TPU v7x, 128 devices: a whole 4x4x4 slice. The times are simulated.
128 devices in a mesh: rep: 16 (over y_lo, z, core), shard: 8 (over x, y_hi).
Axes of the slice: x: 4, y: 4 (y_hi: 2, y_lo: 2; y = y_hi * 2 + y_lo), z: 4, core: 2. Of those that a mesh axis runs over, the one named last changes fastest.
Arguments:
- hidden_in: float32 [16384, 1024], P(('rep', 'shard')), may hold values from -6 to 6
- doc_start: int32 [16384], P(('rep', 'shard')), may hold values from 0 to 127, as said below
- grad_out: float32 [16384, 1024], P(('rep', 'shard')), may hold values from -6 to 6
- w_qkv: bfloat16 [2, 1024, 3072], P(None, 'shard'), may hold values from -0.1875 to 0.1875
- w_proj: bfloat16 [2, 1024, 1024], P(None, 'shard'), may hold values from -0.375 to 0.375
- w_up: bfloat16 [2, 1024, 4096], P(None, 'shard'), may hold values from -0.1875 to 0.1875
- w_down: bfloat16 [2, 4096, 1024], P(None, 'shard'), may hold values from -0.09375 to 0.09375
- norm_gain: bfloat16 [2, 1024, 2], P(None, 'shard'), may hold values from 0.5 to 1.5
- d_bias: bfloat16 [2, 1024, 6], P(None, 'shard'), may hold values from -3 to 3
- up_bias: bfloat16 [2, 4096], P(None, 'shard'), may hold values from -3 to 3
Outputs:
- hidden_out: float32 [16384, 1024], P(('rep', 'shard'))
- grad_in: float32 [16384, 1024], P(('rep', 'shard'))
- grad_qkv: float32 [2, 1024, 3072], P(None, 'shard')
- grad_proj: float32 [2, 1024, 1024], P(None, 'shard')
- grad_up: float32 [2, 1024, 4096], P(None, 'shard')
- grad_down: float32 [2, 4096, 1024], P(None, 'shard')
- grad_gain: float32 [2, 1024, 2], P(None, 'shard')
- grad_dbias: float32 [2, 1024, 6], P(None, 'shard')
- grad_upbias: float32 [2, 4096], P(None, 'shard')
Inputs may be any that keep to these rules, and one draw needn't show every extreme that they name: `doc_start`: each aligned run of 128 slots holds whole documents in order: the value does not fall along a run, is 0 at the run's first slot, and equals the slot's own offset at a document's first token.
All inputs are finite; a program needn't handle non-finite values.
Results may differ from a plain program's by a relative error of at most 0.025.
Values may be sent and summed in bfloat16 or wider, within the bound.
No kernel may reach another device: no remote copies, remote signals or barrier semaphores. Data moves between devices by JAX's collectives and lax.ppermute only.
A program may use at most 256 MiB of HBM per device.

v0:
```python
import jax
import jax.numpy as jnp
from jax import lax
from jax.sharding import PartitionSpec as P

HEADS = 16
HEAD_DIM = 64
LAYERS = 2


epsilon = 1e-05
gelu_coef = 0.7978845608


def in_one_piece(arrays, axis, dim, along):
    both = jnp.concatenate(arrays, axis=along)
    result, at, done = (lax.all_gather(both, axis, axis=dim, tiled=True), 0, [])
    for a in arrays:
        done.append(lax.slice_in_dim(result, at, at + a.shape[along], axis=along))
        at += a.shape[along]
    return tuple(done)


def split_up(shard, dim, length):
    shape = shard.shape
    tiles = shard.reshape(*shape[:dim], length, shape[dim] // length, *shape[dim + 1 :])
    return jnp.moveaxis(tiles, dim, 0)


def sent_and_summed(shard, axis, dim):
    length = lax.axis_size(axis)
    tiles = lax.all_to_all(split_up(shard, dim, length), axis, 0, 0, tiled=True)
    return jnp.sum(tiles.astype(jnp.float32), axis=0)


def sent_together(arrays, axis, dim, along):
    both = jnp.concatenate(arrays, axis=along)
    result, at, done = (sent_and_summed(both, axis, dim), 0, [])
    for a in arrays:
        done.append(lax.slice_in_dim(result, at, at + a.shape[along], axis=along))
        at += a.shape[along]
    return tuple(done)


def batch_prod(form, left, right):
    return jnp.einsum(form, left, right, preferred_element_type=jnp.float32)


def layer_norm(stream, gains, shifts):
    average = jnp.mean(stream, axis=-1, keepdims=True)
    centered = stream - average
    variance = jnp.mean(centered * centered, axis=-1, keepdims=True)
    inv_std = lax.rsqrt(variance + epsilon)
    normed = centered * inv_std
    return (normed * gains + shifts, normed, inv_std)


def norm_back(grad_norm, normed, inv_std, gains):
    scaled = grad_norm * gains
    inner = (
        scaled
        - jnp.mean(scaled, axis=-1, keepdims=True)
        - normed * jnp.mean(scaled * normed, axis=-1, keepdims=True)
    )
    return (inv_std * inner, jnp.sum(grad_norm * normed, axis=0), jnp.sum(grad_norm, axis=0))


def gelu_tanh(values):
    inner = jnp.tanh(gelu_coef * (values + 0.044715 * values * values * values))
    return 0.5 * values * (1.0 + inner)


def gelu_slope(values):
    inner = jnp.tanh(gelu_coef * (values + 0.044715 * values * values * values))
    return 0.5 * (1.0 + inner) + 0.5 * values * (1.0 - inner * inner) * gelu_coef * (
        1.0 + 3.0 * 0.044715 * values * values
    )


def scores_of(query, keys_bf, starts):
    count = query.shape[0]
    query_heads = query.reshape(count, HEADS, HEAD_DIM)
    key_heads = keys_bf.reshape(count, HEADS, HEAD_DIM)
    scores = batch_prod("qhd,khd->hqk", query_heads, key_heads) * HEAD_DIM ** (-0.5)
    offsets = jnp.arange(count, dtype=jnp.int32)
    distance = (offsets[:, None] - offsets[None, :]).astype(jnp.float32)
    head_ids = jnp.arange(HEADS, dtype=jnp.int32).astype(jnp.float32)
    slopes = 2.0 ** (-8.0 * (head_ids + 1.0) / HEADS)
    scores = scores - slopes[:, None, None] * distance[None, :, :]
    visible = (starts[:, None] == starts[None, :]) & (offsets[None, :] <= offsets[:, None])
    return jnp.where(visible[None, :, :], scores, jnp.float32(-1000000000.0))


def layer_forward(stream, starts, wqkv, wproj, wupper, wlower, gains, biases, ubias):
    count, width = stream.shape
    gains = gains.astype(jnp.float32)
    biases = biases.astype(jnp.float32)
    first_f, normed_one, inv_one = layer_norm(stream, gains[:, 0], biases[:, 0])
    first_in = first_f.astype(jnp.bfloat16)
    merged = jnp.dot(first_in, wqkv, preferred_element_type=jnp.float32)
    query = (merged[:, :width] + biases[:, 2]).astype(jnp.bfloat16)
    keys_bf = merged[:, width : 2 * width].astype(jnp.bfloat16)
    values_bf = (merged[:, 2 * width :] + biases[:, 3]).astype(jnp.bfloat16)
    scores = scores_of(query, keys_bf, starts)
    top_score = jnp.max(scores, axis=-1, keepdims=True)
    log_total = top_score + jnp.log(jnp.sum(jnp.exp(scores - top_score), axis=-1, keepdims=True))
    weights_bf = jnp.exp(scores - log_total).astype(jnp.bfloat16)
    context = batch_prod("hqk,khd->qhd", weights_bf, values_bf.reshape(count, HEADS, HEAD_DIM))
    context = context.reshape(count, width).astype(jnp.bfloat16)
    middle = stream + jnp.dot(context, wproj, preferred_element_type=jnp.float32) + biases[:, 4]
    second_f, normed_two, inv_two = layer_norm(middle, gains[:, 1], biases[:, 1])
    second_in = second_f.astype(jnp.bfloat16)
    upper = jnp.dot(second_in, wupper, preferred_element_type=jnp.float32) + ubias.astype(
        jnp.float32
    )
    activ = gelu_tanh(upper).astype(jnp.bfloat16)
    result = middle + jnp.dot(activ, wlower, preferred_element_type=jnp.float32) + biases[:, 5]
    kept = (
        first_in,
        normed_one,
        inv_one,
        query,
        keys_bf,
        values_bf,
        log_total,
        context,
        second_in,
        normed_two,
        inv_two,
        upper,
        activ,
    )
    return (result, kept)


def layer_backward(
    grad_y, starts, kept, wqkv, wproj, wupper, wlower, gains, biases, ubias, full_terms
):
    (
        first_in,
        normed_one,
        inv_one,
        query,
        keys_bf,
        values_bf,
        log_total,
        context,
        second_in,
        normed_two,
        inv_two,
        upper,
        activ,
    ) = kept
    count, width = grad_y.shape
    gains = gains.astype(jnp.float32)
    grad_yb = grad_y.astype(jnp.bfloat16)
    g_bdown = jnp.sum(grad_y, axis=0)
    grad_act = jnp.dot(grad_yb, wlower.T, preferred_element_type=jnp.float32)
    grad_upper = grad_act * gelu_slope(upper)
    g_ubias = jnp.sum(grad_upper, axis=0)
    grad_ub = grad_upper.astype(jnp.bfloat16)
    grad_two = jnp.dot(grad_ub, wupper.T, preferred_element_type=jnp.float32)
    back_two, g_gain_two, g_shift_two = norm_back(grad_two, normed_two, inv_two, gains[:, 1])
    grad_mid = grad_y + back_two
    grad_midb = grad_mid.astype(jnp.bfloat16)
    g_bproj = jnp.sum(grad_mid, axis=0)
    grad_ctx = jnp.dot(grad_midb, wproj.T, preferred_element_type=jnp.float32).astype(jnp.bfloat16)
    scores = scores_of(query, keys_bf, starts)
    probs = jnp.exp(scores - log_total)
    probs_bf = probs.astype(jnp.bfloat16)
    ctx_heads = grad_ctx.reshape(count, HEADS, HEAD_DIM)
    grad_val = batch_prod("hqk,qhd->khd", probs_bf, ctx_heads)
    grad_prob = batch_prod("qhd,khd->hqk", ctx_heads, values_bf.reshape(count, HEADS, HEAD_DIM))
    delta = jnp.sum(
        ctx_heads.astype(jnp.float32) * context.reshape(count, HEADS, HEAD_DIM).astype(jnp.float32),
        axis=-1,
    )
    grad_score = (probs * (grad_prob - jnp.transpose(delta)[:, :, None])).astype(jnp.bfloat16)
    grad_query = batch_prod(
        "hqk,khd->qhd", grad_score, keys_bf.reshape(count, HEADS, HEAD_DIM)
    ) * HEAD_DIM ** (-0.5)
    grad_key = batch_prod(
        "hqk,qhd->khd", grad_score, query.reshape(count, HEADS, HEAD_DIM)
    ) * HEAD_DIM ** (-0.5)
    grad_query = grad_query.reshape(count, width)
    grad_key = grad_key.reshape(count, width)
    grad_val = grad_val.reshape(count, width)
    g_bquery = jnp.sum(grad_query, axis=0)
    g_bvalue = jnp.sum(grad_val, axis=0)
    grad_merged = jnp.concatenate([grad_query, grad_key, grad_val], axis=1).astype(jnp.bfloat16)
    grad_one = jnp.dot(grad_merged, wqkv.T, preferred_element_type=jnp.float32)
    back_one, g_gain_one, g_shift_one = norm_back(grad_one, normed_one, inv_one, gains[:, 0])
    grad_x = grad_mid + back_one
    g_gain = jnp.stack([g_gain_one, g_gain_two], axis=1)
    g_bias = jnp.stack([g_shift_one, g_shift_two, g_bquery, g_bvalue, g_bproj, g_bdown], axis=1)
    g_down, g_up, g_proj, g_qkv = (None, None, None, None)
    operands = (grad_yb, grad_ub, grad_midb, grad_merged)
    return (grad_x, (g_qkv, g_proj, g_up, g_down, g_gain, g_bias, g_ubias), operands)


def local(hidden_in, doc_start, grad_out, w_qkv, w_proj, w_up, w_down, norm_gain, d_bias, up_bias):
    saved = []
    current = hidden_in
    for layer_no in range(LAYERS):
        whole = (
            *in_one_piece((w_qkv[layer_no], w_proj[layer_no], w_up[layer_no]), "shard", 0, 1),
            lax.all_gather(w_down[layer_no], "shard", axis=0, tiled=True),
            *in_one_piece((norm_gain[layer_no], d_bias[layer_no]), "shard", 0, 1),
            lax.all_gather(up_bias[layer_no], "shard", axis=0, tiled=True),
        )
        current, kept = layer_forward(current, doc_start, *whole)
        saved.append(kept)
    running = grad_out
    owned = [None] * LAYERS
    for layer_no in reversed(range(LAYERS)):
        whole = (
            *in_one_piece((w_qkv[layer_no], w_proj[layer_no], w_up[layer_no]), "shard", 0, 1),
            lax.all_gather(w_down[layer_no], "shard", axis=0, tiled=True),
            *in_one_piece((norm_gain[layer_no], d_bias[layer_no]), "shard", 0, 1),
            lax.all_gather(up_bias[layer_no], "shard", axis=0, tiled=True),
        )
        kept = saved[layer_no]
        running, terms, operands = layer_backward(running, doc_start, kept, *whole, False)
        joined = in_one_piece((operands[0], operands[1], operands[2], operands[3]), "shard", 0, 1)
        pieces = (
            lax.all_to_all(kept[0], "shard", split_axis=1, concat_axis=0, tiled=True),
            lax.all_to_all(kept[7], "shard", split_axis=1, concat_axis=0, tiled=True),
            lax.all_to_all(kept[8], "shard", split_axis=1, concat_axis=0, tiled=True),
            lax.all_to_all(kept[12], "shard", split_axis=1, concat_axis=0, tiled=True),
        )
        own_qkv = jnp.dot(pieces[0].T, joined[3], preferred_element_type=jnp.float32)
        own_proj = jnp.dot(pieces[1].T, joined[2], preferred_element_type=jnp.float32)
        own_up = jnp.dot(pieces[2].T, joined[1], preferred_element_type=jnp.float32)
        own_down = jnp.dot(pieces[3].T, joined[0], preferred_element_type=jnp.float32)
        small = (
            *sent_together(
                (terms[4].astype(jnp.bfloat16), terms[5].astype(jnp.bfloat16)), "shard", 0, 1
            ),
            sent_and_summed(terms[6].astype(jnp.bfloat16), "shard", 0),
        )
        shares = (own_qkv, own_proj, own_up, own_down, small[0], small[1], small[2])
        shares = (
            lax.psum(shares[0].astype(jnp.bfloat16), "rep").astype(jnp.float32),
            lax.psum(shares[1].astype(jnp.bfloat16), "rep").astype(jnp.float32),
            lax.psum(shares[2].astype(jnp.bfloat16), "rep").astype(jnp.float32),
            lax.psum(shares[3].astype(jnp.bfloat16), "rep").astype(jnp.float32),
            lax.psum(shares[4].astype(jnp.bfloat16), "rep").astype(jnp.float32),
            lax.psum(shares[5].astype(jnp.bfloat16), "rep").astype(jnp.float32),
            lax.psum(shares[6].astype(jnp.bfloat16), "rep").astype(jnp.float32),
        )
        owned[layer_no] = shares
    stacked = [
        jnp.stack([owned[layer_no][slot] for layer_no in range(LAYERS)]) for slot in range(7)
    ]
    return (
        current,
        running,
        stacked[0],
        stacked[1],
        stacked[2],
        stacked[3],
        stacked[4],
        stacked[5],
        stacked[6],
    )


def solution(mesh):
    placed = (
        P(("rep", "shard"), None),
        P(("rep", "shard")),
        P(("rep", "shard"), None),
        P(None, "shard", None),
        P(None, "shard", None),
        P(None, "shard", None),
        P(None, "shard", None),
        P(None, "shard", None),
        P(None, "shard", None),
        P(None, "shard"),
    )
    return jax.shard_map(
        local,
        mesh=mesh,
        in_specs=placed,
        out_specs=(
            P(("rep", "shard"), None),
            P(("rep", "shard"), None),
            P(None, "shard", None),
            P(None, "shard", None),
            P(None, "shard", None),
            P(None, "shard", None),
            P(None, "shard", None),
            P(None, "shard", None),
            P(None, "shard"),
        ),
        check_vma=False,
    )
```

profile of v0, /device:TPU:1, one launch (start us, length us, event | category | flops | bytes accessed | tf_op | source)
XLA Modules:
  0.0 1300.9 jit_solution(16757099356191935756)
XLA Ops:
  17.2 26.8 %all-gather = bf16[1,4096]{1,0:T(2,128)(2,1)S(1)} all-gather(bf16[1,512]{1,0:T(2,128)(2,1)S(1)} %get-tuple-element.107), channel_id=2, replica_groups=mesh['rep'=16,'shard'=8] {'shard'}, dimensions={1}, use_global_device_ids=true | all-gather | bytes 9216 | tf_op jit(solution)/shard_map/all_gather | solution.py:209
  44.1 26.4 %all-gather.2 = bf16[1,4096]{1,0:T(2,128)(2,1)S(1)} all-gather(bf16[1,512]{1,0:T(2,128)(2,1)S(1)} %get-tuple-element.106), channel_id=4, replica_groups=mesh['rep'=16,'shard'=8] {'shard'}, dimensions={1}, use_global_device_ids=true | all-gather | bytes 9216 | tf_op jit(solution)/shard_map/all_gather | solution.py:209
  70.7 26.3 %all_gather.36 = bf16[1024,8]{0,1:T(8,128)(2,1)S(1)} all-gather(bf16[128,8]{0,1:T(8,128)(2,1)S(1)} %pad_maximum_fusion.2), channel_id=1, replica_groups=mesh['rep'=16,'shard'=8] {'shard'}, dimensions={0}, use_global_device_ids=true | all-gather | bytes 18432 | tf_op jit(solution)/shard_map/all_gather | solution.py:17
  97.0 26.2 %all_gather.40 = bf16[1024,8]{0,1:T(8,128)(2,1)S(1)} all-gather(bf16[128,8]{0,1:T(8,128)(2,1)S(1)} %pad_maximum_fusion.3), channel_id=1, replica_groups=mesh['rep'=16,'shard'=8] {'shard'}, dimensions={0}, use_global_device_ids=true | all-gather | bytes 18432 | tf_op jit(solution)/shard_map/all_gather | solution.py:17
  124.4 77.1 %all-gather.11.cloned.1.call-done = bf16[1024,8192]{1,0:T(8,128)(2,1)} async-done(((bf16[128,8192]{1,0:T(8,128)(2,1)}), bf16[1024,8192]{1,0:T(8,128)(2,1)}) %all-gather.11.cloned.1.call-update) | async-done | bytes 16777232 | tf_op jit(solution)/shard_map/all_gather | solution.py:17
  201.5 3.8 fusion.30
  209.4 7.5 multiply_convert_fusion.1
  216.9 93.8 %all-gather.19.cloned.1.call-done = bf16[1,4096,1024]{2,1,0:T(8,128)(2,1)} async-done(((bf16[1,512,1024]{2,1,0:T(8,128)(2,1)}), bf16[1,4096,1024]{2,1,0:T(8,128)(2,1)}) %all-gather.19.cloned.1.call-update) | async-done | bytes 8388624 | tf_op jit(solution)/shard_map/all_gather | solution.py:207
  310.6 5.1 fusion.207
  315.9 181.5 %all-gather.13.cloned.1.call-done = bf16[1024,8192]{1,0:T(8,128)(2,1)} async-done(((bf16[128,8192]{1,0:T(8,128)(2,1)}), bf16[1024,8192]{1,0:T(8,128)(2,1)}) %all-gather.13.cloned.1.call-update) | async-done | bytes 16777232 | tf_op jit(solution)/shard_map/all_gather | solution.py:17
  497.4 3.8 fusion.26
  507.1 7.9 multiply_convert_fusion
  515.0 91.5 %all-gather.21.cloned.1.call-done = bf16[1,4096,1024]{2,1,0:T(8,128)(2,1)} async-done(((bf16[1,512,1024]{2,1,0:T(8,128)(2,1)}), bf16[1,4096,1024]{2,1,0:T(8,128)(2,1)}) %all-gather.21.cloned.1.call-update) | async-done | bytes 8388624 | tf_op jit(solution)/shard_map/all_gather | solution.py:207
  606.4 8.9 convert_dynamic-update-slice_fusion.1
  615.3 7.0 fusion.12
  633.5 5.2 fusion.24
  640.6 3.5 convert_dynamic-update-slice_fusion
  644.1 8.0 fusion.16
  670.8 3.4 all-to-all-start.4
  675.0 6.5 all-to-all-done.4
  681.5 4.0 all-to-all-start.5
  685.6 5.0 fusion.28
  694.3 4.8 all-to-all-start
  703.7 4.2 all-to-all-done
  707.9 4.3 all-to-all-start.6
  712.2 173.1 %all-gather.15.cloned.1.call-done = bf16[1024,9216]{1,0:T(8,128)(2,1)} async-done(((bf16[128,9216]{1,0:T(8,128)(2,1)}), bf16[1024,9216]{1,0:T(8,128)(2,1)}) %all-gather.15.cloned.1.call-update) | async-done | bytes 18874384 | tf_op jit(solution)/shard_map/all_gather | solution.py:17
  885.3 4.8 fusion.65
  890.2 5.6 fusion.53
  895.8 3.8 all-to-all-start.7
  899.6 4.7 fusion.103
  904.3 198.0 %all-gather.17.cloned.1.call-done = bf16[1024,9216]{1,0:T(8,128)(2,1)} async-done(((bf16[128,9216]{1,0:T(8,128)(2,1)}), bf16[1024,9216]{1,0:T(8,128)(2,1)}) %all-gather.17.cloned.1.call-update) | async-done | bytes 18874384 | tf_op jit(solution)/shard_map/all_gather | solution.py:17
  1102.3 5.7 fusion.50
  1109.0 3.4 all-to-all-start.2
  1112.4 4.1 fusion.100
  1119.7 3.4 all-to-all-start.3
  1125.9 4.6 all-to-all-done.3
  1130.5 3.4 all-to-all-start.1
  1136.7 4.4 all-to-all-done.1
  1141.1 4.7 fusion.62
  1153.2 5.5 fusion.135
  1161.8 6.5 all-to-all-start.11
  1169.0 5.9 all-to-all-done.11
  1178.8 5.9 all-to-all-done.8
  1184.7 3.3 all-to-all-start.9
  1189.2 5.3 all-to-all-done.9
  1194.6 36.0 %all-reduce = (bf16[1,128,2]{1,2,0:T(2,128)(2,1)S(1)}, bf16[1,128,2]{1,2,0:T(2,128)(2,1)S(1)}, bf16[1,128,6]{1,2,0:T(8,128)(2,1)S(1)}, bf16[1,128,6]{1,2,0:T(8,1...) all-reduce(bf16[1,128,2]{1,2,0:T(2,128)(2,1)S(1)} %slice_bitcast_fu, ...), channel_id=1, replica_groups=mesh['rep'=16,'shard'=8] {'rep'}, use_global_device_ids=true, to_apply=%region_49.50 | all-reduce | flops 3072 | bytes 12288 | tf_op jit(solution)/shard_map/psum | solution.py:247
  1232.4 51.5 %all-reduce.4.cloned.1.call-done = (bf16[1,128,3072]{2,1,0:T(8,128)(2,1)}, bf16[1,128,3072]{2,1,0:T(8,128)(2,1)}, bf16[1,128,1024]{2,1,0:T(8,128)(2,1)}, bf16[1,...) async-done(((bf16[1,128,3072]{2,1,0:T(8,128)(2,1)}, ...) | async-done | bytes 6291472 | tf_op jit(solution)/shard_map/psum | solution.py:243
  1283.9 4.0 maximum_convert_fusion.1
  (344 shorter events, 94.9 us)
Async XLA Ops:
  7.2 194.3 %all-gather.11.cloned.1.call-start = ((), (), s32[]{:S(2)}) async-start(), calls=%async_computation.12 | async-start | bytes 18874368 | tf_op jit(solution)/shard_map/all_gather | solution.py:17
  11.8 298.8 %all-gather.19.cloned.1.call-start = ((), (), s32[]{:S(2)}) async-start(), calls=%async_computation.16 | async-start | bytes 9437184 | tf_op jit(solution)/shard_map/all_gather | solution.py:207
  15.0 482.4 %all-gather.13.cloned.1.call-start = ((), (), s32[]{:S(2)}) async-start(), calls=%async_computation.13 | async-start | bytes 18874368 | tf_op jit(solution)/shard_map/all_gather | solution.py:17
  16.5 54.0 %copy-start = (f32[128,1024]{1,0:T(8,128)S(1)}, f32[128,1024]{1,0:T(8,128)}, u32[]{:S(2)}) copy-start(f32[128,1024]{1,0:T(8,128)} %param.10) | copy-start | bytes 1572868
  16.5 54.1 %copy-start.74 = (bf16[2,128,2]{1,2,0:T(2,128)(2,1)S(1)}, bf16[2,128,2]{1,2,0:T(2,128)(2,1)}, u32[]{:S(2)}) copy-start(bf16[2,128,2]{1,2,0:T(2,128)(2,1)} %param.17) | copy-start | bytes 3076
  16.5 107.0 %copy-start.69 = (s32[128]{0:T(128)S(1)}, s32[128]{0:T(128)}, u32[]{:S(2)}) copy-start(s32[128]{0:T(128)} %param.11) | copy-start | bytes 1540
  16.5 107.2 %copy-start.21 = (f32[128,1024]{1,0:T(8,128)S(1)}, f32[128,1024]{1,0:T(8,128)}, u32[]{:S(2)}) copy-start(f32[128,1024]{1,0:T(8,128)} %param.12) | copy-start | bytes 1572868
  16.5 589.9 %all-gather.21.cloned.1.call-start = ((), (), s32[]{:S(2)}) async-start(), calls=%async_computation.17 | async-start | bytes 9437184 | tf_op jit(solution)/shard_map/all_gather | solution.py:207
  17.1 868.2 %all-gather.15.cloned.1.call-start = ((), (), s32[]{:S(2)}) async-start(), calls=%async_computation.14 | async-start | bytes 21233664 | tf_op jit(solution)/shard_map/all_gather | solution.py:17
  123.2 82.9 %copy-start.75 = (f32[16]{0:T(128)}, f32[16]{0:T(128)S(1)}, u32[]{:S(2)}) copy-start(f32[16]{0:T(128)S(1)} %multiply_power_fusion) | copy-start | bytes 196
  123.2 82.2 %copy-start.61 = (f32[128]{0:T(128)}, f32[128]{0:T(128)S(1)}, u32[]{:S(2)}) copy-start(f32[128]{0:T(128)S(1)} %broadcast_multiply_fusion.11) | copy-start | bytes 1540
  123.4 81.9 %copy-start.67 = (f32[128]{0:T(128)}, f32[128]{0:T(128)S(1)}, u32[]{:S(2)}) copy-start(f32[128]{0:T(128)S(1)} %add_rsqrt_fusion.3) | copy-start | bytes 1540
  209.2 101.5 %copy-start.1 = (f32[128,1024]{1,0:T(8,128)}, f32[128,1024]{1,0:T(8,128)S(1)}, u32[]{:S(2)}) copy-start(f32[128,1024]{1,0:T(8,128)S(1)} %get-tuple-element.113) | copy-start | bytes 1572868
  209.2 7.7 copy-start.63
  209.4 7.5 copy-start.70
  315.7 185.6 %copy-start.3 = (f32[128,1024]{1,0:T(8,128)}, f32[128,1024]{1,0:T(8,128)S(1)}, u32[]{:S(2)}) copy-start(f32[128,1024]{1,0:T(8,128)S(1)} %get-tuple-element.117) | copy-start | bytes 1572868
  315.7 185.6 %copy-start.65 = (f32[128]{0:T(128)}, f32[128]{0:T(128)S(1)}, u32[]{:S(2)}) copy-start(f32[128]{0:T(128)S(1)} %broadcast_multiply_fusion.9) | copy-start | bytes 1540
  315.9 185.3 %copy-start.72 = (f32[128]{0:T(128)}, f32[128]{0:T(128)S(1)}, u32[]{:S(2)}) copy-start(f32[128]{0:T(128)S(1)} %add_rsqrt_fusion.1) | copy-start | bytes 1540
  615.3 7.1 copy-start.25
  615.3 8.1 copy-start.22
  633.5 6.6 slice-start
  644.0 8.1 copy-start.26
  644.0 9.1 copy-start.18
  644.0 8.1 copy-start.2
  644.0 8.1 copy-start.64
  644.1 8.1 copy-start.71
  653.4 8.3 copy-start.8
  666.1 436.3 %all-gather.17.cloned.1.call-start = ((), (), s32[]{:S(2)}) async-start(), calls=%async_computation.15 | async-start | bytes 21233664 | tf_op jit(solution)/shard_map/all_gather | solution.py:17
  670.0 15.5 %copy-start.45 = (bf16[128,16,64]{0,2,1:T(8,128)(2,1)S(1)}, bf16[128,16,64]{0,2,1:T(8,128)(2,1)}, u32[]{:S(2)}) copy-start(bf16[128,16,64]{0,2,1:T(8,128)(2,1)} %get-tuple-element.80) | copy-start | bytes 786436
  670.0 15.5 %copy-start.47 = (bf16[16,64,128]{2,1,0:T(8,128)(2,1)S(1)}, bf16[16,64,128]{2,1,0:T(8,128)(2,1)}, u32[]{:S(2)}) copy-start(bf16[16,64,128]{2,1,0:T(8,128)(2,1)} %fusion.139) | copy-start | bytes 786436
  670.0 15.5 %copy-start.48 = (bf16[128,16,64]{0,2,1:T(8,128)(2,1)S(1)}, bf16[128,16,64]{0,2,1:T(8,128)(2,1)}, u32[]{:S(2)}) copy-start(bf16[128,16,64]{0,2,1:T(8,128)(2,1)} %get-tuple-element.78) | copy-start | bytes 786436
  670.8 10.7 all-to-all-start.4
  681.5 12.9 all-to-all-start.5
  691.4 7.7 copy-start.7
  691.4 8.8 copy-start.6
  694.3 13.5 %all-to-all-start = ((bf16[128,8,128]{2,0,1:T(8,128)(2,1)}), bf16[128,8,128]{2,0,1:T(8,128)(2,1)}, u32[]{:S(2)}, u32[]{:S(2)}) async-start(bf16[128,8,128]{2,0,1:T(8,128)(2,1)} %bitcast.263), calls=%async_computation | async-start | bytes 524288 | tf_op jit(solution)/shard_map/all_to_all | solution.py:226
  707.9 187.9 %all-to-all-start.6 = ((bf16[128,8,512]{2,0,1:T(8,128)(2,1)}), bf16[128,8,512]{2,0,1:T(8,128)(2,1)}, u32[]{:S(2)}, u32[]{:S(2)}) async-start(bf16[128,8,512]{2,0,1:T(8,128)(2,1)} %bitcast.235), calls=%async_computation.6 | async-start | bytes 2097152 | tf_op jit(solution)/shard_map/all_to_all | solution.py:229
  895.8 212.2 %all-to-all-start.7 = ((bf16[128,8,512]{2,0,1:T(8,128)(2,1)}), bf16[128,8,512]{2,0,1:T(8,128)(2,1)S(1)}, u32[]{:S(2)}, u32[]{:S(2)}) async-start(bf16[128,8,512]{2,0,1:T(8,128)(2,1)} %bitcast.234), calls=%async_computation.7 | async-start | bytes 2097152 | tf_op jit(solution)/shard_map/all_to_all | solution.py:229
  1109.0 10.7 all-to-all-start.2
  1119.7 10.8 all-to-all-start.3
  1130.5 10.6 all-to-all-start.1
  1133.9 150.0 %all-reduce.4.cloned.1.call-start = ((), (), s32[]{:S(2)}) async-start(), calls=%async_computation.18 | async-start | bytes 12582912 | tf_op jit(solution)/shard_map/psum | solution.py:243
  1149.7 12.1 all-to-all-start.10
  1158.7 29.4 %copy-start.9 = (f32[128,1024]{1,0:T(8,128)S(1)}, f32[128,1024]{1,0:T(8,128)}, u32[]{:S(2)}) copy-start(f32[128,1024]{1,0:T(8,128)} %copy-done.8) | copy-start | bytes 1572868
  1158.7 29.4 %copy-start.24 = (f32[128,1024]{1,0:T(8,128)S(1)}, f32[128,1024]{1,0:T(8,128)}, u32[]{:S(2)}) copy-start(f32[128,1024]{1,0:T(8,128)} %copy-done.23) | copy-start | bytes 1572868
  1161.8 13.1 %all-to-all-start.11 = ((bf16[8,2,256]{2,1,0:T(2,128)(2,1)}), bf16[8,2,256]{2,1,0:T(2,128)(2,1)S(1)}, u32[]{:S(2)}, u32[]{:S(2)}) async-start(bf16[8,2,256]{2,1,0:T(2,128)(2,1)} %reshape.400), calls=%async_computation.11 | async-start | bytes 16384 | tf_op jit(solution)/shard_map/all_to_all | solution.py:32
  1174.9 9.8 all-to-all-start.8
  1184.7 9.8 all-to-all-start.9
  (50 other events, 143.5 us)
Sparse Core Ops, SparseCore 0:
  11.9 189.5 all-gather.10
  203.8 106.7 all-gather.18
  313.5 183.8 all-gather.12
  499.6 106.7 all-gather.20
  666.2 219.1 all-gather.14
  888.1 214.1 all-gather.16
  1146.0 137.8 all-reduce.3
where the time goes:
time: 1310 us; the launch traced here: 1300 us
  waiting for transfers between devices  909 us (69%)
  blocking collectives  142 us (11%)
  matrix products  127 us (10%)
  starting transfers between devices  47.4 us (4%)
  local copies, waits for them, and re-layouts  32.1 us (2%)
  other arithmetic  28.5 us (2%)
  between operations  15.8 us (1%)
    all_gather x4, waiting for transfers between devices, in_one_piece(): result, at, done = (lax.all_gather(both, axis, axis=dim, tiled=True), 0, [])  630 us
    all_gather x2, waiting for transfers between devices, local(): lax.all_gather(w_down[layer_no], 'shard', axis=0, tiled=True)  185 us
    all_gather x2, blocking collectives, local(): lax.all_gather(up_bias[layer_no], 'shard', axis=0, tiled=True)  53.2 us
    all_gather x2, blocking collectives, in_one_piece(): result, at, done = (lax.all_gather(both, axis, axis=dim, tiled=True), 0, [])  52.5 us
    psum x1, waiting for transfers between devices, local(): lax.psum(shares[0].astype(jnp.bfloat16), 'rep').astype(jnp.float32)  51.5 us
    psum x1, blocking collectives, local(): lax.psum(shares[4].astype(jnp.bfloat16), 'rep').astype(jnp.float32)  36 us
  transfers between devices with their start and end apart: 19, of which 16 were waited for; matrix products, arithmetic and copies ran while one was open for 8% of the time, Pallas kernels for 0%

commit v1 on v0

v1 whole, which is shorter than its diff:
```python
import jax
import jax.numpy as jnp
from jax import lax
from jax.experimental import pallas as pl
from jax.experimental.pallas import tpu as pltpu
from jax.sharding import Mesh
from jax.sharding import PartitionSpec as P

HEADS = 16
HEAD_DIM = 64
LAYERS = 2
D = 1024
RUN = 128

epsilon = 1e-05
gelu_coef = 0.7978845608
f32 = jnp.float32
bf16 = jnp.bfloat16

AXES = ("ylo", "z", "core", "x", "yhi")


def ring(step):
    return [(i, (i + step) % 4) for i in range(4)]


def x_up(a):
    return lax.ppermute(a, "x", ring(1))


def x_down(a):
    return lax.ppermute(a, "x", ring(3))


def x_far(a):
    return lax.ppermute(a, "x", ring(2))


def z_up(a):
    return lax.ppermute(a, "z", ring(1))


def z_down(a):
    return lax.ppermute(a, "z", ring(3))


def z_far(a):
    return lax.ppermute(a, "z", ring(2))


def y_pair(a):
    return lax.ppermute(a, ("ylo", "yhi"), [(0, 3), (3, 0), (1, 2), (2, 1)])


def y_copy(a):
    return lax.ppermute(a, "ylo", [(0, 1), (1, 0)])


def swap(a):
    return lax.ppermute(a, "core", [(0, 1), (1, 0)])


def ring_gather(a, up, down):
    half = a.shape[0] // 2
    previous = up(a)
    following = down(a)
    top = up(previous[:half])
    bottom = down(following[half:])
    return a, following, (top, bottom), previous


def ring_scatter(parts, up, down):
    own, following, far, previous = parts
    half = own.shape[0] // 2
    from_previous = up(far[:half])
    from_following = down(far[half:])
    go_up = jnp.concatenate(
        [(following[:half].astype(f32) + from_previous.astype(f32)).astype(bf16), following[half:]]
    )
    go_down = jnp.concatenate(
        [previous[:half], (previous[half:].astype(f32) + from_following.astype(f32)).astype(bf16)]
    )
    got_up = up(go_up)
    got_down = down(go_down)
    return own.astype(f32) + got_up.astype(f32) + got_down.astype(f32)


def rolled(stack, start):
    return lax.dynamic_slice_in_dim(jnp.concatenate([stack, stack[:3]]), start, 4, axis=0)


def ordered_by_core(own, core, axis):
    other = swap(own)
    first = jnp.where(core == 0, own, other)
    second = jnp.where(core == 0, other, own)
    return jnp.stack([first, second], axis=axis)


def take_kernel(order_ref, in_ref, out_ref):
    for block in range(8):
        at = pl.multiple_of(order_ref[block] * 128, 128)
        out_ref[:, block * 128 : (block + 1) * 128] = in_ref[:, pl.ds(at, 128)]


def take_blocks(a, order):
    return pl.pallas_call(
        take_kernel,
        out_shape=jax.ShapeDtypeStruct(a.shape, a.dtype),
        grid_spec=pltpu.PrefetchScalarGridSpec(
            num_scalar_prefetch=1,
            grid=(1,),
            in_specs=[pl.BlockSpec(a.shape, lambda i, order: (0, 0))],
            out_specs=pl.BlockSpec(a.shape, lambda i, order: (0, 0)),
        ),
        compiler_params=pltpu.CompilerParams(vmem_limit_bytes=4 * 1024 * 1024),
        cost_estimate=pl.CostEstimate(flops=0, bytes_accessed=2 * a.size * a.dtype.itemsize, transcendentals=0),
    )(order, a)


def head_scores(q, k, seen, distance, slope):
    s = lax.dot_general(q, k, (((1,), (1,)), ((), ())), preferred_element_type=f32) * HEAD_DIM ** (-0.5)
    s = s - slope * distance
    return jnp.where(seen, s, f32(-1000000000.0))


def visibility(row_start, col_start):
    row = lax.broadcasted_iota(jnp.int32, (RUN, RUN), 0)
    col = lax.broadcasted_iota(jnp.int32, (RUN, RUN), 1)
    seen = (row_start == col_start) & (col <= row)
    return seen, (row - col).astype(f32)


def attend_kernel(slope_ref, rows_ref, cols_ref, qkv_ref, ctx_ref):
    pair = pl.program_id(1)
    seen, distance = visibility(rows_ref[0], cols_ref[0])
    done = []
    for e in range(2):
        q = qkv_ref[:, e * 64 : e * 64 + 64]
        k = qkv_ref[:, 128 + e * 64 : 192 + e * 64]
        v = qkv_ref[:, 256 + e * 64 : 320 + e * 64]
        s = head_scores(q, k, seen, distance, slope_ref[pair * 2 + e])
        top = jnp.max(s, axis=-1, keepdims=True)
        lse = top + jnp.log(jnp.sum(jnp.exp(s - top), axis=-1, keepdims=True))
        p = jnp.exp(s - lse).astype(bf16)
        done.append(jnp.dot(p, v, preferred_element_type=f32))
    ctx_ref[...] = jnp.concatenate(done, axis=1).astype(bf16)


def attend_back_kernel(slope_ref, rows_ref, cols_ref, qkv_ref, ctx_ref, dctx_ref, dqkv_ref, dq_ref, dv_ref):
    pair = pl.program_id(1)
    seen, distance = visibility(rows_ref[0], cols_ref[0])
    dqs, dks, dvs = [], [], []
    tn = (((0,), (0,)), ((), ()))
    nt = (((1,), (1,)), ((), ()))
    for e in range(2):
        lanes = slice(e * 64, e * 64 + 64)
        q = qkv_ref[:, e * 64 : e * 64 + 64]
        k = qkv_ref[:, 128 + e * 64 : 192 + e * 64]
        v = qkv_ref[:, 256 + e * 64 : 320 + e * 64]
        s = head_scores(q, k, seen, distance, slope_ref[pair * 2 + e])
        top = jnp.max(s, axis=-1, keepdims=True)
        lse = top + jnp.log(jnp.sum(jnp.exp(s - top), axis=-1, keepdims=True))
        p = jnp.exp(s - lse)
        dctx = dctx_ref[:, lanes]
        dv = lax.dot_general(p.astype(bf16), dctx, tn, preferred_element_type=f32)
        dp = lax.dot_general(dctx, v, nt, preferred_element_type=f32)
        delta = jnp.sum(dctx.astype(f32) * ctx_ref[:, lanes].astype(f32), axis=-1, keepdims=True)
        ds = (p * (dp - delta)).astype(bf16)
        dqs.append(jnp.dot(ds, k, preferred_element_type=f32) * HEAD_DIM ** (-0.5))
        dks.append(lax.dot_general(ds, q, tn, preferred_element_type=f32) * HEAD_DIM ** (-0.5))
        dvs.append(dv)
    dq = jnp.concatenate(dqs, axis=1)
    dv = jnp.concatenate(dvs, axis=1)
    dqkv_ref[:, 0:128] = dq.astype(bf16)
    dqkv_ref[:, 128:256] = jnp.concatenate(dks, axis=1).astype(bf16)
    dqkv_ref[:, 256:384] = dv.astype(bf16)
    dq_ref[0, 0] = jnp.sum(dq, axis=0, keepdims=True)
    dv_ref[0, 0] = jnp.sum(dv, axis=0, keepdims=True)


def attend(qkv, rows, cols, slopes):
    return pl.pallas_call(
        attend_kernel,
        out_shape=jax.ShapeDtypeStruct((2 * RUN, 512), bf16),
        grid=(2, 4),
        in_specs=[
            pl.BlockSpec(memory_space=pltpu.SMEM),
            pl.BlockSpec((1, RUN, 1), lambda r, p: (r, 0, 0)),
            pl.BlockSpec((1, 1, RUN), lambda r, p: (r, 0, 0)),
            pl.BlockSpec((RUN, 384), lambda r, p: (r, p)),
        ],
        out_specs=pl.BlockSpec((RUN, 128), lambda r, p: (r, p)),
        compiler_params=pltpu.CompilerParams(vmem_limit_bytes=8 * 1024 * 1024),
        cost_estimate=pl.CostEstimate(flops=4 * 16 * RUN * RUN * 64, bytes_accessed=1 << 20, transcendentals=32 * RUN * RUN),
    )(slopes, rows, cols, qkv)


def attend_back(qkv, ctx, dctx, rows, cols, slopes):
    row_block = pl.BlockSpec((RUN, 128), lambda r, p: (r, p))
    sums = pl.BlockSpec((1, 1, 1, 128), lambda r, p: (r, p, 0, 0))
    return pl.pallas_call(
        attend_back_kernel,
        out_shape=(
            jax.ShapeDtypeStruct((2 * RUN, 1536), bf16),
            jax.ShapeDtypeStruct((2, 4, 1, 128), f32),
            jax.ShapeDtypeStruct((2, 4, 1, 128), f32),
        ),
        grid=(2, 4),
        in_specs=[
            pl.BlockSpec(memory_space=pltpu.SMEM),
            pl.BlockSpec((1, RUN, 1), lambda r, p: (r, 0, 0)),
            pl.BlockSpec((1, 1, RUN), lambda r, p: (r, 0, 0)),
            pl.BlockSpec((RUN, 384), lambda r, p: (r, p)),
            row_block,
            row_block,
        ],
        out_specs=(pl.BlockSpec((RUN, 384), lambda r, p: (r, p)), sums, sums),
        compiler_params=pltpu.CompilerParams(vmem_limit_bytes=8 * 1024 * 1024),
        cost_estimate=pl.CostEstimate(flops=10 * 16 * RUN * RUN * 64, bytes_accessed=1 << 21, transcendentals=32 * RUN * RUN),
    )(slopes, rows, cols, qkv, ctx, dctx)


def layer_norm(stream, gains, shifts):
    average = jnp.mean(stream, axis=-1, keepdims=True)
    centered = stream - average
    variance = jnp.mean(centered * centered, axis=-1, keepdims=True)
    inv_std = lax.rsqrt(variance + epsilon)
    normed = centered * inv_std
    return (normed * gains + shifts, normed, inv_std)


def norm_back(grad_norm, normed, inv_std, gains):
    scaled = grad_norm * gains
    inner = (
        scaled
        - jnp.mean(scaled, axis=-1, keepdims=True)
        - normed * jnp.mean(scaled * normed, axis=-1, keepdims=True)
    )
    return (inv_std * inner, jnp.sum(grad_norm * normed, axis=0), jnp.sum(grad_norm, axis=0))


def gelu_tanh(values):
    inner = jnp.tanh(gelu_coef * (values + 0.044715 * values * values * values))
    return 0.5 * values * (1.0 + inner)


def gelu_slope(values):
    inner = jnp.tanh(gelu_coef * (values + 0.044715 * values * values * values))
    return 0.5 * (1.0 + inner) + 0.5 * values * (1.0 - inner * inner) * gelu_coef * (
        1.0 + 3.0 * 0.044715 * values * values
    )


def dot(a, b):
    return jnp.dot(a, b, preferred_element_type=f32)


def dot_nt(a, b):
    return lax.dot_general(a, b, (((1,), (1,)), ((), ())), preferred_element_type=f32)


def dot_tn(a, b):
    return lax.dot_general(a, b, (((0,), (0,)), ((), ())), preferred_element_type=f32)


def local(hidden_in, doc_start, grad_out, w_qkv, w_proj, w_up, w_down, norm_gain, d_bias, up_bias):
    x, z, core, yhi = (lax.axis_index(n) for n in ("x", "z", "core", "yhi"))
    index = jnp.arange(8, dtype=jnp.int32)
    to_rel = ((x + index // 2) % 4) * 2 + (yhi ^ (index % 2))
    to_abs = ((index // 2 - x) % 4) * 2 + ((index % 2) ^ yhi)

    def both(own):
        return jnp.concatenate([own, swap(own)], axis=0)

    def halves_summed(partial):
        return partial[:RUN] + swap(partial[RUN:])

    small = jnp.concatenate(
        [
            jnp.transpose(jnp.concatenate([norm_gain, d_bias], axis=2), (0, 2, 1)).reshape(16, 128),
            up_bias.reshape(8, 128),
        ]
    )
    small = jnp.stack([small, y_pair(small)])
    small = jnp.where(yhi == 0, small, small[::-1])
    small = rolled(jnp.stack([small, x_down(small), x_far(small), x_up(small)]), (4 - x) % 4).astype(f32)
    wide = jnp.transpose(small[:, :, :16], (2, 0, 1, 3)).reshape(LAYERS, 8, D)
    hidden_bias = small[:, :, 16:].reshape(4, 2, LAYERS, 2, 256)

    def core_heads(vector):
        picked = lax.dynamic_index_in_dim(vector.reshape(4, 2, 2, 64), core, axis=2, keepdims=False)
        return rolled(picked.reshape(4, 128), z)

    def gather_layer(layer):
        qkv = w_qkv[layer].reshape(128, 3, 4, 2, 2, 64)
        qkv = lax.dynamic_index_in_dim(qkv, z, axis=2, keepdims=False)
        qkv = lax.dynamic_index_in_dim(qkv, core, axis=3, keepdims=False).reshape(128, 384)
        up = w_up[layer].reshape(128, 4, 2, 2, 256)
        up = lax.dynamic_index_in_dim(up, z, axis=1, keepdims=False)
        up = lax.dynamic_index_in_dim(up, core, axis=2, keepdims=False).reshape(128, 512)
        proj = lax.dynamic_index_in_dim(w_proj[layer].reshape(2, 64, D), core, axis=0, keepdims=False)
        down = lax.dynamic_index_in_dim(w_down[layer].reshape(2, 256, D), core, axis=0, keepdims=False)

        def by_z(piece):
            piece = jnp.concatenate([piece, y_pair(piece)])
            own, following, (top, bottom), previous = ring_gather(piece, x_up, x_down)
            piece = jnp.concatenate([own, following, top, bottom, previous])
            own, following, (top, bottom), previous = ring_gather(piece, z_up, z_down)
            return own, following, jnp.concatenate([top, bottom]), previous

        def by_x(piece):
            other = y_pair(piece)
            first = jnp.where(yhi == 0, piece, other)
            second = jnp.where(yhi == 0, other, piece)
            piece = jnp.concatenate([first, second])
            own, following, (top, bottom), previous = ring_gather(piece, x_up, x_down)
            stack = jnp.stack([own, following, jnp.concatenate([top, bottom]), previous])
            return rolled(stack, (z - x) % 4).reshape(4 * piece.shape[0], D)

        qkv = jnp.concatenate(by_z(qkv), axis=1)
        proj = by_x(proj)
        up = jnp.concatenate(by_z(up), axis=1)
        down = by_x(down)
        return qkv, proj, up, down

    weights = [gather_layer(layer) for layer in range(LAYERS)]

    starts = both(doc_start.reshape(1, RUN))
    rows, cols = starts.reshape(2, RUN, 1), starts.reshape(2, 1, RUN)
    head = 4 * ((z + index // 2) % 4) + 2 * (index % 2) + core
    slopes = 2.0 ** (-8.0 * (head.astype(f32) + 1.0) / HEADS)

    kept = []
    current = hidden_in
    for layer in range(LAYERS):
        wqkv, wproj, wup, wdown = weights[layer]
        gain_one, gain_two, shift_one, shift_two, bq, bv, bproj, bdown = (wide[layer, i] for i in range(8))
        bq, bv = core_heads(bq), core_heads(bv)
        bqkv = jnp.stack([bq, jnp.zeros_like(bq), bv], axis=1).reshape(1536)
        ubias = lax.dynamic_index_in_dim(hidden_bias[:, :, layer], core, axis=2, keepdims=False)
        ubias = rolled(ubias.reshape(4, 512), z).reshape(2048)
        first_f, normed_one, inv_one = layer_norm(current, gain_one, shift_one)
        first_in = both(take_blocks(first_f.astype(bf16), to_rel))
        qkv = (dot(first_in, wqkv) + bqkv).astype(bf16)
        ctx = attend(qkv, rows, cols, slopes)
        middle = current + halves_summed(dot(ctx, wproj)) + bproj
        second_f, normed_two, inv_two = layer_norm(middle, gain_two, shift_two)
        second_in = both(take_blocks(second_f.astype(bf16), to_rel))
        upper = dot(second_in, wup) + ubias
        activ = gelu_tanh(upper).astype(bf16)
        current = middle + halves_summed(dot(activ, wdown)) + bdown
        kept.append((first_in, normed_one, inv_one, qkv, ctx, second_in, normed_two, inv_two, upper, activ, gain_one, gain_two))
    hidden_out = current

    def blocks_by_z(left, right, width):
        parts = [dot_tn(left, right[:, i * width : (i + 1) * width]).astype(bf16) for i in range(4)]
        part = ring_scatter(parts, z_up, z_down).astype(bf16)
        part = ring_scatter([part[i * 256 : (i + 1) * 256] for i in range(4)], x_up, x_down).astype(bf16)
        part = part[:128].astype(f32) + y_pair(part[128:]).astype(f32)
        return part.astype(bf16)

    def blocks_by_x(left, right, width):
        parts = []
        for i in range(4):
            at = ((x + i - z) % 4) * width
            parts.append(dot_tn(lax.dynamic_slice_in_dim(left, at, width, axis=1), right).astype(bf16))
        part = ring_scatter(parts, x_up, x_down).astype(bf16).reshape(2, width // 2, D)
        keep = lax.dynamic_index_in_dim(part, yhi, axis=0, keepdims=False)
        give = lax.dynamic_index_in_dim(part, 1 - yhi, axis=0, keepdims=False)
        part = (keep.astype(f32) + y_pair(give).astype(f32)).astype(bf16).reshape(4, width // 8, D)
        parts = rolled(part, z)
        return ring_scatter([parts[i] for i in range(4)], z_up, z_down).astype(bf16)

    def shared(part):
        part = (part.astype(f32) + y_copy(part).astype(f32)).astype(bf16)
        own, following, (top, bottom), previous = ring_gather(part, z_up, z_down)
        stack = rolled(jnp.stack([own, following, jnp.concatenate([top, bottom]), previous]), (4 - z) % 4)
        return ordered_by_core(stack, core, 0)

    grads = [None] * LAYERS
    small_grads = [None] * LAYERS
    running = grad_out
    for layer in reversed(range(LAYERS)):
        wqkv, wproj, wup, wdown = weights[layer]
        first_in, normed_one, inv_one, qkv, ctx, second_in, normed_two, inv_two, upper, activ, gain_one, gain_two = kept[layer]
        g_bdown = jnp.sum(running, axis=0)
        grad_yb = both(running.astype(bf16))
        grad_upper = dot_nt(grad_yb, wdown) * gelu_slope(upper)
        g_ubias = jnp.sum(grad_upper, axis=0)
        grad_ub = grad_upper.astype(bf16)
        p_down = blocks_by_x(activ, grad_yb, 512)
        p_up = blocks_by_z(second_in, grad_ub, 512)
        grad_two = take_blocks(halves_summed(dot_nt(grad_ub, wup)), to_abs)
        back_two, g_gain_two, g_shift_two = norm_back(grad_two, normed_two, inv_two, gain_two)
        grad_mid = running + back_two
        g_bproj = jnp.sum(grad_mid, axis=0)
        grad_midb = both(grad_mid.astype(bf16))
        grad_ctx = dot_nt(grad_midb, wproj).astype(bf16)
        p_proj = blocks_by_x(ctx, grad_midb, 128)
        grad_qkv, g_bq, g_bv = attend_back(qkv, ctx, grad_ctx, rows, cols, slopes)
        p_qkv = blocks_by_z(first_in, grad_qkv, 384)
        grad_one = take_blocks(halves_summed(dot_nt(grad_qkv, wqkv)), to_abs)
        back_one, g_gain_one, g_shift_one = norm_back(grad_one, normed_one, inv_one, gain_one)
        running = grad_mid + back_one

        def spread_heads(sums):
            sums = rolled(jnp.sum(sums, axis=0).reshape(4, 128), (4 - z) % 4).reshape(4, 2, 1, 64)
            mine = lax.broadcasted_iota(jnp.int32, (4, 2, 2, 64), 2) == core
            return jnp.where(mine, sums, 0.0).reshape(D)

        hidden = rolled(g_ubias.reshape(4, 512), (4 - z) % 4).reshape(4, 2, 1, 256)
        mine = lax.broadcasted_iota(jnp.int32, (4, 2, 2, 256), 2) == core
        hidden = jnp.where(mine, hidden, 0.0).reshape(4, 2, 4, 128)
        thin = jnp.stack([g_gain_one, g_gain_two, g_shift_one, g_shift_two, spread_heads(g_bq), spread_heads(g_bv), g_bproj, g_bdown])
        thin = jnp.transpose(thin.reshape(8, 4, 2, 128), (1, 2, 0, 3))
        small_grads[layer] = jnp.concatenate([thin, hidden], axis=2)

        by_x = shared(jnp.concatenate([p_down, p_proj]))
        by_z = shared(jnp.concatenate([p_up, p_qkv], axis=1))
        g_down = by_x[:, :, :64].reshape(512, D)
        g_proj = by_x[:, :, 64:].reshape(128, D)
        g_up = jnp.transpose(by_z[..., :512].reshape(2, 4, 128, 2, 256), (2, 1, 3, 0, 4)).reshape(128, 4096)
        g_qkv = jnp.transpose(by_z[..., 512:].reshape(2, 4, 128, 3, 2, 64), (2, 3, 1, 4, 0, 5)).reshape(128, 3072)
        grads[layer] = (g_qkv, g_proj, g_up, g_down)

    part = jnp.concatenate(small_grads, axis=2)
    part = rolled(part, x)
    part = part[0] + x_up(part[1]) + x_far(part[2]) + x_down(part[3])
    keep = lax.dynamic_index_in_dim(part, yhi, axis=0, keepdims=False)
    give = lax.dynamic_index_in_dim(part, 1 - yhi, axis=0, keepdims=False)
    part = keep + y_pair(give)
    part = part + y_copy(part)
    part = part + swap(part)
    part = rolled(jnp.stack([part, z_down(part), z_far(part), z_up(part)]), (4 - z) % 4)
    part = part[0] + part[1] + part[2] + part[3]
    part = part.reshape(LAYERS, 12, 128)
    g_wide = jnp.transpose(part[:, :8], (0, 2, 1))
    stacked = [jnp.stack([grads[layer][slot] for layer in range(LAYERS)]).astype(f32) for slot in range(4)]
    return (hidden_out, running, *stacked, g_wide[:, :, :2], g_wide[:, :, 2:], part[:, 8:].reshape(LAYERS, 512))


def solution(mesh):
    fine = Mesh(mesh.devices.reshape(2, 4, 2, 4, 2), AXES)
    tokens = P(AXES)
    wide_tokens = P(AXES, None)
    params = P(None, ("x", "yhi"), None)
    return jax.shard_map(
        local,
        mesh=fine,
        in_specs=(wide_tokens, tokens, wide_tokens, params, params, params, params, params, params, P(None, ("x", "yhi"))),
        out_specs=(wide_tokens, wide_tokens, params, params, params, params, params, params, P(None, ("x", "yhi"))),
        check_vma=False,
    )
```

time: 1310 us -> 726 us (0.55)
  waiting for transfers between devices: 909 us -> 174 us
  starting transfers between devices: 47.4 us -> 285 us
  blocking collectives: 142 us -> 0 us
  matrix products: 127 us -> 52.3 us
  local copies, waits for them, and re-layouts: 32.1 us -> 86.9 us
  Pallas kernels: 0 us -> 42.8 us
  other arithmetic: 28.5 us -> 67.2 us
    all_gather x6 -> x0, waiting for transfers between devices: 815 us -> none  [the longest x4 630 us: in_one_piece(): result, at, done = (lax.all_gather(both, axis, axis=dim, tiled=True), 0, [])]
    ppermute x0 -> x182, starting transfers between devices: none -> 285 us  [the longest x22 95.2 us: swap(): return lax.ppermute(a, 'core', [(0, 1), (1, 0)])]
    ppermute x0 -> x182, waiting for transfers between devices: none -> 174 us  [the longest x33 65.6 us: z_up(): return lax.ppermute(a, 'z', ring(1))]
    all_gather x4 -> x0, blocking collectives: 106 us -> none  [the longest x2 53.2 us: local(): lax.all_gather(up_bias[layer_no], 'shard', axis=0, tiled=True)]
    dot_general x36 -> x48, matrix products: 127 us -> 52.3 us  [the longest x32 27.7 us: dot_tn(): lax.dot_general(a, b, (((0,), (0,)), ((), ())), preferred_element_type=f32)]
    psum x1 -> x0, waiting for transfers between devices: 51.5 us -> none  [local(): lax.psum(shares[0].astype(jnp.bfloat16), 'rep').astype(jnp.float32)]
    all_to_all x12 -> x0, starting transfers between devices: 47.2 us -> none  [the longest x4 16.5 us: sent_and_summed(): tiles = lax.all_to_all(split_up(shard, dim, length), axis, 0, 0, tiled=True)]
    pallas_call x0 -> x12, Pallas kernels: none -> 42.8 us  [the longest x2 22 us: attend_back(): pl.pallas_call(attend_back_kernel, out_shape=(jax.ShapeDtypeStruct((2 * R...]
  transfers between devices with their start and end apart: 19 -> 182, of which waited for: 16 -> 64; matrix products, arithmetic and copies ran while one was open for 8% -> 25% of each run, Pallas kernels for 0% -> 6%
where the time goes in v1:
time: 726 us; the launch traced here: 715 us
  starting transfers between devices  285 us (39%)
  waiting for transfers between devices  174 us (24%)
  local copies, waits for them, and re-layouts  86.9 us (12%)
  other arithmetic  67.2 us (9%)
  matrix products  52.3 us (7%)
  Pallas kernels  42.8 us (6%)
    ppermute x22, starting transfers between devices, swap(): return lax.ppermute(a, 'core', [(0, 1), (1, 0)])  95.2 us
    ppermute x34, starting transfers between devices, x_down(): return lax.ppermute(a, 'x', ring(3))  70.6 us
    ppermute x33, waiting for transfers between devices, z_up(): return lax.ppermute(a, 'z', ring(1))  65.6 us
    ppermute x33, starting transfers between devices, z_down(): return lax.ppermute(a, 'z', ring(3))  60.3 us
    ppermute x34, waiting for transfers between devices, x_up(): return lax.ppermute(a, 'x', ring(1))  52.8 us
    unnamed x455, local copies, waits for them, and re-layouts  28.8 us
    dot_general x32, matrix products, dot_tn(): lax.dot_general(a, b, (((0,), (0,)), ((), ())), preferred_element_type=f32)  27.7 us
    ppermute x18, starting transfers between devices, y_pair(): return lax.ppermute(a, ('ylo', 'yhi'), [(0, 3), (3, 0), (1, 2), (2, 1)])  23.1 us
  transfers between devices with their start and end apart: 182, of which 64 were waited for; matrix products, arithmetic and copies ran while one was open for 25% of the time, Pallas kernels for 6%

profile of v1, /device:TPU:1, one launch (start us, length us, event | category | flops | bytes accessed | tf_op | source)
XLA Modules:
  0.0 715.2 jit_solution(11468102000806830309)
XLA Ops:
  3.3 3.6 collective-permute-start.1
  44.9 3.5 collective-permute-done.4
  70.4 3.0 collective-permute-start.23
  73.7 6.3 collective-permute-done.40
  81.6 2.9 collective-permute-start.55
  91.2 5.6 collective-permute-done.56
  114.7 3.8 collective-permute-start.11
  120.5 3.2 collective-permute-done.12
  127.6 10.8 %collective-permute-done.57 = bf16[128,512]{0,1:T(8,128)(2,1)S(1)} collective-permute-done((bf16[128,512]{0,1:T(8,128)(2,1)S(1)}, bf16[128,512]{0,1:T(8,128)(2,1)S(1)}, u32[]{:S(2)}, u32[]{:S(2)}) %collective-permute-start.57) | collective-permute-done | bytes 131104 | tf_op jit(solution)/shard_map/ppermute | solution.py:28
  141.4 14.2 %collective-permute-start.5 = (bf16[128,1024]{1,0:T(8,128)(2,1)S(1)}, bf16[128,1024]{1,0:T(8,128)(2,1)S(1)}, u32[]{:S(2)}, u32[]{:S(2)}) collective-permute-start(bf16[128,1024]{1,0:T(8,128)(2,1)S(1)} %shard_map.169), channel_id=1, source_target_pairs={{0,8},{8,0},{1,9},{9,1},{2,10},{10,2},{3,11},{11,3},{4,12},{12,4},... | collective-permute-start | bytes 786440 | tf_op jit(solution)/shard_map/ppermute | solution.py:60
  159.9 8.0 %shard_map.170.ctx_ref = bf16[256,512]{1,0:T(8,128)(2,1)S(1)} custom-call(f32[8]{0:T(128)S(1)} %multiply_power_fusion.slope_ref, s32[2,128,1]{2,1,0:T(8,128)S(1)} %copy.52.rows_ref, s32[2,1,128]{2,1,0:T(1,128)S(1)} %bitcast.433, bf16[256,1536]{1,0:T(8,128)(2,1)S(1)} %fusion.qkv_ref), custom_call_target="tpu_custom_call" | custom-call | flops 67108864 | bytes 1048576 | tf_op jit(solution)/shard_map/pallas_call | solution.py:182
  170.9 12.2 %collective-permute-start.20 = (f32[128,1024]{1,0:T(8,128)S(1)}, f32[128,1024]{1,0:T(8,128)S(1)}, u32[]{:S(2)}, u32[]{:S(2)}) collective-permute-start(f32[128,1024]{1,0:T(8,128)S(1)} %slice.1212), channel_id=1, source_target_pairs={{0,8},{8,0},{1,9},{9,1},{2,10},{10,2},{3,11},{11,3},{4,12},{12,4},... | collective-permute-start | bytes 1572872 | tf_op jit(solution)/shard_map/ppermute | solution.py:60
  188.5 4.7 collective-permute-start.64
  193.3 3.1 multiply_convert_fusion.1
  197.8 4.0 collective-permute-start.36
  205.0 7.0 collective-permute-done.64
  212.1 3.1 collective-permute-done.65
  218.8 9.4 %collective-permute-done.60 = bf16[1024,512]{0,1:T(8,128)(2,1)S(1)} collective-permute-done((bf16[1024,512]{0,1:T(8,128)(2,1)S(1)}, bf16[1024,512]{0,1:T(8,128)(2,1)S(1)}, u32[]{:S(2)}, u32[]{:S(2)}) %collective-permute-start.60) | collective-permute-done | bytes 1048608 | tf_op jit(solution)/shard_map/ppermute | solution.py:40
  231.9 4.7 collective-permute-done.45
  239.5 8.0 %shard_map.173.ctx_ref = bf16[256,512]{1,0:T(8,128)(2,1)S(1)} custom-call(f32[8]{0:T(128)S(1)} %multiply_power_fusion.slope_ref, s32[2,128,1]{2,1,0:T(8,128)S(1)} %copy.52.rows_ref, s32[2,1,128]{2,1,0:T(1,128)S(1)} %bitcast.434, bf16[256,1536]{1,0:T(8,128)(2,1)S(1)} %fusion.1.qkv_ref), custom_call_target="tpu_custom_call" | custom-call | flops 67108864 | bytes 1048576 | tf_op jit(solution)/shard_map/pallas_call | solution.py:182
  259.4 2.9 fusion.162
  276.6 4.3 collective-permute-start.151
  301.4 11.0 %shard_map.176 = (bf16[256,1536]{1,0:T(8,128)(2,1)S(1)}, f32[2,4,1,128]{3,2,1,0:T(1,128)S(1)}, f32[2,4,1,128]{3,2,1,0:T(1,128)S(1)}) custom-call(f32[8]{0:T(128)S(1)} %multiply_power_fusion.slope_ref, s32[2,128,1]{2,1,0:T(8,128)S(1)} %copy.52.rows_ref, s32[2,1,128]{2,1,0:T(1,128)S(1)} %bitcast.435, bf16[256,1536]{1,0:T(8,128)(2,1)S(1)} %fusion.1.qkv_ref, ...), custom_call_target="tpu_custom_call" | custom-call | flops 167772160 | bytes 2097152 | tf_op jit(solution)/shard_map/pallas_call | solution.py:201
  349.9 4.6 collective-permute-done.112
  373.3 15.4 %collective-permute-done.102 = bf16[1024,512]{1,0:T(8,128)(2,1)} collective-permute-done((bf16[1024,512]{1,0:T(8,128)(2,1)}, bf16[1024,512]{1,0:T(8,128)(2,1)}, u32[]{:S(2)}, u32[]{:S(2)}) %collective-permute-start.102) | collective-permute-done | bytes 1048608 | tf_op jit(solution)/shard_map/ppermute | solution.py:40
  388.7 7.4 %collective-permute-start.74 = (f32[128,1024]{1,0:T(8,128)S(1)}, f32[128,1024]{1,0:T(8,128)S(1)}, u32[]{:S(2)}, u32[]{:S(2)}) collective-permute-start(f32[128,1024]{1,0:T(8,128)S(1)} %slice.1257), channel_id=1, source_target_pairs={{0,8},{8,0},{1,9},{9,1},{2,10},{10,2},{3,11},{11,3},{4,12},{12,4},... | collective-permute-start | bytes 1572872 | tf_op jit(solution)/shard_map/ppermute | solution.py:60
  415.1 12.3 %collective-permute-done.106 = bf16[256,512]{1,0:T(8,128)(2,1)S(1)} collective-permute-done((bf16[256,512]{1,0:T(8,128)(2,1)S(1)}, bf16[256,512]{1,0:T(8,128)(2,1)S(1)}, u32[]{:S(2)}, u32[]{:S(2)}) %collective-permute-start.106) | collective-permute-done | bytes 262176 | tf_op jit(solution)/shard_map/ppermute | solution.py:28
  440.2 3.8 collective-permute-done.153
  448.3 5.7 collective-permute-start.75
  471.3 11.0 %shard_map.179 = (bf16[256,1536]{1,0:T(8,128)(2,1)S(1)}, f32[2,4,1,128]{3,2,1,0:T(1,128)S(1)}, f32[2,4,1,128]{3,2,1,0:T(1,128)S(1)}) custom-call(f32[8]{0:T(128)S(1)} %multiply_power_fusion.slope_ref, s32[2,128,1]{2,1,0:T(8,128)S(1)} %copy.52.rows_ref, s32[2,1,128]{2,1,0:T(1,128)S(1)} %bitcast.436, bf16[256,1536]{1,0:T(8,128)(2,1)S(1)} %fusion.qkv_ref, ...), custom_call_target="tpu_custom_call" | custom-call | flops 167772160 | bytes 2097152 | tf_op jit(solution)/shard_map/pallas_call | solution.py:201
  482.8 3.0 fusion.150
  506.8 5.1 collective-permute-done.169
  514.7 2.8 collective-permute-done.170
  525.1 6.8 collective-permute-start.76
  535.8 3.3 collective-permute-done.121
  559.8 3.5 collective-permute-done.176
  571.8 10.2 %collective-permute-start.178 = (f32[24,128]{1,0:T(8,128)S(1)}, f32[24,128]{1,0:T(8,128)S(1)}, u32[]{:S(2)}, u32[]{:S(2)}) collective-permute-start(f32[24,128]{1,0:T(8,128)S(1)} %add.933), channel_id=1, source_target_pairs={{0,8},{8,0},{1,9},{9,1},{2,10},{10,2},{3,11},{11,3},{4,12},{12,4},... | collective-permute-start | bytes 36872 | tf_op jit(solution)/shard_map/ppermute | solution.py:60
  583.9 4.9 collective-permute-done.179
  590.0 2.9 collective-permute-done.180
  593.8 3.0 collective-permute-done.181
  596.8 11.1 %collective-permute-start.172 = (bf16[4,80,1024]{2,1,0:T(8,128)(2,1)}, bf16[4,80,1024]{2,1,0:T(8,128)(2,1)}, u32[]{:S(2)}, u32[]{:S(2)}) collective-permute-start(bf16[4,80,1024]{2,1,0:T(8,128)(2,1)} %constant_dynamic-slice_fusion.19), channel_id=1, source_target_pairs={{0,8},{8,0},{1,9},{9,1},{2,10},{10,2},{3,11},{11,3},{4,12},{12,4},... | collective-permute-start | bytes 1966088 | tf_op jit(solution)/shard_map/ppermute | solution.py:60
  624.7 5.7 collective-permute-done.87
  640.2 3.5 collective-permute-start.93
  658.4 2.8 collective-permute-start.144
  672.2 8.2 %collective-permute-start.148 = (bf16[4,80,1024]{2,1,0:T(8,128)(2,1)}, bf16[4,80,1024]{2,1,0:T(8,128)(2,1)}, u32[]{:S(2)}, u32[]{:S(2)}) collective-permute-start(bf16[4,80,1024]{2,1,0:T(8,128)(2,1)} %constant_dynamic-slice_fusion.22), channel_id=1, source_target_pairs={{0,8},{8,0},{1,9},{9,1},{2,10},{10,2},{3,11},{11,3},{4,12},{12,4},... | collective-permute-start | bytes 1966088 | tf_op jit(solution)/shard_map/ppermute | solution.py:60
  680.5 3.1 collective-permute-start.99
  683.7 3.4 collective-permute-done.98
  710.9 3.8 maximum_convert_fusion
  (1250 shorter events, 422.6 us)
Async XLA Ops:
  3.3 30.7 %collective-permute-start.1 = (bf16[24,128]{1,0:T(8,128)(2,1)}, bf16[24,128]{1,0:T(8,128)(2,1)}, u32[]{:S(2)}, u32[]{:S(2)}) collective-permute-start(bf16[24,128]{1,0:T(8,128)(2,1)} %get-tuple-element.209), channel_id=1, source_target_pairs={{0,65},{65,0},{1,64},{64,1},{2,67},{67,2},{3,66},{66,3},{4,69},{69... | collective-permute-start | bytes 18440 | tf_op jit(solution)/shard_map/ppermute | solution.py:52
  9.4 44.8 %collective-permute-start.6 = (bf16[128,384]{0,1:T(8,128)(2,1)}, bf16[128,384]{0,1:T(8,128)(2,1)}, u32[]{:S(2)}, u32[]{:S(2)}) collective-permute-start(bf16[128,384]{0,1:T(8,128)(2,1)} %bitcast.15), channel_id=1, source_target_pairs={{0,65},{65,0},{1,64},{64,1},{2,67},{67,2},{3,66},{66,3},{4,69},{69... | collective-permute-start | bytes 294920 | tf_op jit(solution)/shard_map/ppermute | solution.py:52
  13.9 52.5 %collective-permute-start.22 = (bf16[128,512]{0,1:T(8,128)(2,1)}, bf16[128,512]{0,1:T(8,128)(2,1)}, u32[]{:S(2)}, u32[]{:S(2)}) collective-permute-start(bf16[128,512]{0,1:T(8,128)(2,1)} %bitcast.29), channel_id=1, source_target_pairs={{0,65},{65,0},{1,64},{64,1},{2,67},{67,2},{3,66},{66,3},{4,69},{69... | collective-permute-start | bytes 393224 | tf_op jit(solution)/shard_map/ppermute | solution.py:52
  17.6 41.8 %collective-permute-start.38 = (bf16[128,384]{0,1:T(8,128)(2,1)}, bf16[128,384]{0,1:T(8,128)(2,1)}, u32[]{:S(2)}, u32[]{:S(2)}) collective-permute-start(bf16[128,384]{0,1:T(8,128)(2,1)} %bitcast.41), channel_id=1, source_target_pairs={{0,65},{65,0},{1,64},{64,1},{2,67},{67,2},{3,66},{66,3},{4,69},{69... | collective-permute-start | bytes 294920 | tf_op jit(solution)/shard_map/ppermute | solution.py:52
  18.3 49.2 %collective-permute-start.54 = (bf16[128,512]{0,1:T(8,128)(2,1)S(1)}, bf16[128,512]{0,1:T(8,128)(2,1)S(1)}, u32[]{:S(2)}, u32[]{:S(2)}) collective-permute-start(bf16[128,512]{0,1:T(8,128)(2,1)S(1)} %bitcast.467), channel_id=1, source_target_pairs={{0,65},{65,0},{1,64},{64,1},{2,67},{67,2},{3,66},{66,3},{4,69},{69... | collective-permute-start | bytes 393224 | tf_op jit(solution)/shard_map/ppermute | solution.py:52
  85.5 34.9 %collective-permute-start.63 = (bf16[256,1024]{1,0:T(8,128)(2,1)S(1)}, bf16[256,1024]{1,0:T(8,128)(2,1)S(1)}, u32[]{:S(2)}, u32[]{:S(2)}) collective-permute-start(bf16[256,1024]{1,0:T(8,128)(2,1)S(1)} %copy-done.79), channel_id=1, source_target_pairs={{0,65},{65,0},{1,64},{64,1},{2,67},{67,2},{3,66},{66,3},{4,69},{69... | collective-permute-start | bytes 1572872 | tf_op jit(solution)/shard_map/ppermute | solution.py:52
  118.6 21.1 %collective-permute-start.32 = (bf16[512,1024]{1,0:T(8,128)(2,1)S(1)}, bf16[512,1024]{1,0:T(8,128)(2,1)S(1)}, u32[]{:S(2)}, u32[]{:S(2)}) collective-permute-start(bf16[512,1024]{1,0:T(8,128)(2,1)S(1)} %pad_maximum_fusion.8), channel_id=1, source_target_pairs={{0,6},{2,0},{4,2},{6,4},{1,7},{3,1},{5,3},{7,5},{8,14},{10,8},{12,... | collective-permute-start | bytes 3145736 | tf_op jit(solution)/shard_map/ppermute | solution.py:32
  118.8 22.6 %collective-permute-start.33 = (bf16[512,1024]{1,0:T(8,128)(2,1)S(1)}, bf16[512,1024]{1,0:T(8,128)(2,1)S(1)}, u32[]{:S(2)}, u32[]{:S(2)}) collective-permute-start(bf16[512,1024]{1,0:T(8,128)(2,1)S(1)} %pad_maximum_fusion.8), channel_id=1, source_target_pairs={{0,2},{2,4},{4,6},{6,0},{1,3},{3,5},{5,7},{7,1},{8,10},{10,12},{12... | collective-permute-start | bytes 3145736 | tf_op jit(solution)/shard_map/ppermute | solution.py:28
  120.4 35.2 %collective-permute-start.28 = (bf16[1024,512]{0,1:T(8,128)(2,1)S(1)}, bf16[1024,512]{0,1:T(8,128)(2,1)S(1)}, u32[]{:S(2)}, u32[]{:S(2)}) collective-permute-start(bf16[1024,512]{0,1:T(8,128)(2,1)S(1)} %constant_dynamic-update-slice_fusion.15), channel_id=1, source_target_pairs={{0,16},{16,32},{32,48},{48,0},{1,17},{17,33},{33,49},{49,1},{2,18}... | collective-permute-start | bytes 3145736 | tf_op jit(solution)/shard_map/ppermute | solution.py:40
  123.7 32.6 %collective-permute-start.27 = (bf16[1024,512]{0,1:T(8,128)(2,1)S(1)}, bf16[1024,512]{0,1:T(8,128)(2,1)S(1)}, u32[]{:S(2)}, u32[]{:S(2)}) collective-permute-start(bf16[1024,512]{0,1:T(8,128)(2,1)S(1)} %constant_dynamic-update-slice_fusion.15), channel_id=1, source_target_pairs={{0,48},{16,0},{32,16},{48,32},{1,49},{17,1},{33,17},{49,33},{2,50}... | collective-permute-start | bytes 3145736 | tf_op jit(solution)/shard_map/ppermute | solution.py:44
  155.6 42.1 %collective-permute-start.58 = (bf16[128,512]{0,1:T(8,128)(2,1)S(1)}, bf16[128,512]{0,1:T(8,128)(2,1)S(1)}, u32[]{:S(2)}, u32[]{:S(2)}) collective-permute-start(bf16[128,512]{0,1:T(8,128)(2,1)S(1)} %slice.1243), channel_id=1, source_target_pairs={{0,6},{2,0},{4,2},{6,4},{1,7},{3,1},{5,3},{7,5},{8,14},{10,8},{12,... | collective-permute-start | bytes 393224 | tf_op jit(solution)/shard_map/ppermute | solution.py:32
  156.3 45.8 %collective-permute-start.44 = (bf16[1024,384]{0,1:T(8,128)(2,1)S(1)}, bf16[1024,384]{0,1:T(8,128)(2,1)S(1)}, u32[]{:S(2)}, u32[]{:S(2)}) collective-permute-start(bf16[1024,384]{0,1:T(8,128)(2,1)S(1)} %constant_dynamic-update-slice_fusion.21), channel_id=1, source_target_pairs={{0,16},{16,32},{32,48},{48,0},{1,17},{17,33},{33,49},{49,1},{2,18}... | collective-permute-start | bytes 2359304 | tf_op jit(solution)/shard_map/ppermute | solution.py:40
  158.2 28.8 %collective-permute-start.29 = (bf16[512,512]{0,1:T(8,128)(2,1)S(1)}, bf16[512,512]{0,1:T(8,128)(2,1)S(1)}, u32[]{:S(2)}, u32[]{:S(2)}) collective-permute-start(bf16[512,512]{0,1:T(8,128)(2,1)S(1)} %slice.1218), channel_id=1, source_target_pairs={{0,16},{16,32},{32,48},{48,0},{1,17},{17,33},{33,49},{49,1},{2,18}... | collective-permute-start | bytes 1572872 | tf_op jit(solution)/shard_map/ppermute | solution.py:40
  188.5 23.5 %collective-permute-start.64 = (bf16[512,1024]{1,0:T(8,128)(2,1)S(1)}, bf16[512,1024]{1,0:T(8,128)(2,1)S(1)}, u32[]{:S(2)}, u32[]{:S(2)}) collective-permute-start(bf16[512,1024]{1,0:T(8,128)(2,1)S(1)} %pad_maximum_fusion.9), channel_id=1, source_target_pairs={{0,6},{2,0},{4,2},{6,4},{1,7},{3,1},{5,3},{7,5},{8,14},{10,8},{12,... | collective-permute-start | bytes 3145736 | tf_op jit(solution)/shard_map/ppermute | solution.py:32
  193.3 21.9 %collective-permute-start.65 = (bf16[512,1024]{1,0:T(8,128)(2,1)S(1)}, bf16[512,1024]{1,0:T(8,128)(2,1)S(1)}, u32[]{:S(2)}, u32[]{:S(2)}) collective-permute-start(bf16[512,1024]{1,0:T(8,128)(2,1)S(1)} %pad_maximum_fusion.9), channel_id=1, source_target_pairs={{0,2},{2,4},{4,6},{6,0},{1,3},{3,5},{5,7},{7,1},{8,10},{10,12},{12... | collective-permute-start | bytes 3145736 | tf_op jit(solution)/shard_map/ppermute | solution.py:28
  202.1 26.1 %collective-permute-start.60 = (bf16[1024,512]{0,1:T(8,128)(2,1)S(1)}, bf16[1024,512]{0,1:T(8,128)(2,1)S(1)}, u32[]{:S(2)}, u32[]{:S(2)}) collective-permute-start(bf16[1024,512]{0,1:T(8,128)(2,1)S(1)} %constant_dynamic-update-slice_fusion.29), channel_id=1, source_target_pairs={{0,16},{16,32},{32,48},{48,0},{1,17},{17,33},{33,49},{49,1},{2,18}... | collective-permute-start | bytes 3145736 | tf_op jit(solution)/shard_map/ppermute | solution.py:40
  203.6 24.5 %collective-permute-start.59 = (bf16[1024,512]{0,1:T(8,128)(2,1)S(1)}, bf16[1024,512]{0,1:T(8,128)(2,1)S(1)}, u32[]{:S(2)}, u32[]{:S(2)}) collective-permute-start(bf16[1024,512]{0,1:T(8,128)(2,1)S(1)} %constant_dynamic-update-slice_fusion.29), channel_id=1, source_target_pairs={{0,48},{16,0},{32,16},{48,32},{1,49},{17,1},{33,17},{49,33},{2,50}... | collective-permute-start | bytes 3145736 | tf_op jit(solution)/shard_map/ppermute | solution.py:44
  212.0 24.6 %collective-permute-start.45 = (bf16[512,384]{0,1:T(8,128)(2,1)S(1)}, bf16[512,384]{0,1:T(8,128)(2,1)S(1)}, u32[]{:S(2)}, u32[]{:S(2)}) collective-permute-start(bf16[512,384]{0,1:T(8,128)(2,1)S(1)} %slice.1231), channel_id=1, source_target_pairs={{0,16},{16,32},{32,48},{48,0},{1,17},{17,33},{33,49},{49,1},{2,18}... | collective-permute-start | bytes 1179656 | tf_op jit(solution)/shard_map/ppermute | solution.py:40
  230.5 28.9 %collective-permute-start.69 = (bf16[128,1024]{1,0:T(8,128)(2,1)S(1)}, bf16[128,1024]{1,0:T(8,128)(2,1)S(1)}, u32[]{:S(2)}, u32[]{:S(2)}) collective-permute-start(bf16[128,1024]{1,0:T(8,128)(2,1)S(1)} %get-tuple-element.151), channel_id=1, source_target_pairs={{0,8},{8,0},{1,9},{9,1},{2,10},{10,2},{3,11},{11,3},{4,12},{12,4},... | collective-permute-start | bytes 786440 | tf_op jit(solution)/shard_map/ppermute | solution.py:60
  230.6 23.8 %collective-permute-start.61 = (bf16[512,512]{0,1:T(8,128)(2,1)S(1)}, bf16[512,512]{0,1:T(8,128)(2,1)S(1)}, u32[]{:S(2)}, u32[]{:S(2)}) collective-permute-start(bf16[512,512]{0,1:T(8,128)(2,1)S(1)} %slice.1244), channel_id=1, source_target_pairs={{0,16},{16,32},{32,48},{48,0},{1,17},{17,33},{33,49},{49,1},{2,18}... | collective-permute-start | bytes 1572872 | tf_op jit(solution)/shard_map/ppermute | solution.py:40
  259.0 30.3 %collective-permute-start.68 = (f32[128,1024]{1,0:T(8,128)}, f32[128,1024]{1,0:T(8,128)}, u32[]{:S(2)}, u32[]{:S(2)}) collective-permute-start(f32[128,1024]{1,0:T(8,128)} %slice.1250), channel_id=1, source_target_pairs={{0,8},{8,0},{1,9},{9,1},{2,10},{10,2},{3,11},{11,3},{4,12},{12,4},... | collective-permute-start | bytes 1572872 | tf_op jit(solution)/shard_map/ppermute | solution.py:60
  265.5 20.3 %collective-permute-start.70 = (f32[128,1024]{1,0:T(8,128)}, f32[128,1024]{1,0:T(8,128)}, u32[]{:S(2)}, u32[]{:S(2)}) collective-permute-start(f32[128,1024]{1,0:T(8,128)} %slice.1253), channel_id=1, source_target_pairs={{0,8},{8,0},{1,9},{9,1},{2,10},{10,2},{3,11},{11,3},{4,12},{12,4},... | collective-permute-start | bytes 1572872 | tf_op jit(solution)/shard_map/ppermute | solution.py:60
  294.3 106.9 %collective-permute-start.150 = (bf16[512,1024]{1,0:T(8,128)(2,1)}, bf16[512,1024]{1,0:T(8,128)(2,1)}, u32[]{:S(2)}, u32[]{:S(2)}) collective-permute-start(bf16[512,1024]{1,0:T(8,128)(2,1)} %pad_maximum_fusion.16), channel_id=1, source_target_pairs={{0,2},{2,4},{4,6},{6,0},{1,3},{3,5},{5,7},{7,1},{8,10},{10,12},{12... | collective-permute-start | bytes 3145736 | tf_op jit(solution)/shard_map/ppermute | solution.py:28
  297.4 104.0 %collective-permute-start.152 = (bf16[512,1024]{1,0:T(8,128)(2,1)}, bf16[512,1024]{1,0:T(8,128)(2,1)}, u32[]{:S(2)}, u32[]{:S(2)}) collective-permute-start(bf16[512,1024]{1,0:T(8,128)(2,1)} %pad_maximum_fusion.17), channel_id=1, source_target_pairs={{0,6},{2,0},{4,2},{6,4},{1,7},{3,1},{5,3},{7,5},{8,14},{10,8},{12,... | collective-permute-start | bytes 3145736 | tf_op jit(solution)/shard_map/ppermute | solution.py:32
  320.5 25.9 %collective-permute-start.110 = (bf16[512,384]{1,0:T(8,128)(2,1)}, bf16[512,384]{1,0:T(8,128)(2,1)}, u32[]{:S(2)}, u32[]{:S(2)}) collective-permute-start(bf16[512,384]{1,0:T(8,128)(2,1)} %get-tuple-element.148), channel_id=1, source_target_pairs={{0,16},{16,32},{32,48},{48,0},{1,17},{17,33},{33,49},{49,1},{2,18}... | collective-permute-start | bytes 1179656 | tf_op jit(solution)/shard_map/ppermute | solution.py:40
  365.0 23.7 %collective-permute-start.102 = (bf16[1024,512]{1,0:T(8,128)(2,1)}, bf16[1024,512]{1,0:T(8,128)(2,1)}, u32[]{:S(2)}, u32[]{:S(2)}) collective-permute-start(bf16[1024,512]{1,0:T(8,128)(2,1)} %pad_maximum_fusion.12), channel_id=1, source_target_pairs={{0,16},{16,32},{32,48},{48,0},{1,17},{17,33},{33,49},{49,1},{2,18}... | collective-permute-start | bytes 3145736 | tf_op jit(solution)/shard_map/ppermute | solution.py:40
  365.0 23.7 %collective-permute-start.104 = (bf16[1024,512]{1,0:T(8,128)(2,1)}, bf16[1024,512]{1,0:T(8,128)(2,1)}, u32[]{:S(2)}, u32[]{:S(2)}) collective-permute-start(bf16[1024,512]{1,0:T(8,128)(2,1)} %pad_maximum_fusion.13), channel_id=1, source_target_pairs={{0,48},{16,0},{32,16},{48,32},{1,49},{17,1},{33,17},{49,33},{2,50}... | collective-permute-start | bytes 3145736 | tf_op jit(solution)/shard_map/ppermute | solution.py:44
  368.3 42.3 %collective-permute-start.111 = (bf16[1024,384]{1,0:T(8,128)(2,1)}, bf16[1024,384]{1,0:T(8,128)(2,1)}, u32[]{:S(2)}, u32[]{:S(2)}) collective-permute-start(bf16[1024,384]{1,0:T(8,128)(2,1)} %pad_maximum_fusion.22), channel_id=1, source_target_pairs={{0,16},{16,32},{32,48},{48,0},{1,17},{17,33},{33,49},{49,1},{2,18}... | collective-permute-start | bytes 2359304 | tf_op jit(solution)/shard_map/ppermute | solution.py:40
  388.7 22.0 %collective-permute-start.113 = (bf16[1024,384]{1,0:T(8,128)(2,1)}, bf16[1024,384]{1,0:T(8,128)(2,1)S(1)}, u32[]{:S(2)}, u32[]{:S(2)}) collective-permute-start(bf16[1024,384]{1,0:T(8,128)(2,1)} %pad_maximum_fusion.23), channel_id=1, source_target_pairs={{0,48},{16,0},{32,16},{48,32},{1,49},{17,1},{33,17},{49,33},{2,50}... | collective-permute-start | bytes 2359304 | tf_op jit(solution)/shard_map/ppermute | solution.py:44
  388.7 45.3 %collective-permute-start.74 = (f32[128,1024]{1,0:T(8,128)S(1)}, f32[128,1024]{1,0:T(8,128)S(1)}, u32[]{:S(2)}, u32[]{:S(2)}) collective-permute-start(f32[128,1024]{1,0:T(8,128)S(1)} %slice.1257), channel_id=1, source_target_pairs={{0,8},{8,0},{1,9},{9,1},{2,10},{10,2},{3,11},{11,3},{4,12},{12,4},... | collective-permute-start | bytes 1572872 | tf_op jit(solution)/shard_map/ppermute | solution.py:60
  407.8 30.1 %collective-permute-start.125 = (bf16[256,1024]{1,0:T(8,128)(2,1)S(1)}, bf16[256,1024]{1,0:T(8,128)(2,1)S(1)}, u32[]{:S(2)}, u32[]{:S(2)}) collective-permute-start(bf16[256,1024]{1,0:T(8,128)(2,1)S(1)} %get-tuple-element.110), channel_id=1, source_target_pairs={{0,2},{2,4},{4,6},{6,0},{1,3},{3,5},{5,7},{7,1},{8,10},{10,12},{12... | collective-permute-start | bytes 1572872 | tf_op jit(solution)/shard_map/ppermute | solution.py:28
  407.8 37.6 %collective-permute-start.127 = (bf16[256,1024]{1,0:T(8,128)(2,1)S(1)}, bf16[256,1024]{1,0:T(8,128)(2,1)S(1)}, u32[]{:S(2)}, u32[]{:S(2)}) collective-permute-start(bf16[256,1024]{1,0:T(8,128)(2,1)S(1)} %get-tuple-element.111), channel_id=1, source_target_pairs={{0,6},{2,0},{4,2},{6,4},{1,7},{3,1},{5,3},{7,5},{8,14},{10,8},{12,... | collective-permute-start | bytes 1572872 | tf_op jit(solution)/shard_map/ppermute | solution.py:32
  434.0 22.4 %collective-permute-start.79 = (bf16[512,512]{1,0:T(8,128)(2,1)S(1)}, bf16[512,512]{1,0:T(8,128)(2,1)S(1)}, u32[]{:S(2)}, u32[]{:S(2)}) collective-permute-start(bf16[512,512]{1,0:T(8,128)(2,1)S(1)} %get-tuple-element.121), channel_id=1, source_target_pairs={{0,48},{16,0},{32,16},{48,32},{1,49},{17,1},{33,17},{49,33},{2,50}... | collective-permute-start | bytes 1572872 | tf_op jit(solution)/shard_map/ppermute | solution.py:44
  437.8 20.4 %collective-permute-start.109 = (bf16[128,512]{1,0:T(8,128)(2,1)S(1)}, bf16[128,512]{1,0:T(8,128)(2,1)S(1)}, u32[]{:S(2)}, u32[]{:S(2)}) collective-permute-start(bf16[128,512]{1,0:T(8,128)(2,1)S(1)} %slice.1314), channel_id=1, source_target_pairs={{0,65},{65,0},{1,64},{64,1},{2,67},{67,2},{3,66},{66,3},{4,69},{69... | collective-permute-start | bytes 393224 | tf_op jit(solution)/shard_map/ppermute | solution.py:52
  448.3 22.5 %collective-permute-start.75 = (bf16[128,1024]{1,0:T(8,128)(2,1)S(1)}, bf16[128,1024]{1,0:T(8,128)(2,1)S(1)}, u32[]{:S(2)}, u32[]{:S(2)}) collective-permute-start(bf16[128,1024]{1,0:T(8,128)(2,1)S(1)} %convert_element_type.814), channel_id=1, source_target_pairs={{0,8},{8,0},{1,9},{9,1},{2,10},{10,2},{3,11},{11,3},{4,12},{12,4},... | collective-permute-start | bytes 786440 | tf_op jit(solution)/shard_map/ppermute | solution.py:60
  460.8 153.9 %collective-permute-start.126 = (bf16[512,1024]{1,0:T(8,128)(2,1)}, bf16[512,1024]{1,0:T(8,128)(2,1)}, u32[]{:S(2)}, u32[]{:S(2)}) collective-permute-start(bf16[512,1024]{1,0:T(8,128)(2,1)} %pad_maximum_fusion.14), channel_id=1, source_target_pairs={{0,2},{2,4},{4,6},{6,0},{1,3},{3,5},{5,7},{7,1},{8,10},{10,12},{12... | collective-permute-start | bytes 3145736 | tf_op jit(solution)/shard_map/ppermute | solution.py:28
  461.7 153.5 %collective-permute-start.128 = (bf16[512,1024]{1,0:T(8,128)(2,1)}, bf16[512,1024]{1,0:T(8,128)(2,1)}, u32[]{:S(2)}, u32[]{:S(2)}) collective-permute-start(bf16[512,1024]{1,0:T(8,128)(2,1)} %pad_maximum_fusion.15), channel_id=1, source_target_pairs={{0,6},{2,0},{4,2},{6,4},{1,7},{3,1},{5,3},{7,5},{8,14},{10,8},{12,... | collective-permute-start | bytes 3145736 | tf_op jit(solution)/shard_map/ppermute | solution.py:32
  469.1 25.0 %collective-permute-start.118 = (bf16[128,384]{1,0:T(8,128)(2,1)}, bf16[128,384]{1,0:T(8,128)(2,1)}, u32[]{:S(2)}, u32[]{:S(2)}) collective-permute-start(bf16[128,384]{1,0:T(8,128)(2,1)} %slice.1329), channel_id=1, source_target_pairs={{0,65},{65,0},{1,64},{64,1},{2,67},{67,2},{3,66},{66,3},{4,69},{69... | collective-permute-start | bytes 294920 | tf_op jit(solution)/shard_map/ppermute | solution.py:52
  470.3 27.4 %collective-permute-start.167 = (bf16[80,1024]{1,0:T(8,128)(2,1)}, bf16[80,1024]{1,0:T(8,128)(2,1)}, u32[]{:S(2)}, u32[]{:S(2)}) collective-permute-start(bf16[80,1024]{1,0:T(8,128)(2,1)} %pad_maximum_fusion.55), channel_id=1, source_target_pairs={{0,64},{64,0},{1,65},{65,1},{2,66},{66,2},{3,67},{67,3},{4,68},{68... | collective-permute-start | bytes 491528 | tf_op jit(solution)/shard_map/ppermute | solution.py:56
  497.7 21.9 %collective-permute-start.86 = (bf16[512,384]{1,0:T(8,128)(2,1)}, bf16[512,384]{1,0:T(8,128)(2,1)S(1)}, u32[]{:S(2)}, u32[]{:S(2)}) collective-permute-start(bf16[512,384]{1,0:T(8,128)(2,1)} %get-tuple-element.140), channel_id=1, source_target_pairs={{0,16},{16,32},{32,48},{48,0},{1,17},{17,33},{33,49},{49,1},{2,18}... | collective-permute-start | bytes 1179656 | tf_op jit(solution)/shard_map/ppermute | solution.py:40
  568.8 41.0 %collective-permute-start.78 = (bf16[1024,512]{1,0:T(8,128)(2,1)}, bf16[1024,512]{1,0:T(8,128)(2,1)}, u32[]{:S(2)}, u32[]{:S(2)}) collective-permute-start(bf16[1024,512]{1,0:T(8,128)(2,1)} %pad_maximum_fusion.10), channel_id=1, source_target_pairs={{0,16},{16,32},{32,48},{48,0},{1,17},{17,33},{33,49},{49,1},{2,18}... | collective-permute-start | bytes 3145736 | tf_op jit(solution)/shard_map/ppermute | solution.py:40
  569.6 40.2 %collective-permute-start.80 = (bf16[1024,512]{1,0:T(8,128)(2,1)}, bf16[1024,512]{1,0:T(8,128)(2,1)}, u32[]{:S(2)}, u32[]{:S(2)}) collective-permute-start(bf16[1024,512]{1,0:T(8,128)(2,1)} %pad_maximum_fusion.11), channel_id=1, source_target_pairs={{0,48},{16,0},{32,16},{48,32},{1,49},{17,1},{33,17},{49,33},{2,50}... | collective-permute-start | bytes 3145736 | tf_op jit(solution)/shard_map/ppermute | solution.py:44
  596.8 25.8 %collective-permute-start.172 = (bf16[4,80,1024]{2,1,0:T(8,128)(2,1)}, bf16[4,80,1024]{2,1,0:T(8,128)(2,1)}, u32[]{:S(2)}, u32[]{:S(2)}) collective-permute-start(bf16[4,80,1024]{2,1,0:T(8,128)(2,1)} %constant_dynamic-slice_fusion.19), channel_id=1, source_target_pairs={{0,8},{8,0},{1,9},{9,1},{2,10},{10,2},{3,11},{11,3},{4,12},{12,4},... | collective-permute-start | bytes 1966088 | tf_op jit(solution)/shard_map/ppermute | solution.py:60
  609.8 20.6 %collective-permute-start.87 = (bf16[1024,384]{1,0:T(8,128)(2,1)}, bf16[1024,384]{1,0:T(8,128)(2,1)S(1)}, u32[]{:S(2)}, u32[]{:S(2)}) collective-permute-start(bf16[1024,384]{1,0:T(8,128)(2,1)} %pad_maximum_fusion.20), channel_id=1, source_target_pairs={{0,16},{16,32},{32,48},{48,0},{1,17},{17,33},{33,49},{49,1},{2,18}... | collective-permute-start | bytes 2359304 | tf_op jit(solution)/shard_map/ppermute | solution.py:40
  609.8 23.3 %collective-permute-start.89 = (bf16[1024,384]{1,0:T(8,128)(2,1)}, bf16[1024,384]{1,0:T(8,128)(2,1)S(1)}, u32[]{:S(2)}, u32[]{:S(2)}) collective-permute-start(bf16[1024,384]{1,0:T(8,128)(2,1)} %pad_maximum_fusion.21), channel_id=1, source_target_pairs={{0,48},{16,0},{32,16},{48,32},{1,49},{17,1},{33,17},{49,33},{2,50}... | collective-permute-start | bytes 2359304 | tf_op jit(solution)/shard_map/ppermute | solution.py:44
  620.5 32.4 %collective-permute-start.124 = (bf16[4,128,896]{2,1,0:T(8,128)(2,1)S(1)}, bf16[4,128,896]{2,1,0:T(8,128)(2,1)S(1)}, u32[]{:S(2)}, u32[]{:S(2)}) collective-permute-start(bf16[4,128,896]{2,1,0:T(8,128)(2,1)S(1)} %constant_dynamic-slice_fusion.24), channel_id=1, source_target_pairs={{0,8},{8,0},{1,9},{9,1},{2,10},{10,2},{3,11},{11,3},{4,12},{12,4},... | collective-permute-start | bytes 2752520 | tf_op jit(solution)/shard_map/ppermute | solution.py:60
  621.9 21.8 %collective-permute-start.129 = (bf16[256,1024]{1,0:T(8,128)(2,1)S(1)}, bf16[256,1024]{1,0:T(8,128)(2,1)S(1)}, u32[]{:S(2)}, u32[]{:S(2)}) collective-permute-start(bf16[256,1024]{1,0:T(8,128)(2,1)S(1)} %dynamic-slice_bitcast_fusion.1), channel_id=1, source_target_pairs={{0,65},{65,0},{1,64},{64,1},{2,67},{67,2},{3,66},{66,3},{4,69},{69... | collective-permute-start | bytes 1572872 | tf_op jit(solution)/shard_map/ppermute | solution.py:52
  672.2 24.0 %collective-permute-start.148 = (bf16[4,80,1024]{2,1,0:T(8,128)(2,1)}, bf16[4,80,1024]{2,1,0:T(8,128)(2,1)}, u32[]{:S(2)}, u32[]{:S(2)}) collective-permute-start(bf16[4,80,1024]{2,1,0:T(8,128)(2,1)} %constant_dynamic-slice_fusion.22), channel_id=1, source_target_pairs={{0,8},{8,0},{1,9},{9,1},{2,10},{10,2},{3,11},{11,3},{4,12},{12,4},... | collective-permute-start | bytes 1966088 | tf_op jit(solution)/shard_map/ppermute | solution.py:60
  (334 other events, 3635.8 us)

commit v2 on v1

--- a/solution.py
+++ b/solution.py
@@ -54,6 +54,10 @@
 
 def y_copy(a):
     return lax.ppermute(a, "ylo", [(0, 1), (1, 0)])
+
+
+def y_far(a):
+    return lax.ppermute(a, "yhi", [(0, 1), (1, 0)])
 
 
 def swap(a):
@@ -96,6 +100,55 @@
     return jnp.stack([first, second], axis=axis)
 
 
+def after(a, earlier):
+    there = jnp.abs(earlier[0, 0].astype(f32)) < 1e30
+    return jnp.where(there, a, jnp.zeros_like(a))
+
+
+def select_kernel(at_ref, up_a, up_b, q_ref, k_ref, v_ref, down_ref, proj_ref, by_z_ref, by_x_ref):
+    first = at_ref[1] == 0
+    by_z_ref[0, :, 0:256] = up_a[0]
+    by_z_ref[0, :, 256:512] = up_b[0]
+    for t, ref in enumerate((q_ref, k_ref, v_ref)):
+        low = jnp.where(first, ref[0, :, 0:64].astype(f32), ref[0, :, 64:128].astype(f32))
+        high = jnp.where(first, ref[0, :, 128:192].astype(f32), ref[0, :, 192:256].astype(f32))
+        by_z_ref[0, :, 512 + t * 128 : 640 + t * 128] = jnp.concatenate([low, high], axis=1).astype(bf16)
+    by_x_ref[0, 0:256] = down_ref[0]
+    by_x_ref[0, 256:320] = proj_ref[0]
+
+
+def select_weights(at, w_qkv, w_proj, w_up, w_down):
+    def lanes(block):
+        return pl.BlockSpec((1, 128, 256), lambda l, at: (l, 0, block(at)))
+
+    return pl.pallas_call(
+        select_kernel,
+        out_shape=(
+            jax.ShapeDtypeStruct((LAYERS, 128, 896), bf16),
+            jax.ShapeDtypeStruct((LAYERS, 320, D), bf16),
+        ),
+        grid_spec=pltpu.PrefetchScalarGridSpec(
+            num_scalar_prefetch=1,
+            grid=(LAYERS,),
+            in_specs=[
+                lanes(lambda at: 4 * at[0] + at[1]),
+                lanes(lambda at: 4 * at[0] + 2 + at[1]),
+                lanes(lambda at: at[0]),
+                lanes(lambda at: 4 + at[0]),
+                lanes(lambda at: 8 + at[0]),
+                pl.BlockSpec((1, 256, D), lambda l, at: (l, at[1], 0)),
+                pl.BlockSpec((1, 64, D), lambda l, at: (l, at[1], 0)),
+            ],
+            out_specs=(
+                pl.BlockSpec((1, 128, 896), lambda l, at: (l, 0, 0)),
+                pl.BlockSpec((1, 320, D), lambda l, at: (l, 0, 0)),
+            ),
+        ),
+        compiler_params=pltpu.CompilerParams(vmem_limit_bytes=8 * 1024 * 1024),
+        cost_estimate=pl.CostEstimate(flops=0, bytes_accessed=4 * 1024 * 1024, transcendentals=0),
+    )(at, w_up, w_up, w_qkv, w_qkv, w_qkv, w_down, w_proj)
+
+
 def take_kernel(order_ref, in_ref, out_ref):
     for block in range(8):
         at = pl.multiple_of(order_ref[block] * 128, 128)
@@ -131,14 +184,15 @@
 
 
 def attend_kernel(slope_ref, rows_ref, cols_ref, qkv_ref, ctx_ref):
-    pair = pl.program_id(1)
+    first = pl.program_id(1) * 4
     seen, distance = visibility(rows_ref[0], cols_ref[0])
     done = []
-    for e in range(2):
-        q = qkv_ref[:, e * 64 : e * 64 + 64]
-        k = qkv_ref[:, 128 + e * 64 : 192 + e * 64]
-        v = qkv_ref[:, 256 + e * 64 : 320 + e * 64]
-        s = head_scores(q, k, seen, distance, slope_ref[pair * 2 + e])
+    for i in range(4):
+        at = (i // 2) * 384 + (i % 2) * 64
+        q = qkv_ref[:, at : at + 64]
+        k = qkv_ref[:, at + 128 : at + 192]
+        v = qkv_ref[:, at + 256 : at + 320]
+        s = head_scores(q, k, seen, distance, slope_ref[first + i])
         top = jnp.max(s, axis=-1, keepdims=True)
         lse = top + jnp.log(jnp.sum(jnp.exp(s - top), axis=-1, keepdims=True))
         p = jnp.exp(s - lse).astype(bf16)
@@ -147,17 +201,18 @@
 
 
 def attend_back_kernel(slope_ref, rows_ref, cols_ref, qkv_ref, ctx_ref, dctx_ref, dqkv_ref, dq_ref, dv_ref):
-    pair = pl.program_id(1)
+    first = pl.program_id(1) * 4
     seen, distance = visibility(rows_ref[0], cols_ref[0])
     dqs, dks, dvs = [], [], []
     tn = (((0,), (0,)), ((), ()))
     nt = (((1,), (1,)), ((), ()))
-    for e in range(2):
-        lanes = slice(e * 64, e * 64 + 64)
-        q = qkv_ref[:, e * 64 : e * 64 + 64]
-        k = qkv_ref[:, 128 + e * 64 : 192 + e * 64]
-        v = qkv_ref[:, 256 + e * 64 : 320 + e * 64]
-        s = head_scores(q, k, seen, distance, slope_ref[pair * 2 + e])
+    for i in range(4):
+        lanes = slice(i * 64, i * 64 + 64)
+        at = (i // 2) * 384 + (i % 2) * 64
+        q = qkv_ref[:, at : at + 64]
+        k = qkv_ref[:, at + 128 : at + 192]
+        v = qkv_ref[:, at + 256 : at + 320]
+        s = head_scores(q, k, seen, distance, slope_ref[first + i])
         top = jnp.max(s, axis=-1, keepdims=True)
         lse = top + jnp.log(jnp.sum(jnp.exp(s - top), axis=-1, keepdims=True))
         p = jnp.exp(s - lse)
@@ -169,52 +224,55 @@
         dqs.append(jnp.dot(ds, k, preferred_element_type=f32) * HEAD_DIM ** (-0.5))
         dks.append(lax.dot_general(ds, q, tn, preferred_element_type=f32) * HEAD_DIM ** (-0.5))
         dvs.append(dv)
-    dq = jnp.concatenate(dqs, axis=1)
-    dv = jnp.concatenate(dvs, axis=1)
-    dqkv_ref[:, 0:128] = dq.astype(bf16)
-    dqkv_ref[:, 128:256] = jnp.concatenate(dks, axis=1).astype(bf16)
-    dqkv_ref[:, 256:384] = dv.astype(bf16)
-    dq_ref[0, 0] = jnp.sum(dq, axis=0, keepdims=True)
-    dv_ref[0, 0] = jnp.sum(dv, axis=0, keepdims=True)
+    for pair in range(2):
+        at = pair * 384
+        dq = jnp.concatenate(dqs[2 * pair : 2 * pair + 2], axis=1)
+        dk = jnp.concatenate(dks[2 * pair : 2 * pair + 2], axis=1)
+        dv = jnp.concatenate(dvs[2 * pair : 2 * pair + 2], axis=1)
+        dqkv_ref[:, at : at + 128] = dq.astype(bf16)
+        dqkv_ref[:, at + 128 : at + 256] = dk.astype(bf16)
+        dqkv_ref[:, at + 256 : at + 384] = dv.astype(bf16)
+        dq_ref[0, 0, :, pair * 128 : pair * 128 + 128] = jnp.sum(dq, axis=0, keepdims=True)
+        dv_ref[0, 0, :, pair * 128 : pair * 128 + 128] = jnp.sum(dv, axis=0, keepdims=True)
 
 
 def attend(qkv, rows, cols, slopes):
     return pl.pallas_call(
         attend_kernel,
         out_shape=jax.ShapeDtypeStruct((2 * RUN, 512), bf16),
-        grid=(2, 4),
+        grid=(2, 2),
         in_specs=[
             pl.BlockSpec(memory_space=pltpu.SMEM),
             pl.BlockSpec((1, RUN, 1), lambda r, p: (r, 0, 0)),
             pl.BlockSpec((1, 1, RUN), lambda r, p: (r, 0, 0)),
-            pl.BlockSpec((RUN, 384), lambda r, p: (r, p)),
+            pl.BlockSpec((RUN, 768), lambda r, p: (r, p)),
         ],
-        out_specs=pl.BlockSpec((RUN, 128), lambda r, p: (r, p)),
+        out_specs=pl.BlockSpec((RUN, 256), lambda r, p: (r, p)),
         compiler_params=pltpu.CompilerParams(vmem_limit_bytes=8 * 1024 * 1024),
         cost_estimate=pl.CostEstimate(flops=4 * 16 * RUN * RUN * 64, bytes_accessed=1 << 20, transcendentals=32 * RUN * RUN),
     )(slopes, rows, cols, qkv)
 
 
 def attend_back(qkv, ctx, dctx, rows, cols, slopes):
-    row_block = pl.BlockSpec((RUN, 128), lambda r, p: (r, p))
-    sums = pl.BlockSpec((1, 1, 1, 128), lambda r, p: (r, p, 0, 0))
+    row_block = pl.BlockSpec((RUN, 256), lambda r, p: (r, p))
+    sums = pl.BlockSpec((1, 1, 1, 256), lambda r, p: (r, p, 0, 0))
     return pl.pallas_call(
         attend_back_kernel,
         out_shape=(
             jax.ShapeDtypeStruct((2 * RUN, 1536), bf16),
-            jax.ShapeDtypeStruct((2, 4, 1, 128), f32),
-            jax.ShapeDtypeStruct((2, 4, 1, 128), f32),
+            jax.ShapeDtypeStruct((2, 2, 1, 256), f32),
+            jax.ShapeDtypeStruct((2, 2, 1, 256), f32),
         ),
-        grid=(2, 4),
+        grid=(2, 2),
         in_specs=[
             pl.BlockSpec(memory_space=pltpu.SMEM),
             pl.BlockSpec((1, RUN, 1), lambda r, p: (r, 0, 0)),
             pl.BlockSpec((1, 1, RUN), lambda r, p: (r, 0, 0)),
-            pl.BlockSpec((RUN, 384), lambda r, p: (r, p)),
+            pl.BlockSpec((RUN, 768), lambda r, p: (r, p)),
             row_block,
             row_block,
         ],
-        out_specs=(pl.BlockSpec((RUN, 384), lambda r, p: (r, p)), sums, sums),
+        out_specs=(pl.BlockSpec((RUN, 768), lambda r, p: (r, p)), sums, sums),
         compiler_params=pltpu.CompilerParams(vmem_limit_bytes=8 * 1024 * 1024),
         cost_estimate=pl.CostEstimate(flops=10 * 16 * RUN * RUN * 64, bytes_accessed=1 << 21, transcendentals=32 * RUN * RUN),
     )(slopes, rows, cols, qkv, ctx, dctx)
@@ -291,39 +349,37 @@
         picked = lax.dynamic_index_in_dim(vector.reshape(4, 2, 2, 64), core, axis=2, keepdims=False)
         return rolled(picked.reshape(4, 128), z)
 
-    def gather_layer(layer):
-        qkv = w_qkv[layer].reshape(128, 3, 4, 2, 2, 64)
-        qkv = lax.dynamic_index_in_dim(qkv, z, axis=2, keepdims=False)
-        qkv = lax.dynamic_index_in_dim(qkv, core, axis=3, keepdims=False).reshape(128, 384)
-        up = w_up[layer].reshape(128, 4, 2, 2, 256)
-        up = lax.dynamic_index_in_dim(up, z, axis=1, keepdims=False)
-        up = lax.dynamic_index_in_dim(up, core, axis=2, keepdims=False).reshape(128, 512)
-        proj = lax.dynamic_index_in_dim(w_proj[layer].reshape(2, 64, D), core, axis=0, keepdims=False)
-        down = lax.dynamic_index_in_dim(w_down[layer].reshape(2, 256, D), core, axis=0, keepdims=False)
-
-        def by_z(piece):
-            piece = jnp.concatenate([piece, y_pair(piece)])
-            own, following, (top, bottom), previous = ring_gather(piece, x_up, x_down)
-            piece = jnp.concatenate([own, following, top, bottom, previous])
-            own, following, (top, bottom), previous = ring_gather(piece, z_up, z_down)
-            return own, following, jnp.concatenate([top, bottom]), previous
-
-        def by_x(piece):
-            other = y_pair(piece)
-            first = jnp.where(yhi == 0, piece, other)
-            second = jnp.where(yhi == 0, other, piece)
-            piece = jnp.concatenate([first, second])
-            own, following, (top, bottom), previous = ring_gather(piece, x_up, x_down)
-            stack = jnp.stack([own, following, jnp.concatenate([top, bottom]), previous])
-            return rolled(stack, (z - x) % 4).reshape(4 * piece.shape[0], D)
-
-        qkv = jnp.concatenate(by_z(qkv), axis=1)
-        proj = by_x(proj)
-        up = jnp.concatenate(by_z(up), axis=1)
-        down = by_x(down)
-        return qkv, proj, up, down
-
-    weights = [gather_layer(layer) for layer in range(LAYERS)]
+    at = jnp.stack([z, core]).astype(jnp.int32)
+    mine_z, mine_x = select_weights(at, w_qkv, w_proj, w_up, w_down)
+
+    def gather_layer(layer, earlier):
+        piece_z, piece_x = mine_z[layer], mine_x[layer]
+        if earlier:
+            piece_z, piece_x = after(piece_z, earlier[0]), after(piece_x, earlier[0])
+        piece_z = jnp.concatenate([piece_z, y_pair(piece_z)])
+        other = y_pair(piece_x)
+        piece_x = jnp.concatenate([jnp.where(yhi == 0, piece_x, other), jnp.where(yhi == 0, other, piece_x)])
+        own, following, (top, bottom), previous = ring_gather(piece_z, x_up, x_down)
+        near = top
+        piece_z = jnp.concatenate([own, following, top, bottom, previous])
+        if earlier:
+            piece_z, piece_x = after(piece_z, earlier[1]), after(piece_x, earlier[2])
+        own, following, (top, bottom), previous = ring_gather(piece_z, z_up, z_down)
+        far_z = top
+        blocks = (own, following, jnp.concatenate([top, bottom]), previous)
+        up = jnp.concatenate([block[:, :512] for block in blocks], axis=1)
+        qkv = jnp.concatenate([block[:, 512:] for block in blocks], axis=1)
+        own, following, (top, bottom), previous = ring_gather(piece_x, x_up, x_down)
+        stack = jnp.stack([own, following, jnp.concatenate([top, bottom]), previous])
+        stack = rolled(stack, (z - x) % 4).reshape(4, 2, 320, D)
+        down = stack[:, :, :256].reshape(2048, D)
+        proj = stack[:, :, 256:].reshape(512, D)
+        return (qkv, proj, up, down), (near, far_z, top)
+
+    weights, earlier = [], ()
+    for layer in range(LAYERS):
+        gathered, earlier = gather_layer(layer, earlier)
+        weights.append(gathered)
 
     starts = both(doc_start.reshape(1, RUN))
     rows, cols = starts.reshape(2, RUN, 1), starts.reshape(2, 1, RUN)
@@ -352,33 +408,44 @@
         kept.append((first_in, normed_one, inv_one, qkv, ctx, second_in, normed_two, inv_two, upper, activ, gain_one, gain_two))
     hidden_out = current
 
-    def blocks_by_z(left, right, width):
-        parts = [dot_tn(left, right[:, i * width : (i + 1) * width]).astype(bf16) for i in range(4)]
+    def over_y(part):
+        keep = lax.dynamic_index_in_dim(part, yhi, axis=0, keepdims=False)
+        give = lax.dynamic_index_in_dim(part, 1 - yhi, axis=0, keepdims=False)
+        near = keep.astype(f32) + y_copy(keep).astype(f32)
+        return (near + (y_pair(give).astype(f32) + y_far(give).astype(f32))).astype(bf16)
+
+    def over_z_pieces(part):
+        stack = jnp.stack([part, z_down(part), z_far(part), z_up(part)])
+        return ordered_by_core(rolled(stack, (4 - z) % 4), core, 0)
+
+    def blocks_by_z(pairs):
+        parts = []
+        for i in range(4):
+            parts.append(
+                jnp.concatenate(
+                    [dot_tn(left, right[:, i * w : (i + 1) * w]).astype(bf16) for left, right, w in pairs], axis=1
+                )
+            )
         part = ring_scatter(parts, z_up, z_down).astype(bf16)
         part = ring_scatter([part[i * 256 : (i + 1) * 256] for i in range(4)], x_up, x_down).astype(bf16)
-        part = part[:128].astype(f32) + y_pair(part[128:]).astype(f32)
-        return part.astype(bf16)
-
-    def blocks_by_x(left, right, width):
+        part = part.reshape(2, 128, part.shape[1])
+        return over_z_pieces(over_y(jnp.where(yhi == 0, part, part[::-1])))
+
+    def blocks_by_x(pairs):
         parts = []
         for i in range(4):
-            at = ((x + i - z) % 4) * width
-            parts.append(dot_tn(lax.dynamic_slice_in_dim(left, at, width, axis=1), right).astype(bf16))
-        part = ring_scatter(parts, x_up, x_down).astype(bf16).reshape(2, width // 2, D)
-        keep = lax.dynamic_index_in_dim(part, yhi, axis=0, keepdims=False)
-        give = lax.dynamic_index_in_dim(part, 1 - yhi, axis=0, keepdims=False)
-        part = (keep.astype(f32) + y_pair(give).astype(f32)).astype(bf16).reshape(4, width // 8, D)
-        parts = rolled(part, z)
-        return ring_scatter([parts[i] for i in range(4)], z_up, z_down).astype(bf16)
-
-    def shared(part):
-        part = (part.astype(f32) + y_copy(part).astype(f32)).astype(bf16)
-        own, following, (top, bottom), previous = ring_gather(part, z_up, z_down)
-        stack = rolled(jnp.stack([own, following, jnp.concatenate([top, bottom]), previous]), (4 - z) % 4)
-        return ordered_by_core(stack, core, 0)
+            block = []
+            for left, right, w in pairs:
+                own = lax.dynamic_slice_in_dim(left, ((x + i - z) % 4) * w, w, axis=1)
+                block.append(dot_tn(own, right).astype(bf16).reshape(2, 4, w // 8, D))
+            parts.append(jnp.concatenate(block, axis=2).reshape(640, D))
+        part = ring_scatter(parts, x_up, x_down).astype(bf16).reshape(2, 4, 80, D)
+        parts = rolled(jnp.transpose(part, (1, 0, 2, 3)), z).reshape(4, 160, D)
+        part = ring_scatter([parts[i] for i in range(4)], z_up, z_down).astype(bf16)
+        return over_z_pieces(over_y(part.reshape(2, 80, D)))
 
     grads = [None] * LAYERS
-    small_grads = [None] * LAYERS
+    thin_grads, head_grads, unit_grads = [None] * LAYERS, [None] * LAYERS, [None] * LAYERS
     running = grad_out
     for layer in reversed(range(LAYERS)):
         wqkv, wproj, wup, wdown = weights[layer]
@@ -388,48 +455,47 @@
         grad_upper = dot_nt(grad_yb, wdown) * gelu_slope(upper)
         g_ubias = jnp.sum(grad_upper, axis=0)
         grad_ub = grad_upper.astype(bf16)
-        p_down = blocks_by_x(activ, grad_yb, 512)
-        p_up = blocks_by_z(second_in, grad_ub, 512)
         grad_two = take_blocks(halves_summed(dot_nt(grad_ub, wup)), to_abs)
         back_two, g_gain_two, g_shift_two = norm_back(grad_two, normed_two, inv_two, gain_two)
         grad_mid = running + back_two
         g_bproj = jnp.sum(grad_mid, axis=0)
         grad_midb = both(grad_mid.astype(bf16))
         grad_ctx = dot_nt(grad_midb, wproj).astype(bf16)
-        p_proj = blocks_by_x(ctx, grad_midb, 128)
+        by_x = blocks_by_x([(activ, grad_yb, 512), (ctx, grad_midb, 128)])
         grad_qkv, g_bq, g_bv = attend_back(qkv, ctx, grad_ctx, rows, cols, slopes)
-        p_qkv = blocks_by_z(first_in, grad_qkv, 384)
+        by_z = blocks_by_z([(second_in, grad_ub, 512), (first_in, grad_qkv, 384)])
         grad_one = take_blocks(halves_summed(dot_nt(grad_qkv, wqkv)), to_abs)
         back_one, g_gain_one, g_shift_one = norm_back(grad_one, normed_one, inv_one, gain_one)
         running = grad_mid + back_one
 
-        def spread_heads(sums):
-            sums = rolled(jnp.sum(sums, axis=0).reshape(4, 128), (4 - z) % 4).reshape(4, 2, 1, 64)
-            mine = lax.broadcasted_iota(jnp.int32, (4, 2, 2, 64), 2) == core
-            return jnp.where(mine, sums, 0.0).reshape(D)
-
-        hidden = rolled(g_ubias.reshape(4, 512), (4 - z) % 4).reshape(4, 2, 1, 256)
-        mine = lax.broadcasted_iota(jnp.int32, (4, 2, 2, 256), 2) == core
-        hidden = jnp.where(mine, hidden, 0.0).reshape(4, 2, 4, 128)
-        thin = jnp.stack([g_gain_one, g_gain_two, g_shift_one, g_shift_two, spread_heads(g_bq), spread_heads(g_bv), g_bproj, g_bdown])
-        thin = jnp.transpose(thin.reshape(8, 4, 2, 128), (1, 2, 0, 3))
-        small_grads[layer] = jnp.concatenate([thin, hidden], axis=2)
-
-        by_x = shared(jnp.concatenate([p_down, p_proj]))
-        by_z = shared(jnp.concatenate([p_up, p_qkv], axis=1))
+        thin_grads[layer] = [g_gain_one, g_gain_two, g_shift_one, g_shift_two, g_bproj, g_bdown]
+        head_grads[layer] = [jnp.sum(g, axis=0).reshape(4, 128) for g in (g_bq, g_bv)]
+        unit_grads[layer] = g_ubias.reshape(4, 512)
+
         g_down = by_x[:, :, :64].reshape(512, D)
         g_proj = by_x[:, :, 64:].reshape(128, D)
         g_up = jnp.transpose(by_z[..., :512].reshape(2, 4, 128, 2, 256), (2, 1, 3, 0, 4)).reshape(128, 4096)
         g_qkv = jnp.transpose(by_z[..., 512:].reshape(2, 4, 128, 3, 2, 64), (2, 3, 1, 4, 0, 5)).reshape(128, 3072)
         grads[layer] = (g_qkv, g_proj, g_up, g_down)
 
-    part = jnp.concatenate(small_grads, axis=2)
+    thin = jnp.stack(thin_grads[0] + thin_grads[1]).reshape(LAYERS, 6, 4, 2, 128)
+    heads = jnp.stack(head_grads[0] + head_grads[1], axis=1)
+    heads = rolled(heads, (4 - z) % 4).reshape(4, LAYERS, 2, 2, 1, 64)
+    mine = lax.broadcasted_iota(jnp.int32, (4, LAYERS, 2, 2, 2, 64), 4) == core
+    heads = jnp.where(mine, heads, 0.0).reshape(4, LAYERS, 2, 2, 128)
+    units = rolled(jnp.stack(unit_grads, axis=1), (4 - z) % 4).reshape(4, LAYERS, 2, 1, 256)
+    mine = lax.broadcasted_iota(jnp.int32, (4, LAYERS, 2, 2, 256), 3) == core
+    units = jnp.where(mine, units, 0.0).reshape(4, LAYERS, 2, 4, 128)
+    thin = jnp.transpose(thin, (2, 3, 0, 1, 4))
+    heads = jnp.transpose(heads, (0, 3, 1, 2, 4))
+    units = jnp.transpose(units, (0, 2, 1, 3, 4))
+    part = jnp.concatenate([thin[:, :, :, :4], heads, thin[:, :, :, 4:], units], axis=3)
+    part = part.reshape(4, 2, 24, 128)
     part = rolled(part, x)
     part = part[0] + x_up(part[1]) + x_far(part[2]) + x_down(part[3])
     keep = lax.dynamic_index_in_dim(part, yhi, axis=0, keepdims=False)
     give = lax.dynamic_index_in_dim(part, 1 - yhi, axis=0, keepdims=False)
-    part = keep + y_pair(give)
-    part = part + y_copy(part)
+    part = (keep + y_copy(keep)) + (y_pair(give) + y_far(give))
     part = part + swap(part)
     part = rolled(jnp.stack([part, z_down(part), z_far(part), z_up(part)]), (4 - z) % 4)
     part = part[0] + part[1] + part[2] + part[3]

time: 726 us -> 712 us (0.981)
  starting transfers between devices: 285 us -> 166 us
  waiting for transfers between devices: 174 us -> 212 us
  local copies, waits for them, and re-layouts: 86.9 us -> 112 us
  matrix products: 52.3 us -> 75.8 us
  other arithmetic: 67.2 us -> 89.1 us
    ppermute x22, starting transfers between devices: 95.2 us -> 49.9 us  [swap(): return lax.ppermute(a, 'core', [(0, 1), (1, 0)])]
    ppermute x34 -> x18, starting transfers between devices: 70.6 us -> 36.8 us  [x_down(): return lax.ppermute(a, 'x', ring(3))]
    ppermute x33 -> x17, waiting for transfers between devices: 16.5 us -> 46.1 us  [z_down(): return lax.ppermute(a, 'z', ring(3))]
    ppermute x33 -> x17, starting transfers between devices: 60.3 us -> 33.8 us  [z_down(): return lax.ppermute(a, 'z', ring(3))]
    dot_general x32, matrix products: 27.7 us -> 48.4 us  [dot_tn(): lax.dot_general(a, b, (((0,), (0,)), ((), ())), preferred_element_type=f32)]
    slice x33 -> x29, local copies, waits for them, and re-layouts: 6.56 us -> 26.2 us  [the longest x8 10.6 us: gather_layer(): qkv = jnp.concatenate([block[:, 512:] for block in blocks], axis=1)]
    concatenate x12 -> x16, other arithmetic: 3.86 us -> 16.9 us  [the longest x8 7.89 us: blocks_by_x(): parts.append(jnp.concatenate(block, axis=2).reshape(640, D))]
    unnamed x455 -> x412, local copies, waits for them, and re-layouts: 28.8 us -> 41.8 us
  transfers between devices with their start and end apart: 182 -> 119, of which waited for: 64 -> 49; matrix products, arithmetic and copies ran while one was open for 25% -> 34% of each run, Pallas kernels for 6% -> 3%
where the time goes in v2:
time: 712 us; the launch traced here: 700 us
  waiting for transfers between devices  212 us (30%)
  starting transfers between devices  166 us (23%)
  local copies, waits for them, and re-layouts  112 us (16%)
  other arithmetic  89.1 us (13%)
  matrix products  75.8 us (11%)
  Pallas kernels  38.9 us (5%)
    ppermute x17, waiting for transfers between devices, z_up(): return lax.ppermute(a, 'z', ring(1))  66.2 us
    ppermute x22, starting transfers between devices, swap(): return lax.ppermute(a, 'core', [(0, 1), (1, 0)])  49.9 us
    dot_general x32, matrix products, dot_tn(): lax.dot_general(a, b, (((0,), (0,)), ((), ())), preferred_element_type=f32)  48.4 us
    ppermute x18, waiting for transfers between devices, x_up(): return lax.ppermute(a, 'x', ring(1))  47.3 us
    ppermute x17, waiting for transfers between devices, z_down(): return lax.ppermute(a, 'z', ring(3))  46.1 us
    unnamed x412, local copies, waits for them, and re-layouts  41.8 us
    ppermute x18, starting transfers between devices, x_down(): return lax.ppermute(a, 'x', ring(3))  36.8 us
    ppermute x17, starting transfers between devices, z_down(): return lax.ppermute(a, 'z', ring(3))  33.8 us
  transfers between devices with their start and end apart: 119, of which 49 were waited for; matrix products, arithmetic and copies ran while one was open for 34% of the time, Pallas kernels for 3%

profile of v2, /device:TPU:1, one launch (start us, length us, event | category | flops | bytes accessed | tf_op | source)
XLA Modules:
  0.0 700.4 jit_solution(13685470542248219746)
XLA Ops:
  7.6 3.6 collective-permute-start.6
  20.4 2.9 collective-permute-done.3
  25.2 9.5 %collective-permute-done.8 = bf16[256,896]{1,0:T(8,128)(2,1)S(1)} collective-permute-done((bf16[256,896]{1,0:T(8,128)(2,1)}, bf16[256,896]{1,0:T(8,128)(2,1)S(1)}, u32[]{:S(2)}, u32[]{:S(2)}) %collective-permute-start.8) | collective-permute-done | bytes 458784 | tf_op jit(solution)/shard_map/ppermute | solution.py:28
  37.9 2.7 collective-permute-start.7
  64.9 2.7 collective-permute-start.16
  101.3 12.3 %collective-permute-start.5 = (bf16[128,1024]{1,0:T(8,128)(2,1)S(1)}, bf16[128,1024]{1,0:T(8,128)(2,1)}, u32[]{:S(2)}, u32[]{:S(2)}) collective-permute-start(bf16[128,1024]{1,0:T(8,128)(2,1)S(1)} %shard_map.169), channel_id=1, source_target_pairs={{0,8},{8,0},{1,9},{9,1},{2,10},{10,2},{3,11},{11,3},{4,12},{12,4},... | collective-permute-start | bytes 786440 | tf_op jit(solution)/shard_map/ppermute | solution.py:64
  117.7 3.6 collective-permute-start.28
  132.3 17.9 %collective-permute-done.13 = bf16[512,896]{1,0:T(8,128)(2,1)S(1)} collective-permute-done((bf16[512,896]{1,0:T(8,128)(2,1)}, bf16[512,896]{1,0:T(8,128)(2,1)S(1)}, u32[]{:S(2)}, u32[]{:S(2)}) %collective-permute-start.13) | collective-permute-done | bytes 917536 | tf_op jit(solution)/shard_map/ppermute | solution.py:40
  154.4 7.0 %shard_map.171.ctx_ref = bf16[256,512]{1,0:T(8,128)(2,1)S(1)} custom-call(f32[8]{0:T(128)S(1)} %multiply_power_fusion.slope_ref, s32[2,128,1]{2,1,0:T(8,128)S(1)} %copy.69.rows_ref, s32[2,1,128]{2,1,0:T(1,128)S(1)} %bitcast.393, bf16[256,1536]{1,0:T(8,128)(2,1)S(1)} %fusion.8.qkv_ref), custom_call_target="tpu_custom_call" | custom-call | flops 67108864 | bytes 1048576 | tf_op jit(solution)/shard_map/pallas_call | solution.py:240
  178.6 2.9 multiply_convert_fusion.1
  185.3 2.8 collective-permute-start.29
  191.6 9.9 %collective-permute-done.34 = bf16[640,1024]{1,0:T(8,128)(2,1)} collective-permute-done((bf16[640,1024]{1,0:T(8,128)(2,1)}, bf16[640,1024]{1,0:T(8,128)(2,1)}, u32[]{:S(2)}, u32[]{:S(2)}) %collective-permute-start.34) | collective-permute-done | bytes 1310752 | tf_op jit(solution)/shard_map/ppermute | solution.py:32
  202.6 2.7 collective-permute-start.37
  212.5 6.1 collective-permute-done.37
  218.6 4.7 collective-permute-done.36
  227.7 3.4 collective-permute-start.32
  235.5 10.3 %collective-permute-done.31 = bf16[512,896]{1,0:T(8,128)(2,1)S(1)} collective-permute-done((bf16[512,896]{1,0:T(8,128)(2,1)S(1)}, bf16[512,896]{1,0:T(8,128)(2,1)S(1)}, u32[]{:S(2)}, u32[]{:S(2)}) %collective-permute-start.31) | collective-permute-done | bytes 917536 | tf_op jit(solution)/shard_map/ppermute | solution.py:40
  245.9 3.8 collective-permute-done.32
  251.5 7.0 shard_map.174.ctx_ref
  271.4 2.8 slice.924
  280.4 3.9 fusion.178
  305.0 2.8 convolution_convert_fusion
  310.8 9.4 %shard_map.177 = (bf16[256,1536]{1,0:T(8,128)(2,1)S(1)}, f32[2,2,1,256]{3,2,1,0:T(1,128)S(1)}, f32[2,2,1,256]{3,2,1,0:T(1,128)S(1)}) custom-call(f32[8]{0:T(128)S(1)} %multiply_power_fusion.slope_ref, s32[2,128,1]{2,1,0:T(8,128)S(1)} %copy.69.rows_ref, s32[2,1,128]{2,1,0:T(1,128)S(1)} %bitcast.395, bf16[256,1536]{1,0:T(8,128)(2,1)S(1)} %fusion.9.qkv_ref, ...), custom_call_target="tpu_custom_call" | custom-call | flops 167772160 | bytes 2097152 | tf_op jit(solution)/shard_map/pallas_call | solution.py:259
  332.8 3.6 collective-permute-start.66
  385.9 9.4 %shard_map.180 = (bf16[256,1536]{1,0:T(8,128)(2,1)S(1)}, f32[2,2,1,256]{3,2,1,0:T(1,128)S(1)}, f32[2,2,1,256]{3,2,1,0:T(1,128)S(1)}) custom-call(f32[8]{0:T(128)S(1)} %multiply_power_fusion.slope_ref, s32[2,128,1]{2,1,0:T(8,128)S(1)} %copy.69.rows_ref, s32[2,1,128]{2,1,0:T(1,128)S(1)} %bitcast.396, bf16[256,1536]{1,0:T(8,128)(2,1)S(1)} %fusion.8.qkv_ref, ...), custom_call_target="tpu_custom_call" | custom-call | flops 167772160 | bytes 2097152 | tf_op jit(solution)/shard_map/pallas_call | solution.py:259
  422.3 2.7 collective-permute-start.67
  434.6 3.2 collective-permute-start.115
  440.2 23.1 %collective-permute-done.116 = f32[24,128]{1,0:T(8,128)S(1)} collective-permute-done((f32[24,128]{1,0:T(8,128)S(1)}, f32[24,128]{1,0:T(8,128)S(1)}, u32[]{:S(2)}, u32[]{:S(2)}) %collective-permute-start.116) | collective-permute-done | bytes 12320 | tf_op jit(solution)/shard_map/ppermute | solution.py:44
  463.3 2.7 collective-permute-start.117
  468.6 3.5 collective-permute-done.118
  484.8 3.0 add_convert_fusion
  488.0 3.2 collective-permute-done.49
  491.6 19.7 %collective-permute-done.68 = bf16[128,896]{0,1:T(8,128)(2,1)S(1)} collective-permute-done((bf16[128,896]{0,1:T(8,128)(2,1)S(1)}, bf16[128,896]{0,1:T(8,128)(2,1)S(1)}, u32[]{:S(2)}, u32[]{:S(2)}) %collective-permute-start.68) | collective-permute-done | bytes 229408 | tf_op jit(solution)/shard_map/ppermute | solution.py:28
  514.0 2.8 collective-permute-start.71
  538.7 18.5 %collective-permute-done.83 = bf16[80,1024]{1,0:T(8,128)(2,1)S(1)} collective-permute-done((bf16[80,1024]{1,0:T(8,128)(2,1)S(1)}, bf16[80,1024]{1,0:T(8,128)(2,1)S(1)}, u32[]{:S(2)}, u32[]{:S(2)}) %collective-permute-start.83) | collective-permute-done | bytes 163872 | tf_op jit(solution)/shard_map/ppermute | solution.py:40
  565.4 2.7 collective-permute-done.75
  569.8 5.2 collective-permute-start.86
  578.0 3.0 collective-permute-done.86
  583.8 4.2 collective-permute-done.101
  588.2 4.3 collective-permute-done.87
  595.9 4.4 collective-permute-done.102
  600.3 17.6 %collective-permute-start.78 = (bf16[4,128,896]{2,1,0:T(8,128)(2,1)S(1)}, bf16[4,128,896]{2,1,0:T(8,128)(2,1)S(1)}, u32[]{:S(2)}, u32[]{:S(2)}) collective-permute-start(bf16[4,128,896]{2,1,0:T(8,128)(2,1)S(1)} %constant_dynamic-slice_fusion.24), channel_id=1, source_target_pairs={{0,8},{8,0},{1,9},{9,1},{2,10},{10,2},{3,11},{11,3},{4,12},{12,4},... | collective-permute-start | bytes 2752520 | tf_op jit(solution)/shard_map/ppermute | solution.py:64
  622.0 3.0 add_convert_fusion.1
  637.7 2.7 collective-permute-start.56
  643.8 5.6 collective-permute-done.54
  658.6 2.8 collective-permute-done.57
  672.4 5.9 collective-permute-done.62
  690.2 5.7 copy.100
  (977 shorter events, 396.8 us)
Async XLA Ops:
  58.9 25.6 %collective-permute-start.17 = (bf16[640,1024]{1,0:T(8,128)(2,1)}, bf16[640,1024]{1,0:T(8,128)(2,1)S(1)}, u32[]{:S(2)}, u32[]{:S(2)}) collective-permute-start(bf16[640,1024]{1,0:T(8,128)(2,1)} %pad_maximum_fusion.6), channel_id=1, source_target_pairs={{0,2},{2,4},{4,6},{6,0},{1,3},{3,5},{5,7},{7,1},{8,10},{10,12},{12... | collective-permute-start | bytes 3932168 | tf_op jit(solution)/shard_map/ppermute | solution.py:28
  61.1 56.6 %collective-permute-start.12 = (bf16[1024,896]{1,0:T(8,128)(2,1)}, bf16[1024,896]{1,0:T(8,128)(2,1)}, u32[]{:S(2)}, u32[]{:S(2)}) collective-permute-start(bf16[1024,896]{1,0:T(8,128)(2,1)} %constant_dynamic-update-slice_fusion.7), channel_id=1, source_target_pairs={{0,16},{16,32},{32,48},{48,0},{1,17},{17,33},{33,49},{49,1},{2,18}... | collective-permute-start | bytes 5505032 | tf_op jit(solution)/shard_map/ppermute | solution.py:40
  62.8 51.6 %collective-permute-start.11 = (bf16[1024,896]{1,0:T(8,128)(2,1)}, bf16[1024,896]{1,0:T(8,128)(2,1)}, u32[]{:S(2)}, u32[]{:S(2)}) collective-permute-start(bf16[1024,896]{1,0:T(8,128)(2,1)} %constant_dynamic-update-slice_fusion.7), channel_id=1, source_target_pairs={{0,48},{16,0},{32,16},{48,32},{1,49},{17,1},{33,17},{49,33},{2,50}... | collective-permute-start | bytes 5505032 | tf_op jit(solution)/shard_map/ppermute | solution.py:44
  64.9 25.9 %collective-permute-start.16 = (bf16[640,1024]{1,0:T(8,128)(2,1)}, bf16[640,1024]{1,0:T(8,128)(2,1)}, u32[]{:S(2)}, u32[]{:S(2)}) collective-permute-start(bf16[640,1024]{1,0:T(8,128)(2,1)} %pad_maximum_fusion.6), channel_id=1, source_target_pairs={{0,6},{2,0},{4,2},{6,4},{1,7},{3,1},{5,3},{7,5},{8,14},{10,8},{12,... | collective-permute-start | bytes 3932168 | tf_op jit(solution)/shard_map/ppermute | solution.py:32
  94.0 33.1 %collective-permute-start.18 = (bf16[320,1024]{1,0:T(8,128)(2,1)S(1)}, bf16[320,1024]{1,0:T(8,128)(2,1)S(1)}, u32[]{:S(2)}, u32[]{:S(2)}) collective-permute-start(bf16[320,1024]{1,0:T(8,128)(2,1)S(1)} %slice.878), channel_id=1, source_target_pairs={{0,2},{2,4},{4,6},{6,0},{1,3},{3,5},{5,7},{7,1},{8,10},{10,12},{12... | collective-permute-start | bytes 1966088 | tf_op jit(solution)/shard_map/ppermute | solution.py:28
  96.2 31.0 %collective-permute-start.19 = (bf16[320,1024]{1,0:T(8,128)(2,1)S(1)}, bf16[320,1024]{1,0:T(8,128)(2,1)S(1)}, u32[]{:S(2)}, u32[]{:S(2)}) collective-permute-start(bf16[320,1024]{1,0:T(8,128)(2,1)S(1)} %slice.879), channel_id=1, source_target_pairs={{0,6},{2,0},{4,2},{6,4},{1,7},{3,1},{5,3},{7,5},{8,14},{10,8},{12,... | collective-permute-start | bytes 1966088 | tf_op jit(solution)/shard_map/ppermute | solution.py:32
  101.3 50.7 %collective-permute-start.5 = (bf16[128,1024]{1,0:T(8,128)(2,1)S(1)}, bf16[128,1024]{1,0:T(8,128)(2,1)}, u32[]{:S(2)}, u32[]{:S(2)}) collective-permute-start(bf16[128,1024]{1,0:T(8,128)(2,1)S(1)} %shard_map.169), channel_id=1, source_target_pairs={{0,8},{8,0},{1,9},{9,1},{2,10},{10,2},{3,11},{11,3},{4,12},{12,4},... | collective-permute-start | bytes 786440 | tf_op jit(solution)/shard_map/ppermute | solution.py:64
  114.3 48.8 %collective-permute-start.27 = (bf16[128,896]{1,0:T(8,128)(2,1)}, bf16[128,896]{1,0:T(8,128)(2,1)}, u32[]{:S(2)}, u32[]{:S(2)}) collective-permute-start(bf16[128,896]{1,0:T(8,128)(2,1)} %slice.900), channel_id=1, source_target_pairs={{0,2},{2,4},{4,6},{6,0},{1,3},{3,5},{5,7},{7,1},{8,10},{10,12},{12... | collective-permute-start | bytes 688136 | tf_op jit(solution)/shard_map/ppermute | solution.py:28
  117.7 46.4 %collective-permute-start.28 = (bf16[128,896]{1,0:T(8,128)(2,1)}, bf16[128,896]{1,0:T(8,128)(2,1)}, u32[]{:S(2)}, u32[]{:S(2)}) collective-permute-start(bf16[128,896]{1,0:T(8,128)(2,1)} %slice.901), channel_id=1, source_target_pairs={{0,6},{2,0},{4,2},{6,4},{1,7},{3,1},{5,3},{7,5},{8,14},{10,8},{12,... | collective-permute-start | bytes 688136 | tf_op jit(solution)/shard_map/ppermute | solution.py:32
  127.0 23.2 %collective-permute-start.13 = (bf16[512,896]{1,0:T(8,128)(2,1)}, bf16[512,896]{1,0:T(8,128)(2,1)S(1)}, u32[]{:S(2)}, u32[]{:S(2)}) collective-permute-start(bf16[512,896]{1,0:T(8,128)(2,1)} %slice.872), channel_id=1, source_target_pairs={{0,16},{16,32},{32,48},{48,0},{1,17},{17,33},{33,49},{49,1},{2,18}... | collective-permute-start | bytes 2752520 | tf_op jit(solution)/shard_map/ppermute | solution.py:40
  127.1 23.2 %collective-permute-start.14 = (bf16[512,896]{1,0:T(8,128)(2,1)S(1)}, bf16[512,896]{1,0:T(8,128)(2,1)}, u32[]{:S(2)}, u32[]{:S(2)}) collective-permute-start(bf16[512,896]{1,0:T(8,128)(2,1)S(1)} %slice.873), channel_id=1, source_target_pairs={{0,48},{16,0},{32,16},{48,32},{1,49},{17,1},{33,17},{49,33},{2,50}... | collective-permute-start | bytes 2752520 | tf_op jit(solution)/shard_map/ppermute | solution.py:44
  170.8 30.7 %collective-permute-start.34 = (bf16[640,1024]{1,0:T(8,128)(2,1)}, bf16[640,1024]{1,0:T(8,128)(2,1)}, u32[]{:S(2)}, u32[]{:S(2)}) collective-permute-start(bf16[640,1024]{1,0:T(8,128)(2,1)} %maximum_select_fusion.1), channel_id=1, source_target_pairs={{0,6},{2,0},{4,2},{6,4},{1,7},{3,1},{5,3},{7,5},{8,14},{10,8},{12,... | collective-permute-start | bytes 3932168 | tf_op jit(solution)/shard_map/ppermute | solution.py:32
  172.2 33.1 %collective-permute-start.35 = (bf16[640,1024]{1,0:T(8,128)(2,1)}, bf16[640,1024]{1,0:T(8,128)(2,1)}, u32[]{:S(2)}, u32[]{:S(2)}) collective-permute-start(bf16[640,1024]{1,0:T(8,128)(2,1)} %maximum_select_fusion.1), channel_id=1, source_target_pairs={{0,2},{2,4},{4,6},{6,0},{1,3},{3,5},{5,7},{7,1},{8,10},{10,12},{12... | collective-permute-start | bytes 3932168 | tf_op jit(solution)/shard_map/ppermute | solution.py:28
  178.5 45.0 %collective-permute-start.30 = (bf16[1024,896]{1,0:T(8,128)(2,1)}, bf16[1024,896]{1,0:T(8,128)(2,1)}, u32[]{:S(2)}, u32[]{:S(2)}) collective-permute-start(bf16[1024,896]{1,0:T(8,128)(2,1)} %broadcast_select_fusion), channel_id=1, source_target_pairs={{0,16},{16,32},{32,48},{48,0},{1,17},{17,33},{33,49},{49,1},{2,18}... | collective-permute-start | bytes 5505032 | tf_op jit(solution)/shard_map/ppermute | solution.py:40
  184.6 23.9 %collective-permute-start.22 = (f32[128,1024]{1,0:T(8,128)}, f32[128,1024]{1,0:T(8,128)}, u32[]{:S(2)}, u32[]{:S(2)}) collective-permute-start(f32[128,1024]{1,0:T(8,128)} %slice.894), channel_id=1, source_target_pairs={{0,8},{8,0},{1,9},{9,1},{2,10},{10,2},{3,11},{11,3},{4,12},{12,4},... | collective-permute-start | bytes 1572872 | tf_op jit(solution)/shard_map/ppermute | solution.py:64
  185.3 42.4 %collective-permute-start.29 = (bf16[1024,896]{1,0:T(8,128)(2,1)}, bf16[1024,896]{1,0:T(8,128)(2,1)S(1)}, u32[]{:S(2)}, u32[]{:S(2)}) collective-permute-start(bf16[1024,896]{1,0:T(8,128)(2,1)} %broadcast_select_fusion), channel_id=1, source_target_pairs={{0,48},{16,0},{32,16},{48,32},{1,49},{17,1},{33,17},{49,33},{2,50}... | collective-permute-start | bytes 5505032 | tf_op jit(solution)/shard_map/ppermute | solution.py:44
  211.3 38.6 %collective-permute-start.23 = (bf16[128,1024]{1,0:T(8,128)(2,1)S(1)}, bf16[128,1024]{1,0:T(8,128)(2,1)S(1)}, u32[]{:S(2)}, u32[]{:S(2)}) collective-permute-start(bf16[128,1024]{1,0:T(8,128)(2,1)S(1)} %shard_map.173), channel_id=1, source_target_pairs={{0,8},{8,0},{1,9},{9,1},{2,10},{10,2},{3,11},{11,3},{4,12},{12,4},... | collective-permute-start | bytes 786440 | tf_op jit(solution)/shard_map/ppermute | solution.py:64
  224.7 21.1 %collective-permute-start.31 = (bf16[512,896]{1,0:T(8,128)(2,1)S(1)}, bf16[512,896]{1,0:T(8,128)(2,1)S(1)}, u32[]{:S(2)}, u32[]{:S(2)}) collective-permute-start(bf16[512,896]{1,0:T(8,128)(2,1)S(1)} %slice.904), channel_id=1, source_target_pairs={{0,16},{16,32},{32,48},{48,0},{1,17},{17,33},{33,49},{49,1},{2,18}... | collective-permute-start | bytes 2752520 | tf_op jit(solution)/shard_map/ppermute | solution.py:40
  227.7 22.0 %collective-permute-start.32 = (bf16[512,896]{1,0:T(8,128)(2,1)S(1)}, bf16[512,896]{1,0:T(8,128)(2,1)S(1)}, u32[]{:S(2)}, u32[]{:S(2)}) collective-permute-start(bf16[512,896]{1,0:T(8,128)(2,1)S(1)} %slice.905), channel_id=1, source_target_pairs={{0,48},{16,0},{32,16},{48,32},{1,49},{17,1},{33,17},{49,33},{2,50}... | collective-permute-start | bytes 2752520 | tf_op jit(solution)/shard_map/ppermute | solution.py:44
  280.0 23.1 %collective-permute-start.40 = (f32[128,1024]{1,0:T(8,128)S(1)}, f32[128,1024]{1,0:T(8,128)S(1)}, u32[]{:S(2)}, u32[]{:S(2)}) collective-permute-start(f32[128,1024]{1,0:T(8,128)S(1)} %slice.926), channel_id=1, source_target_pairs={{0,8},{8,0},{1,9},{9,1},{2,10},{10,2},{3,11},{11,3},{4,12},{12,4},... | collective-permute-start | bytes 1572872 | tf_op jit(solution)/shard_map/ppermute | solution.py:64
  323.1 21.3 %collective-permute-start.44 = (f32[128,1024]{1,0:T(8,128)}, f32[128,1024]{1,0:T(8,128)}, u32[]{:S(2)}, u32[]{:S(2)}) collective-permute-start(f32[128,1024]{1,0:T(8,128)} %slice.931), channel_id=1, source_target_pairs={{0,8},{8,0},{1,9},{9,1},{2,10},{10,2},{3,11},{11,3},{4,12},{12,4},... | collective-permute-start | bytes 1572872 | tf_op jit(solution)/shard_map/ppermute | solution.py:64
  327.1 22.0 %collective-permute-start.94 = (bf16[320,1024]{1,0:T(8,128)(2,1)S(1)}, bf16[320,1024]{1,0:T(8,128)(2,1)S(1)}, u32[]{:S(2)}, u32[]{:S(2)}) collective-permute-start(bf16[320,1024]{1,0:T(8,128)(2,1)S(1)} %bitcast.446), channel_id=1, source_target_pairs={{0,2},{2,4},{4,6},{6,0},{1,3},{3,5},{5,7},{7,1},{8,10},{10,12},{12... | collective-permute-start | bytes 1966088 | tf_op jit(solution)/shard_map/ppermute | solution.py:28
  327.3 23.2 %collective-permute-start.96 = (bf16[320,1024]{1,0:T(8,128)(2,1)S(1)}, bf16[320,1024]{1,0:T(8,128)(2,1)S(1)}, u32[]{:S(2)}, u32[]{:S(2)}) collective-permute-start(bf16[320,1024]{1,0:T(8,128)(2,1)S(1)} %bitcast.445), channel_id=1, source_target_pairs={{0,6},{2,0},{4,2},{6,4},{1,7},{3,1},{5,3},{7,5},{8,14},{10,8},{12,... | collective-permute-start | bytes 1966088 | tf_op jit(solution)/shard_map/ppermute | solution.py:32
  332.7 44.1 %collective-permute-start.64 = (bf16[512,896]{0,1:T(8,128)(2,1)}, bf16[512,896]{0,1:T(8,128)(2,1)}, u32[]{:S(2)}, u32[]{:S(2)}) collective-permute-start(bf16[512,896]{0,1:T(8,128)(2,1)} %get-tuple-element.122), channel_id=1, source_target_pairs={{0,16},{16,32},{32,48},{48,0},{1,17},{17,33},{33,49},{49,1},{2,18}... | collective-permute-start | bytes 2752520 | tf_op jit(solution)/shard_map/ppermute | solution.py:40
  332.8 42.3 %collective-permute-start.66 = (bf16[512,896]{0,1:T(8,128)(2,1)}, bf16[512,896]{0,1:T(8,128)(2,1)}, u32[]{:S(2)}, u32[]{:S(2)}) collective-permute-start(bf16[512,896]{0,1:T(8,128)(2,1)} %get-tuple-element.123), channel_id=1, source_target_pairs={{0,48},{16,0},{32,16},{48,32},{1,49},{17,1},{33,17},{49,33},{2,50}... | collective-permute-start | bytes 2752520 | tf_op jit(solution)/shard_map/ppermute | solution.py:44
  350.5 77.1 %collective-permute-start.95 = (bf16[640,1024]{1,0:T(8,128)(2,1)}, bf16[640,1024]{1,0:T(8,128)(2,1)}, u32[]{:S(2)}, u32[]{:S(2)}) collective-permute-start(bf16[640,1024]{1,0:T(8,128)(2,1)} %pad_maximum_fusion.11), channel_id=1, source_target_pairs={{0,2},{2,4},{4,6},{6,0},{1,3},{3,5},{5,7},{7,1},{8,10},{10,12},{12... | collective-permute-start | bytes 3932168 | tf_op jit(solution)/shard_map/ppermute | solution.py:28
  351.9 75.7 %collective-permute-start.97 = (bf16[640,1024]{1,0:T(8,128)(2,1)}, bf16[640,1024]{1,0:T(8,128)(2,1)}, u32[]{:S(2)}, u32[]{:S(2)}) collective-permute-start(bf16[640,1024]{1,0:T(8,128)(2,1)} %pad_maximum_fusion.12), channel_id=1, source_target_pairs={{0,6},{2,0},{4,2},{6,4},{1,7},{3,1},{5,3},{7,5},{8,14},{10,8},{12,... | collective-permute-start | bytes 3932168 | tf_op jit(solution)/shard_map/ppermute | solution.py:32
  422.3 60.4 %collective-permute-start.65 = (bf16[1024,896]{0,1:T(8,128)(2,1)}, bf16[1024,896]{0,1:T(8,128)(2,1)}, u32[]{:S(2)}, u32[]{:S(2)}) collective-permute-start(bf16[1024,896]{0,1:T(8,128)(2,1)} %fusion.23), channel_id=1, source_target_pairs={{0,16},{16,32},{32,48},{48,0},{1,17},{17,33},{33,49},{49,1},{2,18}... | collective-permute-start | bytes 5505032 | tf_op jit(solution)/shard_map/ppermute | solution.py:40
  422.3 62.5 %collective-permute-start.67 = (bf16[1024,896]{0,1:T(8,128)(2,1)}, bf16[1024,896]{0,1:T(8,128)(2,1)}, u32[]{:S(2)}, u32[]{:S(2)}) collective-permute-start(bf16[1024,896]{0,1:T(8,128)(2,1)} %pad_maximum_fusion.5), channel_id=1, source_target_pairs={{0,48},{16,0},{32,16},{48,32},{1,49},{17,1},{33,17},{49,33},{2,50}... | collective-permute-start | bytes 5505032 | tf_op jit(solution)/shard_map/ppermute | solution.py:44
  431.9 42.0 %collective-permute-start.79 = (bf16[320,1024]{1,0:T(8,128)(2,1)}, bf16[320,1024]{1,0:T(8,128)(2,1)}, u32[]{:S(2)}, u32[]{:S(2)}) collective-permute-start(bf16[320,1024]{1,0:T(8,128)(2,1)} %bitcast.82), channel_id=1, source_target_pairs={{0,2},{2,4},{4,6},{6,0},{1,3},{3,5},{5,7},{7,1},{8,10},{10,12},{12... | collective-permute-start | bytes 1966088 | tf_op jit(solution)/shard_map/ppermute | solution.py:28
  432.5 46.9 %collective-permute-start.81 = (bf16[320,1024]{1,0:T(8,128)(2,1)}, bf16[320,1024]{1,0:T(8,128)(2,1)}, u32[]{:S(2)}, u32[]{:S(2)}) collective-permute-start(bf16[320,1024]{1,0:T(8,128)(2,1)} %bitcast.88), channel_id=1, source_target_pairs={{0,6},{2,0},{4,2},{6,4},{1,7},{3,1},{5,3},{7,5},{8,14},{10,8},{12,... | collective-permute-start | bytes 1966088 | tf_op jit(solution)/shard_map/ppermute | solution.py:32
  438.6 24.7 %collective-permute-start.116 = (f32[24,128]{1,0:T(8,128)S(1)}, f32[24,128]{1,0:T(8,128)S(1)}, u32[]{:S(2)}, u32[]{:S(2)}) collective-permute-start(f32[24,128]{1,0:T(8,128)S(1)} %get-tuple-element.73), channel_id=1, source_target_pairs={{0,48},{16,0},{32,16},{48,32},{1,49},{17,1},{33,17},{49,33},{2,50}... | collective-permute-start | bytes 36872 | tf_op jit(solution)/shard_map/ppermute | solution.py:44
  472.1 19.1 %collective-permute-start.49 = (bf16[512,896]{0,1:T(8,128)(2,1)}, bf16[512,896]{0,1:T(8,128)(2,1)S(1)}, u32[]{:S(2)}, u32[]{:S(2)}) collective-permute-start(bf16[512,896]{0,1:T(8,128)(2,1)} %get-tuple-element.112), channel_id=1, source_target_pairs={{0,16},{16,32},{32,48},{48,0},{1,17},{17,33},{33,49},{49,1},{2,18}... | collective-permute-start | bytes 2752520 | tf_op jit(solution)/shard_map/ppermute | solution.py:40
  474.0 44.2 %collective-permute-start.51 = (bf16[512,896]{0,1:T(8,128)(2,1)}, bf16[512,896]{0,1:T(8,128)(2,1)S(1)}, u32[]{:S(2)}, u32[]{:S(2)}) collective-permute-start(bf16[512,896]{0,1:T(8,128)(2,1)} %get-tuple-element.113), channel_id=1, source_target_pairs={{0,48},{16,0},{32,16},{48,32},{1,49},{17,1},{33,17},{49,33},{2,50}... | collective-permute-start | bytes 2752520 | tf_op jit(solution)/shard_map/ppermute | solution.py:44
  479.4 49.1 %collective-permute-start.80 = (bf16[640,1024]{1,0:T(8,128)(2,1)}, bf16[640,1024]{1,0:T(8,128)(2,1)}, u32[]{:S(2)}, u32[]{:S(2)}) collective-permute-start(bf16[640,1024]{1,0:T(8,128)(2,1)} %pad_maximum_fusion.8), channel_id=1, source_target_pairs={{0,2},{2,4},{4,6},{6,0},{1,3},{3,5},{5,7},{7,1},{8,10},{10,12},{12... | collective-permute-start | bytes 3932168 | tf_op jit(solution)/shard_map/ppermute | solution.py:28
  482.7 45.9 %collective-permute-start.82 = (bf16[640,1024]{1,0:T(8,128)(2,1)}, bf16[640,1024]{1,0:T(8,128)(2,1)}, u32[]{:S(2)}, u32[]{:S(2)}) collective-permute-start(bf16[640,1024]{1,0:T(8,128)(2,1)} %pad_maximum_fusion.9), channel_id=1, source_target_pairs={{0,6},{2,0},{4,2},{6,4},{1,7},{3,1},{5,3},{7,5},{8,14},{10,8},{12,... | collective-permute-start | bytes 3932168 | tf_op jit(solution)/shard_map/ppermute | solution.py:32
  487.9 23.4 %collective-permute-start.68 = (bf16[128,896]{0,1:T(8,128)(2,1)S(1)}, bf16[128,896]{0,1:T(8,128)(2,1)S(1)}, u32[]{:S(2)}, u32[]{:S(2)}) collective-permute-start(bf16[128,896]{0,1:T(8,128)(2,1)S(1)} %get-tuple-element.118), channel_id=1, source_target_pairs={{0,2},{2,4},{4,6},{6,0},{1,3},{3,5},{5,7},{7,1},{8,10},{10,12},{12... | collective-permute-start | bytes 688136 | tf_op jit(solution)/shard_map/ppermute | solution.py:28
  491.2 21.8 %collective-permute-start.70 = (bf16[128,896]{0,1:T(8,128)(2,1)S(1)}, bf16[128,896]{0,1:T(8,128)(2,1)S(1)}, u32[]{:S(2)}, u32[]{:S(2)}) collective-permute-start(bf16[128,896]{0,1:T(8,128)(2,1)S(1)} %get-tuple-element.119), channel_id=1, source_target_pairs={{0,6},{2,0},{4,2},{6,4},{1,7},{3,1},{5,3},{7,5},{8,14},{10,8},{12,... | collective-permute-start | bytes 688136 | tf_op jit(solution)/shard_map/ppermute | solution.py:32
  518.2 100.3 %collective-permute-start.50 = (bf16[1024,896]{0,1:T(8,128)(2,1)}, bf16[1024,896]{0,1:T(8,128)(2,1)}, u32[]{:S(2)}, u32[]{:S(2)}) collective-permute-start(bf16[1024,896]{0,1:T(8,128)(2,1)} %fusion.21), channel_id=1, source_target_pairs={{0,16},{16,32},{32,48},{48,0},{1,17},{17,33},{33,49},{49,1},{2,18}... | collective-permute-start | bytes 5505032 | tf_op jit(solution)/shard_map/ppermute | solution.py:40
  522.5 97.1 %collective-permute-start.52 = (bf16[1024,896]{0,1:T(8,128)(2,1)}, bf16[1024,896]{0,1:T(8,128)(2,1)}, u32[]{:S(2)}, u32[]{:S(2)}) collective-permute-start(bf16[1024,896]{0,1:T(8,128)(2,1)} %pad_maximum_fusion.4), channel_id=1, source_target_pairs={{0,48},{16,0},{32,16},{48,32},{1,49},{17,1},{33,17},{49,33},{2,50}... | collective-permute-start | bytes 5505032 | tf_op jit(solution)/shard_map/ppermute | solution.py:44
  535.6 21.6 %collective-permute-start.83 = (bf16[80,1024]{1,0:T(8,128)(2,1)S(1)}, bf16[80,1024]{1,0:T(8,128)(2,1)S(1)}, u32[]{:S(2)}, u32[]{:S(2)}) collective-permute-start(bf16[80,1024]{1,0:T(8,128)(2,1)S(1)} %get-tuple-element.128), channel_id=1, source_target_pairs={{0,16},{16,32},{32,48},{48,0},{1,17},{17,33},{33,49},{49,1},{2,18}... | collective-permute-start | bytes 491528 | tf_op jit(solution)/shard_map/ppermute | solution.py:40
  536.1 23.5 %collective-permute-start.85 = (bf16[80,1024]{1,0:T(8,128)(2,1)S(1)}, bf16[80,1024]{1,0:T(8,128)(2,1)S(1)}, u32[]{:S(2)}, u32[]{:S(2)}) collective-permute-start(bf16[80,1024]{1,0:T(8,128)(2,1)S(1)} %get-tuple-element.130), channel_id=1, source_target_pairs={{0,48},{16,0},{32,16},{48,32},{1,49},{17,1},{33,17},{49,33},{2,50}... | collective-permute-start | bytes 491528 | tf_op jit(solution)/shard_map/ppermute | solution.py:44
  538.3 24.9 %collective-permute-start.100 = (bf16[80,1024]{1,0:T(8,128)(2,1)S(1)}, bf16[80,1024]{1,0:T(8,128)(2,1)S(1)}, u32[]{:S(2)}, u32[]{:S(2)}) collective-permute-start(bf16[80,1024]{1,0:T(8,128)(2,1)S(1)} %get-tuple-element.144), channel_id=1, source_target_pairs={{0,48},{16,0},{32,16},{48,32},{1,49},{17,1},{33,17},{49,33},{2,50}... | collective-permute-start | bytes 491528 | tf_op jit(solution)/shard_map/ppermute | solution.py:44
  592.5 25.4 %collective-permute-start.103 = (bf16[80,1024]{1,0:T(8,128)(2,1)S(1)}, bf16[80,1024]{1,0:T(8,128)(2,1)S(1)}, u32[]{:S(2)}, u32[]{:S(2)}) collective-permute-start(bf16[80,1024]{1,0:T(8,128)(2,1)S(1)} %get-tuple-element.167), channel_id=1, source_target_pairs={{0,65},{65,0},{1,64},{64,1},{2,67},{67,2},{3,66},{66,3},{4,69},{69... | collective-permute-start | bytes 491528 | tf_op jit(solution)/shard_map/ppermute | solution.py:52
  595.0 23.4 %collective-permute-start.104 = (bf16[80,1024]{1,0:T(8,128)(2,1)S(1)}, bf16[80,1024]{1,0:T(8,128)(2,1)S(1)}, u32[]{:S(2)}, u32[]{:S(2)}) collective-permute-start(bf16[80,1024]{1,0:T(8,128)(2,1)S(1)} %get-tuple-element.167), channel_id=1, source_target_pairs={{0,1},{1,0},{2,3},{3,2},{4,5},{5,4},{6,7},{7,6},{8,9},{9,8},{10,11... | collective-permute-start | bytes 491528 | tf_op jit(solution)/shard_map/ppermute | solution.py:60
  600.3 43.4 %collective-permute-start.78 = (bf16[4,128,896]{2,1,0:T(8,128)(2,1)S(1)}, bf16[4,128,896]{2,1,0:T(8,128)(2,1)S(1)}, u32[]{:S(2)}, u32[]{:S(2)}) collective-permute-start(bf16[4,128,896]{2,1,0:T(8,128)(2,1)S(1)} %constant_dynamic-slice_fusion.24), channel_id=1, source_target_pairs={{0,8},{8,0},{1,9},{9,1},{2,10},{10,2},{3,11},{11,3},{4,12},{12,4},... | collective-permute-start | bytes 2752520 | tf_op jit(solution)/shard_map/ppermute | solution.py:64
  633.3 31.3 %collective-permute-start.93 = (bf16[4,80,1024]{2,1,0:T(8,128)(2,1)}, bf16[4,80,1024]{2,1,0:T(8,128)(2,1)}, u32[]{:S(2)}, u32[]{:S(2)}) collective-permute-start(bf16[4,80,1024]{2,1,0:T(8,128)(2,1)} %constant_dynamic-slice_fusion.22), channel_id=1, source_target_pairs={{0,8},{8,0},{1,9},{9,1},{2,10},{10,2},{3,11},{11,3},{4,12},{12,4},... | collective-permute-start | bytes 1966088 | tf_op jit(solution)/shard_map/ppermute | solution.py:64
  641.4 39.1 %collective-permute-start.108 = (bf16[4,80,1024]{2,1,0:T(8,128)(2,1)}, bf16[4,80,1024]{2,1,0:T(8,128)(2,1)}, u32[]{:S(2)}, u32[]{:S(2)}) collective-permute-start(bf16[4,80,1024]{2,1,0:T(8,128)(2,1)} %constant_dynamic-slice_fusion.20), channel_id=1, source_target_pairs={{0,8},{8,0},{1,9},{9,1},{2,10},{10,2},{3,11},{11,3},{4,12},{12,4},... | collective-permute-start | bytes 1966088 | tf_op jit(solution)/shard_map/ppermute | solution.py:64
  (249 other events, 1782.4 us)

commit v3 on v2

--- a/solution.py
+++ b/solution.py
@@ -24,18 +24,6 @@
     return [(i, (i + step) % 4) for i in range(4)]
 
 
-def x_up(a):
-    return lax.ppermute(a, "x", ring(1))
-
-
-def x_down(a):
-    return lax.ppermute(a, "x", ring(3))
-
-
-def x_far(a):
-    return lax.ppermute(a, "x", ring(2))
-
-
 def z_up(a):
     return lax.ppermute(a, "z", ring(1))
 
@@ -44,24 +32,20 @@
     return lax.ppermute(a, "z", ring(3))
 
 
-def z_far(a):
-    return lax.ppermute(a, "z", ring(2))
-
-
-def y_pair(a):
-    return lax.ppermute(a, ("ylo", "yhi"), [(0, 3), (3, 0), (1, 2), (2, 1)])
-
-
-def y_copy(a):
-    return lax.ppermute(a, "ylo", [(0, 1), (1, 0)])
-
-
-def y_far(a):
-    return lax.ppermute(a, "yhi", [(0, 1), (1, 0)])
-
-
 def swap(a):
     return lax.ppermute(a, "core", [(0, 1), (1, 0)])
+
+
+SHARD = ("x", "yhi")
+REP = ("ylo", "z", "core")
+
+
+def exchange(blocks, axes):
+    return lax.all_to_all(blocks, axes, 0, 0, tiled=True)
+
+
+def to_all(a, axes, count):
+    return exchange(jnp.broadcast_to(a[None], (count, *a.shape)), axes)
 
 
 def ring_gather(a, up, down):
@@ -91,13 +75,6 @@
 
 def rolled(stack, start):
     return lax.dynamic_slice_in_dim(jnp.concatenate([stack, stack[:3]]), start, 4, axis=0)
-
-
-def ordered_by_core(own, core, axis):
-    other = swap(own)
-    first = jnp.where(core == 0, own, other)
-    second = jnp.where(core == 0, other, own)
-    return jnp.stack([first, second], axis=axis)
 
 
 def after(a, earlier):
@@ -149,25 +126,164 @@
     )(at, w_up, w_up, w_qkv, w_qkv, w_qkv, w_down, w_proj)
 
 
-def take_kernel(order_ref, in_ref, out_ref):
-    for block in range(8):
-        at = pl.multiple_of(order_ref[block] * 128, 128)
-        out_ref[:, block * 128 : (block + 1) * 128] = in_ref[:, pl.ds(at, 128)]
-
-
-def take_blocks(a, order):
+def call(kernel, scalars, operands, out_shape, grid, in_specs, out_specs, flops=0):
+    moved = sum(a.size * a.dtype.itemsize for a in operands) + sum(o.size * o.dtype.itemsize for o in jax.tree.leaves(out_shape))
     return pl.pallas_call(
-        take_kernel,
-        out_shape=jax.ShapeDtypeStruct(a.shape, a.dtype),
+        kernel,
+        out_shape=out_shape,
         grid_spec=pltpu.PrefetchScalarGridSpec(
-            num_scalar_prefetch=1,
-            grid=(1,),
-            in_specs=[pl.BlockSpec(a.shape, lambda i, order: (0, 0))],
-            out_specs=pl.BlockSpec(a.shape, lambda i, order: (0, 0)),
+            num_scalar_prefetch=1, grid=grid, in_specs=in_specs, out_specs=out_specs
         ),
-        compiler_params=pltpu.CompilerParams(vmem_limit_bytes=4 * 1024 * 1024),
-        cost_estimate=pl.CostEstimate(flops=0, bytes_accessed=2 * a.size * a.dtype.itemsize, transcendentals=0),
-    )(order, a)
+        compiler_params=pltpu.CompilerParams(vmem_limit_bytes=20 * 1024 * 1024),
+        cost_estimate=pl.CostEstimate(flops=flops, bytes_accessed=moved, transcendentals=0),
+    )(scalars, *operands)
+
+
+def split_z_kernel(at_ref, own_ref, next_ref, top_ref, bottom_ref, last_ref, up_ref, qkv_ref):
+    step = pl.program_id(0)
+
+    def put(position, block):
+        up_ref[:, position * 512 : position * 512 + 512] = block[:, :512]
+        qkv_ref[:, position * 384 : position * 384 + 384] = block[:, 512:]
+
+    put(0, own_ref)
+    put(1, next_ref)
+    put(3, last_ref)
+
+    @pl.when(step < 4)
+    def _():
+        put(2, top_ref)
+
+    @pl.when(step >= 4)
+    def _():
+        put(2, bottom_ref)
+
+
+def split_z(at, own, following, top, bottom, previous):
+    block = pl.BlockSpec((128, 896), lambda i, at: (i, 0))
+    return call(
+        split_z_kernel,
+        at,
+        (own, following, top, bottom, previous),
+        (jax.ShapeDtypeStruct((D, 2048), bf16), jax.ShapeDtypeStruct((D, 1536), bf16)),
+        (8,),
+        [
+            block,
+            block,
+            pl.BlockSpec((128, 896), lambda i, at: (jnp.minimum(i, 3), 0)),
+            pl.BlockSpec((128, 896), lambda i, at: (jnp.maximum(i - 4, 0), 0)),
+            block,
+        ],
+        (pl.BlockSpec((128, 2048), lambda i, at: (i, 0)), pl.BlockSpec((128, 1536), lambda i, at: (i, 0))),
+    )
+
+
+def split_x_kernel(at_ref, in_ref, down_ref, proj_ref):
+    for e in range(2):
+        down_ref[e * 256 : e * 256 + 256] = in_ref[e, 0:256]
+        proj_ref[e * 64 : e * 64 + 64] = in_ref[e, 256:320]
+
+
+def split_x(at, gathered):
+    return call(
+        split_x_kernel,
+        at,
+        (gathered,),
+        (jax.ShapeDtypeStruct((2048, D), bf16), jax.ShapeDtypeStruct((512, D), bf16)),
+        (4,),
+        [pl.BlockSpec((2, 320, D), lambda i, at: (lax.rem(i + at[0], 4), 0, 0))],
+        (pl.BlockSpec((512, D), lambda i, at: (i, 0)), pl.BlockSpec((128, D), lambda i, at: (i, 0))),
+    )
+
+
+def grad_z_kernel(at_ref, a2_ref, dub_ref, a1_ref, dqkv_ref, out_ref):
+    out_ref[:, :512] = dot_tn(a2_ref[...], dub_ref[...]).astype(bf16)
+    out_ref[:, 512:] = dot_tn(a1_ref[...], dqkv_ref[...]).astype(bf16)
+
+
+def grad_z(at, a2, dub, a1, dqkv, block):
+    rows = pl.BlockSpec((256, 256), lambda i, at: (0, i))
+    return call(
+        grad_z_kernel,
+        at,
+        (a2, dub, a1, dqkv),
+        jax.ShapeDtypeStruct((D, 896), bf16),
+        (4,),
+        [
+            rows,
+            pl.BlockSpec((256, 512), lambda i, at: (0, block)),
+            rows,
+            pl.BlockSpec((256, 384), lambda i, at: (0, block)),
+        ],
+        pl.BlockSpec((256, 896), lambda i, at: (i, 0)),
+        flops=2 * 256 * D * 896,
+    )
+
+
+def grad_x_kernel(at_ref, m_ref, dy_ref, ctx_ref, dr_ref, out_ref):
+    for e in range(2):
+        out_ref[e, 0:256] = dot_tn(m_ref[:, e * 256 : e * 256 + 256], dy_ref[...]).astype(bf16)
+        out_ref[e, 256:320] = dot_tn(ctx_ref[:, e * 64 : e * 64 + 64], dr_ref[...]).astype(bf16)
+
+
+def grad_x(at, m, dy, ctx, dr):
+    whole = pl.BlockSpec((256, D), lambda i, at: (0, 0))
+    return call(
+        grad_x_kernel,
+        at,
+        (m, dy, ctx, dr),
+        jax.ShapeDtypeStruct((8, 320, D), bf16),
+        (4,),
+        [
+            pl.BlockSpec((256, 512), lambda i, at: (0, i)),
+            whole,
+            pl.BlockSpec((256, 128), lambda i, at: (0, i)),
+            whole,
+        ],
+        pl.BlockSpec((2, 320, D), lambda i, at: (lax.rem(i + at[0], 4), 0, 0)),
+        flops=2 * 256 * D * 2560,
+    )
+
+
+def assemble_kernel(at_ref, first_ref, second_ref, up_ref, qkv_ref):
+    def put(ref):
+        for j in range(4):
+            for e in range(2):
+                for core in range(2):
+                    at = j * 1024 + e * 512 + core * 256
+                    up_ref[0, :, at : at + 256] = ref[0, j, core, :, e * 256 : e * 256 + 256].astype(f32)
+                for t in range(3):
+                    lane = 512 + t * 128 + e * 64
+                    both = [ref[0, j, core, :, lane : lane + 64].astype(f32) for core in range(2)]
+                    at = t * 1024 + j * 256 + e * 128
+                    qkv_ref[0, :, at : at + 128] = jnp.concatenate(both, axis=1)
+
+    @pl.when(pl.program_id(0) == 0)
+    def _():
+        put(first_ref)
+
+    @pl.when(pl.program_id(0) == 1)
+    def _():
+        put(second_ref)
+
+
+def assemble(at, first, second):
+    block = (1, 4, 2, 64, 896)
+    return call(
+        assemble_kernel,
+        at,
+        (first, second),
+        (jax.ShapeDtypeStruct((LAYERS, 128, 4096), f32), jax.ShapeDtypeStruct((LAYERS, 128, 3072), f32)),
+        (LAYERS, 2),
+        [
+            pl.BlockSpec(block, lambda l, h, at: (h, 0, 0, 0, 0)),
+            pl.BlockSpec(block, lambda l, h, at: (h, 0, 0, 0, 0)),
+        ],
+        (
+            pl.BlockSpec((1, 64, 4096), lambda l, h, at: (l, h, 0)),
+            pl.BlockSpec((1, 64, 3072), lambda l, h, at: (l, h, 0)),
+        ),
+    )
 
 
 def head_scores(q, k, seen, distance, slope):
@@ -322,10 +438,9 @@
 
 
 def local(hidden_in, doc_start, grad_out, w_qkv, w_proj, w_up, w_down, norm_gain, d_bias, up_bias):
-    x, z, core, yhi = (lax.axis_index(n) for n in ("x", "z", "core", "yhi"))
+    z, core = lax.axis_index("z"), lax.axis_index("core")
+    at = jnp.stack([z, core]).astype(jnp.int32)
     index = jnp.arange(8, dtype=jnp.int32)
-    to_rel = ((x + index // 2) % 4) * 2 + (yhi ^ (index % 2))
-    to_abs = ((index // 2 - x) % 4) * 2 + ((index % 2) ^ yhi)
 
     def both(own):
         return jnp.concatenate([own, swap(own)], axis=0)
@@ -339,9 +454,7 @@
             up_bias.reshape(8, 128),
         ]
     )
-    small = jnp.stack([small, y_pair(small)])
-    small = jnp.where(yhi == 0, small, small[::-1])
-    small = rolled(jnp.stack([small, x_down(small), x_far(small), x_up(small)]), (4 - x) % 4).astype(f32)
+    small = to_all(small, SHARD, 8).reshape(4, 2, 24, 128).astype(f32)
     wide = jnp.transpose(small[:, :, :16], (2, 0, 1, 3)).reshape(LAYERS, 8, D)
     hidden_bias = small[:, :, 16:].reshape(4, 2, LAYERS, 2, 256)
 
@@ -349,37 +462,22 @@
         picked = lax.dynamic_index_in_dim(vector.reshape(4, 2, 2, 64), core, axis=2, keepdims=False)
         return rolled(picked.reshape(4, 128), z)
 
-    at = jnp.stack([z, core]).astype(jnp.int32)
     mine_z, mine_x = select_weights(at, w_qkv, w_proj, w_up, w_down)
-
-    def gather_layer(layer, earlier):
+    weights, earlier = [], None
+    for layer in range(LAYERS):
         piece_z, piece_x = mine_z[layer], mine_x[layer]
-        if earlier:
-            piece_z, piece_x = after(piece_z, earlier[0]), after(piece_x, earlier[0])
-        piece_z = jnp.concatenate([piece_z, y_pair(piece_z)])
-        other = y_pair(piece_x)
-        piece_x = jnp.concatenate([jnp.where(yhi == 0, piece_x, other), jnp.where(yhi == 0, other, piece_x)])
-        own, following, (top, bottom), previous = ring_gather(piece_z, x_up, x_down)
-        near = top
-        piece_z = jnp.concatenate([own, following, top, bottom, previous])
-        if earlier:
-            piece_z, piece_x = after(piece_z, earlier[1]), after(piece_x, earlier[2])
-        own, following, (top, bottom), previous = ring_gather(piece_z, z_up, z_down)
-        far_z = top
-        blocks = (own, following, jnp.concatenate([top, bottom]), previous)
-        up = jnp.concatenate([block[:, :512] for block in blocks], axis=1)
-        qkv = jnp.concatenate([block[:, 512:] for block in blocks], axis=1)
-        own, following, (top, bottom), previous = ring_gather(piece_x, x_up, x_down)
-        stack = jnp.stack([own, following, jnp.concatenate([top, bottom]), previous])
-        stack = rolled(stack, (z - x) % 4).reshape(4, 2, 320, D)
-        down = stack[:, :, :256].reshape(2048, D)
-        proj = stack[:, :, 256:].reshape(512, D)
-        return (qkv, proj, up, down), (near, far_z, top)
-
-    weights, earlier = [], ()
-    for layer in range(LAYERS):
-        gathered, earlier = gather_layer(layer, earlier)
-        weights.append(gathered)
+        if earlier is not None:
+            piece_z, piece_x = after(piece_z, earlier[0]), after(piece_x, earlier[1])
+        block_z = to_all(piece_z, SHARD, 8).reshape(D, 896)
+        all_x = lax.all_gather(piece_x, SHARD, axis=0)
+        earlier_z = block_z
+        if earlier is not None:
+            block_z = after(block_z, earlier[2])
+        own, following, (top, bottom), previous = ring_gather(block_z, z_up, z_down)
+        earlier = (earlier_z, all_x[0], top)
+        wup, wqkv = split_z(at, own, following, top, bottom, previous)
+        wdown, wproj = split_x(at, all_x)
+        weights.append((wqkv, wproj, wup, wdown))
 
     starts = both(doc_start.reshape(1, RUN))
     rows, cols = starts.reshape(2, RUN, 1), starts.reshape(2, 1, RUN)
@@ -396,55 +494,38 @@
         ubias = lax.dynamic_index_in_dim(hidden_bias[:, :, layer], core, axis=2, keepdims=False)
         ubias = rolled(ubias.reshape(4, 512), z).reshape(2048)
         first_f, normed_one, inv_one = layer_norm(current, gain_one, shift_one)
-        first_in = both(take_blocks(first_f.astype(bf16), to_rel))
+        first_in = both(first_f.astype(bf16))
         qkv = (dot(first_in, wqkv) + bqkv).astype(bf16)
         ctx = attend(qkv, rows, cols, slopes)
         middle = current + halves_summed(dot(ctx, wproj)) + bproj
         second_f, normed_two, inv_two = layer_norm(middle, gain_two, shift_two)
-        second_in = both(take_blocks(second_f.astype(bf16), to_rel))
+        second_in = both(second_f.astype(bf16))
         upper = dot(second_in, wup) + ubias
         activ = gelu_tanh(upper).astype(bf16)
         current = middle + halves_summed(dot(activ, wdown)) + bdown
         kept.append((first_in, normed_one, inv_one, qkv, ctx, second_in, normed_two, inv_two, upper, activ, gain_one, gain_two))
     hidden_out = current
 
-    def over_y(part):
-        keep = lax.dynamic_index_in_dim(part, yhi, axis=0, keepdims=False)
-        give = lax.dynamic_index_in_dim(part, 1 - yhi, axis=0, keepdims=False)
-        near = keep.astype(f32) + y_copy(keep).astype(f32)
-        return (near + (y_pair(give).astype(f32) + y_far(give).astype(f32))).astype(bf16)
-
-    def over_z_pieces(part):
-        stack = jnp.stack([part, z_down(part), z_far(part), z_up(part)])
-        return ordered_by_core(rolled(stack, (4 - z) % 4), core, 0)
-
-    def blocks_by_z(pairs):
-        parts = []
-        for i in range(4):
-            parts.append(
-                jnp.concatenate(
-                    [dot_tn(left, right[:, i * w : (i + 1) * w]).astype(bf16) for left, right, w in pairs], axis=1
-                )
-            )
+    def summed(blocks):
+        return jnp.sum(blocks.astype(f32), axis=0).astype(bf16)
+
+    def reduce_z(a2, dub, a1, dqkv):
+        parts = [grad_z(at, a2, dub, a1, dqkv, i) for i in (2, 1, 3, 0)]
+        parts = [parts[i] for i in (3, 1, 0, 2)]
         part = ring_scatter(parts, z_up, z_down).astype(bf16)
-        part = ring_scatter([part[i * 256 : (i + 1) * 256] for i in range(4)], x_up, x_down).astype(bf16)
-        part = part.reshape(2, 128, part.shape[1])
-        return over_z_pieces(over_y(jnp.where(yhi == 0, part, part[::-1])))
-
-    def blocks_by_x(pairs):
-        parts = []
-        for i in range(4):
-            block = []
-            for left, right, w in pairs:
-                own = lax.dynamic_slice_in_dim(left, ((x + i - z) % 4) * w, w, axis=1)
-                block.append(dot_tn(own, right).astype(bf16).reshape(2, 4, w // 8, D))
-            parts.append(jnp.concatenate(block, axis=2).reshape(640, D))
-        part = ring_scatter(parts, x_up, x_down).astype(bf16).reshape(2, 4, 80, D)
-        parts = rolled(jnp.transpose(part, (1, 0, 2, 3)), z).reshape(4, 160, D)
-        part = ring_scatter([parts[i] for i in range(4)], z_up, z_down).astype(bf16)
-        return over_z_pieces(over_y(part.reshape(2, 80, D)))
-
-    grads = [None] * LAYERS
+        part = jnp.transpose(part.reshape(8, 2, 64, 896), (1, 0, 2, 3)).reshape(16, 64, 896)
+        part = summed(exchange(part, ("ylo", "x", "yhi")))
+        return lax.all_gather(part, REP, axis=0).reshape(2, 4, 2, 64, 896)
+
+    def reduce_x(m, dy, ctx, dr):
+        part = lax.psum_scatter(grad_x(at, m, dy, ctx, dr), SHARD, scatter_dimension=0, tiled=True)[0]
+        part = jnp.concatenate([part[:256].reshape(8, 32, D), part[256:].reshape(8, 8, D)], axis=1)
+        part = summed(exchange(part, ("ylo", "z")))
+        part = lax.all_gather(part, REP, axis=0).reshape(8, 2, 40, D)
+        part = jnp.transpose(part, (1, 0, 2, 3))
+        return part[:, :, :32].reshape(512, D), part[:, :, 32:].reshape(128, D)
+
+    grads_x, grads_z = [None] * LAYERS, [None] * LAYERS
     thin_grads, head_grads, unit_grads = [None] * LAYERS, [None] * LAYERS, [None] * LAYERS
     running = grad_out
     for layer in reversed(range(LAYERS)):
@@ -455,28 +536,22 @@
         grad_upper = dot_nt(grad_yb, wdown) * gelu_slope(upper)
         g_ubias = jnp.sum(grad_upper, axis=0)
         grad_ub = grad_upper.astype(bf16)
-        grad_two = take_blocks(halves_summed(dot_nt(grad_ub, wup)), to_abs)
+        grad_two = halves_summed(dot_nt(grad_ub, wup))
         back_two, g_gain_two, g_shift_two = norm_back(grad_two, normed_two, inv_two, gain_two)
         grad_mid = running + back_two
         g_bproj = jnp.sum(grad_mid, axis=0)
         grad_midb = both(grad_mid.astype(bf16))
         grad_ctx = dot_nt(grad_midb, wproj).astype(bf16)
-        by_x = blocks_by_x([(activ, grad_yb, 512), (ctx, grad_midb, 128)])
+        grads_x[layer] = reduce_x(activ, grad_yb, ctx, grad_midb)
         grad_qkv, g_bq, g_bv = attend_back(qkv, ctx, grad_ctx, rows, cols, slopes)
-        by_z = blocks_by_z([(second_in, grad_ub, 512), (first_in, grad_qkv, 384)])
-        grad_one = take_blocks(halves_summed(dot_nt(grad_qkv, wqkv)), to_abs)
+        grads_z[layer] = reduce_z(second_in, grad_ub, first_in, grad_qkv)
+        grad_one = halves_summed(dot_nt(grad_qkv, wqkv))
         back_one, g_gain_one, g_shift_one = norm_back(grad_one, normed_one, inv_one, gain_one)
         running = grad_mid + back_one
 
         thin_grads[layer] = [g_gain_one, g_gain_two, g_shift_one, g_shift_two, g_bproj, g_bdown]
         head_grads[layer] = [jnp.sum(g, axis=0).reshape(4, 128) for g in (g_bq, g_bv)]
         unit_grads[layer] = g_ubias.reshape(4, 512)
-
-        g_down = by_x[:, :, :64].reshape(512, D)
-        g_proj = by_x[:, :, 64:].reshape(128, D)
-        g_up = jnp.transpose(by_z[..., :512].reshape(2, 4, 128, 2, 256), (2, 1, 3, 0, 4)).reshape(128, 4096)
-        g_qkv = jnp.transpose(by_z[..., 512:].reshape(2, 4, 128, 3, 2, 64), (2, 3, 1, 4, 0, 5)).reshape(128, 3072)
-        grads[layer] = (g_qkv, g_proj, g_up, g_down)
 
     thin = jnp.stack(thin_grads[0] + thin_grads[1]).reshape(LAYERS, 6, 4, 2, 128)
     heads = jnp.stack(head_grads[0] + head_grads[1], axis=1)
@@ -490,19 +565,22 @@
     heads = jnp.transpose(heads, (0, 3, 1, 2, 4))
     units = jnp.transpose(units, (0, 2, 1, 3, 4))
     part = jnp.concatenate([thin[:, :, :, :4], heads, thin[:, :, :, 4:], units], axis=3)
-    part = part.reshape(4, 2, 24, 128)
-    part = rolled(part, x)
-    part = part[0] + x_up(part[1]) + x_far(part[2]) + x_down(part[3])
-    keep = lax.dynamic_index_in_dim(part, yhi, axis=0, keepdims=False)
-    give = lax.dynamic_index_in_dim(part, 1 - yhi, axis=0, keepdims=False)
-    part = (keep + y_copy(keep)) + (y_pair(give) + y_far(give))
-    part = part + swap(part)
-    part = rolled(jnp.stack([part, z_down(part), z_far(part), z_up(part)]), (4 - z) % 4)
-    part = part[0] + part[1] + part[2] + part[3]
-    part = part.reshape(LAYERS, 12, 128)
+    part = jnp.sum(exchange(part.reshape(8, 24, 128), SHARD), axis=0)
+    part = jnp.sum(to_all(part, REP, 16), axis=0).reshape(LAYERS, 12, 128)
     g_wide = jnp.transpose(part[:, :8], (0, 2, 1))
-    stacked = [jnp.stack([grads[layer][slot] for layer in range(LAYERS)]).astype(f32) for slot in range(4)]
-    return (hidden_out, running, *stacked, g_wide[:, :, :2], g_wide[:, :, 2:], part[:, 8:].reshape(LAYERS, 512))
+    g_up, g_qkv = assemble(at, grads_z[0], grads_z[1])
+    g_down, g_proj = (jnp.stack([grads_x[layer][i] for layer in range(LAYERS)]).astype(f32) for i in range(2))
+    return (
+        hidden_out,
+        running,
+        g_qkv,
+        g_proj,
+        g_up,
+        g_down,
+        g_wide[:, :, :2],
+        g_wide[:, :, 2:],
+        part[:, 8:].reshape(LAYERS, 512),
+    )
 
 
 def solution(mesh):

time: 712 us -> 723 us (1.015)
  waiting for transfers between devices: 212 us -> 362 us
  starting transfers between devices: 166 us -> 76.5 us
  other arithmetic: 89.1 us -> 41.6 us
  local copies, waits for them, and re-layouts: 112 us -> 66.8 us
  matrix products: 75.8 us -> 32 us
  blocking collectives: 0 us -> 40.1 us
  Pallas kernels: 38.9 us -> 74.6 us
  between operations: 6.76 us -> 18.7 us
    all_gather x0 -> x6, waiting for transfers between devices: none -> 164 us  [the longest x2 89.3 us: local(): all_x = lax.all_gather(piece_x, SHARD, axis=0)]
    ppermute x63 -> x0, waiting for transfers between devices: 98.2 us -> none  [the longest x18 47.3 us: x_up(): return lax.ppermute(a, 'x', ring(1))]
    ppermute x63 -> x0, starting transfers between devices: 75.2 us -> none  [the longest x18 36.8 us: x_down(): return lax.ppermute(a, 'x', ring(3))]
    dot_general x32 -> x0, matrix products: 48.4 us -> none  [dot_tn(): lax.dot_general(a, b, (((0,), (0,)), ((), ())), preferred_element_type=f32)]
    all_to_all x0 -> x7, waiting for transfers between devices: none -> 40.2 us  [exchange(): return lax.all_to_all(blocks, axes, 0, 0, tiled=True)]
    all_to_all x0 -> x2, blocking collectives: none -> 40.1 us  [exchange(): return lax.all_to_all(blocks, axes, 0, 0, tiled=True)]
    pallas_call x8 -> x15, Pallas kernels: 4.93 us -> 40.6 us  [call(): pl.pallas_call(kernel, out_shape=out_shape, grid_spec=pltpu.PrefetchScala...]
    all_to_all x0 -> x7, starting transfers between devices: none -> 32.4 us  [exchange(): return lax.all_to_all(blocks, axes, 0, 0, tiled=True)]
  transfers between devices with their start and end apart: 119 -> 48, of which waited for: 49 -> 32; matrix products, arithmetic and copies ran while one was open for 34% -> 13% of each run, Pallas kernels for 3% -> 10%
where the time goes in v3:
time: 723 us; the launch traced here: 712 us
  waiting for transfers between devices  362 us (50%)
  starting transfers between devices  76.5 us (11%)
  Pallas kernels  74.6 us (10%)
  local copies, waits for them, and re-layouts  66.8 us (9%)
  other arithmetic  41.6 us (6%)
  blocking collectives  40.1 us (6%)
  matrix products  32 us (4%)
  between operations  18.7 us (3%)
    ppermute x8, waiting for transfers between devices, z_up(): return lax.ppermute(a, 'z', ring(1))  92.4 us
    all_gather x2, waiting for transfers between devices, local(): all_x = lax.all_gather(piece_x, SHARD, axis=0)  89.3 us
    all_gather x2, waiting for transfers between devices, reduce_x(): part = lax.all_gather(part, REP, axis=0).reshape(8, 2, 40, D)  57.8 us
    ppermute x8, waiting for transfers between devices, z_down(): return lax.ppermute(a, 'z', ring(3))  53.8 us
    pallas_call x15, Pallas kernels, call(): pl.pallas_call(kernel, out_shape=out_shape, grid_spec=pltpu.PrefetchScala...  40.6 us
    all_to_all x7, waiting for transfers between devices, exchange(): return lax.all_to_all(blocks, axes, 0, 0, tiled=True)  40.2 us
    all_to_all x2, blocking collectives, exchange(): return lax.all_to_all(blocks, axes, 0, 0, tiled=True)  40.1 us
    unnamed x250, local copies, waits for them, and re-layouts  33 us
  transfers between devices with their start and end apart: 48, of which 32 were waited for; matrix products, arithmetic and copies ran while one was open for 13% of the time, Pallas kernels for 10%

profile of v3, /device:TPU:1, one launch (start us, length us, event | category | flops | bytes accessed | tf_op | source)
XLA Modules:
  0.0 712.4 jit_solution(11549501767824391255)
XLA Ops:
  16.6 7.5 %all-to-all-start.1 = ((bf16[8,128,896]{2,1,0:T(8,128)(2,1)}), bf16[8,128,896]{2,1,0:T(8,128)(2,1)S(1)}, u32[]{:S(2)}, u32[]{:S(2)}) async-start(bf16[8,128,896]{2,1,0:T(8,128)(2,1)} %broadcast_in_dim.86), calls=%async_computation.1 | async-start | bytes 3670016 | tf_op jit(solution)/shard_map/all_to_all | solution.py:44
  24.2 89.3 %all-gather.11.cloned.1.call-done.in_ref = bf16[8,320,1024]{2,1,0:T(8,128)(2,1)} async-done(((bf16[1,320,1024]{2,1,0:T(8,128)(2,1)}), bf16[8,320,1024]{2,1,0:T(8,128)(2,1)}) %all-gather.11.cloned.1.call-update) | async-done | bytes 5242896 | tf_op jit(solution)/shard_map/all_gather | solution.py:472
  121.3 3.3 all-to-all-start
  127.5 3.8 all-to-all-done
  137.0 23.8 %collective-permute-done.3.last_ref = bf16[1024,896]{1,0:T(8,128)(2,1)} collective-permute-done((bf16[1024,896]{1,0:T(8,128)(2,1)S(1)}, bf16[1024,896]{1,0:T(8,128)(2,1)}, u32[]{:S(2)}, u32[]{:S(2)}) %collective-permute-start.3) | collective-permute-done | bytes 1835040 | tf_op jit(solution)/shard_map/ppermute | solution.py:28
  169.4 4.3 all-to-all-start.2
  174.5 11.1 %collective-permute-done.4.top_ref = bf16[512,896]{1,0:T(8,128)(2,1)S(1)} collective-permute-done((bf16[512,896]{1,0:T(8,128)(2,1)}, bf16[512,896]{1,0:T(8,128)(2,1)S(1)}, u32[]{:S(2)}, u32[]{:S(2)}) %collective-permute-start.4) | collective-permute-done | bytes 917536 | tf_op jit(solution)/shard_map/ppermute | solution.py:28
  186.8 7.3 %shard_map.170 = (bf16[1024,2048]{1,0:T(8,128)(2,1)S(1)}, bf16[1024,1536]{1,0:T(8,128)(2,1)}) custom-call(s32[2]{0:T(128)S(1)} %pad_add_fusion.1.at_ref, bf16[1024,896]{1,0:T(8,128)(2,1)S(1)} %bitcast.140, bf16[1024,896]{1,0:T(8,128)(2,1)} %collective-permute-done.2.next_ref, bf16[512,896]{1,0:T(8,128)(2,1)S(1)} %collective-permute-done.4.top_ref, ...), custom_call_target="tpu_custom_call" | custom-call | bytes 14680064 | tf_op jit(solution)/shard_map/pallas_call | solution.py:131
  194.1 4.5 fusion.qkv_ref
  198.6 7.0 shard_map.171.ctx_ref
  228.3 3.2 multiply_convert_fusion.1
  233.7 31.3 %collective-permute-done.11.last_ref = bf16[1024,896]{1,0:T(8,128)(2,1)S(1)} collective-permute-done((bf16[1024,896]{1,0:T(8,128)(2,1)S(1)}, bf16[1024,896]{1,0:T(8,128)(2,1)S(1)}, u32[]{:S(2)}, u32[]{:S(2)}) %collective-permute-start.11) | collective-permute-done | bytes 1835040 | tf_op jit(solution)/shard_map/ppermute | solution.py:28
  272.3 16.5 %collective-permute-done.12.top_ref = bf16[512,896]{1,0:T(8,128)(2,1)S(1)} collective-permute-done((bf16[512,896]{1,0:T(8,128)(2,1)}, bf16[512,896]{1,0:T(8,128)(2,1)S(1)}, u32[]{:S(2)}, u32[]{:S(2)}) %collective-permute-start.12) | collective-permute-done | bytes 917536 | tf_op jit(solution)/shard_map/ppermute | solution.py:28
  292.0 3.9 shard_map.173
  299.7 7.0 shard_map.174.ctx_ref
  319.2 3.0 fusion.65
  330.9 3.2 shard_map.188
  338.2 9.4 %shard_map.176 = (bf16[256,1536]{1,0:T(8,128)(2,1)S(1)}, f32[2,2,1,256]{3,2,1,0:T(1,128)S(1)}, f32[2,2,1,256]{3,2,1,0:T(1,128)S(1)}) custom-call(f32[8]{0:T(128)S(1)} %fusion.51.slope_ref, s32[2,128,1]{2,1,0:T(8,128)S(1)} %copy.67.rows_ref, s32[2,1,128]{2,1,0:T(1,128)S(1)} %bitcast.148, bf16[256,1536]{1,0:T(8,128)(2,1)S(1)} %copy-done.17, ...), custom_call_target="tpu_custom_call" | custom-call | flops 167772160 | bytes 2097152 | tf_op jit(solution)/shard_map/pallas_call | solution.py:375
  347.6 3.2 fusion.77
  356.2 3.0 fusion.66
  366.7 3.2 shard_map.187
  377.6 3.5 collective-permute-start.31
  385.7 15.0 %collective-permute-done.31 = bf16[512,896]{1,0:T(8,128)(2,1)S(1)} collective-permute-done((bf16[512,896]{1,0:T(8,128)(2,1)S(1)}, bf16[512,896]{1,0:T(8,128)(2,1)S(1)}, u32[]{:S(2)}, u32[]{:S(2)}) %collective-permute-start.31) | collective-permute-done | bytes 917536 | tf_op jit(solution)/shard_map/ppermute | solution.py:32
  401.0 3.5 collective-permute-start.32
  407.1 9.3 %shard_map.177 = (bf16[256,1536]{1,0:T(8,128)(2,1)S(1)}, f32[2,2,1,256]{3,2,1,0:T(1,128)S(1)}, f32[2,2,1,256]{3,2,1,0:T(1,128)S(1)}) custom-call(f32[8]{0:T(128)S(1)} %fusion.51.slope_ref, s32[2,128,1]{2,1,0:T(8,128)S(1)} %copy.67.rows_ref, s32[2,1,128]{2,1,0:T(1,128)S(1)} %bitcast.149, bf16[256,1536]{1,0:T(8,128)(2,1)S(1)} %copy-done.15, ...), custom_call_target="tpu_custom_call" | custom-call | flops 167772160 | bytes 2097152 | tf_op jit(solution)/shard_map/pallas_call | solution.py:375
  424.5 18.3 %collective-permute-done.32 = bf16[1024,896]{1,0:T(8,128)(2,1)S(1)} collective-permute-done((bf16[1024,896]{1,0:T(8,128)(2,1)S(1)}, bf16[1024,896]{1,0:T(8,128)(2,1)S(1)}, u32[]{:S(2)}, u32[]{:S(2)}) %collective-permute-start.32) | collective-permute-done | bytes 1835040 | tf_op jit(solution)/shard_map/ppermute | solution.py:32
  442.8 3.7 collective-permute-done.30
  448.7 4.6 all-to-all-start.4
  457.8 4.9 collective-permute-done.27
  465.4 3.4 collective-permute-start.28
  471.6 15.9 %all-to-all-done.4 = bf16[16,64,896]{2,1,0:T(8,128)(2,1)} async-done(((bf16[16,64,896]{2,1,0:T(8,128)(2,1)}), bf16[16,64,896]{2,1,0:T(8,128)(2,1)}, u32[]{:S(2)}, u32[]{:S(2)}) %all-to-all-start.4) | async-done | bytes 1835040 | tf_op jit(solution)/shard_map/all_to_all | solution.py:44
  492.1 14.3 %collective-permute-done.28 = bf16[1024,896]{1,0:T(8,128)(2,1)} collective-permute-done((bf16[1024,896]{1,0:T(8,128)(2,1)}, bf16[1024,896]{1,0:T(8,128)(2,1)}, u32[]{:S(2)}, u32[]{:S(2)}) %collective-permute-start.28) | collective-permute-done | bytes 1835040 | tf_op jit(solution)/shard_map/ppermute | solution.py:32
  506.5 5.9 collective-permute-done.26
  512.4 2.7 add_convert_fusion.1
  515.3 29.4 %all_to_all.45 = bf16[16,64,896]{2,1,0:T(8,128)(2,1)S(1)} all-to-all(bf16[16,64,896]{2,1,0:T(8,128)(2,1)S(1)} %bitcast.153), channel_id=1, replica_groups=mesh['ylo'=2,'z'=4,'core'=2,'x'=4,'yhi'=2] {'ylo','x','yhi'}, dimensions={0} | all-to-all | bytes 3670016 | tf_op jit(solution)/shard_map/all_to_all | solution.py:44
  547.8 10.6 %all_to_all.46 = bf16[8,40,1024]{2,1,0:T(8,128)(2,1)S(1)} all-to-all(bf16[8,40,1024]{2,1,0:T(8,128)(2,1)S(1)} %pad_maximum_fusion.5), channel_id=1, replica_groups=mesh['ylo'=2,'z'=4,'core'=2,'x'=4,'yhi'=2] {'ylo','z'}, dimensions={0} | all-to-all | bytes 1310720 | tf_op jit(solution)/shard_map/all_to_all | solution.py:44
  562.4 3.8 all-to-all-start.5
  567.9 7.3 %all-to-all-done.5 = bf16[8,40,1024]{2,1,0:T(8,128)(2,1)S(1)} async-done(((bf16[8,40,1024]{2,1,0:T(8,128)(2,1)}), bf16[8,40,1024]{2,1,0:T(8,128)(2,1)S(1)}, u32[]{:S(2)}, u32[]{:S(2)}) %all-to-all-start.5) | async-done | bytes 655392 | tf_op jit(solution)/shard_map/all_to_all | solution.py:44
  576.0 3.0 fusion.79
  579.1 7.4 %collective-permute-start.24 = (f32[128,1024]{1,0:T(8,128)S(1)}, f32[128,1024]{1,0:T(8,128)S(1)}, u32[]{:S(2)}, u32[]{:S(2)}) collective-permute-start(f32[128,1024]{1,0:T(8,128)S(1)} %slice.399), channel_id=1, source_target_pairs={{0,8},{8,0},{1,9},{9,1},{2,10},{10,2},{3,11},{11,3},{4,12},{12,4},... | collective-permute-start | bytes 1572872 | tf_op jit(solution)/shard_map/ppermute | solution.py:36
  589.3 3.4 all-to-all-start.7
  592.7 6.6 all-to-all-done.7
  600.0 5.5 all-to-all-start.8
  606.6 6.6 all-to-all-done.8
  615.0 17.1 %all-gather.15.cloned.1.call-done = bf16[1024,896]{1,0:T(8,128)(2,1)} async-done(((bf16[64,896]{1,0:T(8,128)(2,1)}), bf16[1024,896]{1,0:T(8,128)(2,1)}) %all-gather.15.cloned.1.call-update) | async-done | bytes 1835024 | tf_op jit(solution)/shard_map/all_gather | solution.py:518
  635.1 4.1 shard_map.186
  639.2 25.6 %all-gather.21.cloned.1.call-done = bf16[640,1024]{1,0:T(8,128)(2,1)} async-done(((bf16[40,1024]{1,0:T(8,128)(2,1)}), bf16[640,1024]{1,0:T(8,128)(2,1)}) %all-gather.21.cloned.1.call-update) | async-done | bytes 1310736 | tf_op jit(solution)/shard_map/all_gather | solution.py:524
  667.2 32.2 %all-gather.19.cloned.1.call-done = bf16[640,1024]{1,0:T(8,128)(2,1)} async-done(((bf16[40,1024]{1,0:T(8,128)(2,1)}), bf16[640,1024]{1,0:T(8,128)(2,1)}) %all-gather.19.cloned.1.call-update) | async-done | bytes 1310736 | tf_op jit(solution)/shard_map/all_gather | solution.py:524
  (541 shorter events, 177.4 us)
Async XLA Ops:
  7.2 106.2 %all-gather.11.cloned.1.call-start = ((), (), s32[]{:S(2)}) async-start(), calls=%async_computation.11 | async-start | bytes 5898240 | tf_op jit(solution)/shard_map/all_gather | solution.py:472
  16.6 101.3 %all-to-all-start.1 = ((bf16[8,128,896]{2,1,0:T(8,128)(2,1)}), bf16[8,128,896]{2,1,0:T(8,128)(2,1)S(1)}, u32[]{:S(2)}, u32[]{:S(2)}) async-start(bf16[8,128,896]{2,1,0:T(8,128)(2,1)} %broadcast_in_dim.86), calls=%async_computation.1 | async-start | bytes 3670016 | tf_op jit(solution)/shard_map/all_to_all | solution.py:44
  24.1 283.5 %all-gather.13.cloned.1.call-start = ((), (), s32[]{:S(2)}) async-start(), calls=%async_computation.12 | async-start | bytes 5898240 | tf_op jit(solution)/shard_map/all_gather | solution.py:472
  116.7 10.6 %collective-permute-start = (s32[1,128]{1,0:T(1,128)S(1)}, s32[1,128]{1,0:T(1,128)S(1)}, u32[]{:S(2)}, u32[]{:S(2)}) collective-permute-start(s32[1,128]{1,0:T(1,128)S(1)} %bitcast.218), channel_id=1, source_target_pairs={{0,8},{8,0},{1,9},{9,1},{2,10},{10,2},{3,11},{11,3},{4,12},{12,4},... | collective-permute-start | bytes 1544 | tf_op jit(solution)/shard_map/ppermute | solution.py:36
  117.9 43.0 %collective-permute-start.3 = (bf16[1024,896]{1,0:T(8,128)(2,1)S(1)}, bf16[1024,896]{1,0:T(8,128)(2,1)}, u32[]{:S(2)}, u32[]{:S(2)}) collective-permute-start(bf16[1024,896]{1,0:T(8,128)(2,1)S(1)} %bitcast.137), channel_id=1, source_target_pairs={{0,16},{16,32},{32,48},{48,0},{1,17},{17,33},{33,49},{49,1},{2,18}... | collective-permute-start | bytes 5505032 | tf_op jit(solution)/shard_map/ppermute | solution.py:28
  119.2 43.9 %collective-permute-start.2 = (bf16[1024,896]{1,0:T(8,128)(2,1)S(1)}, bf16[1024,896]{1,0:T(8,128)(2,1)}, u32[]{:S(2)}, u32[]{:S(2)}) collective-permute-start(bf16[1024,896]{1,0:T(8,128)(2,1)S(1)} %bitcast.138), channel_id=1, source_target_pairs={{0,48},{16,0},{32,16},{48,32},{1,49},{17,1},{33,17},{49,33},{2,50}... | collective-permute-start | bytes 5505032 | tf_op jit(solution)/shard_map/ppermute | solution.py:32
  121.3 9.9 %all-to-all-start = ((bf16[8,24,128]{2,1,0:T(8,128)(2,1)}), bf16[8,24,128]{2,1,0:T(8,128)(2,1)S(1)}, u32[]{:S(2)}, u32[]{:S(2)}) async-start(bf16[8,24,128]{2,1,0:T(8,128)(2,1)} %broadcast_in_dim.84), calls=%async_computation | async-start | bytes 98304 | tf_op jit(solution)/shard_map/all_to_all | solution.py:44
  134.1 60.0 %collective-permute-start.1 = (bf16[128,1024]{1,0:T(8,128)(2,1)}, bf16[128,1024]{1,0:T(8,128)(2,1)}, u32[]{:S(2)}, u32[]{:S(2)}) collective-permute-start(bf16[128,1024]{1,0:T(8,128)(2,1)} %add_convert_fusion.9), channel_id=1, source_target_pairs={{0,8},{8,0},{1,9},{9,1},{2,10},{10,2},{3,11},{11,3},{4,12},{12,4},... | collective-permute-start | bytes 786440 | tf_op jit(solution)/shard_map/ppermute | solution.py:36
  163.1 22.6 %collective-permute-start.4 = (bf16[512,896]{1,0:T(8,128)(2,1)}, bf16[512,896]{1,0:T(8,128)(2,1)S(1)}, u32[]{:S(2)}, u32[]{:S(2)}) collective-permute-start(bf16[512,896]{1,0:T(8,128)(2,1)} %slice.359), channel_id=1, source_target_pairs={{0,16},{16,32},{32,48},{48,0},{1,17},{17,33},{33,49},{49,1},{2,18}... | collective-permute-start | bytes 2752520 | tf_op jit(solution)/shard_map/ppermute | solution.py:28
  165.3 21.5 %collective-permute-start.5 = (bf16[512,896]{1,0:T(8,128)(2,1)}, bf16[512,896]{1,0:T(8,128)(2,1)}, u32[]{:S(2)}, u32[]{:S(2)}) collective-permute-start(bf16[512,896]{1,0:T(8,128)(2,1)} %slice.360), channel_id=1, source_target_pairs={{0,48},{16,0},{32,16},{48,32},{1,49},{17,1},{33,17},{49,33},{2,50}... | collective-permute-start | bytes 2752520 | tf_op jit(solution)/shard_map/ppermute | solution.py:32
  169.4 49.8 %all-to-all-start.2 = ((bf16[8,128,896]{2,1,0:T(8,128)(2,1)}), bf16[8,128,896]{2,1,0:T(8,128)(2,1)}, u32[]{:S(2)}, u32[]{:S(2)}) async-start(bf16[8,128,896]{2,1,0:T(8,128)(2,1)} %broadcast_in_dim.89), calls=%async_computation.2 | async-start | bytes 3670016 | tf_op jit(solution)/shard_map/all_to_all | solution.py:44
  173.7 372.0 %reduce-scatter.5.cloned.1.call-start = ((), (), s32[]{:S(2)}) async-start(), calls=%async_computation.14 | async-start | bytes 5898240 | tf_op jit(solution)/shard_map/reduce_scatter | solution.py:521
  215.3 9.4 %collective-permute-start.6 = (f32[128,1024]{1,0:T(8,128)}, f32[128,1024]{1,0:T(8,128)}, u32[]{:S(2)}, u32[]{:S(2)}) collective-permute-start(f32[128,1024]{1,0:T(8,128)} %slice.364), channel_id=1, source_target_pairs={{0,8},{8,0},{1,9},{9,1},{2,10},{10,2},{3,11},{11,3},{4,12},{12,4},... | collective-permute-start | bytes 1572872 | tf_op jit(solution)/shard_map/ppermute | solution.py:36
  221.1 43.9 %collective-permute-start.11 = (bf16[1024,896]{1,0:T(8,128)(2,1)S(1)}, bf16[1024,896]{1,0:T(8,128)(2,1)S(1)}, u32[]{:S(2)}, u32[]{:S(2)}) collective-permute-start(bf16[1024,896]{1,0:T(8,128)(2,1)S(1)} %bitcast.141), channel_id=1, source_target_pairs={{0,16},{16,32},{32,48},{48,0},{1,17},{17,33},{33,49},{49,1},{2,18}... | collective-permute-start | bytes 5505032 | tf_op jit(solution)/shard_map/ppermute | solution.py:28
  222.0 44.1 %collective-permute-start.10 = (bf16[1024,896]{1,0:T(8,128)(2,1)S(1)}, bf16[1024,896]{1,0:T(8,128)(2,1)S(1)}, u32[]{:S(2)}, u32[]{:S(2)}) collective-permute-start(bf16[1024,896]{1,0:T(8,128)(2,1)S(1)} %bitcast.142), channel_id=1, source_target_pairs={{0,48},{16,0},{32,16},{48,32},{1,49},{17,1},{33,17},{49,33},{2,50}... | collective-permute-start | bytes 5505032 | tf_op jit(solution)/shard_map/ppermute | solution.py:32
  226.8 1.5 collective-permute-start.7
  232.9 37.0 %collective-permute-start.8 = (f32[128,1024]{1,0:T(8,128)S(1)}, f32[128,1024]{1,0:T(8,128)S(1)}, u32[]{:S(2)}, u32[]{:S(2)}) collective-permute-start(f32[128,1024]{1,0:T(8,128)S(1)} %slice.371), channel_id=1, source_target_pairs={{0,8},{8,0},{1,9},{9,1},{2,10},{10,2},{3,11},{11,3},{4,12},{12,4},... | collective-permute-start | bytes 1572872 | tf_op jit(solution)/shard_map/ppermute | solution.py:36
  266.1 22.7 %collective-permute-start.12 = (bf16[512,896]{1,0:T(8,128)(2,1)}, bf16[512,896]{1,0:T(8,128)(2,1)S(1)}, u32[]{:S(2)}, u32[]{:S(2)}) collective-permute-start(bf16[512,896]{1,0:T(8,128)(2,1)} %slice.377), channel_id=1, source_target_pairs={{0,16},{16,32},{32,48},{48,0},{1,17},{17,33},{33,49},{49,1},{2,18}... | collective-permute-start | bytes 2752520 | tf_op jit(solution)/shard_map/ppermute | solution.py:28
  267.2 21.8 %collective-permute-start.13 = (bf16[512,896]{1,0:T(8,128)(2,1)}, bf16[512,896]{1,0:T(8,128)(2,1)}, u32[]{:S(2)}, u32[]{:S(2)}) collective-permute-start(bf16[512,896]{1,0:T(8,128)(2,1)} %slice.378), channel_id=1, source_target_pairs={{0,48},{16,0},{32,16},{48,32},{1,49},{17,1},{33,17},{49,33},{2,50}... | collective-permute-start | bytes 2752520 | tf_op jit(solution)/shard_map/ppermute | solution.py:32
  271.1 24.9 %collective-permute-start.9 = (bf16[128,1024]{1,0:T(8,128)(2,1)S(1)}, bf16[128,1024]{1,0:T(8,128)(2,1)}, u32[]{:S(2)}, u32[]{:S(2)}) collective-permute-start(bf16[128,1024]{1,0:T(8,128)(2,1)S(1)} %add_convert_fusion.7), channel_id=1, source_target_pairs={{0,8},{8,0},{1,9},{9,1},{2,10},{10,2},{3,11},{11,3},{4,12},{12,4},... | collective-permute-start | bytes 786440 | tf_op jit(solution)/shard_map/ppermute | solution.py:36
  311.6 3.4 collective-permute-start.14
  315.6 1.6 collective-permute-start.15
  316.7 2.5 collective-permute-start.17
  323.6 2.2 collective-permute-start.18
  325.4 2.2 collective-permute-start.16
  329.2 1.6 collective-permute-start.19
  336.5 223.0 %reduce-scatter.3.cloned.1.call-start = ((), (), s32[]{:S(2)}) async-start(), calls=%async_computation.13 | async-start | bytes 5898240 | tf_op jit(solution)/shard_map/reduce_scatter | solution.py:521
  350.9 2.0 collective-permute-start.20
  354.6 1.6 collective-permute-start.21
  360.6 2.0 collective-permute-start.22
  364.4 1.6 collective-permute-start.23
  377.6 23.1 %collective-permute-start.31 = (bf16[512,896]{1,0:T(8,128)(2,1)S(1)}, bf16[512,896]{1,0:T(8,128)(2,1)S(1)}, u32[]{:S(2)}, u32[]{:S(2)}) collective-permute-start(bf16[512,896]{1,0:T(8,128)(2,1)S(1)} %get-tuple-element.131), channel_id=1, source_target_pairs={{0,48},{16,0},{32,16},{48,32},{1,49},{17,1},{33,17},{49,33},{2,50}... | collective-permute-start | bytes 2752520 | tf_op jit(solution)/shard_map/ppermute | solution.py:32
  381.0 23.5 %collective-permute-start.29 = (bf16[512,896]{1,0:T(8,128)(2,1)S(1)}, bf16[512,896]{1,0:T(8,128)(2,1)S(1)}, u32[]{:S(2)}, u32[]{:S(2)}) collective-permute-start(bf16[512,896]{1,0:T(8,128)(2,1)S(1)} %get-tuple-element.130), channel_id=1, source_target_pairs={{0,16},{16,32},{32,48},{48,0},{1,17},{17,33},{33,49},{49,1},{2,18}... | collective-permute-start | bytes 2752520 | tf_op jit(solution)/shard_map/ppermute | solution.py:28
  401.0 41.8 %collective-permute-start.32 = (bf16[1024,896]{1,0:T(8,128)(2,1)S(1)}, bf16[1024,896]{1,0:T(8,128)(2,1)S(1)}, u32[]{:S(2)}, u32[]{:S(2)}) collective-permute-start(bf16[1024,896]{1,0:T(8,128)(2,1)S(1)} %pad_maximum_fusion.3), channel_id=1, source_target_pairs={{0,48},{16,0},{32,16},{48,32},{1,49},{17,1},{33,17},{49,33},{2,50}... | collective-permute-start | bytes 5505032 | tf_op jit(solution)/shard_map/ppermute | solution.py:32
  404.9 41.7 %collective-permute-start.30 = (bf16[1024,896]{1,0:T(8,128)(2,1)S(1)}, bf16[1024,896]{1,0:T(8,128)(2,1)S(1)}, u32[]{:S(2)}, u32[]{:S(2)}) collective-permute-start(bf16[1024,896]{1,0:T(8,128)(2,1)S(1)} %pad_maximum_fusion.2), channel_id=1, source_target_pairs={{0,16},{16,32},{32,48},{48,0},{1,17},{17,33},{33,49},{49,1},{2,18}... | collective-permute-start | bytes 5505032 | tf_op jit(solution)/shard_map/ppermute | solution.py:28
  420.0 42.6 %collective-permute-start.27 = (bf16[512,896]{1,0:T(8,128)(2,1)}, bf16[512,896]{1,0:T(8,128)(2,1)}, u32[]{:S(2)}, u32[]{:S(2)}) collective-permute-start(bf16[512,896]{1,0:T(8,128)(2,1)} %get-tuple-element.133), channel_id=1, source_target_pairs={{0,48},{16,0},{32,16},{48,32},{1,49},{17,1},{33,17},{49,33},{2,50}... | collective-permute-start | bytes 2752520 | tf_op jit(solution)/shard_map/ppermute | solution.py:32
  424.4 44.4 %collective-permute-start.25 = (bf16[512,896]{1,0:T(8,128)(2,1)}, bf16[512,896]{1,0:T(8,128)(2,1)}, u32[]{:S(2)}, u32[]{:S(2)}) collective-permute-start(bf16[512,896]{1,0:T(8,128)(2,1)} %get-tuple-element.132), channel_id=1, source_target_pairs={{0,16},{16,32},{32,48},{48,0},{1,17},{17,33},{33,49},{49,1},{2,18}... | collective-permute-start | bytes 2752520 | tf_op jit(solution)/shard_map/ppermute | solution.py:28
  448.7 38.8 %all-to-all-start.4 = ((bf16[16,64,896]{2,1,0:T(8,128)(2,1)}), bf16[16,64,896]{2,1,0:T(8,128)(2,1)}, u32[]{:S(2)}, u32[]{:S(2)}) async-start(bf16[16,64,896]{2,1,0:T(8,128)(2,1)} %bitcast.152), calls=%async_computation.4 | async-start | bytes 3670016 | tf_op jit(solution)/shard_map/all_to_all | solution.py:44
  453.3 161.8 %all-gather.17.cloned.1.call-start = ((), (), s32[]{:S(2)}) async-start(), calls=%async_computation.16 | async-start | bytes 1949696 | tf_op jit(solution)/shard_map/all_gather | solution.py:518
  465.4 41.1 %collective-permute-start.28 = (bf16[1024,896]{1,0:T(8,128)(2,1)}, bf16[1024,896]{1,0:T(8,128)(2,1)}, u32[]{:S(2)}, u32[]{:S(2)}) collective-permute-start(bf16[1024,896]{1,0:T(8,128)(2,1)} %pad_maximum_fusion.1), channel_id=1, source_target_pairs={{0,48},{16,0},{32,16},{48,32},{1,49},{17,1},{33,17},{49,33},{2,50}... | collective-permute-start | bytes 5505032 | tf_op jit(solution)/shard_map/ppermute | solution.py:32
  471.6 40.8 %collective-permute-start.26 = (bf16[1024,896]{1,0:T(8,128)(2,1)}, bf16[1024,896]{1,0:T(8,128)(2,1)}, u32[]{:S(2)}, u32[]{:S(2)}) collective-permute-start(bf16[1024,896]{1,0:T(8,128)(2,1)} %pad_maximum_fusion), channel_id=1, source_target_pairs={{0,16},{16,32},{32,48},{48,0},{1,17},{17,33},{33,49},{49,1},{2,18}... | collective-permute-start | bytes 5505032 | tf_op jit(solution)/shard_map/ppermute | solution.py:28
  490.0 142.2 %all-gather.15.cloned.1.call-start = ((), (), s32[]{:S(2)}) async-start(), calls=%async_computation.15 | async-start | bytes 1949696 | tf_op jit(solution)/shard_map/all_gather | solution.py:518
  545.7 119.1 %all-gather.21.cloned.1.call-start = ((), (), s32[]{:S(2)}) async-start(), calls=%async_computation.18 | async-start | bytes 1392640 | tf_op jit(solution)/shard_map/all_gather | solution.py:524
  562.4 12.8 %all-to-all-start.5 = ((bf16[8,40,1024]{2,1,0:T(8,128)(2,1)}), bf16[8,40,1024]{2,1,0:T(8,128)(2,1)S(1)}, u32[]{:S(2)}, u32[]{:S(2)}) async-start(bf16[8,40,1024]{2,1,0:T(8,128)(2,1)} %pad_maximum_fusion.4), calls=%async_computation.6 | async-start | bytes 1310720 | tf_op jit(solution)/shard_map/all_to_all | solution.py:44
  566.2 133.2 %all-gather.19.cloned.1.call-start = ((), (), s32[]{:S(2)}) async-start(), calls=%async_computation.17 | async-start | bytes 1392640 | tf_op jit(solution)/shard_map/all_gather | solution.py:524
  579.1 8.9 %collective-permute-start.24 = (f32[128,1024]{1,0:T(8,128)S(1)}, f32[128,1024]{1,0:T(8,128)S(1)}, u32[]{:S(2)}, u32[]{:S(2)}) collective-permute-start(f32[128,1024]{1,0:T(8,128)S(1)} %slice.399), channel_id=1, source_target_pairs={{0,8},{8,0},{1,9},{9,1},{2,10},{10,2},{3,11},{11,3},{4,12},{12,4},... | collective-permute-start | bytes 1572872 | tf_op jit(solution)/shard_map/ppermute | solution.py:36
  589.3 10.0 %all-to-all-start.7 = ((f32[8,24,128]{2,1,0:T(8,128)}), f32[8,24,128]{2,1,0:T(8,128)S(1)}, u32[]{:S(2)}, u32[]{:S(2)}) async-start(f32[8,24,128]{2,1,0:T(8,128)} %copy.79), calls=%async_computation.9 | async-start | bytes 196608 | tf_op jit(solution)/shard_map/all_to_all | solution.py:44
  600.0 13.2 %all-to-all-start.8 = ((f32[16,24,128]{2,1,0:T(8,128)}), f32[16,24,128]{2,1,0:T(8,128)S(1)}, u32[]{:S(2)}, u32[]{:S(2)}) async-start(f32[16,24,128]{2,1,0:T(8,128)} %broadcast_in_dim.100), calls=%async_computation.10 | async-start | bytes 393216 | tf_op jit(solution)/shard_map/all_to_all | solution.py:44
  (120 other events, 1306.5 us)
Sparse Core Ops, SparseCore 0:
  15.2 98.1 all-gather.10
  116.8 96.2 all-gather.12
  336.6 88.6 reduce-scatter.4
  429.6 129.8 reduce-scatter.2
  561.0 33.5 all-gather.16
  596.8 35.2 all-gather.14
  633.8 30.8 all-gather.20
  666.5 32.9 all-gather.18

commit v4 on v3

--- a/solution.py
+++ b/solution.py
@@ -70,15 +70,16 @@
     )
     got_up = up(go_up)
     got_down = down(go_down)
-    return own.astype(f32) + got_up.astype(f32) + got_down.astype(f32)
+    total = own.astype(f32) + got_up.astype(f32) + got_down.astype(f32)
+    return total, (following, previous), (from_previous, from_following), (got_up, got_down)
 
 
 def rolled(stack, start):
     return lax.dynamic_slice_in_dim(jnp.concatenate([stack, stack[:3]]), start, 4, axis=0)
 
 
-def after(a, earlier):
-    there = jnp.abs(earlier[0, 0].astype(f32)) < 1e30
+def after(a, *earlier):
+    there = sum(jnp.abs(e[0, 0].astype(f32)) * 2.0**-40 for e in earlier) < 1e30
     return jnp.where(there, a, jnp.zeros_like(a))
 
 
@@ -466,15 +467,16 @@
     weights, earlier = [], None
     for layer in range(LAYERS):
         piece_z, piece_x = mine_z[layer], mine_x[layer]
-        if earlier is not None:
-            piece_z, piece_x = after(piece_z, earlier[0]), after(piece_x, earlier[1])
-        block_z = to_all(piece_z, SHARD, 8).reshape(D, 896)
-        all_x = lax.all_gather(piece_x, SHARD, axis=0)
-        earlier_z = block_z
-        if earlier is not None:
-            block_z = after(block_z, earlier[2])
+        if earlier is None:
+            block_z = to_all(piece_z, SHARD, 8).reshape(D, 896)
+            all_x = to_all(after(piece_x, block_z), SHARD, 8)
+            first_z = block_z
+        else:
+            block_z = to_all(after(piece_z, first_z), SHARD, 8).reshape(D, 896)
+            all_x = lax.all_gather(after(piece_x, first_z), SHARD, axis=0)
+            block_z = after(block_z, earlier)
         own, following, (top, bottom), previous = ring_gather(block_z, z_up, z_down)
-        earlier = (earlier_z, all_x[0], top)
+        earlier = top
         wup, wqkv = split_z(at, own, following, top, bottom, previous)
         wdown, wproj = split_x(at, all_x)
         weights.append((wqkv, wproj, wup, wdown))
@@ -512,13 +514,14 @@
     def reduce_z(a2, dub, a1, dqkv):
         parts = [grad_z(at, a2, dub, a1, dqkv, i) for i in (2, 1, 3, 0)]
         parts = [parts[i] for i in (3, 1, 0, 2)]
-        part = ring_scatter(parts, z_up, z_down).astype(bf16)
+        total, sent, near, got = ring_scatter(parts, z_up, z_down)
+        part = total.astype(bf16)
         part = jnp.transpose(part.reshape(8, 2, 64, 896), (1, 0, 2, 3)).reshape(16, 64, 896)
         part = summed(exchange(part, ("ylo", "x", "yhi")))
-        return lax.all_gather(part, REP, axis=0).reshape(2, 4, 2, 64, 896)
-
-    def reduce_x(m, dy, ctx, dr):
-        part = lax.psum_scatter(grad_x(at, m, dy, ctx, dr), SHARD, scatter_dimension=0, tiled=True)[0]
+        return lax.all_gather(part, REP, axis=0).reshape(2, 4, 2, 64, 896), (sent, near, got)
+
+    def finish_x(blocks, later):
+        part = summed(after(blocks, later))
         part = jnp.concatenate([part[:256].reshape(8, 32, D), part[256:].reshape(8, 8, D)], axis=1)
         part = summed(exchange(part, ("ylo", "z")))
         part = lax.all_gather(part, REP, axis=0).reshape(8, 2, 40, D)
@@ -527,10 +530,12 @@
 
     grads_x, grads_z = [None] * LAYERS, [None] * LAYERS
     thin_grads, head_grads, unit_grads = [None] * LAYERS, [None] * LAYERS, [None] * LAYERS
-    running = grad_out
+    running, ring_state = grad_out, None
     for layer in reversed(range(LAYERS)):
         wqkv, wproj, wup, wdown = weights[layer]
         first_in, normed_one, inv_one, qkv, ctx, second_in, normed_two, inv_two, upper, activ, gain_one, gain_two = kept[layer]
+        if ring_state is not None:
+            running = after(running, *ring_state[0])
         g_bdown = jnp.sum(running, axis=0)
         grad_yb = both(running.astype(bf16))
         grad_upper = dot_nt(grad_yb, wdown) * gelu_slope(upper)
@@ -540,11 +545,17 @@
         back_two, g_gain_two, g_shift_two = norm_back(grad_two, normed_two, inv_two, gain_two)
         grad_mid = running + back_two
         g_bproj = jnp.sum(grad_mid, axis=0)
-        grad_midb = both(grad_mid.astype(bf16))
+        grad_midb = grad_mid.astype(bf16)
+        if ring_state is not None:
+            grad_midb = after(grad_midb, *ring_state[1])
+            grads_x[layer + 1] = finish_x(waiting_x, grad_midb)
+        grad_midb = both(grad_midb)
         grad_ctx = dot_nt(grad_midb, wproj).astype(bf16)
-        grads_x[layer] = reduce_x(activ, grad_yb, ctx, grad_midb)
+        waiting_x = exchange(grad_x(at, activ, grad_yb, ctx, grad_midb), SHARD)
         grad_qkv, g_bq, g_bv = attend_back(qkv, ctx, grad_ctx, rows, cols, slopes)
-        grads_z[layer] = reduce_z(second_in, grad_ub, first_in, grad_qkv)
+        if ring_state is not None:
+            grad_qkv = after(grad_qkv, *ring_state[2])
+        grads_z[layer], ring_state = reduce_z(second_in, grad_ub, first_in, grad_qkv)
         grad_one = halves_summed(dot_nt(grad_qkv, wqkv))
         back_one, g_gain_one, g_shift_one = norm_back(grad_one, normed_one, inv_one, gain_one)
         running = grad_mid + back_one
@@ -552,6 +563,8 @@
         thin_grads[layer] = [g_gain_one, g_gain_two, g_shift_one, g_shift_two, g_bproj, g_bdown]
         head_grads[layer] = [jnp.sum(g, axis=0).reshape(4, 128) for g in (g_bq, g_bv)]
         unit_grads[layer] = g_ubias.reshape(4, 512)
+
+    grads_x[0] = finish_x(waiting_x, running)
 
     thin = jnp.stack(thin_grads[0] + thin_grads[1]).reshape(LAYERS, 6, 4, 2, 128)
     heads = jnp.stack(head_grads[0] + head_grads[1], axis=1)

time: 723 us -> 689 us (0.953)
  waiting for transfers between devices: 362 us -> 264 us
  blocking collectives: 40.1 us -> 66.5 us
  starting transfers between devices: 76.5 us -> 95.6 us
  other arithmetic: 41.6 us -> 58.2 us
  matrix products: 32 us -> 23.9 us
    all_gather x6 -> x5, waiting for transfers between devices: 164 us -> 0.05 us  [the longest x2 0.02 us: finish_x(): part = lax.all_gather(part, REP, axis=0).reshape(8, 2, 40, D)]
    all_to_all x7 -> x9, waiting for transfers between devices: 40.2 us -> 111 us  [exchange(): return lax.all_to_all(blocks, axes, 0, 0, tiled=True)]
    all_to_all x2 -> x3, blocking collectives: 40.1 us -> 66.5 us  [exchange(): return lax.all_to_all(blocks, axes, 0, 0, tiled=True)]
    ppermute x8, waiting for transfers between devices: 92.4 us -> 110 us  [z_up(): return lax.ppermute(a, 'z', ring(1))]
    all_to_all x7 -> x9, starting transfers between devices: 32.4 us -> 48.3 us  [exchange(): return lax.all_to_all(blocks, axes, 0, 0, tiled=True)]
    ppermute x8, waiting for transfers between devices: 53.8 us -> 38.2 us  [z_down(): return lax.ppermute(a, 'z', ring(3))]
    reduce_sum x4 -> x6, other arithmetic: 4.8 us -> 14.8 us  [summed(): return jnp.sum(blocks.astype(f32), axis=0).astype(bf16)]
    unnamed x250 -> x266, local copies, waits for them, and re-layouts: 33 us -> 33.4 us
  transfers between devices with their start and end apart: 48 -> 47, of which waited for: 32 -> 22; matrix products, arithmetic and copies ran while one was open for 13% -> 16% of each run, Pallas kernels for 10% -> 9%
where the time goes in v4:
time: 689 us; the launch traced here: 679 us
  waiting for transfers between devices  264 us (38%)
  starting transfers between devices  95.6 us (14%)
  Pallas kernels  76.1 us (11%)
  local copies, waits for them, and re-layouts  71.3 us (10%)
  blocking collectives  66.5 us (10%)
  other arithmetic  58.2 us (8%)
  matrix products  23.9 us (3%)
  between operations  23.3 us (3%)
    all_to_all x9, waiting for transfers between devices, exchange(): return lax.all_to_all(blocks, axes, 0, 0, tiled=True)  111 us
    ppermute x8, waiting for transfers between devices, z_up(): return lax.ppermute(a, 'z', ring(1))  110 us
    all_to_all x3, blocking collectives, exchange(): return lax.all_to_all(blocks, axes, 0, 0, tiled=True)  66.5 us
    all_to_all x9, starting transfers between devices, exchange(): return lax.all_to_all(blocks, axes, 0, 0, tiled=True)  48.3 us
    pallas_call x15, Pallas kernels, call(): pl.pallas_call(kernel, out_shape=out_shape, grid_spec=pltpu.PrefetchScala...  42.2 us
    ppermute x8, waiting for transfers between devices, z_down(): return lax.ppermute(a, 'z', ring(3))  38.2 us
    unnamed x266, local copies, waits for them, and re-layouts  33.4 us
    ppermute x17, starting transfers between devices, swap(): return lax.ppermute(a, 'core', [(0, 1), (1, 0)])  24 us
  transfers between devices with their start and end apart: 47, of which 22 were waited for; matrix products, arithmetic and copies ran while one was open for 16% of the time, Pallas kernels for 9%

profile of v4, /device:TPU:1, one launch (start us, length us, event | category | flops | bytes accessed | tf_op | source)
XLA Modules:
  0.0 679.2 jit_solution(13384469044865910076)
XLA Ops:
  16.3 7.6 %all-to-all-start.1 = ((bf16[8,128,896]{2,1,0:T(8,128)(2,1)}), bf16[8,128,896]{2,1,0:T(8,128)(2,1)S(1)}, u32[]{:S(2)}, u32[]{:S(2)}) async-start(bf16[8,128,896]{2,1,0:T(8,128)(2,1)} %broadcast_in_dim.100), calls=%async_computation.1 | async-start | bytes 3670016 | tf_op jit(solution)/shard_map/all_to_all | solution.py:44
  24.0 26.6 %all-to-all-done.1 = bf16[8,128,896]{2,1,0:T(8,128)(2,1)S(1)} async-done(((bf16[8,128,896]{2,1,0:T(8,128)(2,1)}), bf16[8,128,896]{2,1,0:T(8,128)(2,1)S(1)}, u32[]{:S(2)}, u32[]{:S(2)}) %all-to-all-start.1) | async-done | bytes 1835040 | tf_op jit(solution)/shard_map/all_to_all | solution.py:44
  51.3 3.3 all-to-all-start
  56.9 4.2 all-to-all-done
  61.1 4.1 broadcast_in_dim.102
  65.2 4.8 all-to-all-start.2
  74.7 3.1 collective-permute-start
  81.2 31.0 %collective-permute-done.3.last_ref = bf16[1024,896]{1,0:T(8,128)(2,1)} collective-permute-done((bf16[1024,896]{1,0:T(8,128)(2,1)S(1)}, bf16[1024,896]{1,0:T(8,128)(2,1)}, u32[]{:S(2)}, u32[]{:S(2)}) %collective-permute-start.3) | collective-permute-done | bytes 1835040 | tf_op jit(solution)/shard_map/ppermute | solution.py:28
  119.3 30.4 %all-to-all-done.2.in_ref = bf16[8,320,1024]{2,1,0:T(8,128)(2,1)} async-done(((bf16[8,320,1024]{2,1,0:T(8,128)(2,1)}), bf16[8,320,1024]{2,1,0:T(8,128)(2,1)}, u32[]{:S(2)}, u32[]{:S(2)}) %all-to-all-start.2) | async-done | bytes 5242912 | tf_op jit(solution)/shard_map/all_to_all | solution.py:44
  151.1 4.5 all-to-all-start.3
  155.8 5.9 shard_map.170
  164.8 7.0 %shard_map.171.ctx_ref = bf16[256,512]{1,0:T(8,128)(2,1)S(1)} custom-call(f32[8]{0:T(128)S(1)} %fusion.51.slope_ref, s32[2,128,1]{2,1,0:T(8,128)S(1)} %copy.67.rows_ref, s32[2,1,128]{2,1,0:T(1,128)S(1)} %bitcast.150, bf16[256,1536]{1,0:T(8,128)(2,1)S(1)} %fusion.qkv_ref), custom_call_target="tpu_custom_call" | custom-call | flops 67108864 | bytes 1048576 | tf_op jit(solution)/shard_map/pallas_call | solution.py:357
  172.7 3.9 shard_map.172
  196.3 3.1 multiply_convert_fusion.1
  201.2 29.6 %collective-permute-done.11.last_ref = bf16[1024,896]{1,0:T(8,128)(2,1)S(1)} collective-permute-done((bf16[1024,896]{1,0:T(8,128)(2,1)S(1)}, bf16[1024,896]{1,0:T(8,128)(2,1)S(1)}, u32[]{:S(2)}, u32[]{:S(2)}) %collective-permute-start.11) | collective-permute-done | bytes 1835040 | tf_op jit(solution)/shard_map/ppermute | solution.py:28
  236.9 3.9 collective-permute-start.9
  240.8 11.2 %collective-permute-done.12.top_ref = bf16[512,896]{1,0:T(8,128)(2,1)S(1)} collective-permute-done((bf16[512,896]{1,0:T(8,128)(2,1)}, bf16[512,896]{1,0:T(8,128)(2,1)S(1)}, u32[]{:S(2)}, u32[]{:S(2)}) %collective-permute-start.12) | collective-permute-done | bytes 917536 | tf_op jit(solution)/shard_map/ppermute | solution.py:28
  255.1 3.9 shard_map.173
  262.2 7.0 %shard_map.174.ctx_ref = bf16[256,512]{1,0:T(8,128)(2,1)S(1)} custom-call(f32[8]{0:T(128)S(1)} %fusion.51.slope_ref, s32[2,128,1]{2,1,0:T(8,128)S(1)} %copy.67.rows_ref, s32[2,1,128]{2,1,0:T(1,128)S(1)} %bitcast.151, bf16[256,1536]{1,0:T(8,128)(2,1)S(1)} %fusion.1.qkv_ref), custom_call_target="tpu_custom_call" | custom-call | flops 67108864 | bytes 1048576 | tf_op jit(solution)/shard_map/pallas_call | solution.py:357
  273.2 4.5 collective-permute-start.14
  295.1 9.4 %shard_map.176 = (bf16[256,1536]{1,0:T(8,128)(2,1)S(1)}, f32[2,2,1,256]{3,2,1,0:T(1,128)S(1)}, f32[2,2,1,256]{3,2,1,0:T(1,128)S(1)}) custom-call(f32[8]{0:T(128)S(1)} %fusion.51.slope_ref, s32[2,128,1]{2,1,0:T(8,128)S(1)} %copy.67.rows_ref, s32[2,1,128]{2,1,0:T(1,128)S(1)} %bitcast.152, bf16[256,1536]{1,0:T(8,128)(2,1)S(1)} %fusion.1.qkv_ref, ...), custom_call_target="tpu_custom_call" | custom-call | flops 167772160 | bytes 2097152 | tf_op jit(solution)/shard_map/pallas_call | solution.py:376
  306.8 3.2 shard_map.188
  312.3 8.4 %all-to-all-start.8 = ((bf16[8,320,1024]{2,1,0:T(8,128)(2,1)}), bf16[8,320,1024]{2,1,0:T(8,128)(2,1)}, u32[]{:S(2)}, u32[]{:S(2)}) async-start(bf16[8,320,1024]{2,1,0:T(8,128)(2,1)} %copy-done), calls=%async_computation.8 | async-start | bytes 10485760 | tf_op jit(solution)/shard_map/all_to_all | solution.py:44
  333.8 3.5 collective-permute-start.25
  337.4 3.0 fusion.66
  343.1 15.0 %collective-permute-done.23 = bf16[512,896]{1,0:T(8,128)(2,1)S(1)} collective-permute-done((bf16[512,896]{1,0:T(8,128)(2,1)S(1)}, bf16[512,896]{1,0:T(8,128)(2,1)S(1)}, u32[]{:S(2)}, u32[]{:S(2)}) %collective-permute-start.23) | collective-permute-done | bytes 917536 | tf_op jit(solution)/shard_map/ppermute | solution.py:28
  366.1 27.7 %all-to-all-done.8 = bf16[8,320,1024]{2,1,0:T(8,128)(2,1)} async-done(((bf16[8,320,1024]{2,1,0:T(8,128)(2,1)}), bf16[8,320,1024]{2,1,0:T(8,128)(2,1)}, u32[]{:S(2)}, u32[]{:S(2)}) %all-to-all-start.8) | async-done | bytes 5242912 | tf_op jit(solution)/shard_map/all_to_all | solution.py:44
  393.8 3.8 select_reduce_fusion
  398.6 5.0 all-to-all-start.9
  409.3 3.2 shard_map.187
  414.8 5.6 all-to-all-start.6
  425.5 9.4 %shard_map.180 = (bf16[256,1536]{1,0:T(8,128)(2,1)S(1)}, f32[2,2,1,256]{3,2,1,0:T(1,128)S(1)}, f32[2,2,1,256]{3,2,1,0:T(1,128)S(1)}) custom-call(f32[8]{0:T(128)S(1)} %fusion.51.slope_ref, s32[2,128,1]{2,1,0:T(8,128)S(1)} %copy-done.24, s32[2,1,128]{2,1,0:T(1,128)S(1)} %bitcast.153, bf16[256,1536]{1,0:T(8,128)(2,1)S(1)} %copy-done.26, ...), custom_call_target="tpu_custom_call" | custom-call | flops 167772160 | bytes 2097152 | tf_op jit(solution)/shard_map/pallas_call | solution.py:376
  434.8 18.8 %collective-permute-done.24 = bf16[1024,896]{1,0:T(8,128)(2,1)} collective-permute-done((bf16[1024,896]{1,0:T(8,128)(2,1)}, bf16[1024,896]{1,0:T(8,128)(2,1)}, u32[]{:S(2)}, u32[]{:S(2)}) %collective-permute-start.24) | collective-permute-done | bytes 1835040 | tf_op jit(solution)/shard_map/ppermute | solution.py:28
  455.5 6.3 collective-permute-done.26
  465.9 3.4 collective-permute-start.28
  475.8 16.8 %all-to-all-done.6 = bf16[8,320,1024]{2,1,0:T(8,128)(2,1)} async-done(((bf16[8,320,1024]{2,1,0:T(8,128)(2,1)}), bf16[8,320,1024]{2,1,0:T(8,128)(2,1)}, u32[]{:S(2)}, u32[]{:S(2)}) %all-to-all-start.6) | async-done | bytes 5242912 | tf_op jit(solution)/shard_map/all_to_all | solution.py:44
  492.6 3.9 select_reduce_fusion.1
  497.4 4.2 all-to-all-start.7
  511.3 3.0 fusion.67
  521.8 4.9 all-to-all-start.5
  531.2 5.1 collective-permute-done.31
  544.3 3.2 all-to-all-done.5
  552.4 26.7 %collective-permute-done.32 = bf16[1024,896]{1,0:T(8,128)(2,1)} collective-permute-done((bf16[1024,896]{1,0:T(8,128)(2,1)}, bf16[1024,896]{1,0:T(8,128)(2,1)}, u32[]{:S(2)}, u32[]{:S(2)}) %collective-permute-start.32) | collective-permute-done | bytes 1835040 | tf_op jit(solution)/shard_map/ppermute | solution.py:32
  579.1 4.0 collective-permute-done.30
  586.1 41.2 %all_to_all.60 = bf16[16,64,896]{2,1,0:T(8,128)(2,1)S(1)} all-to-all(bf16[16,64,896]{2,1,0:T(8,128)(2,1)S(1)} %bitcast.157), channel_id=1, replica_groups=mesh['ylo'=2,'z'=4,'core'=2,'x'=4,'yhi'=2] {'ylo','x','yhi'}, dimensions={0} | all-to-all | bytes 3670016 | tf_op jit(solution)/shard_map/all_to_all | solution.py:44
  629.7 10.9 %all_to_all.61 = f32[8,24,128]{2,1,0:T(8,128)S(1)} all-to-all(f32[8,24,128]{2,1,0:T(8,128)S(1)} %copy.79), channel_id=1, replica_groups=mesh['ylo'=2,'z'=4,'core'=2,'x'=4,'yhi'=2] {'x','yhi'}, dimensions={0} | all-to-all | bytes 196608 | tf_op jit(solution)/shard_map/all_to_all | solution.py:44
  640.7 14.4 %all_to_all.62 = f32[16,24,128]{2,1,0:T(8,128)S(1)} all-to-all(f32[16,24,128]{2,1,0:T(8,128)S(1)} %broadcast_in_dim.118), channel_id=1, replica_groups=mesh['ylo'=2,'z'=4,'core'=2,'x'=4,'yhi'=2] {'ylo','z','core'}, dimensions={0} | all-to-all | bytes 393216 | tf_op jit(solution)/shard_map/all_to_all | solution.py:44
  668.1 4.1 shard_map.186
  (564 shorter events, 188.4 us)
Async XLA Ops:
  16.3 34.3 %all-to-all-start.1 = ((bf16[8,128,896]{2,1,0:T(8,128)(2,1)}), bf16[8,128,896]{2,1,0:T(8,128)(2,1)S(1)}, u32[]{:S(2)}, u32[]{:S(2)}) async-start(bf16[8,128,896]{2,1,0:T(8,128)(2,1)} %broadcast_in_dim.100), calls=%async_computation.1 | async-start | bytes 3670016 | tf_op jit(solution)/shard_map/all_to_all | solution.py:44
  51.3 9.9 %all-to-all-start = ((bf16[8,24,128]{2,1,0:T(8,128)(2,1)}), bf16[8,24,128]{2,1,0:T(8,128)(2,1)S(1)}, u32[]{:S(2)}, u32[]{:S(2)}) async-start(bf16[8,24,128]{2,1,0:T(8,128)(2,1)} %broadcast_in_dim.98), calls=%async_computation | async-start | bytes 98304 | tf_op jit(solution)/shard_map/all_to_all | solution.py:44
  65.2 84.4 %all-to-all-start.2 = ((bf16[8,320,1024]{2,1,0:T(8,128)(2,1)}), bf16[8,320,1024]{2,1,0:T(8,128)(2,1)}, u32[]{:S(2)}, u32[]{:S(2)}) async-start(bf16[8,320,1024]{2,1,0:T(8,128)(2,1)} %broadcast_in_dim.102), calls=%async_computation.2 | async-start | bytes 10485760 | tf_op jit(solution)/shard_map/all_to_all | solution.py:44
  70.0 199.2 %all-gather.10.cloned.1.call-start = ((), (), s32[]{:S(2)}) async-start(), calls=%async_computation.12 | async-start | bytes 5898240 | tf_op jit(solution)/shard_map/all_gather | solution.py:476
  70.7 41.5 %collective-permute-start.3 = (bf16[1024,896]{1,0:T(8,128)(2,1)S(1)}, bf16[1024,896]{1,0:T(8,128)(2,1)}, u32[]{:S(2)}, u32[]{:S(2)}) collective-permute-start(bf16[1024,896]{1,0:T(8,128)(2,1)S(1)} %bitcast.142), channel_id=1, source_target_pairs={{0,16},{16,32},{32,48},{48,0},{1,17},{17,33},{33,49},{49,1},{2,18}... | collective-permute-start | bytes 5505032 | tf_op jit(solution)/shard_map/ppermute | solution.py:28
  72.4 42.0 %collective-permute-start.2 = (bf16[1024,896]{1,0:T(8,128)(2,1)S(1)}, bf16[1024,896]{1,0:T(8,128)(2,1)}, u32[]{:S(2)}, u32[]{:S(2)}) collective-permute-start(bf16[1024,896]{1,0:T(8,128)(2,1)S(1)} %bitcast.143), channel_id=1, source_target_pairs={{0,48},{16,0},{32,16},{48,32},{1,49},{17,1},{33,17},{49,33},{2,50}... | collective-permute-start | bytes 5505032 | tf_op jit(solution)/shard_map/ppermute | solution.py:32
  74.7 4.0 collective-permute-start
  78.8 216.3 %copy-start.23 = (s32[2,128,1]{2,1,0:T(8,128)}, s32[2,128,1]{2,1,0:T(8,128)S(1)}, u32[]{:S(2)}) copy-start(s32[2,128,1]{2,1,0:T(8,128)S(1)} %copy.67.rows_ref) | copy-start | bytes 3076
  81.0 80.7 %collective-permute-start.1 = (bf16[128,1024]{1,0:T(8,128)(2,1)S(1)}, bf16[128,1024]{1,0:T(8,128)(2,1)}, u32[]{:S(2)}, u32[]{:S(2)}) collective-permute-start(bf16[128,1024]{1,0:T(8,128)(2,1)S(1)} %add_convert_fusion.9), channel_id=1, source_target_pairs={{0,8},{8,0},{1,9},{9,1},{2,10},{10,2},{3,11},{11,3},{4,12},{12,4},... | collective-permute-start | bytes 786440 | tf_op jit(solution)/shard_map/ppermute | solution.py:36
  114.4 41.4 %collective-permute-start.4 = (bf16[512,896]{1,0:T(8,128)(2,1)}, bf16[512,896]{1,0:T(8,128)(2,1)S(1)}, u32[]{:S(2)}, u32[]{:S(2)}) collective-permute-start(bf16[512,896]{1,0:T(8,128)(2,1)} %slice.381), channel_id=1, source_target_pairs={{0,16},{16,32},{32,48},{48,0},{1,17},{17,33},{33,49},{49,1},{2,18}... | collective-permute-start | bytes 2752520 | tf_op jit(solution)/shard_map/ppermute | solution.py:28
  116.6 39.2 %collective-permute-start.5 = (bf16[512,896]{1,0:T(8,128)(2,1)}, bf16[512,896]{1,0:T(8,128)(2,1)}, u32[]{:S(2)}, u32[]{:S(2)}) collective-permute-start(bf16[512,896]{1,0:T(8,128)(2,1)} %slice.382), channel_id=1, source_target_pairs={{0,48},{16,0},{32,16},{48,32},{1,49},{17,1},{33,17},{49,33},{2,50}... | collective-permute-start | bytes 2752520 | tf_op jit(solution)/shard_map/ppermute | solution.py:32
  151.1 34.7 %all-to-all-start.3 = ((bf16[8,128,896]{2,1,0:T(8,128)(2,1)}), bf16[8,128,896]{2,1,0:T(8,128)(2,1)}, u32[]{:S(2)}, u32[]{:S(2)}) async-start(bf16[8,128,896]{2,1,0:T(8,128)(2,1)} %broadcast_in_dim.105), calls=%async_computation.3 | async-start | bytes 3670016 | tf_op jit(solution)/shard_map/all_to_all | solution.py:44
  180.7 9.7 %collective-permute-start.6 = (f32[128,1024]{1,0:T(8,128)}, f32[128,1024]{1,0:T(8,128)}, u32[]{:S(2)}, u32[]{:S(2)}) collective-permute-start(f32[128,1024]{1,0:T(8,128)} %slice.387), channel_id=1, source_target_pairs={{0,8},{8,0},{1,9},{9,1},{2,10},{10,2},{3,11},{11,3},{4,12},{12,4},... | collective-permute-start | bytes 1572872 | tf_op jit(solution)/shard_map/ppermute | solution.py:36
  187.7 44.3 %collective-permute-start.10 = (bf16[1024,896]{1,0:T(8,128)(2,1)S(1)}, bf16[1024,896]{1,0:T(8,128)(2,1)S(1)}, u32[]{:S(2)}, u32[]{:S(2)}) collective-permute-start(bf16[1024,896]{1,0:T(8,128)(2,1)S(1)} %bitcast.145), channel_id=1, source_target_pairs={{0,48},{16,0},{32,16},{48,32},{1,49},{17,1},{33,17},{49,33},{2,50}... | collective-permute-start | bytes 5505032 | tf_op jit(solution)/shard_map/ppermute | solution.py:32
  190.4 40.4 %collective-permute-start.11 = (bf16[1024,896]{1,0:T(8,128)(2,1)S(1)}, bf16[1024,896]{1,0:T(8,128)(2,1)S(1)}, u32[]{:S(2)}, u32[]{:S(2)}) collective-permute-start(bf16[1024,896]{1,0:T(8,128)(2,1)S(1)} %bitcast.146), channel_id=1, source_target_pairs={{0,16},{16,32},{32,48},{48,0},{1,17},{17,33},{33,49},{49,1},{2,18}... | collective-permute-start | bytes 5505032 | tf_op jit(solution)/shard_map/ppermute | solution.py:28
  192.6 3.7 collective-permute-start.7
  200.8 34.9 %collective-permute-start.8 = (f32[128,1024]{1,0:T(8,128)S(1)}, f32[128,1024]{1,0:T(8,128)S(1)}, u32[]{:S(2)}, u32[]{:S(2)}) collective-permute-start(f32[128,1024]{1,0:T(8,128)S(1)} %slice.394), channel_id=1, source_target_pairs={{0,8},{8,0},{1,9},{9,1},{2,10},{10,2},{3,11},{11,3},{4,12},{12,4},... | collective-permute-start | bytes 1572872 | tf_op jit(solution)/shard_map/ppermute | solution.py:36
  231.9 20.0 %collective-permute-start.12 = (bf16[512,896]{1,0:T(8,128)(2,1)}, bf16[512,896]{1,0:T(8,128)(2,1)S(1)}, u32[]{:S(2)}, u32[]{:S(2)}) collective-permute-start(bf16[512,896]{1,0:T(8,128)(2,1)} %slice.399), channel_id=1, source_target_pairs={{0,16},{16,32},{32,48},{48,0},{1,17},{17,33},{33,49},{49,1},{2,18}... | collective-permute-start | bytes 2752520 | tf_op jit(solution)/shard_map/ppermute | solution.py:28
  233.0 19.1 %collective-permute-start.13 = (bf16[512,896]{1,0:T(8,128)(2,1)}, bf16[512,896]{1,0:T(8,128)(2,1)}, u32[]{:S(2)}, u32[]{:S(2)}) collective-permute-start(bf16[512,896]{1,0:T(8,128)(2,1)} %slice.400), channel_id=1, source_target_pairs={{0,48},{16,0},{32,16},{48,32},{1,49},{17,1},{33,17},{49,33},{2,50}... | collective-permute-start | bytes 2752520 | tf_op jit(solution)/shard_map/ppermute | solution.py:32
  236.9 22.2 %collective-permute-start.9 = (bf16[128,1024]{1,0:T(8,128)(2,1)S(1)}, bf16[128,1024]{1,0:T(8,128)(2,1)S(1)}, u32[]{:S(2)}, u32[]{:S(2)}) collective-permute-start(bf16[128,1024]{1,0:T(8,128)(2,1)S(1)} %add_convert_fusion.7), channel_id=1, source_target_pairs={{0,8},{8,0},{1,9},{9,1},{2,10},{10,2},{3,11},{11,3},{4,12},{12,4},... | collective-permute-start | bytes 786440 | tf_op jit(solution)/shard_map/ppermute | solution.py:36
  273.2 6.1 collective-permute-start.14
  279.8 1.6 collective-permute-start.15
  281.0 2.4 collective-permute-start.17
  287.6 2.0 collective-permute-start.18
  289.4 2.0 collective-permute-start.16
  293.0 1.6 collective-permute-start.19
  306.5 23.5 %collective-permute-start.20 = (f32[128,1024]{1,0:T(8,128)}, f32[128,1024]{1,0:T(8,128)}, u32[]{:S(2)}, u32[]{:S(2)}) collective-permute-start(f32[128,1024]{1,0:T(8,128)} %slice.417), channel_id=1, source_target_pairs={{0,8},{8,0},{1,9},{9,1},{2,10},{10,2},{3,11},{11,3},{4,12},{12,4},... | collective-permute-start | bytes 1572872 | tf_op jit(solution)/shard_map/ppermute | solution.py:36
  312.3 81.5 %all-to-all-start.8 = ((bf16[8,320,1024]{2,1,0:T(8,128)(2,1)}), bf16[8,320,1024]{2,1,0:T(8,128)(2,1)}, u32[]{:S(2)}, u32[]{:S(2)}) async-start(bf16[8,320,1024]{2,1,0:T(8,128)(2,1)} %copy-done), calls=%async_computation.8 | async-start | bytes 10485760 | tf_op jit(solution)/shard_map/all_to_all | solution.py:44
  332.9 4.4 collective-permute-start.21
  333.8 24.3 %collective-permute-start.23 = (bf16[512,896]{1,0:T(8,128)(2,1)S(1)}, bf16[512,896]{1,0:T(8,128)(2,1)S(1)}, u32[]{:S(2)}, u32[]{:S(2)}) collective-permute-start(bf16[512,896]{1,0:T(8,128)(2,1)S(1)} %get-tuple-element.133), channel_id=1, source_target_pairs={{0,16},{16,32},{32,48},{48,0},{1,17},{17,33},{33,49},{49,1},{2,18}... | collective-permute-start | bytes 2752520 | tf_op jit(solution)/shard_map/ppermute | solution.py:28
  333.8 25.4 %collective-permute-start.25 = (bf16[512,896]{1,0:T(8,128)(2,1)S(1)}, bf16[512,896]{1,0:T(8,128)(2,1)S(1)}, u32[]{:S(2)}, u32[]{:S(2)}) collective-permute-start(bf16[512,896]{1,0:T(8,128)(2,1)S(1)} %get-tuple-element.132), channel_id=1, source_target_pairs={{0,48},{16,0},{32,16},{48,32},{1,49},{17,1},{33,17},{49,33},{2,50}... | collective-permute-start | bytes 2752520 | tf_op jit(solution)/shard_map/ppermute | solution.py:32
  341.8 18.7 %collective-permute-start.22 = (f32[128,1024]{1,0:T(8,128)S(1)}, f32[128,1024]{1,0:T(8,128)S(1)}, u32[]{:S(2)}, u32[]{:S(2)}) collective-permute-start(f32[128,1024]{1,0:T(8,128)S(1)} %slice.419), channel_id=1, source_target_pairs={{0,8},{8,0},{1,9},{9,1},{2,10},{10,2},{3,11},{11,3},{4,12},{12,4},... | collective-permute-start | bytes 1572872 | tf_op jit(solution)/shard_map/ppermute | solution.py:36
  363.8 44.4 %collective-permute-start.27 = (bf16[128,1024]{1,0:T(8,128)(2,1)}, bf16[128,1024]{1,0:T(8,128)(2,1)}, u32[]{:S(2)}, u32[]{:S(2)}) collective-permute-start(bf16[128,1024]{1,0:T(8,128)(2,1)} %convert_select_fusion), channel_id=1, source_target_pairs={{0,8},{8,0},{1,9},{9,1},{2,10},{10,2},{3,11},{11,3},{4,12},{12,4},... | collective-permute-start | bytes 786440 | tf_op jit(solution)/shard_map/ppermute | solution.py:36
  398.6 16.2 %all-to-all-start.9 = ((bf16[8,40,1024]{2,1,0:T(8,128)(2,1)}), bf16[8,40,1024]{2,1,0:T(8,128)(2,1)}, u32[]{:S(2)}, u32[]{:S(2)}) async-start(bf16[8,40,1024]{2,1,0:T(8,128)(2,1)} %pad_maximum_fusion.5), calls=%async_computation.9 | async-start | bytes 1310720 | tf_op jit(solution)/shard_map/all_to_all | solution.py:44
  406.7 47.0 %collective-permute-start.24 = (bf16[1024,896]{1,0:T(8,128)(2,1)}, bf16[1024,896]{1,0:T(8,128)(2,1)}, u32[]{:S(2)}, u32[]{:S(2)}) collective-permute-start(bf16[1024,896]{1,0:T(8,128)(2,1)} %pad_maximum_fusion), channel_id=1, source_target_pairs={{0,16},{16,32},{32,48},{48,0},{1,17},{17,33},{33,49},{49,1},{2,18}... | collective-permute-start | bytes 5505032 | tf_op jit(solution)/shard_map/ppermute | solution.py:28
  414.8 77.8 %all-to-all-start.6 = ((bf16[8,320,1024]{2,1,0:T(8,128)(2,1)}), bf16[8,320,1024]{2,1,0:T(8,128)(2,1)}, u32[]{:S(2)}, u32[]{:S(2)}) async-start(bf16[8,320,1024]{2,1,0:T(8,128)(2,1)} %copy-done.1), calls=%async_computation.6 | async-start | bytes 10485760 | tf_op jit(solution)/shard_map/all_to_all | solution.py:44
  420.4 236.5 %all-gather.18.cloned.1.call-start = ((), (), s32[]{:S(2)}) async-start(), calls=%async_computation.16 | async-start | bytes 1392640 | tf_op jit(solution)/shard_map/all_gather | solution.py:527
  422.4 39.4 %collective-permute-start.26 = (bf16[1024,896]{1,0:T(8,128)(2,1)S(1)}, bf16[1024,896]{1,0:T(8,128)(2,1)S(1)}, u32[]{:S(2)}, u32[]{:S(2)}) collective-permute-start(bf16[1024,896]{1,0:T(8,128)(2,1)S(1)} %pad_maximum_fusion.1), channel_id=1, source_target_pairs={{0,48},{16,0},{32,16},{48,32},{1,49},{17,1},{33,17},{49,33},{2,50}... | collective-permute-start | bytes 5505032 | tf_op jit(solution)/shard_map/ppermute | solution.py:32
  465.9 5.2 collective-permute-start.28
  497.4 11.9 %all-to-all-start.7 = ((bf16[8,40,1024]{2,1,0:T(8,128)(2,1)}), bf16[8,40,1024]{2,1,0:T(8,128)(2,1)}, u32[]{:S(2)}, u32[]{:S(2)}) async-start(bf16[8,40,1024]{2,1,0:T(8,128)(2,1)} %pad_maximum_fusion.4), calls=%async_computation.7 | async-start | bytes 1310720 | tf_op jit(solution)/shard_map/all_to_all | solution.py:44
  501.7 157.7 %all-gather.16.cloned.1.call-start = ((), (), s32[]{:S(2)}) async-start(), calls=%async_computation.15 | async-start | bytes 1392640 | tf_op jit(solution)/shard_map/all_gather | solution.py:527
  514.3 22.0 %collective-permute-start.31 = (bf16[512,896]{1,0:T(8,128)(2,1)}, bf16[512,896]{1,0:T(8,128)(2,1)}, u32[]{:S(2)}, u32[]{:S(2)}) collective-permute-start(bf16[512,896]{1,0:T(8,128)(2,1)} %get-tuple-element.131), channel_id=1, source_target_pairs={{0,48},{16,0},{32,16},{48,32},{1,49},{17,1},{33,17},{49,33},{2,50}... | collective-permute-start | bytes 2752520 | tf_op jit(solution)/shard_map/ppermute | solution.py:32
  518.1 21.6 %collective-permute-start.29 = (bf16[512,896]{1,0:T(8,128)(2,1)}, bf16[512,896]{1,0:T(8,128)(2,1)}, u32[]{:S(2)}, u32[]{:S(2)}) collective-permute-start(bf16[512,896]{1,0:T(8,128)(2,1)} %get-tuple-element.130), channel_id=1, source_target_pairs={{0,16},{16,32},{32,48},{48,0},{1,17},{17,33},{33,49},{49,1},{2,18}... | collective-permute-start | bytes 2752520 | tf_op jit(solution)/shard_map/ppermute | solution.py:28
  521.8 25.7 %all-to-all-start.5 = ((bf16[16,64,896]{2,1,0:T(8,128)(2,1)}), bf16[16,64,896]{2,1,0:T(8,128)(2,1)}, u32[]{:S(2)}, u32[]{:S(2)}) async-start(bf16[16,64,896]{2,1,0:T(8,128)(2,1)} %bitcast.156), calls=%async_computation.5 | async-start | bytes 3670016 | tf_op jit(solution)/shard_map/all_to_all | solution.py:44
  526.7 138.4 %all-gather.14.cloned.1.call-start = ((), (), s32[]{:S(2)}) async-start(), calls=%async_computation.14 | async-start | bytes 1949696 | tf_op jit(solution)/shard_map/all_gather | solution.py:521
  539.1 40.1 %collective-permute-start.32 = (bf16[1024,896]{1,0:T(8,128)(2,1)}, bf16[1024,896]{1,0:T(8,128)(2,1)}, u32[]{:S(2)}, u32[]{:S(2)}) collective-permute-start(bf16[1024,896]{1,0:T(8,128)(2,1)} %pad_maximum_fusion.3), channel_id=1, source_target_pairs={{0,48},{16,0},{32,16},{48,32},{1,49},{17,1},{33,17},{49,33},{2,50}... | collective-permute-start | bytes 5505032 | tf_op jit(solution)/shard_map/ppermute | solution.py:32
  542.5 40.7 %collective-permute-start.30 = (bf16[1024,896]{1,0:T(8,128)(2,1)}, bf16[1024,896]{1,0:T(8,128)(2,1)}, u32[]{:S(2)}, u32[]{:S(2)}) collective-permute-start(bf16[1024,896]{1,0:T(8,128)(2,1)} %pad_maximum_fusion.2), channel_id=1, source_target_pairs={{0,16},{16,32},{32,48},{48,0},{1,17},{17,33},{33,49},{49,1},{2,18}... | collective-permute-start | bytes 5505032 | tf_op jit(solution)/shard_map/ppermute | solution.py:28
  550.0 115.1 %all-gather.12.cloned.1.call-start = ((), (), s32[]{:S(2)}) async-start(), calls=%async_computation.13 | async-start | bytes 1949696 | tf_op jit(solution)/shard_map/all_gather | solution.py:521
  (129 other events, 1322.0 us)
Sparse Core Ops, SparseCore 0:
  73.1 147.3 all-gather.9
  471.3 34.1 all-gather.17
  511.4 44.7 all-gather.15
  558.3 40.2 all-gather.13
  628.5 34.9 all-gather.11

commit v5 on v4

--- a/solution.py
+++ b/solution.py
@@ -62,16 +62,13 @@
     half = own.shape[0] // 2
     from_previous = up(far[:half])
     from_following = down(far[half:])
-    go_up = jnp.concatenate(
-        [(following[:half].astype(f32) + from_previous.astype(f32)).astype(bf16), following[half:]]
-    )
-    go_down = jnp.concatenate(
-        [previous[:half], (previous[half:].astype(f32) + from_following.astype(f32)).astype(bf16)]
-    )
-    got_up = up(go_up)
-    got_down = down(go_down)
-    total = own.astype(f32) + got_up.astype(f32) + got_down.astype(f32)
-    return total, (following, previous), (from_previous, from_following), (got_up, got_down)
+    plain_up = up(following[half:])
+    plain_down = down(previous[:half])
+    sum_up = up((following[:half].astype(f32) + from_previous.astype(f32)).astype(bf16))
+    sum_down = down((previous[half:].astype(f32) + from_following.astype(f32)).astype(bf16))
+    top = own[:half].astype(f32) + sum_up.astype(f32) + plain_down.astype(f32)
+    bottom = own[half:].astype(f32) + plain_up.astype(f32) + sum_down.astype(f32)
+    return (top, bottom), (following, previous), (from_previous, from_following), (sum_up, sum_down)
 
 
 def rolled(stack, start):
@@ -192,7 +189,7 @@
         (gathered,),
         (jax.ShapeDtypeStruct((2048, D), bf16), jax.ShapeDtypeStruct((512, D), bf16)),
         (4,),
-        [pl.BlockSpec((2, 320, D), lambda i, at: (lax.rem(i + at[0], 4), 0, 0))],
+        [pl.BlockSpec((2, gathered.shape[1], D), lambda i, at: (lax.rem(i + at[0], 4), 0, 0))],
         (pl.BlockSpec((512, D), lambda i, at: (i, 0)), pl.BlockSpec((128, D), lambda i, at: (i, 0))),
     )
 
@@ -446,8 +443,9 @@
     def both(own):
         return jnp.concatenate([own, swap(own)], axis=0)
 
-    def halves_summed(partial):
-        return partial[:RUN] + swap(partial[RUN:])
+    def halves_summed(product, a, w):
+        theirs = swap(product(a[RUN:], w))
+        return product(a[:RUN], w) + theirs
 
     small = jnp.concatenate(
         [
@@ -455,31 +453,30 @@
             up_bias.reshape(8, 128),
         ]
     )
-    small = to_all(small, SHARD, 8).reshape(4, 2, 24, 128).astype(f32)
+
+    mine_z, mine_x = select_weights(at, w_qkv, w_proj, w_up, w_down)
+    weights = []
+    piece_x = jnp.concatenate([mine_x[0], small.reshape(3, D), jnp.zeros((5, D), bf16)])
+    block_z = to_all(mine_z[0], SHARD, 8).reshape(D, 896)
+    all_x = to_all(after(piece_x, block_z), SHARD, 8)
+    all_small = all_x[:, 320:323]
+    next_z = lax.all_gather(after(mine_z[1], block_z), SHARD, axis=0).reshape(D, 896)
+    for layer in range(LAYERS):
+        own, following, (top, bottom), previous = ring_gather(block_z, z_up, z_down)
+        wup, wqkv = split_z(at, own, following, top, bottom, previous)
+        wdown, wproj = split_x(at, all_x)
+        weights.append((wqkv, wproj, wup, wdown))
+        if layer == 0:
+            block_z = after(next_z, top)
+            all_x = lax.all_gather(after(mine_x[1], previous, following, all_x[0]), SHARD, axis=0)
+
+    small = all_small.reshape(4, 2, 24, 128).astype(f32)
     wide = jnp.transpose(small[:, :, :16], (2, 0, 1, 3)).reshape(LAYERS, 8, D)
     hidden_bias = small[:, :, 16:].reshape(4, 2, LAYERS, 2, 256)
 
     def core_heads(vector):
         picked = lax.dynamic_index_in_dim(vector.reshape(4, 2, 2, 64), core, axis=2, keepdims=False)
         return rolled(picked.reshape(4, 128), z)
-
-    mine_z, mine_x = select_weights(at, w_qkv, w_proj, w_up, w_down)
-    weights, earlier = [], None
-    for layer in range(LAYERS):
-        piece_z, piece_x = mine_z[layer], mine_x[layer]
-        if earlier is None:
-            block_z = to_all(piece_z, SHARD, 8).reshape(D, 896)
-            all_x = to_all(after(piece_x, block_z), SHARD, 8)
-            first_z = block_z
-        else:
-            block_z = to_all(after(piece_z, first_z), SHARD, 8).reshape(D, 896)
-            all_x = lax.all_gather(after(piece_x, first_z), SHARD, axis=0)
-            block_z = after(block_z, earlier)
-        own, following, (top, bottom), previous = ring_gather(block_z, z_up, z_down)
-        earlier = top
-        wup, wqkv = split_z(at, own, following, top, bottom, previous)
-        wdown, wproj = split_x(at, all_x)
-        weights.append((wqkv, wproj, wup, wdown))
 
     starts = both(doc_start.reshape(1, RUN))
     rows, cols = starts.reshape(2, RUN, 1), starts.reshape(2, 1, RUN)
@@ -499,34 +496,36 @@
         first_in = both(first_f.astype(bf16))
         qkv = (dot(first_in, wqkv) + bqkv).astype(bf16)
         ctx = attend(qkv, rows, cols, slopes)
-        middle = current + halves_summed(dot(ctx, wproj)) + bproj
+        middle = current + halves_summed(dot, ctx, wproj) + bproj
         second_f, normed_two, inv_two = layer_norm(middle, gain_two, shift_two)
         second_in = both(second_f.astype(bf16))
         upper = dot(second_in, wup) + ubias
         activ = gelu_tanh(upper).astype(bf16)
-        current = middle + halves_summed(dot(activ, wdown)) + bdown
+        current = middle + halves_summed(dot, activ, wdown) + bdown
         kept.append((first_in, normed_one, inv_one, qkv, ctx, second_in, normed_two, inv_two, upper, activ, gain_one, gain_two))
     hidden_out = current
 
     def summed(blocks):
         return jnp.sum(blocks.astype(f32), axis=0).astype(bf16)
 
-    def reduce_z(a2, dub, a1, dqkv):
+    def ring_z(a2, dub, a1, dqkv):
         parts = [grad_z(at, a2, dub, a1, dqkv, i) for i in (2, 1, 3, 0)]
         parts = [parts[i] for i in (3, 1, 0, 2)]
-        total, sent, near, got = ring_scatter(parts, z_up, z_down)
-        part = total.astype(bf16)
-        part = jnp.transpose(part.reshape(8, 2, 64, 896), (1, 0, 2, 3)).reshape(16, 64, 896)
-        part = summed(exchange(part, ("ylo", "x", "yhi")))
-        return lax.all_gather(part, REP, axis=0).reshape(2, 4, 2, 64, 896), (sent, near, got)
+        (top, bottom), sent, near, got = ring_scatter(parts, z_up, z_down)
+        part = jnp.concatenate([top.astype(bf16).reshape(8, 64, 896), bottom.astype(bf16).reshape(8, 64, 896)])
+        return part, (sent, near, got)
 
     def finish_x(blocks, later):
         part = summed(after(blocks, later))
-        part = jnp.concatenate([part[:256].reshape(8, 32, D), part[256:].reshape(8, 8, D)], axis=1)
-        part = summed(exchange(part, ("ylo", "z")))
-        part = lax.all_gather(part, REP, axis=0).reshape(8, 2, 40, D)
-        part = jnp.transpose(part, (1, 0, 2, 3))
-        return part[:, :, :32].reshape(512, D), part[:, :, 32:].reshape(128, D)
+        part = jnp.concatenate([part[:256].reshape(8, 32, D), part[256:320].reshape(8, 8, D)], axis=1)
+        return summed(exchange(part, ("ylo", "z")))
+
+    def share(part_z, part_x, *earlier):
+        part = jnp.concatenate([part_z.reshape(56, D), part_x])
+        parts = lax.all_gather(after(part, *earlier) if earlier else part, REP, axis=0)
+        by_z = parts[:, :56].reshape(2, 4, 2, 64, 896)
+        by_x = jnp.transpose(parts[:, 56:].reshape(8, 2, 40, D), (1, 0, 2, 3))
+        return by_z, (by_x[:, :, :32].reshape(512, D), by_x[:, :, 32:].reshape(128, D))
 
     grads_x, grads_z = [None] * LAYERS, [None] * LAYERS
     thin_grads, head_grads, unit_grads = [None] * LAYERS, [None] * LAYERS, [None] * LAYERS
@@ -541,22 +540,29 @@
         grad_upper = dot_nt(grad_yb, wdown) * gelu_slope(upper)
         g_ubias = jnp.sum(grad_upper, axis=0)
         grad_ub = grad_upper.astype(bf16)
-        grad_two = halves_summed(dot_nt(grad_ub, wup))
+        grad_two = halves_summed(dot_nt, grad_ub, wup)
         back_two, g_gain_two, g_shift_two = norm_back(grad_two, normed_two, inv_two, gain_two)
         grad_mid = running + back_two
         g_bproj = jnp.sum(grad_mid, axis=0)
         grad_midb = grad_mid.astype(bf16)
         if ring_state is not None:
             grad_midb = after(grad_midb, *ring_state[1])
-            grads_x[layer + 1] = finish_x(waiting_x, grad_midb)
+            later_x = waiting_x
         grad_midb = both(grad_midb)
         grad_ctx = dot_nt(grad_midb, wproj).astype(bf16)
         waiting_x = exchange(grad_x(at, activ, grad_yb, ctx, grad_midb), SHARD)
         grad_qkv, g_bq, g_bv = attend_back(qkv, ctx, grad_ctx, rows, cols, slopes)
         if ring_state is not None:
             grad_qkv = after(grad_qkv, *ring_state[2])
-        grads_z[layer], ring_state = reduce_z(second_in, grad_ub, first_in, grad_qkv)
-        grad_one = halves_summed(dot_nt(grad_qkv, wqkv))
+            later_x = finish_x(later_x, grad_ctx)
+            later_z = lax.psum_scatter(after(part_z, grad_ctx), ("x", "yhi", "ylo"), scatter_dimension=0, tiled=True)[0]
+        part_z, ring_state = ring_z(second_in, grad_ub, first_in, grad_qkv)
+        if layer == 0:
+            grad_qkv = after(grad_qkv, *ring_state[0])
+        grad_one = halves_summed(dot_nt, grad_qkv, wqkv)
+        if layer == 0:
+            grad_one = after(grad_one, *ring_state[1])
+            grads_z[1], grads_x[1] = share(later_z, later_x, *ring_state[1])
         back_one, g_gain_one, g_shift_one = norm_back(grad_one, normed_one, inv_one, gain_one)
         running = grad_mid + back_one
 
@@ -564,7 +570,9 @@
         head_grads[layer] = [jnp.sum(g, axis=0).reshape(4, 128) for g in (g_bq, g_bv)]
         unit_grads[layer] = g_ubias.reshape(4, 512)
 
-    grads_x[0] = finish_x(waiting_x, running)
+    part_x = finish_x(waiting_x, running)
+    part_z = summed(exchange(after(part_z, part_x), ("x", "yhi", "ylo")))
+    grads_z[0], grads_x[0] = share(part_z, part_x)
 
     thin = jnp.stack(thin_grads[0] + thin_grads[1]).reshape(LAYERS, 6, 4, 2, 128)
     heads = jnp.stack(head_grads[0] + head_grads[1], axis=1)

time: 689 us -> 750 us (1.089)
  waiting for transfers between devices: 264 us -> 312 us
  blocking collectives: 66.5 us -> 37.3 us
  local copies, waits for them, and re-layouts: 71.3 us -> 97.3 us
  matrix products: 23.9 us -> 47.1 us
  other arithmetic: 58.2 us -> 48.6 us
    unnamed x5 -> x6, waiting for transfers between devices: 0.75 us -> 61.4 us
    ppermute x8 -> x10, waiting for transfers between devices: 110 us -> 155 us  [z_up(): return lax.ppermute(a, 'z', ring(1))]
    all_to_all x9 -> x7, waiting for transfers between devices: 111 us -> 68.9 us  [exchange(): return lax.all_to_all(blocks, axes, 0, 0, tiled=True)]
    all_to_all x3 -> x2, blocking collectives: 66.5 us -> 37.3 us  [exchange(): return lax.all_to_all(blocks, axes, 0, 0, tiled=True)]
    ppermute x8 -> x10, waiting for transfers between devices: 38.2 us -> 22.4 us  [z_down(): return lax.ppermute(a, 'z', ring(3))]
    dot_general x8 -> x12, matrix products: 12.6 us -> 25.7 us  [dot_nt(): lax.dot_general(a, b, (((1,), (1,)), ((), ())), preferred_element_type=f32)]
    all_to_all x9 -> x7, starting transfers between devices: 48.3 us -> 36.8 us  [exchange(): return lax.all_to_all(blocks, axes, 0, 0, tiled=True)]
    dot_general x8 -> x12, matrix products: 11.3 us -> 21.3 us  [dot(): return jnp.dot(a, b, preferred_element_type=f32)]
  transfers between devices with their start and end apart: 47 -> 49, of which waited for: 22 -> 26; matrix products, arithmetic and copies ran while one was open for 16% -> 17% of each run, Pallas kernels for 9% -> 8%
where the time goes in v5:
time: 750 us; the launch traced here: 739 us
  waiting for transfers between devices  312 us (42%)
  local copies, waits for them, and re-layouts  97.3 us (13%)
  starting transfers between devices  94.5 us (13%)
  Pallas kernels  73.2 us (10%)
  other arithmetic  48.6 us (6%)
  matrix products  47.1 us (6%)
  blocking collectives  37.3 us (5%)
  between operations  28.7 us (4%)
    ppermute x10, waiting for transfers between devices, z_up(): return lax.ppermute(a, 'z', ring(1))  155 us
    all_to_all x7, waiting for transfers between devices, exchange(): return lax.all_to_all(blocks, axes, 0, 0, tiled=True)  68.9 us
    unnamed x6, waiting for transfers between devices  61.4 us
    pallas_call x15, Pallas kernels, call(): pl.pallas_call(kernel, out_shape=out_shape, grid_spec=pltpu.PrefetchScala...  39.3 us
    unnamed x310, local copies, waits for them, and re-layouts  37.9 us
    all_to_all x2, blocking collectives, exchange(): return lax.all_to_all(blocks, axes, 0, 0, tiled=True)  37.3 us
    all_to_all x7, starting transfers between devices, exchange(): return lax.all_to_all(blocks, axes, 0, 0, tiled=True)  36.8 us
    ppermute x17, starting transfers between devices, swap(): return lax.ppermute(a, 'core', [(0, 1), (1, 0)])  26.5 us
  transfers between devices with their start and end apart: 49, of which 26 were waited for; matrix products, arithmetic and copies ran while one was open for 17% of the time, Pallas kernels for 8%

profile of v5, /device:TPU:1, one launch (start us, length us, event | category | flops | bytes accessed | tf_op | source)
XLA Modules:
  0.0 739.1 jit_solution(16470716770519189232)
XLA Ops:
  16.3 7.6 %all-to-all-start = ((bf16[8,128,896]{2,1,0:T(8,128)(2,1)}), bf16[8,128,896]{2,1,0:T(8,128)(2,1)S(1)}, u32[]{:S(2)}, u32[]{:S(2)}) async-start(bf16[8,128,896]{2,1,0:T(8,128)(2,1)} %broadcast_in_dim.89), calls=%async_computation | async-start | bytes 3670016 | tf_op jit(solution)/shard_map/all_to_all | solution.py:44
  25.0 25.6 %all-to-all-done = bf16[8,128,896]{2,1,0:T(8,128)(2,1)S(1)} async-done(((bf16[8,128,896]{2,1,0:T(8,128)(2,1)}), bf16[8,128,896]{2,1,0:T(8,128)(2,1)S(1)}, u32[]{:S(2)}, u32[]{:S(2)}) %all-to-all-start) | async-done | bytes 1835040 | tf_op jit(solution)/shard_map/all_to_all | solution.py:44
  53.2 3.1 broadcast_in_dim.92
  56.3 4.7 all-to-all-start.1
  66.6 38.7 %collective-permute-done.3.last_ref = bf16[1024,896]{1,0:T(8,128)(2,1)S(1)} collective-permute-done((bf16[1024,896]{1,0:T(8,128)(2,1)S(1)}, bf16[1024,896]{1,0:T(8,128)(2,1)S(1)}, u32[]{:S(2)}, u32[]{:S(2)}) %collective-permute-start.3) | collective-permute-done | bytes 1835040 | tf_op jit(solution)/shard_map/ppermute | solution.py:28
  108.6 34.2 %all-to-all-done.1.in_ref = bf16[8,328,1024]{2,1,0:T(8,128)(2,1)} async-done(((bf16[8,328,1024]{2,1,0:T(8,128)(2,1)}), bf16[8,328,1024]{2,1,0:T(8,128)(2,1)}, u32[]{:S(2)}, u32[]{:S(2)}) %all-to-all-start.1) | async-done | bytes 5373984 | tf_op jit(solution)/shard_map/all_to_all | solution.py:44
  148.6 3.5 collective-permute-start.5
  152.1 3.9 collective-permute-start
  157.7 9.2 %collective-permute-done.4.top_ref = bf16[512,896]{1,0:T(8,128)(2,1)S(1)} collective-permute-done((bf16[512,896]{1,0:T(8,128)(2,1)S(1)}, bf16[512,896]{1,0:T(8,128)(2,1)S(1)}, u32[]{:S(2)}, u32[]{:S(2)}) %collective-permute-start.4) | collective-permute-done | bytes 917536 | tf_op jit(solution)/shard_map/ppermute | solution.py:28
  188.5 4.6 collective-permute-start.1
  198.6 3.9 shard_map.172
  204.7 7.0 shard_map.171.ctx_ref
  216.7 3.3 collective-permute-start.10
  224.4 3.1 multiply_convert_fusion.1
  228.9 33.2 %collective-permute-done.11.last_ref = bf16[1024,896]{1,0:T(8,128)(2,1)} collective-permute-done((bf16[1024,896]{1,0:T(8,128)(2,1)S(1)}, bf16[1024,896]{1,0:T(8,128)(2,1)}, u32[]{:S(2)}, u32[]{:S(2)}) %collective-permute-start.11) | collective-permute-done | bytes 1835040 | tf_op jit(solution)/shard_map/ppermute | solution.py:28
  273.4 12.6 %collective-permute-done.12.top_ref = bf16[512,896]{1,0:T(8,128)(2,1)S(1)} collective-permute-done((bf16[512,896]{1,0:T(8,128)(2,1)}, bf16[512,896]{1,0:T(8,128)(2,1)S(1)}, u32[]{:S(2)}, u32[]{:S(2)}) %collective-permute-start.12) | collective-permute-done | bytes 917536 | tf_op jit(solution)/shard_map/ppermute | solution.py:28
  287.3 5.7 shard_map.173
  297.1 7.0 shard_map.174.ctx_ref
  316.7 3.0 fusion.84
  329.0 9.4 %shard_map.176 = (bf16[256,1536]{1,0:T(8,128)(2,1)S(1)}, f32[2,2,1,256]{3,2,1,0:T(1,128)S(1)}, f32[2,2,1,256]{3,2,1,0:T(1,128)S(1)}) custom-call(f32[8]{0:T(128)S(1)} %fusion.76.slope_ref, s32[2,128,1]{2,1,0:T(8,128)S(1)} %copy.63.rows_ref, s32[2,1,128]{2,1,0:T(1,128)S(1)} %bitcast.150, bf16[256,1536]{1,0:T(8,128)(2,1)S(1)} %fusion.1.qkv_ref, ...), custom_call_target="tpu_custom_call" | custom-call | flops 167772160 | bytes 2097152 | tf_op jit(solution)/shard_map/pallas_call | solution.py:373
  351.3 3.2 shard_map.187
  356.9 4.7 all-to-all-start.5
  363.9 3.1 multiply_reduce_fusion.1
  368.4 3.5 collective-permute-start.25
  379.3 12.9 %collective-permute-done.23 = bf16[512,896]{1,0:T(8,128)(2,1)S(1)} collective-permute-done((bf16[512,896]{1,0:T(8,128)(2,1)S(1)}, bf16[512,896]{1,0:T(8,128)(2,1)S(1)}, u32[]{:S(2)}, u32[]{:S(2)}) %collective-permute-start.23) | collective-permute-done | bytes 917536 | tf_op jit(solution)/shard_map/ppermute | solution.py:28
  407.7 3.1 collective-permute-done.35
  411.9 19.7 %collective-permute-done.24 = bf16[512,896]{1,0:T(8,128)(2,1)S(1)} collective-permute-done((bf16[512,896]{1,0:T(8,128)(2,1)S(1)}, bf16[512,896]{1,0:T(8,128)(2,1)S(1)}, u32[]{:S(2)}, u32[]{:S(2)}) %collective-permute-start.24) | collective-permute-done | bytes 917536 | tf_op jit(solution)/shard_map/ppermute | solution.py:28
  435.1 3.8 select_reduce_fusion
  440.0 4.7 all-to-all-start.6
  446.7 3.2 shard_map.184
  454.4 6.5 all-to-all-start.2
  463.3 9.4 %shard_map.180 = (bf16[256,1536]{1,0:T(8,128)(2,1)S(1)}, f32[2,2,1,256]{3,2,1,0:T(1,128)S(1)}, f32[2,2,1,256]{3,2,1,0:T(1,128)S(1)}) custom-call(f32[8]{0:T(128)S(1)} %fusion.76.slope_ref, s32[2,128,1]{2,1,0:T(8,128)S(1)} %copy.63.rows_ref, s32[2,1,128]{2,1,0:T(1,128)S(1)} %bitcast.151, bf16[256,1536]{1,0:T(8,128)(2,1)S(1)} %copy-done.50, ...), custom_call_target="tpu_custom_call" | custom-call | flops 167772160 | bytes 2097152 | tf_op jit(solution)/shard_map/pallas_call | solution.py:373
  492.2 8.1 %collective-permute-done.28 = bf16[512,896]{1,0:T(8,128)(2,1)S(1)} collective-permute-done((bf16[512,896]{1,0:T(8,128)(2,1)S(1)}, bf16[512,896]{1,0:T(8,128)(2,1)S(1)}, u32[]{:S(2)}, u32[]{:S(2)}) %collective-permute-start.28) | collective-permute-done | bytes 917536 | tf_op jit(solution)/shard_map/ppermute | solution.py:28
  504.8 61.3 %reduce-scatter.4.cloned.1.call-done = bf16[1,64,896]{2,1,0:T(8,128)(2,1)} async-done(((bf16[16,64,896]{2,1,0:T(8,128)(2,1)}), bf16[1,64,896]{2,1,0:T(8,128)(2,1)}) %reduce-scatter.4.cloned.1.call-update) | async-done | bytes 114704
  568.0 3.3 fusion.33
  588.5 3.9 select_reduce_fusion.1
  593.3 3.5 all-to-all-start.3
  599.1 17.1 %collective-permute-done.32 = bf16[512,896]{1,0:T(8,128)(2,1)} collective-permute-done((bf16[512,896]{1,0:T(8,128)(2,1)}, bf16[512,896]{1,0:T(8,128)(2,1)}, u32[]{:S(2)}, u32[]{:S(2)}) %collective-permute-start.32) | collective-permute-done | bytes 917536 | tf_op jit(solution)/shard_map/ppermute | solution.py:32
  616.2 19.5 %collective-permute-done.31 = bf16[512,896]{1,0:T(8,128)(2,1)} collective-permute-done((bf16[512,896]{1,0:T(8,128)(2,1)}, bf16[512,896]{1,0:T(8,128)(2,1)}, u32[]{:S(2)}, u32[]{:S(2)}) %collective-permute-start.31) | collective-permute-done | bytes 917536 | tf_op jit(solution)/shard_map/ppermute | solution.py:28
  641.9 27.5 %all_to_all.45 = bf16[16,64,896]{2,1,0:T(8,128)(2,1)S(1)} all-to-all(bf16[16,64,896]{2,1,0:T(8,128)(2,1)S(1)} %maximum_select_fusion), channel_id=1, replica_groups=mesh['ylo'=2,'z'=4,'core'=2,'x'=4,'yhi'=2] {'x','yhi','ylo'}, dimensions={0} | all-to-all | bytes 3670016 | tf_op jit(solution)/shard_map/all_to_all | solution.py:44
  673.9 3.4 collective-permute-start.16
  678.5 9.8 %all_to_all.46 = f32[8,24,128]{2,1,0:T(8,128)S(1)} all-to-all(f32[8,24,128]{2,1,0:T(8,128)S(1)} %copy.72), channel_id=1, replica_groups=mesh['ylo'=2,'z'=4,'core'=2,'x'=4,'yhi'=2] {'x','yhi'}, dimensions={0} | all-to-all | bytes 196608 | tf_op jit(solution)/shard_map/all_to_all | solution.py:44
  689.0 5.1 all-to-all-start.8
  694.1 3.8 fusion.19
  697.9 4.5 all-to-all-done.8
  707.9 3.6 reshape.396.second_ref
  718.8 4.4 reshape.391.first_ref
  724.8 4.1 shard_map.188
  (622 shorter events, 226.5 us)
Async XLA Ops:
  16.3 34.3 %all-to-all-start = ((bf16[8,128,896]{2,1,0:T(8,128)(2,1)}), bf16[8,128,896]{2,1,0:T(8,128)(2,1)S(1)}, u32[]{:S(2)}, u32[]{:S(2)}) async-start(bf16[8,128,896]{2,1,0:T(8,128)(2,1)} %broadcast_in_dim.89), calls=%async_computation | async-start | bytes 3670016 | tf_op jit(solution)/shard_map/all_to_all | solution.py:44
  56.3 86.5 %all-to-all-start.1 = ((bf16[8,328,1024]{2,1,0:T(8,128)(2,1)}), bf16[8,328,1024]{2,1,0:T(8,128)(2,1)}, u32[]{:S(2)}, u32[]{:S(2)}) async-start(bf16[8,328,1024]{2,1,0:T(8,128)(2,1)} %broadcast_in_dim.92), calls=%async_computation.1 | async-start | bytes 10747904 | tf_op jit(solution)/shard_map/all_to_all | solution.py:44
  60.9 154.0 %all-gather.6.cloned.1.call-start = ((), (), s32[]{:S(2)}) async-start(), calls=%async_computation.10 | async-start | bytes 2064384 | tf_op jit(solution)/shard_map/all_gather | solution.py:463
  62.7 241.5 %all-gather.8.cloned.1.call-start = ((), (), s32[]{:S(2)}) async-start(), calls=%async_computation.11 | async-start | bytes 5898240 | tf_op jit(solution)/shard_map/all_gather | solution.py:471
  62.7 42.6 %collective-permute-start.3 = (bf16[1024,896]{1,0:T(8,128)(2,1)S(1)}, bf16[1024,896]{1,0:T(8,128)(2,1)S(1)}, u32[]{:S(2)}, u32[]{:S(2)}) collective-permute-start(bf16[1024,896]{1,0:T(8,128)(2,1)S(1)} %bitcast.142), channel_id=1, source_target_pairs={{0,16},{16,32},{32,48},{48,0},{1,17},{17,33},{33,49},{49,1},{2,18}... | collective-permute-start | bytes 5505032 | tf_op jit(solution)/shard_map/ppermute | solution.py:28
  64.4 42.2 %collective-permute-start.2 = (bf16[1024,896]{1,0:T(8,128)(2,1)S(1)}, bf16[1024,896]{1,0:T(8,128)(2,1)S(1)}, u32[]{:S(2)}, u32[]{:S(2)}) collective-permute-start(bf16[1024,896]{1,0:T(8,128)(2,1)S(1)} %bitcast.143), channel_id=1, source_target_pairs={{0,48},{16,0},{32,16},{48,32},{1,49},{17,1},{33,17},{49,33},{2,50}... | collective-permute-start | bytes 5505032 | tf_op jit(solution)/shard_map/ppermute | solution.py:32
  146.2 20.7 %collective-permute-start.4 = (bf16[512,896]{1,0:T(8,128)(2,1)S(1)}, bf16[512,896]{1,0:T(8,128)(2,1)S(1)}, u32[]{:S(2)}, u32[]{:S(2)}) collective-permute-start(bf16[512,896]{1,0:T(8,128)(2,1)S(1)} %slice.457), channel_id=1, source_target_pairs={{0,16},{16,32},{32,48},{48,0},{1,17},{17,33},{33,49},{49,1},{2,18}... | collective-permute-start | bytes 2752520 | tf_op jit(solution)/shard_map/ppermute | solution.py:28
  148.6 19.9 %collective-permute-start.5 = (bf16[512,896]{1,0:T(8,128)(2,1)}, bf16[512,896]{1,0:T(8,128)(2,1)S(1)}, u32[]{:S(2)}, u32[]{:S(2)}) collective-permute-start(bf16[512,896]{1,0:T(8,128)(2,1)} %slice.458), channel_id=1, source_target_pairs={{0,48},{16,0},{32,16},{48,32},{1,49},{17,1},{33,17},{49,33},{2,50}... | collective-permute-start | bytes 2752520 | tf_op jit(solution)/shard_map/ppermute | solution.py:32
  152.1 5.4 collective-permute-start
  188.5 14.0 %collective-permute-start.1 = (bf16[128,1024]{1,0:T(8,128)(2,1)S(1)}, bf16[128,1024]{1,0:T(8,128)(2,1)}, u32[]{:S(2)}, u32[]{:S(2)}) collective-permute-start(bf16[128,1024]{1,0:T(8,128)(2,1)S(1)} %add_convert_fusion.11), channel_id=1, source_target_pairs={{0,8},{8,0},{1,9},{9,1},{2,10},{10,2},{3,11},{11,3},{4,12},{12,4},... | collective-permute-start | bytes 786440 | tf_op jit(solution)/shard_map/ppermute | solution.py:36
  212.9 7.1 collective-permute-start.6
  216.7 47.6 %collective-permute-start.10 = (bf16[1024,896]{1,0:T(8,128)(2,1)S(1)}, bf16[1024,896]{1,0:T(8,128)(2,1)}, u32[]{:S(2)}, u32[]{:S(2)}) collective-permute-start(bf16[1024,896]{1,0:T(8,128)(2,1)S(1)} %bitcast.145), channel_id=1, source_target_pairs={{0,48},{16,0},{32,16},{48,32},{1,49},{17,1},{33,17},{49,33},{2,50}... | collective-permute-start | bytes 5505032 | tf_op jit(solution)/shard_map/ppermute | solution.py:32
  220.0 42.2 %collective-permute-start.11 = (bf16[1024,896]{1,0:T(8,128)(2,1)S(1)}, bf16[1024,896]{1,0:T(8,128)(2,1)}, u32[]{:S(2)}, u32[]{:S(2)}) collective-permute-start(bf16[1024,896]{1,0:T(8,128)(2,1)S(1)} %bitcast.146), channel_id=1, source_target_pairs={{0,16},{16,32},{32,48},{48,0},{1,17},{17,33},{33,49},{49,1},{2,18}... | collective-permute-start | bytes 5505032 | tf_op jit(solution)/shard_map/ppermute | solution.py:28
  222.5 1.9 collective-permute-start.7
  228.3 40.9 %collective-permute-start.8 = (f32[128,1024]{1,0:T(8,128)S(1)}, f32[128,1024]{1,0:T(8,128)S(1)}, u32[]{:S(2)}, u32[]{:S(2)}) collective-permute-start(f32[128,1024]{1,0:T(8,128)S(1)} %fusion.30), channel_id=1, source_target_pairs={{0,8},{8,0},{1,9},{9,1},{2,10},{10,2},{3,11},{11,3},{4,12},{12,4},... | collective-permute-start | bytes 1572872 | tf_op jit(solution)/shard_map/ppermute | solution.py:36
  264.3 21.7 %collective-permute-start.12 = (bf16[512,896]{1,0:T(8,128)(2,1)}, bf16[512,896]{1,0:T(8,128)(2,1)S(1)}, u32[]{:S(2)}, u32[]{:S(2)}) collective-permute-start(bf16[512,896]{1,0:T(8,128)(2,1)} %slice.474), channel_id=1, source_target_pairs={{0,16},{16,32},{32,48},{48,0},{1,17},{17,33},{33,49},{49,1},{2,18}... | collective-permute-start | bytes 2752520 | tf_op jit(solution)/shard_map/ppermute | solution.py:28
  266.5 20.8 %collective-permute-start.13 = (bf16[512,896]{1,0:T(8,128)(2,1)}, bf16[512,896]{1,0:T(8,128)(2,1)}, u32[]{:S(2)}, u32[]{:S(2)}) collective-permute-start(bf16[512,896]{1,0:T(8,128)(2,1)} %slice.475), channel_id=1, source_target_pairs={{0,48},{16,0},{32,16},{48,32},{1,49},{17,1},{33,17},{49,33},{2,50}... | collective-permute-start | bytes 2752520 | tf_op jit(solution)/shard_map/ppermute | solution.py:32
  271.3 21.7 %collective-permute-start.9 = (bf16[128,1024]{1,0:T(8,128)(2,1)}, bf16[128,1024]{1,0:T(8,128)(2,1)}, u32[]{:S(2)}, u32[]{:S(2)}) collective-permute-start(bf16[128,1024]{1,0:T(8,128)(2,1)} %add_convert_fusion.9), channel_id=1, source_target_pairs={{0,8},{8,0},{1,9},{9,1},{2,10},{10,2},{3,11},{11,3},{4,12},{12,4},... | collective-permute-start | bytes 786440 | tf_op jit(solution)/shard_map/ppermute | solution.py:36
  308.1 4.4 collective-permute-start.14
  313.3 1.6 collective-permute-start.15
  314.4 2.3 collective-permute-start.17
  321.3 2.4 collective-permute-start.18
  340.3 23.5 %collective-permute-start.20 = (f32[128,1024]{1,0:T(8,128)}, f32[128,1024]{1,0:T(8,128)}, u32[]{:S(2)}, u32[]{:S(2)}) collective-permute-start(f32[128,1024]{1,0:T(8,128)} %fusion.36), channel_id=1, source_target_pairs={{0,8},{8,0},{1,9},{9,1},{2,10},{10,2},{3,11},{11,3},{4,12},{12,4},... | collective-permute-start | bytes 1572872 | tf_op jit(solution)/shard_map/ppermute | solution.py:36
  356.9 78.3 %all-to-all-start.5 = ((bf16[8,320,1024]{2,1,0:T(8,128)(2,1)}), bf16[8,320,1024]{2,1,0:T(8,128)(2,1)}, u32[]{:S(2)}, u32[]{:S(2)}) async-start(bf16[8,320,1024]{2,1,0:T(8,128)(2,1)} %copy-done), calls=%async_computation.5 | async-start | bytes 10485760 | tf_op jit(solution)/shard_map/all_to_all | solution.py:44
  361.6 204.6 %reduce-scatter.4.cloned.1.call-start = ((), (), s32[]{:S(2)}) async-start(), calls=%async_computation.14 | async-start | bytes 1949696
  367.9 5.5 collective-permute-start.21
  368.3 24.0 %collective-permute-start.23 = (bf16[512,896]{1,0:T(8,128)(2,1)S(1)}, bf16[512,896]{1,0:T(8,128)(2,1)S(1)}, u32[]{:S(2)}, u32[]{:S(2)}) collective-permute-start(bf16[512,896]{1,0:T(8,128)(2,1)S(1)} %get-tuple-element.127), channel_id=1, source_target_pairs={{0,16},{16,32},{32,48},{48,0},{1,17},{17,33},{33,49},{49,1},{2,18}... | collective-permute-start | bytes 2752520 | tf_op jit(solution)/shard_map/ppermute | solution.py:28
  368.4 25.1 %collective-permute-start.25 = (bf16[512,896]{1,0:T(8,128)(2,1)S(1)}, bf16[512,896]{1,0:T(8,128)(2,1)S(1)}, u32[]{:S(2)}, u32[]{:S(2)}) collective-permute-start(bf16[512,896]{1,0:T(8,128)(2,1)S(1)} %get-tuple-element.126), channel_id=1, source_target_pairs={{0,48},{16,0},{32,16},{48,32},{1,49},{17,1},{33,17},{49,33},{2,50}... | collective-permute-start | bytes 2752520 | tf_op jit(solution)/shard_map/ppermute | solution.py:32
  371.8 39.0 %collective-permute-start.35 = (bf16[512,896]{1,0:T(8,128)(2,1)S(1)}, bf16[512,896]{1,0:T(8,128)(2,1)S(1)}, u32[]{:S(2)}, u32[]{:S(2)}) collective-permute-start(bf16[512,896]{1,0:T(8,128)(2,1)S(1)} %copy-done.92), channel_id=1, source_target_pairs={{0,48},{16,0},{32,16},{48,32},{1,49},{17,1},{33,17},{49,33},{2,50}... | collective-permute-start | bytes 2752520 | tf_op jit(solution)/shard_map/ppermute | solution.py:32
  373.2 38.7 %collective-permute-start.36 = (bf16[512,896]{1,0:T(8,128)(2,1)S(1)}, bf16[512,896]{1,0:T(8,128)(2,1)S(1)}, u32[]{:S(2)}, u32[]{:S(2)}) collective-permute-start(bf16[512,896]{1,0:T(8,128)(2,1)S(1)} %copy-done.91), channel_id=1, source_target_pairs={{0,16},{16,32},{32,48},{48,0},{1,17},{17,33},{33,49},{49,1},{2,18}... | collective-permute-start | bytes 2752520 | tf_op jit(solution)/shard_map/ppermute | solution.py:28
  378.0 19.9 %collective-permute-start.22 = (f32[128,1024]{1,0:T(8,128)S(1)}, f32[128,1024]{1,0:T(8,128)S(1)}, u32[]{:S(2)}, u32[]{:S(2)}) collective-permute-start(f32[128,1024]{1,0:T(8,128)S(1)} %fusion.21), channel_id=1, source_target_pairs={{0,8},{8,0},{1,9},{9,1},{2,10},{10,2},{3,11},{11,3},{4,12},{12,4},... | collective-permute-start | bytes 1572872 | tf_op jit(solution)/shard_map/ppermute | solution.py:36
  394.9 36.7 %collective-permute-start.24 = (bf16[512,896]{1,0:T(8,128)(2,1)S(1)}, bf16[512,896]{1,0:T(8,128)(2,1)S(1)}, u32[]{:S(2)}, u32[]{:S(2)}) collective-permute-start(bf16[512,896]{1,0:T(8,128)(2,1)S(1)} %add_convert_fusion.7), channel_id=1, source_target_pairs={{0,16},{16,32},{32,48},{48,0},{1,17},{17,33},{33,49},{49,1},{2,18}... | collective-permute-start | bytes 2752520 | tf_op jit(solution)/shard_map/ppermute | solution.py:28
  395.2 36.4 %collective-permute-start.26 = (bf16[512,896]{1,0:T(8,128)(2,1)S(1)}, bf16[512,896]{1,0:T(8,128)(2,1)S(1)}, u32[]{:S(2)}, u32[]{:S(2)}) collective-permute-start(bf16[512,896]{1,0:T(8,128)(2,1)S(1)} %add_convert_fusion.6), channel_id=1, source_target_pairs={{0,48},{16,0},{32,16},{48,32},{1,49},{17,1},{33,17},{49,33},{2,50}... | collective-permute-start | bytes 2752520 | tf_op jit(solution)/shard_map/ppermute | solution.py:32
  401.9 4.1 collective-permute-start.27
  440.0 14.4 %all-to-all-start.6 = ((bf16[8,40,1024]{2,1,0:T(8,128)(2,1)}), bf16[8,40,1024]{2,1,0:T(8,128)(2,1)}, u32[]{:S(2)}, u32[]{:S(2)}) async-start(bf16[8,40,1024]{2,1,0:T(8,128)(2,1)} %pad_maximum_fusion.1), calls=%async_computation.6 | async-start | bytes 1310720 | tf_op jit(solution)/shard_map/all_to_all | solution.py:44
  454.4 134.1 %all-to-all-start.2 = ((bf16[8,320,1024]{2,1,0:T(8,128)(2,1)}), bf16[8,320,1024]{2,1,0:T(8,128)(2,1)}, u32[]{:S(2)}, u32[]{:S(2)}) async-start(bf16[8,320,1024]{2,1,0:T(8,128)(2,1)} %copy-done.1), calls=%async_computation.2 | async-start | bytes 10485760 | tf_op jit(solution)/shard_map/all_to_all | solution.py:44
  460.9 243.3 %all-gather.10.cloned.1.call-start = ((), (), s32[]{:S(2)}) async-start(), calls=%async_computation.12 | async-start | bytes 3342336 | tf_op jit(solution)/shard_map/all_gather | solution.py:525
  479.9 20.4 %collective-permute-start.28 = (bf16[512,896]{1,0:T(8,128)(2,1)S(1)}, bf16[512,896]{1,0:T(8,128)(2,1)S(1)}, u32[]{:S(2)}, u32[]{:S(2)}) collective-permute-start(bf16[512,896]{1,0:T(8,128)(2,1)S(1)} %get-tuple-element.125), channel_id=1, source_target_pairs={{0,16},{16,32},{32,48},{48,0},{1,17},{17,33},{33,49},{49,1},{2,18}... | collective-permute-start | bytes 2752520 | tf_op jit(solution)/shard_map/ppermute | solution.py:28
  481.1 20.4 %collective-permute-start.29 = (bf16[512,896]{1,0:T(8,128)(2,1)S(1)}, bf16[512,896]{1,0:T(8,128)(2,1)S(1)}, u32[]{:S(2)}, u32[]{:S(2)}) collective-permute-start(bf16[512,896]{1,0:T(8,128)(2,1)S(1)} %get-tuple-element.124), channel_id=1, source_target_pairs={{0,48},{16,0},{32,16},{48,32},{1,49},{17,1},{33,17},{49,33},{2,50}... | collective-permute-start | bytes 2752520 | tf_op jit(solution)/shard_map/ppermute | solution.py:32
  571.3 7.0 collective-permute-start.30
  575.7 40.5 %collective-permute-start.32 = (bf16[512,896]{1,0:T(8,128)(2,1)}, bf16[512,896]{1,0:T(8,128)(2,1)}, u32[]{:S(2)}, u32[]{:S(2)}) collective-permute-start(bf16[512,896]{1,0:T(8,128)(2,1)} %slice.519), channel_id=1, source_target_pairs={{0,48},{16,0},{32,16},{48,32},{1,49},{17,1},{33,17},{49,33},{2,50}... | collective-permute-start | bytes 2752520 | tf_op jit(solution)/shard_map/ppermute | solution.py:32
  578.3 37.9 %collective-permute-start.33 = (bf16[512,896]{1,0:T(8,128)(2,1)}, bf16[512,896]{1,0:T(8,128)(2,1)}, u32[]{:S(2)}, u32[]{:S(2)}) collective-permute-start(bf16[512,896]{1,0:T(8,128)(2,1)} %slice.521), channel_id=1, source_target_pairs={{0,16},{16,32},{32,48},{48,0},{1,17},{17,33},{33,49},{49,1},{2,18}... | collective-permute-start | bytes 2752520 | tf_op jit(solution)/shard_map/ppermute | solution.py:28
  584.7 51.0 %collective-permute-start.31 = (bf16[512,896]{1,0:T(8,128)(2,1)}, bf16[512,896]{1,0:T(8,128)(2,1)}, u32[]{:S(2)}, u32[]{:S(2)}) collective-permute-start(bf16[512,896]{1,0:T(8,128)(2,1)} %add_convert_fusion.5), channel_id=1, source_target_pairs={{0,16},{16,32},{32,48},{48,0},{1,17},{17,33},{33,49},{49,1},{2,18}... | collective-permute-start | bytes 2752520 | tf_op jit(solution)/shard_map/ppermute | solution.py:28
  585.9 50.0 %collective-permute-start.34 = (bf16[512,896]{1,0:T(8,128)(2,1)}, bf16[512,896]{1,0:T(8,128)(2,1)}, u32[]{:S(2)}, u32[]{:S(2)}) collective-permute-start(bf16[512,896]{1,0:T(8,128)(2,1)} %add_convert_fusion.3), channel_id=1, source_target_pairs={{0,48},{16,0},{32,16},{48,32},{1,49},{17,1},{33,17},{49,33},{2,50}... | collective-permute-start | bytes 2752520 | tf_op jit(solution)/shard_map/ppermute | solution.py:32
  593.3 47.0 %all-to-all-start.3 = ((bf16[8,40,1024]{2,1,0:T(8,128)(2,1)}), bf16[8,40,1024]{2,1,0:T(8,128)(2,1)S(1)}, u32[]{:S(2)}, u32[]{:S(2)}) async-start(bf16[8,40,1024]{2,1,0:T(8,128)(2,1)} %pad_maximum_fusion), calls=%async_computation.3 | async-start | bytes 1310720 | tf_op jit(solution)/shard_map/all_to_all | solution.py:44
  596.9 115.7 %all-gather.12.cloned.1.call-start = ((), (), s32[]{:S(2)}) async-start(), calls=%async_computation.13 | async-start | bytes 3342336 | tf_op jit(solution)/shard_map/all_gather | solution.py:525
  673.9 20.1 %collective-permute-start.16 = (f32[128,1024]{1,0:T(8,128)S(1)}, f32[128,1024]{1,0:T(8,128)S(1)}, u32[]{:S(2)}, u32[]{:S(2)}) collective-permute-start(f32[128,1024]{1,0:T(8,128)S(1)} %fusion.27), channel_id=1, source_target_pairs={{0,8},{8,0},{1,9},{9,1},{2,10},{10,2},{3,11},{11,3},{4,12},{12,4},... | collective-permute-start | bytes 1572872 | tf_op jit(solution)/shard_map/ppermute | solution.py:36
  689.0 13.4 %all-to-all-start.8 = ((f32[16,24,128]{2,1,0:T(8,128)}), f32[16,24,128]{2,1,0:T(8,128)S(1)}, u32[]{:S(2)}, u32[]{:S(2)}) async-start(f32[16,24,128]{2,1,0:T(8,128)} %broadcast_in_dim.106), calls=%async_computation.8 | async-start | bytes 393216 | tf_op jit(solution)/shard_map/all_to_all | solution.py:44
  (152 other events, 1132.5 us)
Sparse Core Ops, SparseCore 0:
  64.7 80.6 all-gather.5
  147.7 78.7 all-gather.7
  434.4 131.6 reduce-scatter.3
  568.0 47.3 all-gather.9
  670.6 38.8 all-gather.11

commit v6 on v5

--- a/solution.py
+++ b/solution.py
@@ -32,6 +32,18 @@
     return lax.ppermute(a, "z", ring(3))
 
 
+def x_up(a):
+    return lax.ppermute(a, "x", ring(1))
+
+
+def x_down(a):
+    return lax.ppermute(a, "x", ring(3))
+
+
+def y_pair(a):
+    return lax.ppermute(a, ("ylo", "yhi"), [(0, 3), (3, 0), (1, 2), (2, 1)])
+
+
 def swap(a):
     return lax.ppermute(a, "core", [(0, 1), (1, 0)])
 
@@ -62,13 +74,16 @@
     half = own.shape[0] // 2
     from_previous = up(far[:half])
     from_following = down(far[half:])
-    plain_up = up(following[half:])
-    plain_down = down(previous[:half])
-    sum_up = up((following[:half].astype(f32) + from_previous.astype(f32)).astype(bf16))
-    sum_down = down((previous[half:].astype(f32) + from_following.astype(f32)).astype(bf16))
-    top = own[:half].astype(f32) + sum_up.astype(f32) + plain_down.astype(f32)
-    bottom = own[half:].astype(f32) + plain_up.astype(f32) + sum_down.astype(f32)
-    return (top, bottom), (following, previous), (from_previous, from_following), (sum_up, sum_down)
+    go_up = jnp.concatenate(
+        [(following[:half].astype(f32) + from_previous.astype(f32)).astype(bf16), following[half:]]
+    )
+    go_down = jnp.concatenate(
+        [previous[:half], (previous[half:].astype(f32) + from_following.astype(f32)).astype(bf16)]
+    )
+    got_up = up(go_up)
+    got_down = down(go_down)
+    total = own.astype(f32) + got_up.astype(f32) + got_down.astype(f32)
+    return total, (following, previous), (from_previous, from_following), (got_up, got_down)
 
 
 def rolled(stack, start):
@@ -436,8 +451,9 @@
 
 
 def local(hidden_in, doc_start, grad_out, w_qkv, w_proj, w_up, w_down, norm_gain, d_bias, up_bias):
-    z, core = lax.axis_index("z"), lax.axis_index("core")
+    x, yhi, z, core = (lax.axis_index(n) for n in ("x", "yhi", "z", "core"))
     at = jnp.stack([z, core]).astype(jnp.int32)
+    at_x = jnp.stack([(z - x + 4) % 4, core]).astype(jnp.int32)
     index = jnp.arange(8, dtype=jnp.int32)
 
     def both(own):
@@ -456,19 +472,23 @@
 
     mine_z, mine_x = select_weights(at, w_qkv, w_proj, w_up, w_down)
     weights = []
-    piece_x = jnp.concatenate([mine_x[0], small.reshape(3, D), jnp.zeros((5, D), bf16)])
-    block_z = to_all(mine_z[0], SHARD, 8).reshape(D, 896)
-    all_x = to_all(after(piece_x, block_z), SHARD, 8)
-    all_small = all_x[:, 320:323]
-    next_z = lax.all_gather(after(mine_z[1], block_z), SHARD, axis=0).reshape(D, 896)
+    thin = jnp.concatenate([small, jnp.zeros((4, 128), bf16)]).reshape(4, 896)
+    first_z = to_all(jnp.concatenate([mine_z[0], thin, jnp.zeros((4, 896), bf16)]), SHARD, 8)
+    all_small = first_z[:, 128:132].reshape(8, 28, 128)[:, :24]
+    block_z = first_z[:, :128].reshape(D, 896)
+    other = y_pair(mine_x[0])
+    piece_x = jnp.concatenate([jnp.where(yhi == 0, mine_x[0], other), jnp.where(yhi == 0, other, mine_x[0])])
+    own, following, (top, bottom), previous = ring_gather(after(piece_x, block_z), x_up, x_down)
+    all_x = jnp.concatenate([own, following, top, bottom, previous]).reshape(8, 320, D)
+    next_x = lax.all_gather(after(mine_x[1], block_z), SHARD, axis=0)
     for layer in range(LAYERS):
         own, following, (top, bottom), previous = ring_gather(block_z, z_up, z_down)
         wup, wqkv = split_z(at, own, following, top, bottom, previous)
-        wdown, wproj = split_x(at, all_x)
+        wdown, wproj = split_x(at_x if layer == 0 else at, all_x)
         weights.append((wqkv, wproj, wup, wdown))
         if layer == 0:
-            block_z = after(next_z, top)
-            all_x = lax.all_gather(after(mine_x[1], previous, following, all_x[0]), SHARD, axis=0)
+            next_z = to_all(after(mine_z[1], previous, following), SHARD, 8).reshape(D, 896)
+            block_z, all_x = after(next_z, top, bottom), next_x
 
     small = all_small.reshape(4, 2, 24, 128).astype(f32)
     wide = jnp.transpose(small[:, :, :16], (2, 0, 1, 3)).reshape(LAYERS, 8, D)
@@ -496,6 +516,8 @@
         first_in = both(first_f.astype(bf16))
         qkv = (dot(first_in, wqkv) + bqkv).astype(bf16)
         ctx = attend(qkv, rows, cols, slopes)
+        if layer == 0:
+            ctx = after(ctx, next_z)
         middle = current + halves_summed(dot, ctx, wproj) + bproj
         second_f, normed_two, inv_two = layer_norm(middle, gain_two, shift_two)
         second_in = both(second_f.astype(bf16))
@@ -511,14 +533,20 @@
     def ring_z(a2, dub, a1, dqkv):
         parts = [grad_z(at, a2, dub, a1, dqkv, i) for i in (2, 1, 3, 0)]
         parts = [parts[i] for i in (3, 1, 0, 2)]
-        (top, bottom), sent, near, got = ring_scatter(parts, z_up, z_down)
-        part = jnp.concatenate([top.astype(bf16).reshape(8, 64, 896), bottom.astype(bf16).reshape(8, 64, 896)])
-        return part, (sent, near, got)
-
-    def finish_x(blocks, later):
-        part = summed(after(blocks, later))
-        part = jnp.concatenate([part[:256].reshape(8, 32, D), part[256:320].reshape(8, 8, D)], axis=1)
-        return summed(exchange(part, ("ylo", "z")))
+        total, sent, near, got = ring_scatter(parts, z_up, z_down)
+        return total.astype(bf16).reshape(16, 64, 896), (sent, near, got)
+
+    def ring_x(m, dy, ctx, dr):
+        parts = grad_x(at_x, m, dy, ctx, dr)
+        total, _, near, got = ring_scatter([parts[2 * i : 2 * i + 2].reshape(640, D) for i in range(4)], x_up, x_down)
+        part = total.astype(bf16).reshape(2, 320, D)
+        part = jnp.concatenate([part[:, :256].reshape(2, 8, 32, D), part[:, 256:].reshape(2, 8, 8, D)], axis=2)
+        return jnp.transpose(part, (1, 0, 2, 3)).reshape(16, 40, D), (near, got)
+
+    def finish(part_z, part_x, *earlier):
+        part_x = summed(exchange(part_x, ("ylo", "z", "yhi")))
+        part_z = exchange(part_z, ("x", "yhi", "ylo"))
+        return summed(after(part_z, *earlier) if earlier else part_z), part_x
 
     def share(part_z, part_x, *earlier):
         part = jnp.concatenate([part_z.reshape(56, D), part_x])
@@ -546,23 +574,23 @@
         g_bproj = jnp.sum(grad_mid, axis=0)
         grad_midb = grad_mid.astype(bf16)
         if ring_state is not None:
-            grad_midb = after(grad_midb, *ring_state[1])
-            later_x = waiting_x
+            grad_midb = after(grad_midb, *ring_state[1], *x_state[0])
+            part_x_before = part_x
+            later_state = x_state
         grad_midb = both(grad_midb)
         grad_ctx = dot_nt(grad_midb, wproj).astype(bf16)
-        waiting_x = exchange(grad_x(at, activ, grad_yb, ctx, grad_midb), SHARD)
+        part_x, x_state = ring_x(activ, grad_yb, ctx, grad_midb)
         grad_qkv, g_bq, g_bv = attend_back(qkv, ctx, grad_ctx, rows, cols, slopes)
         if ring_state is not None:
-            grad_qkv = after(grad_qkv, *ring_state[2])
-            later_x = finish_x(later_x, grad_ctx)
-            later_z = lax.psum_scatter(after(part_z, grad_ctx), ("x", "yhi", "ylo"), scatter_dimension=0, tiled=True)[0]
+            later = (after(part_z, grad_qkv), part_x_before)
+            grad_qkv = after(grad_qkv, *ring_state[2], *later_state[1])
         part_z, ring_state = ring_z(second_in, grad_ub, first_in, grad_qkv)
         if layer == 0:
             grad_qkv = after(grad_qkv, *ring_state[0])
         grad_one = halves_summed(dot_nt, grad_qkv, wqkv)
         if layer == 0:
             grad_one = after(grad_one, *ring_state[1])
-            grads_z[1], grads_x[1] = share(later_z, later_x, *ring_state[1])
+            grads_z[1], grads_x[1] = share(*finish(*later, *ring_state[1]))
         back_one, g_gain_one, g_shift_one = norm_back(grad_one, normed_one, inv_one, gain_one)
         running = grad_mid + back_one
 
@@ -570,9 +598,7 @@
         head_grads[layer] = [jnp.sum(g, axis=0).reshape(4, 128) for g in (g_bq, g_bv)]
         unit_grads[layer] = g_ubias.reshape(4, 512)
 
-    part_x = finish_x(waiting_x, running)
-    part_z = summed(exchange(after(part_z, part_x), ("x", "yhi", "ylo")))
-    grads_z[0], grads_x[0] = share(part_z, part_x)
+    grads_z[0], grads_x[0] = share(*finish(part_z, part_x))
 
     thin = jnp.stack(thin_grads[0] + thin_grads[1]).reshape(LAYERS, 6, 4, 2, 128)
     heads = jnp.stack(head_grads[0] + head_grads[1], axis=1)

time: 750 us -> 691 us (0.921)
  waiting for transfers between devices: 312 us -> 220 us
  starting transfers between devices: 94.5 us -> 117 us
  other arithmetic: 48.6 us -> 60 us
  local copies, waits for them, and re-layouts: 97.3 us -> 107 us
    ppermute x10 -> x8, waiting for transfers between devices: 155 us -> 84.3 us  [z_up(): return lax.ppermute(a, 'z', ring(1))]
    ppermute x0 -> x13, waiting for transfers between devices: none -> 64.7 us  [the longest x6 45.3 us: x_up(): return lax.ppermute(a, 'x', ring(1))]
    unnamed x6 -> x3, waiting for transfers between devices: 61.4 us -> 0.06 us
    all_to_all x7, waiting for transfers between devices: 68.9 us -> 31.6 us  [exchange(): return lax.all_to_all(blocks, axes, 0, 0, tiled=True)]
    ppermute x0 -> x13, starting transfers between devices: none -> 16.5 us  [the longest x6 11.5 us: x_down(): return lax.ppermute(a, 'x', ring(3))]
    ppermute x10 -> x8, waiting for transfers between devices: 22.4 us -> 30.8 us  [z_down(): return lax.ppermute(a, 'z', ring(3))]
    slice x18 -> x21, local copies, waits for them, and re-layouts: 11.7 us -> 19.6 us  [after(): e[0, 0].astype(f32)]
    all_to_all x7, starting transfers between devices: 36.8 us -> 44.6 us  [exchange(): return lax.all_to_all(blocks, axes, 0, 0, tiled=True)]
  transfers between devices with their start and end apart: 49 -> 56, of which waited for: 26 -> 26; matrix products, arithmetic and copies ran while one was open for 17% -> 22% of each run, Pallas kernels for 8% -> 8%
where the time goes in v6:
time: 691 us; the launch traced here: 679 us
  waiting for transfers between devices  220 us (32%)
  starting transfers between devices  117 us (17%)
  local copies, waits for them, and re-layouts  107 us (15%)
  Pallas kernels  73.1 us (11%)
  other arithmetic  60 us (9%)
  matrix products  40 us (6%)
  blocking collectives  32.8 us (5%)
  between operations  30.3 us (4%)
    ppermute x8, waiting for transfers between devices, z_up(): return lax.ppermute(a, 'z', ring(1))  84.3 us
    ppermute x6, waiting for transfers between devices, x_up(): return lax.ppermute(a, 'x', ring(1))  45.3 us
    all_to_all x7, starting transfers between devices, exchange(): return lax.all_to_all(blocks, axes, 0, 0, tiled=True)  44.6 us
    pallas_call x15, Pallas kernels, call(): pl.pallas_call(kernel, out_shape=out_shape, grid_spec=pltpu.PrefetchScala...  39.2 us
    unnamed x268, local copies, waits for them, and re-layouts  37.8 us
    all_to_all x1, blocking collectives, exchange(): return lax.all_to_all(blocks, axes, 0, 0, tiled=True)  32.8 us
    all_to_all x7, waiting for transfers between devices, exchange(): return lax.all_to_all(blocks, axes, 0, 0, tiled=True)  31.6 us
    ppermute x8, waiting for transfers between devices, z_down(): return lax.ppermute(a, 'z', ring(3))  30.8 us
  transfers between devices with their start and end apart: 56, of which 26 were waited for; matrix products, arithmetic and copies ran while one was open for 22% of the time, Pallas kernels for 8%

profile of v6, /device:TPU:1, one launch (start us, length us, event | category | flops | bytes accessed | tf_op | source)
XLA Modules:
  0.0 679.5 jit_solution(2386843711863151073)
XLA Ops:
  17.5 32.8 %all_to_all.40 = bf16[8,136,896]{2,1,0:T(8,128)(2,1)S(1)} all-to-all(bf16[8,136,896]{2,1,0:T(8,128)(2,1)S(1)} %broadcast_in_dim.94), channel_id=1, replica_groups=mesh['ylo'=2,'z'=4,'core'=2,'x'=4,'yhi'=2] {'x','yhi'}, dimensions={0} | all-to-all | bytes 3899392 | tf_op jit(solution)/shard_map/all_to_all | solution.py:56
  57.2 3.8 collective-permute-start.1
  62.4 6.0 collective-permute-done.6
  77.6 26.1 %collective-permute-done.last_ref = bf16[1024,896]{1,0:T(8,128)(2,1)} collective-permute-done((bf16[1024,896]{1,0:T(8,128)(2,1)S(1)}, bf16[1024,896]{1,0:T(8,128)(2,1)}, u32[]{:S(2)}, u32[]{:S(2)}) %collective-permute-start) | collective-permute-done | bytes 1835040 | tf_op jit(solution)/shard_map/ppermute | solution.py:28
  108.9 4.3 all-to-all-start.1
  113.3 4.8 collective-permute-done.8
  133.3 6.7 collective-permute-start.3
  142.6 16.5 %collective-permute-done.9 = bf16[320,1024]{1,0:T(8,128)(2,1)} collective-permute-done((bf16[320,1024]{1,0:T(8,128)(2,1)}, bf16[320,1024]{1,0:T(8,128)(2,1)}, u32[]{:S(2)}, u32[]{:S(2)}) %collective-permute-start.9) | collective-permute-done | bytes 655392 | tf_op jit(solution)/shard_map/ppermute | solution.py:36
  171.0 5.9 shard_map.170
  180.0 7.0 %shard_map.171 = bf16[256,512]{1,0:T(8,128)(2,1)S(1)} custom-call(f32[8]{0:T(128)S(1)} %fusion.85.slope_ref, s32[2,128,1]{2,1,0:T(8,128)S(1)} %copy.66.rows_ref, s32[2,1,128]{2,1,0:T(1,128)S(1)} %bitcast.203, bf16[256,1536]{1,0:T(8,128)(2,1)S(1)} %fusion.4.qkv_ref), custom_call_target="tpu_custom_call" | custom-call | flops 67108864 | bytes 1048576 | tf_op jit(solution)/shard_map/pallas_call | solution.py:369
  203.4 3.1 multiply_convert_fusion.1
  210.5 34.9 %collective-permute-done.16.last_ref = bf16[1024,896]{1,0:T(8,128)(2,1)S(1)} collective-permute-done((bf16[1024,896]{1,0:T(8,128)(2,1)S(1)}, bf16[1024,896]{1,0:T(8,128)(2,1)S(1)}, u32[]{:S(2)}, u32[]{:S(2)}) %collective-permute-start.16) | collective-permute-done | bytes 1835040 | tf_op jit(solution)/shard_map/ppermute | solution.py:28
  254.0 14.2 %collective-permute-done.17.top_ref = bf16[512,896]{1,0:T(8,128)(2,1)S(1)} collective-permute-done((bf16[512,896]{1,0:T(8,128)(2,1)}, bf16[512,896]{1,0:T(8,128)(2,1)S(1)}, u32[]{:S(2)}, u32[]{:S(2)}) %collective-permute-start.17) | collective-permute-done | bytes 917536 | tf_op jit(solution)/shard_map/ppermute | solution.py:28
  272.6 3.9 shard_map.173
  279.6 7.0 %shard_map.174.ctx_ref = bf16[256,512]{1,0:T(8,128)(2,1)S(1)} custom-call(f32[8]{0:T(128)S(1)} %fusion.85.slope_ref, s32[2,128,1]{2,1,0:T(8,128)S(1)} %copy.66.rows_ref, s32[2,1,128]{2,1,0:T(1,128)S(1)} %bitcast.204, bf16[256,1536]{1,0:T(8,128)(2,1)S(1)} %fusion.5.qkv_ref), custom_call_target="tpu_custom_call" | custom-call | flops 67108864 | bytes 1048576 | tf_op jit(solution)/shard_map/pallas_call | solution.py:369
  299.3 3.0 fusion.93
  311.1 9.4 %shard_map.176 = (bf16[256,1536]{1,0:T(8,128)(2,1)S(1)}, f32[2,2,1,256]{3,2,1,0:T(1,128)S(1)}, f32[2,2,1,256]{3,2,1,0:T(1,128)S(1)}) custom-call(f32[8]{0:T(128)S(1)} %fusion.85.slope_ref, s32[2,128,1]{2,1,0:T(8,128)S(1)} %copy.66.rows_ref, s32[2,1,128]{2,1,0:T(1,128)S(1)} %bitcast.205, bf16[256,1536]{1,0:T(8,128)(2,1)S(1)} %fusion.5.qkv_ref, ...), custom_call_target="tpu_custom_call" | custom-call | flops 167772160 | bytes 2097152 | tf_op jit(solution)/shard_map/pallas_call | solution.py:388
  331.4 3.7 collective-permute-start.30
  335.1 3.2 shard_map.180
  345.2 10.6 %collective-permute-done.32 = bf16[320,1024]{1,0:T(8,128)(2,1)S(1)} collective-permute-done((bf16[320,1024]{1,0:T(8,128)(2,1)S(1)}, bf16[320,1024]{1,0:T(8,128)(2,1)S(1)}, u32[]{:S(2)}, u32[]{:S(2)}) %collective-permute-start.32) | collective-permute-done | bytes 655392 | tf_op jit(solution)/shard_map/ppermute | solution.py:36
  361.8 2.9 fusion.94
  380.7 8.4 %collective-permute-done.33 = bf16[640,1024]{1,0:T(8,128)(2,1)S(1)} collective-permute-done((bf16[640,1024]{1,0:T(8,128)(2,1)S(1)}, bf16[640,1024]{1,0:T(8,128)(2,1)S(1)}, u32[]{:S(2)}, u32[]{:S(2)}) %collective-permute-start.33) | collective-permute-done | bytes 1310752 | tf_op jit(solution)/shard_map/ppermute | solution.py:36
  392.1 8.1 %all-to-all-start.5 = ((bf16[16,40,1024]{2,1,0:T(8,128)(2,1)}), bf16[16,40,1024]{2,1,0:T(8,128)(2,1)}, u32[]{:S(2)}, u32[]{:S(2)}) async-start(bf16[16,40,1024]{2,1,0:T(8,128)(2,1)} %bitcast.212), calls=%async_computation.5 | async-start | bytes 2621440 | tf_op jit(solution)/shard_map/all_to_all | solution.py:56
  411.1 9.3 %shard_map.181 = (bf16[256,1536]{1,0:T(8,128)(2,1)S(1)}, f32[2,2,1,256]{3,2,1,0:T(1,128)S(1)}, f32[2,2,1,256]{3,2,1,0:T(1,128)S(1)}) custom-call(f32[8]{0:T(128)S(1)} %fusion.85.slope_ref, s32[2,128,1]{2,1,0:T(8,128)S(1)} %copy.66.rows_ref, s32[2,1,128]{2,1,0:T(1,128)S(1)} %bitcast.206, bf16[256,1536]{1,0:T(8,128)(2,1)S(1)} %copy-done.39, ...), custom_call_target="tpu_custom_call" | custom-call | flops 167772160 | bytes 2097152 | tf_op jit(solution)/shard_map/pallas_call | solution.py:388
  430.1 4.1 fusion.16
  434.2 7.5 %all-to-all-start.4 = ((bf16[16,64,896]{2,1,0:T(8,128)(2,1)}), bf16[16,64,896]{2,1,0:T(8,128)(2,1)}, u32[]{:S(2)}, u32[]{:S(2)}) async-start(bf16[16,64,896]{2,1,0:T(8,128)(2,1)} %bitcast.207), calls=%async_computation.4 | async-start | bytes 3670016 | tf_op jit(solution)/shard_map/all_to_all | solution.py:56
  446.6 3.6 collective-permute-start.38
  450.3 3.2 shard_map.186
  460.9 8.1 %collective-permute-done.37 = bf16[512,896]{1,0:T(8,128)(2,1)} collective-permute-done((bf16[512,896]{1,0:T(8,128)(2,1)}, bf16[512,896]{1,0:T(8,128)(2,1)}, u32[]{:S(2)}, u32[]{:S(2)}) %collective-permute-start.37) | collective-permute-done | bytes 917536 | tf_op jit(solution)/shard_map/ppermute | solution.py:28
  475.4 3.6 collective-permute-done.42
  497.6 13.4 %collective-permute-done.45 = bf16[640,1024]{1,0:T(8,128)(2,1)S(1)} collective-permute-done((bf16[640,1024]{1,0:T(8,128)(2,1)S(1)}, bf16[640,1024]{1,0:T(8,128)(2,1)S(1)}, u32[]{:S(2)}, u32[]{:S(2)}) %collective-permute-start.45) | collective-permute-done | bytes 1310752 | tf_op jit(solution)/shard_map/ppermute | solution.py:40
  514.8 7.9 %all-to-all-start.3 = ((bf16[16,40,1024]{2,1,0:T(8,128)(2,1)}), bf16[16,40,1024]{2,1,0:T(8,128)(2,1)}, u32[]{:S(2)}, u32[]{:S(2)}) async-start(bf16[16,40,1024]{2,1,0:T(8,128)(2,1)} %bitcast.213), calls=%async_computation.3 | async-start | bytes 2621440 | tf_op jit(solution)/shard_map/all_to_all | solution.py:56
  524.8 29.0 %collective-permute-done.41 = bf16[1024,896]{1,0:T(8,128)(2,1)} collective-permute-done((bf16[1024,896]{1,0:T(8,128)(2,1)}, bf16[1024,896]{1,0:T(8,128)(2,1)}, u32[]{:S(2)}, u32[]{:S(2)}) %collective-permute-start.41) | collective-permute-done | bytes 1835040 | tf_op jit(solution)/shard_map/ppermute | solution.py:32
  554.3 3.9 add_convert_fusion.1
  558.2 6.8 all-to-all-start.2
  566.7 20.6 %all-to-all-done.2 = bf16[16,64,896]{2,1,0:T(8,128)(2,1)S(1)} async-done(((bf16[16,64,896]{2,1,0:T(8,128)(2,1)}), bf16[16,64,896]{2,1,0:T(8,128)(2,1)S(1)}, u32[]{:S(2)}, u32[]{:S(2)}) %all-to-all-start.2) | async-done | bytes 1835040 | tf_op jit(solution)/shard_map/all_to_all | solution.py:56
  588.5 2.9 fusion.36
  591.4 5.4 collective-permute-start.21
  599.1 4.4 fusion.28
  613.8 3.3 multiply_reduce_fusion.3
  618.1 3.6 all-to-all-start.6
  621.7 6.7 all-to-all-done.6
  629.1 6.4 all-to-all-start.7
  638.0 4.2 all-to-all-done.7
  649.5 3.6 reshape.403.second_ref
  653.2 2.9 slice.661
  659.4 4.4 reshape.397.first_ref
  665.4 4.1 shard_map.188
  (616 shorter events, 249.6 us)
Async XLA Ops:
  7.2 279.5 %all-gather.6.cloned.1.call-start = ((), (), s32[]{:S(2)}) async-start(), calls=%async_computation.8 | async-start | bytes 5898240 | tf_op jit(solution)/shard_map/all_gather | solution.py:483
  52.9 15.4 %collective-permute-start.6 = (bf16[320,1024]{1,0:T(8,128)(2,1)}, bf16[320,1024]{1,0:T(8,128)(2,1)}, u32[]{:S(2)}, u32[]{:S(2)}) collective-permute-start(bf16[320,1024]{1,0:T(8,128)(2,1)} %get-tuple-element.141), channel_id=1, source_target_pairs={{0,65},{65,0},{1,64},{64,1},{2,67},{67,2},{3,66},{66,3},{4,69},{69... | collective-permute-start | bytes 1966088 | tf_op jit(solution)/shard_map/ppermute | solution.py:44
  53.9 20.5 %collective-permute-start.2 = (s32[1,128]{1,0:T(1,128)S(1)}, s32[1,128]{1,0:T(1,128)S(1)}, u32[]{:S(2)}, u32[]{:S(2)}) collective-permute-start(s32[1,128]{1,0:T(1,128)S(1)} %bitcast.285), channel_id=1, source_target_pairs={{0,8},{8,0},{1,9},{9,1},{2,10},{10,2},{3,11},{11,3},{4,12},{12,4},... | collective-permute-start | bytes 1544 | tf_op jit(solution)/shard_map/ppermute | solution.py:48
  57.2 48.3 %collective-permute-start.1 = (bf16[1024,896]{1,0:T(8,128)(2,1)S(1)}, bf16[1024,896]{1,0:T(8,128)(2,1)}, u32[]{:S(2)}, u32[]{:S(2)}) collective-permute-start(bf16[1024,896]{1,0:T(8,128)(2,1)S(1)} %bitcast.200), channel_id=1, source_target_pairs={{0,48},{16,0},{32,16},{48,32},{1,49},{17,1},{33,17},{49,33},{2,50}... | collective-permute-start | bytes 5505032 | tf_op jit(solution)/shard_map/ppermute | solution.py:32
  61.1 42.6 %collective-permute-start = (bf16[1024,896]{1,0:T(8,128)(2,1)S(1)}, bf16[1024,896]{1,0:T(8,128)(2,1)}, u32[]{:S(2)}, u32[]{:S(2)}) collective-permute-start(bf16[1024,896]{1,0:T(8,128)(2,1)S(1)} %bitcast.201), channel_id=1, source_target_pairs={{0,16},{16,32},{32,48},{48,0},{1,17},{17,33},{33,49},{49,1},{2,18}... | collective-permute-start | bytes 5505032 | tf_op jit(solution)/shard_map/ppermute | solution.py:28
  71.5 46.6 %collective-permute-start.8 = (bf16[640,1024]{1,0:T(8,128)(2,1)}, bf16[640,1024]{1,0:T(8,128)(2,1)}, u32[]{:S(2)}, u32[]{:S(2)}) collective-permute-start(bf16[640,1024]{1,0:T(8,128)(2,1)} %get-tuple-element.117), channel_id=1, source_target_pairs={{0,2},{2,4},{4,6},{6,0},{1,3},{3,5},{5,7},{7,1},{8,10},{10,12},{12... | collective-permute-start | bytes 3932168 | tf_op jit(solution)/shard_map/ppermute | solution.py:36
  71.8 55.3 %collective-permute-start.7 = (bf16[640,1024]{1,0:T(8,128)(2,1)}, bf16[640,1024]{1,0:T(8,128)(2,1)}, u32[]{:S(2)}, u32[]{:S(2)}) collective-permute-start(bf16[640,1024]{1,0:T(8,128)(2,1)} %get-tuple-element.117), channel_id=1, source_target_pairs={{0,6},{2,0},{4,2},{6,4},{1,7},{3,1},{5,3},{7,5},{8,14},{10,8},{12,... | collective-permute-start | bytes 3932168 | tf_op jit(solution)/shard_map/ppermute | solution.py:40
  108.9 79.0 %all-to-all-start.1 = ((bf16[8,128,896]{2,1,0:T(8,128)(2,1)}), bf16[8,128,896]{2,1,0:T(8,128)(2,1)}, u32[]{:S(2)}, u32[]{:S(2)}) async-start(bf16[8,128,896]{2,1,0:T(8,128)(2,1)} %broadcast_in_dim.97), calls=%async_computation.1 | async-start | bytes 3670016 | tf_op jit(solution)/shard_map/all_to_all | solution.py:56
  120.1 39.0 %collective-permute-start.9 = (bf16[320,1024]{1,0:T(8,128)(2,1)}, bf16[320,1024]{1,0:T(8,128)(2,1)}, u32[]{:S(2)}, u32[]{:S(2)}) collective-permute-start(bf16[320,1024]{1,0:T(8,128)(2,1)} %slice.586), channel_id=1, source_target_pairs={{0,2},{2,4},{4,6},{6,0},{1,3},{3,5},{5,7},{7,1},{8,10},{10,12},{12... | collective-permute-start | bytes 1966088 | tf_op jit(solution)/shard_map/ppermute | solution.py:36
  122.3 48.7 %collective-permute-start.4 = (bf16[512,896]{1,0:T(8,128)(2,1)}, bf16[512,896]{1,0:T(8,128)(2,1)}, u32[]{:S(2)}, u32[]{:S(2)}) collective-permute-start(bf16[512,896]{1,0:T(8,128)(2,1)} %slice.580), channel_id=1, source_target_pairs={{0,16},{16,32},{32,48},{48,0},{1,17},{17,33},{33,49},{49,1},{2,18}... | collective-permute-start | bytes 2752520 | tf_op jit(solution)/shard_map/ppermute | solution.py:28
  125.8 45.3 %collective-permute-start.5 = (bf16[512,896]{1,0:T(8,128)(2,1)}, bf16[512,896]{1,0:T(8,128)(2,1)}, u32[]{:S(2)}, u32[]{:S(2)}) collective-permute-start(bf16[512,896]{1,0:T(8,128)(2,1)} %slice.581), channel_id=1, source_target_pairs={{0,48},{16,0},{32,16},{48,32},{1,49},{17,1},{33,17},{49,33},{2,50}... | collective-permute-start | bytes 2752520 | tf_op jit(solution)/shard_map/ppermute | solution.py:32
  129.2 32.0 %collective-permute-start.10 = (bf16[320,1024]{1,0:T(8,128)(2,1)}, bf16[320,1024]{1,0:T(8,128)(2,1)}, u32[]{:S(2)}, u32[]{:S(2)}) collective-permute-start(bf16[320,1024]{1,0:T(8,128)(2,1)} %slice.587), channel_id=1, source_target_pairs={{0,6},{2,0},{4,2},{6,4},{1,7},{3,1},{5,3},{7,5},{8,14},{10,8},{12,... | collective-permute-start | bytes 1966088 | tf_op jit(solution)/shard_map/ppermute | solution.py:40
  133.3 43.7 %collective-permute-start.3 = (bf16[128,1024]{1,0:T(8,128)(2,1)S(1)}, bf16[128,1024]{1,0:T(8,128)(2,1)S(1)}, u32[]{:S(2)}, u32[]{:S(2)}) collective-permute-start(bf16[128,1024]{1,0:T(8,128)(2,1)S(1)} %add_convert_fusion.9), channel_id=1, source_target_pairs={{0,8},{8,0},{1,9},{9,1},{2,10},{10,2},{3,11},{11,3},{4,12},{12,4},... | collective-permute-start | bytes 786440 | tf_op jit(solution)/shard_map/ppermute | solution.py:48
  190.1 6.9 %collective-permute-start.11 = (f32[128,1024]{1,0:T(8,128)S(1)}, f32[128,1024]{1,0:T(8,128)S(1)}, u32[]{:S(2)}, u32[]{:S(2)}) collective-permute-start(f32[128,1024]{1,0:T(8,128)S(1)} %fusion.51), channel_id=1, source_target_pairs={{0,8},{8,0},{1,9},{9,1},{2,10},{10,2},{3,11},{11,3},{4,12},{12,4},... | collective-permute-start | bytes 1572872 | tf_op jit(solution)/shard_map/ppermute | solution.py:48
  200.3 46.2 %collective-permute-start.15 = (bf16[1024,896]{1,0:T(8,128)(2,1)S(1)}, bf16[1024,896]{1,0:T(8,128)(2,1)S(1)}, u32[]{:S(2)}, u32[]{:S(2)}) collective-permute-start(bf16[1024,896]{1,0:T(8,128)(2,1)S(1)} %broadcast_select_fusion.own_ref), channel_id=1, source_target_pairs={{0,48},{16,0},{32,16},{48,32},{1,49},{17,1},{33,17},{49,33},{2,50}... | collective-permute-start | bytes 5505032 | tf_op jit(solution)/shard_map/ppermute | solution.py:32
  203.1 42.3 %collective-permute-start.16 = (bf16[1024,896]{1,0:T(8,128)(2,1)S(1)}, bf16[1024,896]{1,0:T(8,128)(2,1)S(1)}, u32[]{:S(2)}, u32[]{:S(2)}) collective-permute-start(bf16[1024,896]{1,0:T(8,128)(2,1)S(1)} %broadcast_select_fusion.own_ref), channel_id=1, source_target_pairs={{0,16},{16,32},{32,48},{48,0},{1,17},{17,33},{33,49},{49,1},{2,18}... | collective-permute-start | bytes 5505032 | tf_op jit(solution)/shard_map/ppermute | solution.py:28
  246.5 21.7 %collective-permute-start.17 = (bf16[512,896]{1,0:T(8,128)(2,1)}, bf16[512,896]{1,0:T(8,128)(2,1)S(1)}, u32[]{:S(2)}, u32[]{:S(2)}) collective-permute-start(bf16[512,896]{1,0:T(8,128)(2,1)} %slice.601), channel_id=1, source_target_pairs={{0,16},{16,32},{32,48},{48,0},{1,17},{17,33},{33,49},{49,1},{2,18}... | collective-permute-start | bytes 2752520 | tf_op jit(solution)/shard_map/ppermute | solution.py:28
  248.7 20.8 %collective-permute-start.18 = (bf16[512,896]{1,0:T(8,128)(2,1)}, bf16[512,896]{1,0:T(8,128)(2,1)}, u32[]{:S(2)}, u32[]{:S(2)}) collective-permute-start(bf16[512,896]{1,0:T(8,128)(2,1)} %slice.602), channel_id=1, source_target_pairs={{0,48},{16,0},{32,16},{48,32},{1,49},{17,1},{33,17},{49,33},{2,50}... | collective-permute-start | bytes 2752520 | tf_op jit(solution)/shard_map/ppermute | solution.py:32
  251.8 24.7 %collective-permute-start.14 = (bf16[128,1024]{1,0:T(8,128)(2,1)S(1)}, bf16[128,1024]{1,0:T(8,128)(2,1)S(1)}, u32[]{:S(2)}, u32[]{:S(2)}) collective-permute-start(bf16[128,1024]{1,0:T(8,128)(2,1)S(1)} %add_convert_fusion.7), channel_id=1, source_target_pairs={{0,8},{8,0},{1,9},{9,1},{2,10},{10,2},{3,11},{11,3},{4,12},{12,4},... | collective-permute-start | bytes 786440 | tf_op jit(solution)/shard_map/ppermute | solution.py:48
  329.4 12.0 %collective-permute-start.25 = (f32[128,1024]{1,0:T(8,128)S(1)}, f32[128,1024]{1,0:T(8,128)S(1)}, u32[]{:S(2)}, u32[]{:S(2)}) collective-permute-start(f32[128,1024]{1,0:T(8,128)S(1)} %fusion.45), channel_id=1, source_target_pairs={{0,8},{8,0},{1,9},{9,1},{2,10},{10,2},{3,11},{11,3},{4,12},{12,4},... | collective-permute-start | bytes 1572872 | tf_op jit(solution)/shard_map/ppermute | solution.py:48
  331.3 36.9 %collective-permute-start.28 = (bf16[512,896]{1,0:T(8,128)(2,1)S(1)}, bf16[512,896]{1,0:T(8,128)(2,1)S(1)}, u32[]{:S(2)}, u32[]{:S(2)}) collective-permute-start(bf16[512,896]{1,0:T(8,128)(2,1)S(1)} %get-tuple-element.139), channel_id=1, source_target_pairs={{0,16},{16,32},{32,48},{48,0},{1,17},{17,33},{33,49},{49,1},{2,18}... | collective-permute-start | bytes 2752520 | tf_op jit(solution)/shard_map/ppermute | solution.py:28
  331.4 39.6 %collective-permute-start.30 = (bf16[512,896]{1,0:T(8,128)(2,1)S(1)}, bf16[512,896]{1,0:T(8,128)(2,1)S(1)}, u32[]{:S(2)}, u32[]{:S(2)}) collective-permute-start(bf16[512,896]{1,0:T(8,128)(2,1)S(1)} %get-tuple-element.138), channel_id=1, source_target_pairs={{0,48},{16,0},{32,16},{48,32},{1,49},{17,1},{33,17},{49,33},{2,50}... | collective-permute-start | bytes 2752520 | tf_op jit(solution)/shard_map/ppermute | solution.py:32
  338.6 17.2 %collective-permute-start.32 = (bf16[320,1024]{1,0:T(8,128)(2,1)S(1)}, bf16[320,1024]{1,0:T(8,128)(2,1)S(1)}, u32[]{:S(2)}, u32[]{:S(2)}) collective-permute-start(bf16[320,1024]{1,0:T(8,128)(2,1)S(1)} %get-tuple-element.127), channel_id=1, source_target_pairs={{0,2},{2,4},{4,6},{6,0},{1,3},{3,5},{5,7},{7,1},{8,10},{10,12},{12... | collective-permute-start | bytes 1966088 | tf_op jit(solution)/shard_map/ppermute | solution.py:36
  339.0 17.9 %collective-permute-start.34 = (bf16[320,1024]{1,0:T(8,128)(2,1)S(1)}, bf16[320,1024]{1,0:T(8,128)(2,1)S(1)}, u32[]{:S(2)}, u32[]{:S(2)}) collective-permute-start(bf16[320,1024]{1,0:T(8,128)(2,1)S(1)} %get-tuple-element.125), channel_id=1, source_target_pairs={{0,6},{2,0},{4,2},{6,4},{1,7},{3,1},{5,3},{7,5},{8,14},{10,8},{12,... | collective-permute-start | bytes 1966088 | tf_op jit(solution)/shard_map/ppermute | solution.py:40
  344.1 17.6 %collective-permute-start.26 = (bf16[128,1024]{1,0:T(8,128)(2,1)S(1)}, bf16[128,1024]{1,0:T(8,128)(2,1)S(1)}, u32[]{:S(2)}, u32[]{:S(2)}) collective-permute-start(bf16[128,1024]{1,0:T(8,128)(2,1)S(1)} %convert_element_type.319), channel_id=1, source_target_pairs={{0,8},{8,0},{1,9},{9,1},{2,10},{10,2},{3,11},{11,3},{4,12},{12,4},... | collective-permute-start | bytes 786440 | tf_op jit(solution)/shard_map/ppermute | solution.py:48
  358.8 30.4 %collective-permute-start.33 = (bf16[640,1024]{1,0:T(8,128)(2,1)S(1)}, bf16[640,1024]{1,0:T(8,128)(2,1)S(1)}, u32[]{:S(2)}, u32[]{:S(2)}) collective-permute-start(bf16[640,1024]{1,0:T(8,128)(2,1)S(1)} %pad_maximum_fusion.4), channel_id=1, source_target_pairs={{0,2},{2,4},{4,6},{6,0},{1,3},{3,5},{5,7},{7,1},{8,10},{10,12},{12... | collective-permute-start | bytes 3932168 | tf_op jit(solution)/shard_map/ppermute | solution.py:36
  359.0 30.2 %collective-permute-start.35 = (bf16[640,1024]{1,0:T(8,128)(2,1)S(1)}, bf16[640,1024]{1,0:T(8,128)(2,1)S(1)}, u32[]{:S(2)}, u32[]{:S(2)}) collective-permute-start(bf16[640,1024]{1,0:T(8,128)(2,1)S(1)} %pad_maximum_fusion.5), channel_id=1, source_target_pairs={{0,6},{2,0},{4,2},{6,4},{1,7},{3,1},{5,3},{7,5},{8,14},{10,8},{12,... | collective-permute-start | bytes 3932168 | tf_op jit(solution)/shard_map/ppermute | solution.py:40
  366.3 10.5 %collective-permute-start.27 = (f32[128,1024]{1,0:T(8,128)S(1)}, f32[128,1024]{1,0:T(8,128)S(1)}, u32[]{:S(2)}, u32[]{:S(2)}) collective-permute-start(f32[128,1024]{1,0:T(8,128)S(1)} %fusion.30), channel_id=1, source_target_pairs={{0,8},{8,0},{1,9},{9,1},{2,10},{10,2},{3,11},{11,3},{4,12},{12,4},... | collective-permute-start | bytes 1572872 | tf_op jit(solution)/shard_map/ppermute | solution.py:48
  372.2 53.9 %collective-permute-start.29 = (bf16[1024,896]{1,0:T(8,128)(2,1)}, bf16[1024,896]{1,0:T(8,128)(2,1)}, u32[]{:S(2)}, u32[]{:S(2)}) collective-permute-start(bf16[1024,896]{1,0:T(8,128)(2,1)} %pad_maximum_fusion), channel_id=1, source_target_pairs={{0,16},{16,32},{32,48},{48,0},{1,17},{17,33},{33,49},{49,1},{2,18}... | collective-permute-start | bytes 5505032 | tf_op jit(solution)/shard_map/ppermute | solution.py:28
  373.9 54.4 %collective-permute-start.31 = (bf16[1024,896]{1,0:T(8,128)(2,1)}, bf16[1024,896]{1,0:T(8,128)(2,1)}, u32[]{:S(2)}, u32[]{:S(2)}) collective-permute-start(bf16[1024,896]{1,0:T(8,128)(2,1)} %pad_maximum_fusion.1), channel_id=1, source_target_pairs={{0,48},{16,0},{32,16},{48,32},{1,49},{17,1},{33,17},{49,33},{2,50}... | collective-permute-start | bytes 5505032 | tf_op jit(solution)/shard_map/ppermute | solution.py:32
  392.1 42.0 %all-to-all-start.5 = ((bf16[16,40,1024]{2,1,0:T(8,128)(2,1)}), bf16[16,40,1024]{2,1,0:T(8,128)(2,1)}, u32[]{:S(2)}, u32[]{:S(2)}) async-start(bf16[16,40,1024]{2,1,0:T(8,128)(2,1)} %bitcast.212), calls=%async_computation.5 | async-start | bytes 2621440 | tf_op jit(solution)/shard_map/all_to_all | solution.py:56
  401.4 8.4 %collective-permute-start.36 = (bf16[128,1024]{1,0:T(8,128)(2,1)S(1)}, bf16[128,1024]{1,0:T(8,128)(2,1)S(1)}, u32[]{:S(2)}, u32[]{:S(2)}) collective-permute-start(bf16[128,1024]{1,0:T(8,128)(2,1)S(1)} %convert_select_fusion), channel_id=1, source_target_pairs={{0,8},{8,0},{1,9},{9,1},{2,10},{10,2},{3,11},{11,3},{4,12},{12,4},... | collective-permute-start | bytes 786440 | tf_op jit(solution)/shard_map/ppermute | solution.py:48
  434.2 38.5 %all-to-all-start.4 = ((bf16[16,64,896]{2,1,0:T(8,128)(2,1)}), bf16[16,64,896]{2,1,0:T(8,128)(2,1)}, u32[]{:S(2)}, u32[]{:S(2)}) async-start(bf16[16,64,896]{2,1,0:T(8,128)(2,1)} %bitcast.207), calls=%async_computation.4 | async-start | bytes 3670016 | tf_op jit(solution)/shard_map/all_to_all | solution.py:56
  441.7 202.3 %all-gather.10.cloned.1.call-start = ((), (), s32[]{:S(2)}) async-start(), calls=%async_computation.10 | async-start | bytes 3342336 | tf_op jit(solution)/shard_map/all_gather | solution.py:553
  446.6 22.4 %collective-permute-start.37 = (bf16[512,896]{1,0:T(8,128)(2,1)}, bf16[512,896]{1,0:T(8,128)(2,1)}, u32[]{:S(2)}, u32[]{:S(2)}) collective-permute-start(bf16[512,896]{1,0:T(8,128)(2,1)} %get-tuple-element.137), channel_id=1, source_target_pairs={{0,16},{16,32},{32,48},{48,0},{1,17},{17,33},{33,49},{49,1},{2,18}... | collective-permute-start | bytes 2752520 | tf_op jit(solution)/shard_map/ppermute | solution.py:28
  446.6 24.3 %collective-permute-start.38 = (bf16[512,896]{1,0:T(8,128)(2,1)}, bf16[512,896]{1,0:T(8,128)(2,1)}, u32[]{:S(2)}, u32[]{:S(2)}) collective-permute-start(bf16[512,896]{1,0:T(8,128)(2,1)} %get-tuple-element.136), channel_id=1, source_target_pairs={{0,48},{16,0},{32,16},{48,32},{1,49},{17,1},{33,17},{49,33},{2,50}... | collective-permute-start | bytes 2752520 | tf_op jit(solution)/shard_map/ppermute | solution.py:32
  456.6 22.4 %collective-permute-start.42 = (bf16[320,1024]{1,0:T(8,128)(2,1)}, bf16[320,1024]{1,0:T(8,128)(2,1)}, u32[]{:S(2)}, u32[]{:S(2)}) collective-permute-start(bf16[320,1024]{1,0:T(8,128)(2,1)} %get-tuple-element.120), channel_id=1, source_target_pairs={{0,2},{2,4},{4,6},{6,0},{1,3},{3,5},{5,7},{7,1},{8,10},{10,12},{12... | collective-permute-start | bytes 1966088 | tf_op jit(solution)/shard_map/ppermute | solution.py:36
  457.9 21.1 %collective-permute-start.44 = (bf16[320,1024]{1,0:T(8,128)(2,1)}, bf16[320,1024]{1,0:T(8,128)(2,1)}, u32[]{:S(2)}, u32[]{:S(2)}) collective-permute-start(bf16[320,1024]{1,0:T(8,128)(2,1)} %get-tuple-element.121), channel_id=1, source_target_pairs={{0,6},{2,0},{4,2},{6,4},{1,7},{3,1},{5,3},{7,5},{8,14},{10,8},{12,... | collective-permute-start | bytes 1966088 | tf_op jit(solution)/shard_map/ppermute | solution.py:40
  482.5 28.5 %collective-permute-start.45 = (bf16[640,1024]{1,0:T(8,128)(2,1)S(1)}, bf16[640,1024]{1,0:T(8,128)(2,1)S(1)}, u32[]{:S(2)}, u32[]{:S(2)}) collective-permute-start(bf16[640,1024]{1,0:T(8,128)(2,1)S(1)} %pad_maximum_fusion.7), channel_id=1, source_target_pairs={{0,6},{2,0},{4,2},{6,4},{1,7},{3,1},{5,3},{7,5},{8,14},{10,8},{12,... | collective-permute-start | bytes 3932168 | tf_op jit(solution)/shard_map/ppermute | solution.py:40
  482.7 29.7 %collective-permute-start.43 = (bf16[640,1024]{1,0:T(8,128)(2,1)S(1)}, bf16[640,1024]{1,0:T(8,128)(2,1)S(1)}, u32[]{:S(2)}, u32[]{:S(2)}) collective-permute-start(bf16[640,1024]{1,0:T(8,128)(2,1)S(1)} %pad_maximum_fusion.6), channel_id=1, source_target_pairs={{0,2},{2,4},{4,6},{6,0},{1,3},{3,5},{5,7},{7,1},{8,10},{10,12},{12... | collective-permute-start | bytes 3932168 | tf_op jit(solution)/shard_map/ppermute | solution.py:36
  492.3 61.5 %collective-permute-start.41 = (bf16[1024,896]{1,0:T(8,128)(2,1)}, bf16[1024,896]{1,0:T(8,128)(2,1)}, u32[]{:S(2)}, u32[]{:S(2)}) collective-permute-start(bf16[1024,896]{1,0:T(8,128)(2,1)} %pad_maximum_fusion.3), channel_id=1, source_target_pairs={{0,48},{16,0},{32,16},{48,32},{1,49},{17,1},{33,17},{49,33},{2,50}... | collective-permute-start | bytes 5505032 | tf_op jit(solution)/shard_map/ppermute | solution.py:32
  497.6 56.7 %collective-permute-start.40 = (bf16[1024,896]{1,0:T(8,128)(2,1)}, bf16[1024,896]{1,0:T(8,128)(2,1)}, u32[]{:S(2)}, u32[]{:S(2)}) collective-permute-start(bf16[1024,896]{1,0:T(8,128)(2,1)} %pad_maximum_fusion.2), channel_id=1, source_target_pairs={{0,16},{16,32},{32,48},{48,0},{1,17},{17,33},{33,49},{49,1},{2,18}... | collective-permute-start | bytes 5505032 | tf_op jit(solution)/shard_map/ppermute | solution.py:28
  514.8 43.5 %all-to-all-start.3 = ((bf16[16,40,1024]{2,1,0:T(8,128)(2,1)}), bf16[16,40,1024]{2,1,0:T(8,128)(2,1)}, u32[]{:S(2)}, u32[]{:S(2)}) async-start(bf16[16,40,1024]{2,1,0:T(8,128)(2,1)} %bitcast.213), calls=%async_computation.3 | async-start | bytes 2621440 | tf_op jit(solution)/shard_map/all_to_all | solution.py:56
  558.2 29.1 %all-to-all-start.2 = ((bf16[16,64,896]{2,1,0:T(8,128)(2,1)}), bf16[16,64,896]{2,1,0:T(8,128)(2,1)S(1)}, u32[]{:S(2)}, u32[]{:S(2)}) async-start(bf16[16,64,896]{2,1,0:T(8,128)(2,1)} %bitcast.48), calls=%async_computation.2 | async-start | bytes 3670016 | tf_op jit(solution)/shard_map/all_to_all | solution.py:56
  565.0 88.1 %all-gather.8.cloned.1.call-start = ((), (), s32[]{:S(2)}) async-start(), calls=%async_computation.9 | async-start | bytes 3342336 | tf_op jit(solution)/shard_map/all_gather | solution.py:553
  591.4 6.9 %collective-permute-start.21 = (f32[128,1024]{1,0:T(8,128)S(1)}, f32[128,1024]{1,0:T(8,128)S(1)}, u32[]{:S(2)}, u32[]{:S(2)}) collective-permute-start(f32[128,1024]{1,0:T(8,128)S(1)} %fusion.36), channel_id=1, source_target_pairs={{0,8},{8,0},{1,9},{9,1},{2,10},{10,2},{3,11},{11,3},{4,12},{12,4},... | collective-permute-start | bytes 1572872 | tf_op jit(solution)/shard_map/ppermute | solution.py:48
  618.1 10.3 %all-to-all-start.6 = ((f32[8,24,128]{2,1,0:T(8,128)}), f32[8,24,128]{2,1,0:T(8,128)S(1)}, u32[]{:S(2)}, u32[]{:S(2)}) async-start(f32[8,24,128]{2,1,0:T(8,128)} %copy.76), calls=%async_computation.6 | async-start | bytes 196608 | tf_op jit(solution)/shard_map/all_to_all | solution.py:56
  629.1 13.0 %all-to-all-start.7 = ((f32[16,24,128]{2,1,0:T(8,128)}), f32[16,24,128]{2,1,0:T(8,128)S(1)}, u32[]{:S(2)}, u32[]{:S(2)}) async-start(f32[16,24,128]{2,1,0:T(8,128)} %broadcast_in_dim.111), calls=%async_computation.7 | async-start | bytes 393216 | tf_op jit(solution)/shard_map/all_to_all | solution.py:56
  (137 other events, 1229.5 us)
Sparse Core Ops, SparseCore 0:
  62.5 106.7 all-gather.5
  475.5 44.0 all-gather.9
  588.6 39.4 all-gather.7

commit v7 on v6

--- a/solution.py
+++ b/solution.py
@@ -258,7 +258,7 @@
     )
 
 
-def assemble_kernel(at_ref, first_ref, second_ref, up_ref, qkv_ref):
+def assemble_kernel(at_ref, first_ref, second_ref, up_ref, qkv_ref, down_ref, proj_ref):
     def put(ref):
         for j in range(4):
             for e in range(2):
@@ -270,6 +270,14 @@
                     both = [ref[0, j, core, :, lane : lane + 64].astype(f32) for core in range(2)]
                     at = t * 1024 + j * 256 + e * 128
                     qkv_ref[0, :, at : at + 128] = jnp.concatenate(both, axis=1)
+            for core in range(2):
+                rest = ref[0, j, core, :, 896:].astype(f32)
+                for b in range(8):
+                    lanes = slice(b * 128, b * 128 + 128)
+                    for g in range(4):
+                        at = j * 32 + g * 8
+                        down_ref[0, core, 0, at : at + 8, lanes] = rest[b * 8 : b * 8 + 8, g * 128 : g * 128 + 128]
+                    proj_ref[0, core, 0, j * 8 : j * 8 + 8, lanes] = rest[b * 8 : b * 8 + 8, 512:640]
 
     @pl.when(pl.program_id(0) == 0)
     def _():
@@ -281,12 +289,17 @@
 
 
 def assemble(at, first, second):
-    block = (1, 4, 2, 64, 896)
+    block = (1, 4, 2, 64, 1536)
     return call(
         assemble_kernel,
         at,
         (first, second),
-        (jax.ShapeDtypeStruct((LAYERS, 128, 4096), f32), jax.ShapeDtypeStruct((LAYERS, 128, 3072), f32)),
+        (
+            jax.ShapeDtypeStruct((LAYERS, 128, 4096), f32),
+            jax.ShapeDtypeStruct((LAYERS, 128, 3072), f32),
+            jax.ShapeDtypeStruct((LAYERS, 2, 2, 128, D), f32),
+            jax.ShapeDtypeStruct((LAYERS, 2, 2, 32, D), f32),
+        ),
         (LAYERS, 2),
         [
             pl.BlockSpec(block, lambda l, h, at: (h, 0, 0, 0, 0)),
@@ -295,6 +308,8 @@
         (
             pl.BlockSpec((1, 64, 4096), lambda l, h, at: (l, h, 0)),
             pl.BlockSpec((1, 64, 3072), lambda l, h, at: (l, h, 0)),
+            pl.BlockSpec((1, 2, 1, 128, D), lambda l, h, at: (l, 0, h, 0, 0)),
+            pl.BlockSpec((1, 2, 1, 32, D), lambda l, h, at: (l, 0, h, 0, 0)),
         ),
     )
 
@@ -489,6 +504,8 @@
         if layer == 0:
             next_z = to_all(after(mine_z[1], previous, following), SHARD, 8).reshape(D, 896)
             block_z, all_x = after(next_z, top, bottom), next_x
+        else:
+            second_ring = (previous, following)
 
     small = all_small.reshape(4, 2, 24, 128).astype(f32)
     wide = jnp.transpose(small[:, :, :16], (2, 0, 1, 3)).reshape(LAYERS, 8, D)
@@ -514,10 +531,12 @@
         ubias = rolled(ubias.reshape(4, 512), z).reshape(2048)
         first_f, normed_one, inv_one = layer_norm(current, gain_one, shift_one)
         first_in = both(first_f.astype(bf16))
+        if layer == 0:
+            first_in = after(first_in, next_z)
         qkv = (dot(first_in, wqkv) + bqkv).astype(bf16)
         ctx = attend(qkv, rows, cols, slopes)
         if layer == 0:
-            ctx = after(ctx, next_z)
+            ctx = after(ctx, *second_ring)
         middle = current + halves_summed(dot, ctx, wproj) + bproj
         second_f, normed_two, inv_two = layer_norm(middle, gain_two, shift_two)
         second_in = both(second_f.astype(bf16))
@@ -548,14 +567,12 @@
         part_z = exchange(part_z, ("x", "yhi", "ylo"))
         return summed(after(part_z, *earlier) if earlier else part_z), part_x
 
-    def share(part_z, part_x, *earlier):
-        part = jnp.concatenate([part_z.reshape(56, D), part_x])
-        parts = lax.all_gather(after(part, *earlier) if earlier else part, REP, axis=0)
-        by_z = parts[:, :56].reshape(2, 4, 2, 64, 896)
-        by_x = jnp.transpose(parts[:, 56:].reshape(8, 2, 40, D), (1, 0, 2, 3))
-        return by_z, (by_x[:, :, :32].reshape(512, D), by_x[:, :, 32:].reshape(128, D))
-
-    grads_x, grads_z = [None] * LAYERS, [None] * LAYERS
+    def share(part_z, part_x):
+        part_x = jnp.transpose(part_x.reshape(5, 8, 8, 128), (2, 1, 0, 3)).reshape(64, 640)
+        parts = lax.all_gather(jnp.concatenate([part_z, part_x], axis=1), REP, axis=0)
+        return parts.reshape(2, 4, 2, 64, 1536)
+
+    shared = [None] * LAYERS
     thin_grads, head_grads, unit_grads = [None] * LAYERS, [None] * LAYERS, [None] * LAYERS
     running, ring_state = grad_out, None
     for layer in reversed(range(LAYERS)):
@@ -576,21 +593,20 @@
         if ring_state is not None:
             grad_midb = after(grad_midb, *ring_state[1], *x_state[0])
             part_x_before = part_x
-            later_state = x_state
         grad_midb = both(grad_midb)
         grad_ctx = dot_nt(grad_midb, wproj).astype(bf16)
         part_x, x_state = ring_x(activ, grad_yb, ctx, grad_midb)
         grad_qkv, g_bq, g_bv = attend_back(qkv, ctx, grad_ctx, rows, cols, slopes)
         if ring_state is not None:
             later = (after(part_z, grad_qkv), part_x_before)
-            grad_qkv = after(grad_qkv, *ring_state[2], *later_state[1])
+            grad_qkv = after(grad_qkv, *ring_state[2], *x_state[0])
         part_z, ring_state = ring_z(second_in, grad_ub, first_in, grad_qkv)
         if layer == 0:
             grad_qkv = after(grad_qkv, *ring_state[0])
         grad_one = halves_summed(dot_nt, grad_qkv, wqkv)
         if layer == 0:
             grad_one = after(grad_one, *ring_state[1])
-            grads_z[1], grads_x[1] = share(*finish(*later, *ring_state[1]))
+            shared[1] = share(*finish(*later, *ring_state[1]))
         back_one, g_gain_one, g_shift_one = norm_back(grad_one, normed_one, inv_one, gain_one)
         running = grad_mid + back_one
 
@@ -598,7 +614,7 @@
         head_grads[layer] = [jnp.sum(g, axis=0).reshape(4, 128) for g in (g_bq, g_bv)]
         unit_grads[layer] = g_ubias.reshape(4, 512)
 
-    grads_z[0], grads_x[0] = share(*finish(part_z, part_x))
+    shared[0] = share(*finish(part_z, part_x))
 
     thin = jnp.stack(thin_grads[0] + thin_grads[1]).reshape(LAYERS, 6, 4, 2, 128)
     heads = jnp.stack(head_grads[0] + head_grads[1], axis=1)
@@ -615,15 +631,14 @@
     part = jnp.sum(exchange(part.reshape(8, 24, 128), SHARD), axis=0)
     part = jnp.sum(to_all(part, REP, 16), axis=0).reshape(LAYERS, 12, 128)
     g_wide = jnp.transpose(part[:, :8], (0, 2, 1))
-    g_up, g_qkv = assemble(at, grads_z[0], grads_z[1])
-    g_down, g_proj = (jnp.stack([grads_x[layer][i] for layer in range(LAYERS)]).astype(f32) for i in range(2))
+    g_up, g_qkv, g_down, g_proj = assemble(at, shared[0], shared[1])
     return (
         hidden_out,
         running,
         g_qkv,
-        g_proj,
+        g_proj.reshape(LAYERS, 128, D),
         g_up,
-        g_down,
+        g_down.reshape(LAYERS, 512, D),
         g_wide[:, :, :2],
         g_wide[:, :, 2:],
         part[:, 8:].reshape(LAYERS, 512),

time: 691 us -> 669 us (0.968)
  local copies, waits for them, and re-layouts: 107 us -> 90.7 us
  starting transfers between devices: 117 us -> 103 us
  waiting for transfers between devices: 220 us -> 230 us
  other arithmetic: 60 us -> 52.9 us
    ppermute x8, waiting for transfers between devices: 84.3 us -> 69.8 us  [z_up(): return lax.ppermute(a, 'z', ring(1))]
    slice x9 -> x0, local copies, waits for them, and re-layouts: 13.2 us -> none  [the longest x2 5.78 us: share(): by_z = parts[:, :56].reshape(2, 4, 2, 64, 896)]
    ppermute x6, waiting for transfers between devices: 45.3 us -> 57.9 us  [x_up(): return lax.ppermute(a, 'x', ring(1))]
    ppermute x8, waiting for transfers between devices: 30.8 us -> 39.9 us  [z_down(): return lax.ppermute(a, 'z', ring(3))]
    all_to_all x7, starting transfers between devices: 44.6 us -> 35.7 us  [exchange(): return lax.all_to_all(blocks, axes, 0, 0, tiled=True)]
    ppermute x6, waiting for transfers between devices: 13.5 us -> 22.3 us  [x_down(): return lax.ppermute(a, 'x', ring(3))]
    reshape x6 -> x0, local copies, waits for them, and re-layouts: 8.56 us -> none  [the longest x2 8.04 us: share(): by_z = parts[:, :56].reshape(2, 4, 2, 64, 896)]
    unnamed x268 -> x254, local copies, waits for them, and re-layouts: 37.8 us -> 35.9 us
  transfers between devices with their start and end apart: 56 -> 56, of which waited for: 26 -> 27; matrix products, arithmetic and copies ran while one was open for 22% -> 21% of each run, Pallas kernels for 8% -> 8%
where the time goes in v7:
time: 669 us; the launch traced here: 658 us
  waiting for transfers between devices  230 us (34%)
  starting transfers between devices  103 us (15%)
  local copies, waits for them, and re-layouts  90.7 us (14%)
  Pallas kernels  76.3 us (11%)
  other arithmetic  52.9 us (8%)
  matrix products  39.8 us (6%)
  blocking collectives  32.8 us (5%)
  between operations  31.8 us (5%)
    ppermute x8, waiting for transfers between devices, z_up(): return lax.ppermute(a, 'z', ring(1))  69.8 us
    ppermute x6, waiting for transfers between devices, x_up(): return lax.ppermute(a, 'x', ring(1))  57.9 us
    pallas_call x15, Pallas kernels, call(): pl.pallas_call(kernel, out_shape=out_shape, grid_spec=pltpu.PrefetchScala...  42.4 us
    ppermute x8, waiting for transfers between devices, z_down(): return lax.ppermute(a, 'z', ring(3))  39.9 us
    unnamed x254, local copies, waits for them, and re-layouts  35.9 us
    all_to_all x7, starting transfers between devices, exchange(): return lax.all_to_all(blocks, axes, 0, 0, tiled=True)  35.7 us
    all_to_all x1, blocking collectives, exchange(): return lax.all_to_all(blocks, axes, 0, 0, tiled=True)  32.8 us
    all_to_all x7, waiting for transfers between devices, exchange(): return lax.all_to_all(blocks, axes, 0, 0, tiled=True)  31.8 us
  transfers between devices with their start and end apart: 56, of which 27 were waited for; matrix products, arithmetic and copies ran while one was open for 21% of the time, Pallas kernels for 8%

profile of v7, /device:TPU:1, one launch (start us, length us, event | category | flops | bytes accessed | tf_op | source)
XLA Modules:
  0.0 657.8 jit_solution(17227702123131809325)
XLA Ops:
  17.5 32.8 %all_to_all.40 = bf16[8,136,896]{2,1,0:T(8,128)(2,1)S(1)} all-to-all(bf16[8,136,896]{2,1,0:T(8,128)(2,1)S(1)} %broadcast_in_dim.97), channel_id=1, replica_groups=mesh['ylo'=2,'z'=4,'core'=2,'x'=4,'yhi'=2] {'x','yhi'}, dimensions={0} | all-to-all | bytes 3899392 | tf_op jit(solution)/shard_map/all_to_all | solution.py:56
  62.0 31.4 %collective-permute-done.last_ref = bf16[1024,896]{1,0:T(8,128)(2,1)} collective-permute-done((bf16[1024,896]{1,0:T(8,128)(2,1)S(1)}, bf16[1024,896]{1,0:T(8,128)(2,1)}, u32[]{:S(2)}, u32[]{:S(2)}) %collective-permute-start) | collective-permute-done | bytes 1835040 | tf_op jit(solution)/shard_map/ppermute | solution.py:28
  98.6 4.3 all-to-all-start.1
  120.1 4.2 collective-permute-start.7
  131.5 2.9 broadcast_select_fusion.own_ref
  138.0 34.3 %collective-permute-done.10 = bf16[640,1024]{1,0:T(8,128)(2,1)} collective-permute-done((bf16[640,1024]{1,0:T(8,128)(2,1)}, bf16[640,1024]{1,0:T(8,128)(2,1)}, u32[]{:S(2)}, u32[]{:S(2)}) %collective-permute-start.10) | collective-permute-done | bytes 1310752 | tf_op jit(solution)/shard_map/ppermute | solution.py:36
  182.8 7.4 %collective-permute-done.11 = bf16[320,1024]{1,0:T(8,128)(2,1)S(1)} collective-permute-done((bf16[320,1024]{1,0:T(8,128)(2,1)}, bf16[320,1024]{1,0:T(8,128)(2,1)S(1)}, u32[]{:S(2)}, u32[]{:S(2)}) %collective-permute-start.11) | collective-permute-done | bytes 655392 | tf_op jit(solution)/shard_map/ppermute | solution.py:36
  191.1 6.1 collective-permute-done.12
  207.2 5.9 shard_map.170
  216.6 7.0 %shard_map.171 = bf16[256,512]{1,0:T(8,128)(2,1)S(1)} custom-call(f32[8]{0:T(128)S(1)} %fusion.85.slope_ref, s32[2,128,1]{2,1,0:T(8,128)S(1)} %copy.62.rows_ref, s32[2,1,128]{2,1,0:T(1,128)S(1)} %bitcast.219, bf16[256,1536]{1,0:T(8,128)(2,1)S(1)} %fusion.4.qkv_ref), custom_call_target="tpu_custom_call" | custom-call | flops 67108864 | bytes 1048576 | tf_op jit(solution)/shard_map/pallas_call | solution.py:384
  227.7 7.3 %collective-permute-start.13 = (f32[128,1024]{1,0:T(8,128)S(1)}, f32[128,1024]{1,0:T(8,128)S(1)}, u32[]{:S(2)}, u32[]{:S(2)}) collective-permute-start(f32[128,1024]{1,0:T(8,128)S(1)} %fusion.51), channel_id=1, source_target_pairs={{0,8},{8,0},{1,9},{9,1},{2,10},{10,2},{3,11},{11,3},{4,12},{12,4},... | collective-permute-start | bytes 1572872 | tf_op jit(solution)/shard_map/ppermute | solution.py:48
  239.5 3.1 multiply_convert_fusion.1
  254.2 15.0 %collective-permute-done.17.top_ref = bf16[512,896]{1,0:T(8,128)(2,1)S(1)} collective-permute-done((bf16[512,896]{1,0:T(8,128)(2,1)}, bf16[512,896]{1,0:T(8,128)(2,1)S(1)}, u32[]{:S(2)}, u32[]{:S(2)}) %collective-permute-start.17) | collective-permute-done | bytes 917536 | tf_op jit(solution)/shard_map/ppermute | solution.py:28
  270.4 5.7 shard_map.173
  279.2 7.0 %shard_map.174.ctx_ref = bf16[256,512]{1,0:T(8,128)(2,1)S(1)} custom-call(f32[8]{0:T(128)S(1)} %fusion.85.slope_ref, s32[2,128,1]{2,1,0:T(8,128)S(1)} %copy.62.rows_ref, s32[2,1,128]{2,1,0:T(1,128)S(1)} %bitcast.220, bf16[256,1536]{1,0:T(8,128)(2,1)S(1)} %fusion.5.qkv_ref), custom_call_target="tpu_custom_call" | custom-call | flops 67108864 | bytes 1048576 | tf_op jit(solution)/shard_map/pallas_call | solution.py:384
  297.4 3.0 fusion.93
  309.2 9.4 %shard_map.176 = (bf16[256,1536]{1,0:T(8,128)(2,1)S(1)}, f32[2,2,1,256]{3,2,1,0:T(1,128)S(1)}, f32[2,2,1,256]{3,2,1,0:T(1,128)S(1)}) custom-call(f32[8]{0:T(128)S(1)} %fusion.85.slope_ref, s32[2,128,1]{2,1,0:T(8,128)S(1)} %copy.62.rows_ref, s32[2,1,128]{2,1,0:T(1,128)S(1)} %bitcast.221, bf16[256,1536]{1,0:T(8,128)(2,1)S(1)} %fusion.5.qkv_ref, ...), custom_call_target="tpu_custom_call" | custom-call | flops 167772160 | bytes 2097152 | tf_op jit(solution)/shard_map/pallas_call | solution.py:403
  329.4 3.5 collective-permute-start.30
  333.0 3.2 shard_map.180
  343.6 11.1 %collective-permute-done.32 = bf16[320,1024]{1,0:T(8,128)(2,1)S(1)} collective-permute-done((bf16[320,1024]{1,0:T(8,128)(2,1)S(1)}, bf16[320,1024]{1,0:T(8,128)(2,1)S(1)}, u32[]{:S(2)}, u32[]{:S(2)}) %collective-permute-start.32) | collective-permute-done | bytes 655392 | tf_op jit(solution)/shard_map/ppermute | solution.py:36
  360.1 2.9 fusion.94
  378.3 3.2 shard_map.181
  383.8 3.5 collective-permute-done.45
  391.7 4.4 all-to-all-start.5
  396.1 3.1 slice_bitcast_fusion.6
  406.1 9.3 %shard_map.182 = (bf16[256,1536]{1,0:T(8,128)(2,1)S(1)}, f32[2,2,1,256]{3,2,1,0:T(1,128)S(1)}, f32[2,2,1,256]{3,2,1,0:T(1,128)S(1)}) custom-call(f32[8]{0:T(128)S(1)} %fusion.85.slope_ref, s32[2,128,1]{2,1,0:T(8,128)S(1)} %copy.62.rows_ref, s32[2,1,128]{2,1,0:T(1,128)S(1)} %bitcast.222, bf16[256,1536]{1,0:T(8,128)(2,1)S(1)} %copy-done.38, ...), custom_call_target="tpu_custom_call" | custom-call | flops 167772160 | bytes 2097152 | tf_op jit(solution)/shard_map/pallas_call | solution.py:403
  419.7 3.8 collective-permute-done.29
  425.4 4.3 collective-permute-done.31
  431.6 4.1 fusion.16
  435.6 4.9 all-to-all-start.4
  445.4 3.6 collective-permute-start.38
  450.6 17.2 %collective-permute-done.37 = bf16[512,896]{1,0:T(8,128)(2,1)} collective-permute-done((bf16[512,896]{1,0:T(8,128)(2,1)}, bf16[512,896]{1,0:T(8,128)(2,1)}, u32[]{:S(2)}, u32[]{:S(2)}) %collective-permute-start.37) | collective-permute-done | bytes 917536 | tf_op jit(solution)/shard_map/ppermute | solution.py:28
  492.5 12.8 %collective-permute-done.43 = bf16[640,1024]{1,0:T(8,128)(2,1)S(1)} collective-permute-done((bf16[640,1024]{1,0:T(8,128)(2,1)S(1)}, bf16[640,1024]{1,0:T(8,128)(2,1)S(1)}, u32[]{:S(2)}, u32[]{:S(2)}) %collective-permute-start.43) | collective-permute-done | bytes 1310752 | tf_op jit(solution)/shard_map/ppermute | solution.py:40
  505.2 3.1 collective-permute-done.42
  510.7 4.7 all-to-all-start.3
  517.6 34.3 %collective-permute-done.41 = bf16[1024,896]{1,0:T(8,128)(2,1)} collective-permute-done((bf16[1024,896]{1,0:T(8,128)(2,1)}, bf16[1024,896]{1,0:T(8,128)(2,1)}, u32[]{:S(2)}, u32[]{:S(2)}) %collective-permute-start.41) | collective-permute-done | bytes 1835040 | tf_op jit(solution)/shard_map/ppermute | solution.py:32
  551.9 3.9 add_convert_fusion.1
  555.8 6.4 all-to-all-start.2
  564.0 20.0 %all-to-all-done.2 = bf16[16,64,896]{2,1,0:T(8,128)(2,1)S(1)} async-done(((bf16[16,64,896]{2,1,0:T(8,128)(2,1)}), bf16[16,64,896]{2,1,0:T(8,128)(2,1)S(1)}, u32[]{:S(2)}, u32[]{:S(2)}) %all-to-all-start.2) | async-done | bytes 1835040 | tf_op jit(solution)/shard_map/all_to_all | solution.py:56
  585.0 2.9 fusion.36
  587.9 5.7 collective-permute-start.21
  595.9 4.3 fusion.28
  610.5 3.3 multiply_reduce_fusion.3
  614.8 3.4 all-to-all-start.6
  618.2 6.7 %all-to-all-done.6 = f32[8,24,128]{2,1,0:T(8,128)S(1)} async-done(((f32[8,24,128]{2,1,0:T(8,128)}), f32[8,24,128]{2,1,0:T(8,128)S(1)}, u32[]{:S(2)}, u32[]{:S(2)}) %all-to-all-start.6) | async-done | bytes 98336 | tf_op jit(solution)/shard_map/all_to_all | solution.py:56
  625.5 7.6 %all-to-all-start.7 = ((f32[16,24,128]{2,1,0:T(8,128)}), f32[16,24,128]{2,1,0:T(8,128)S(1)}, u32[]{:S(2)}, u32[]{:S(2)}) async-start(f32[16,24,128]{2,1,0:T(8,128)} %broadcast_in_dim.115), calls=%async_computation.7 | async-start | bytes 393216 | tf_op jit(solution)/shard_map/all_to_all | solution.py:56
  635.5 4.3 all-to-all-done.7
  645.4 5.4 shard_map.188
  (590 shorter events, 228.4 us)
Async XLA Ops:
  51.5 41.9 %collective-permute-start = (bf16[1024,896]{1,0:T(8,128)(2,1)S(1)}, bf16[1024,896]{1,0:T(8,128)(2,1)}, u32[]{:S(2)}, u32[]{:S(2)}) collective-permute-start(bf16[1024,896]{1,0:T(8,128)(2,1)S(1)} %bitcast.213), channel_id=1, source_target_pairs={{0,16},{16,32},{32,48},{48,0},{1,17},{17,33},{33,49},{49,1},{2,18}... | collective-permute-start | bytes 5505032 | tf_op jit(solution)/shard_map/ppermute | solution.py:28
  53.2 42.1 %collective-permute-start.2 = (bf16[1024,896]{1,0:T(8,128)(2,1)S(1)}, bf16[1024,896]{1,0:T(8,128)(2,1)}, u32[]{:S(2)}, u32[]{:S(2)}) collective-permute-start(bf16[1024,896]{1,0:T(8,128)(2,1)S(1)} %bitcast.214), channel_id=1, source_target_pairs={{0,48},{16,0},{32,16},{48,32},{1,49},{17,1},{33,17},{49,33},{2,50}... | collective-permute-start | bytes 5505032 | tf_op jit(solution)/shard_map/ppermute | solution.py:32
  55.3 62.1 %collective-permute-start.6 = (s32[1,128]{1,0:T(1,128)S(1)}, s32[1,128]{1,0:T(1,128)S(1)}, u32[]{:S(2)}, u32[]{:S(2)}) collective-permute-start(s32[1,128]{1,0:T(1,128)S(1)} %bitcast.293), channel_id=1, source_target_pairs={{0,8},{8,0},{1,9},{9,1},{2,10},{10,2},{3,11},{11,3},{4,12},{12,4},... | collective-permute-start | bytes 1544 | tf_op jit(solution)/shard_map/ppermute | solution.py:48
  61.4 49.9 %collective-permute-start.8 = (bf16[320,1024]{1,0:T(8,128)(2,1)}, bf16[320,1024]{1,0:T(8,128)(2,1)}, u32[]{:S(2)}, u32[]{:S(2)}) collective-permute-start(bf16[320,1024]{1,0:T(8,128)(2,1)} %get-tuple-element.145), channel_id=1, source_target_pairs={{0,65},{65,0},{1,64},{64,1},{2,67},{67,2},{3,66},{66,3},{4,69},{69... | collective-permute-start | bytes 1966088 | tf_op jit(solution)/shard_map/ppermute | solution.py:44
  98.6 32.9 %all-to-all-start.1 = ((bf16[8,128,896]{2,1,0:T(8,128)(2,1)}), bf16[8,128,896]{2,1,0:T(8,128)(2,1)}, u32[]{:S(2)}, u32[]{:S(2)}) async-start(bf16[8,128,896]{2,1,0:T(8,128)(2,1)} %broadcast_in_dim.100), calls=%async_computation.1 | async-start | bytes 3670016 | tf_op jit(solution)/shard_map/all_to_all | solution.py:56
  103.0 183.3 %all-gather.6.cloned.1.call-start = ((), (), s32[]{:S(2)}) async-start(), calls=%async_computation.8 | async-start | bytes 5898240 | tf_op jit(solution)/shard_map/all_gather | solution.py:498
  106.5 20.4 %collective-permute-start.1 = (bf16[512,896]{1,0:T(8,128)(2,1)}, bf16[512,896]{1,0:T(8,128)(2,1)}, u32[]{:S(2)}, u32[]{:S(2)}) collective-permute-start(bf16[512,896]{1,0:T(8,128)(2,1)} %slice.548), channel_id=1, source_target_pairs={{0,16},{16,32},{32,48},{48,0},{1,17},{17,33},{33,49},{49,1},{2,18}... | collective-permute-start | bytes 2752520 | tf_op jit(solution)/shard_map/ppermute | solution.py:28
  108.7 20.1 %collective-permute-start.3 = (bf16[512,896]{1,0:T(8,128)(2,1)}, bf16[512,896]{1,0:T(8,128)(2,1)}, u32[]{:S(2)}, u32[]{:S(2)}) collective-permute-start(bf16[512,896]{1,0:T(8,128)(2,1)} %slice.550), channel_id=1, source_target_pairs={{0,48},{16,0},{32,16},{48,32},{1,49},{17,1},{33,17},{49,33},{2,50}... | collective-permute-start | bytes 2752520 | tf_op jit(solution)/shard_map/ppermute | solution.py:32
  114.5 57.7 %collective-permute-start.10 = (bf16[640,1024]{1,0:T(8,128)(2,1)}, bf16[640,1024]{1,0:T(8,128)(2,1)}, u32[]{:S(2)}, u32[]{:S(2)}) collective-permute-start(bf16[640,1024]{1,0:T(8,128)(2,1)} %get-tuple-element.121), channel_id=1, source_target_pairs={{0,2},{2,4},{4,6},{6,0},{1,3},{3,5},{5,7},{7,1},{8,10},{10,12},{12... | collective-permute-start | bytes 3932168 | tf_op jit(solution)/shard_map/ppermute | solution.py:36
  116.0 58.3 %collective-permute-start.9 = (bf16[640,1024]{1,0:T(8,128)(2,1)}, bf16[640,1024]{1,0:T(8,128)(2,1)}, u32[]{:S(2)}, u32[]{:S(2)}) collective-permute-start(bf16[640,1024]{1,0:T(8,128)(2,1)} %get-tuple-element.121), channel_id=1, source_target_pairs={{0,6},{2,0},{4,2},{6,4},{1,7},{3,1},{5,3},{7,5},{8,14},{10,8},{12,... | collective-permute-start | bytes 3932168 | tf_op jit(solution)/shard_map/ppermute | solution.py:40
  120.1 95.3 %collective-permute-start.7 = (bf16[128,1024]{1,0:T(8,128)(2,1)S(1)}, bf16[128,1024]{1,0:T(8,128)(2,1)S(1)}, u32[]{:S(2)}, u32[]{:S(2)}) collective-permute-start(bf16[128,1024]{1,0:T(8,128)(2,1)S(1)} %add_convert_fusion.9), channel_id=1, source_target_pairs={{0,8},{8,0},{1,9},{9,1},{2,10},{10,2},{3,11},{11,3},{4,12},{12,4},... | collective-permute-start | bytes 786440 | tf_op jit(solution)/shard_map/ppermute | solution.py:48
  134.4 89.3 %collective-permute-start.4 = (bf16[1024,896]{1,0:T(8,128)(2,1)}, bf16[1024,896]{1,0:T(8,128)(2,1)}, u32[]{:S(2)}, u32[]{:S(2)}) collective-permute-start(bf16[1024,896]{1,0:T(8,128)(2,1)} %broadcast_select_fusion.own_ref), channel_id=1, source_target_pairs={{0,16},{16,32},{32,48},{48,0},{1,17},{17,33},{33,49},{49,1},{2,18}... | collective-permute-start | bytes 5505032 | tf_op jit(solution)/shard_map/ppermute | solution.py:28
  134.4 91.0 %collective-permute-start.5 = (bf16[1024,896]{1,0:T(8,128)(2,1)}, bf16[1024,896]{1,0:T(8,128)(2,1)}, u32[]{:S(2)}, u32[]{:S(2)}) collective-permute-start(bf16[1024,896]{1,0:T(8,128)(2,1)} %broadcast_select_fusion.own_ref), channel_id=1, source_target_pairs={{0,48},{16,0},{32,16},{48,32},{1,49},{17,1},{33,17},{49,33},{2,50}... | collective-permute-start | bytes 5505032 | tf_op jit(solution)/shard_map/ppermute | solution.py:32
  174.3 15.9 %collective-permute-start.11 = (bf16[320,1024]{1,0:T(8,128)(2,1)}, bf16[320,1024]{1,0:T(8,128)(2,1)S(1)}, u32[]{:S(2)}, u32[]{:S(2)}) collective-permute-start(bf16[320,1024]{1,0:T(8,128)(2,1)} %slice.566), channel_id=1, source_target_pairs={{0,2},{2,4},{4,6},{6,0},{1,3},{3,5},{5,7},{7,1},{8,10},{10,12},{12... | collective-permute-start | bytes 1966088 | tf_op jit(solution)/shard_map/ppermute | solution.py:36
  176.3 21.0 %collective-permute-start.12 = (bf16[320,1024]{1,0:T(8,128)(2,1)}, bf16[320,1024]{1,0:T(8,128)(2,1)}, u32[]{:S(2)}, u32[]{:S(2)}) collective-permute-start(bf16[320,1024]{1,0:T(8,128)(2,1)} %slice.567), channel_id=1, source_target_pairs={{0,6},{2,0},{4,2},{6,4},{1,7},{3,1},{5,3},{7,5},{8,14},{10,8},{12,... | collective-permute-start | bytes 1966088 | tf_op jit(solution)/shard_map/ppermute | solution.py:40
  227.7 8.9 %collective-permute-start.13 = (f32[128,1024]{1,0:T(8,128)S(1)}, f32[128,1024]{1,0:T(8,128)S(1)}, u32[]{:S(2)}, u32[]{:S(2)}) collective-permute-start(f32[128,1024]{1,0:T(8,128)S(1)} %fusion.51), channel_id=1, source_target_pairs={{0,8},{8,0},{1,9},{9,1},{2,10},{10,2},{3,11},{11,3},{4,12},{12,4},... | collective-permute-start | bytes 1572872 | tf_op jit(solution)/shard_map/ppermute | solution.py:48
  243.3 7.5 %collective-permute-start.15 = (f32[128,1024]{1,0:T(8,128)S(1)}, f32[128,1024]{1,0:T(8,128)S(1)}, u32[]{:S(2)}, u32[]{:S(2)}) collective-permute-start(f32[128,1024]{1,0:T(8,128)S(1)} %fusion.39), channel_id=1, source_target_pairs={{0,8},{8,0},{1,9},{9,1},{2,10},{10,2},{3,11},{11,3},{4,12},{12,4},... | collective-permute-start | bytes 1572872 | tf_op jit(solution)/shard_map/ppermute | solution.py:48
  245.9 23.2 %collective-permute-start.17 = (bf16[512,896]{1,0:T(8,128)(2,1)}, bf16[512,896]{1,0:T(8,128)(2,1)S(1)}, u32[]{:S(2)}, u32[]{:S(2)}) collective-permute-start(bf16[512,896]{1,0:T(8,128)(2,1)} %slice.579), channel_id=1, source_target_pairs={{0,16},{16,32},{32,48},{48,0},{1,17},{17,33},{33,49},{49,1},{2,18}... | collective-permute-start | bytes 2752520 | tf_op jit(solution)/shard_map/ppermute | solution.py:28
  248.1 22.3 %collective-permute-start.18 = (bf16[512,896]{1,0:T(8,128)(2,1)}, bf16[512,896]{1,0:T(8,128)(2,1)S(1)}, u32[]{:S(2)}, u32[]{:S(2)}) collective-permute-start(bf16[512,896]{1,0:T(8,128)(2,1)} %slice.580), channel_id=1, source_target_pairs={{0,48},{16,0},{32,16},{48,32},{1,49},{17,1},{33,17},{49,33},{2,50}... | collective-permute-start | bytes 2752520 | tf_op jit(solution)/shard_map/ppermute | solution.py:32
  252.7 23.4 %collective-permute-start.16 = (bf16[128,1024]{1,0:T(8,128)(2,1)S(1)}, bf16[128,1024]{1,0:T(8,128)(2,1)S(1)}, u32[]{:S(2)}, u32[]{:S(2)}) collective-permute-start(bf16[128,1024]{1,0:T(8,128)(2,1)S(1)} %add_convert_fusion.7), channel_id=1, source_target_pairs={{0,8},{8,0},{1,9},{9,1},{2,10},{10,2},{3,11},{11,3},{4,12},{12,4},... | collective-permute-start | bytes 786440 | tf_op jit(solution)/shard_map/ppermute | solution.py:48
  327.4 12.7 %collective-permute-start.25 = (f32[128,1024]{1,0:T(8,128)S(1)}, f32[128,1024]{1,0:T(8,128)S(1)}, u32[]{:S(2)}, u32[]{:S(2)}) collective-permute-start(f32[128,1024]{1,0:T(8,128)S(1)} %fusion.45), channel_id=1, source_target_pairs={{0,8},{8,0},{1,9},{9,1},{2,10},{10,2},{3,11},{11,3},{4,12},{12,4},... | collective-permute-start | bytes 1572872 | tf_op jit(solution)/shard_map/ppermute | solution.py:48
  329.3 36.4 %collective-permute-start.28 = (bf16[512,896]{1,0:T(8,128)(2,1)S(1)}, bf16[512,896]{1,0:T(8,128)(2,1)S(1)}, u32[]{:S(2)}, u32[]{:S(2)}) collective-permute-start(bf16[512,896]{1,0:T(8,128)(2,1)S(1)} %get-tuple-element.143), channel_id=1, source_target_pairs={{0,16},{16,32},{32,48},{48,0},{1,17},{17,33},{33,49},{49,1},{2,18}... | collective-permute-start | bytes 2752520 | tf_op jit(solution)/shard_map/ppermute | solution.py:28
  329.4 37.4 %collective-permute-start.30 = (bf16[512,896]{1,0:T(8,128)(2,1)S(1)}, bf16[512,896]{1,0:T(8,128)(2,1)S(1)}, u32[]{:S(2)}, u32[]{:S(2)}) collective-permute-start(bf16[512,896]{1,0:T(8,128)(2,1)S(1)} %get-tuple-element.142), channel_id=1, source_target_pairs={{0,48},{16,0},{32,16},{48,32},{1,49},{17,1},{33,17},{49,33},{2,50}... | collective-permute-start | bytes 2752520 | tf_op jit(solution)/shard_map/ppermute | solution.py:32
  336.5 18.2 %collective-permute-start.32 = (bf16[320,1024]{1,0:T(8,128)(2,1)S(1)}, bf16[320,1024]{1,0:T(8,128)(2,1)S(1)}, u32[]{:S(2)}, u32[]{:S(2)}) collective-permute-start(bf16[320,1024]{1,0:T(8,128)(2,1)S(1)} %get-tuple-element.127), channel_id=1, source_target_pairs={{0,2},{2,4},{4,6},{6,0},{1,3},{3,5},{5,7},{7,1},{8,10},{10,12},{12... | collective-permute-start | bytes 1966088 | tf_op jit(solution)/shard_map/ppermute | solution.py:36
  338.1 17.8 %collective-permute-start.33 = (bf16[320,1024]{1,0:T(8,128)(2,1)S(1)}, bf16[320,1024]{1,0:T(8,128)(2,1)S(1)}, u32[]{:S(2)}, u32[]{:S(2)}) collective-permute-start(bf16[320,1024]{1,0:T(8,128)(2,1)S(1)} %get-tuple-element.126), channel_id=1, source_target_pairs={{0,6},{2,0},{4,2},{6,4},{1,7},{3,1},{5,3},{7,5},{8,14},{10,8},{12,... | collective-permute-start | bytes 1966088 | tf_op jit(solution)/shard_map/ppermute | solution.py:40
  342.8 16.6 %collective-permute-start.26 = (bf16[128,1024]{1,0:T(8,128)(2,1)S(1)}, bf16[128,1024]{1,0:T(8,128)(2,1)S(1)}, u32[]{:S(2)}, u32[]{:S(2)}) collective-permute-start(bf16[128,1024]{1,0:T(8,128)(2,1)S(1)} %convert_element_type.323), channel_id=1, source_target_pairs={{0,8},{8,0},{1,9},{9,1},{2,10},{10,2},{3,11},{11,3},{4,12},{12,4},... | collective-permute-start | bytes 786440 | tf_op jit(solution)/shard_map/ppermute | solution.py:48
  357.8 29.5 %collective-permute-start.45 = (bf16[640,1024]{1,0:T(8,128)(2,1)S(1)}, bf16[640,1024]{1,0:T(8,128)(2,1)S(1)}, u32[]{:S(2)}, u32[]{:S(2)}) collective-permute-start(bf16[640,1024]{1,0:T(8,128)(2,1)S(1)} %pad_maximum_fusion.7), channel_id=1, source_target_pairs={{0,6},{2,0},{4,2},{6,4},{1,7},{3,1},{5,3},{7,5},{8,14},{10,8},{12,... | collective-permute-start | bytes 3932168 | tf_op jit(solution)/shard_map/ppermute | solution.py:40
  359.2 30.1 %collective-permute-start.44 = (bf16[640,1024]{1,0:T(8,128)(2,1)S(1)}, bf16[640,1024]{1,0:T(8,128)(2,1)S(1)}, u32[]{:S(2)}, u32[]{:S(2)}) collective-permute-start(bf16[640,1024]{1,0:T(8,128)(2,1)S(1)} %pad_maximum_fusion.6), channel_id=1, source_target_pairs={{0,2},{2,4},{4,6},{6,0},{1,3},{3,5},{5,7},{7,1},{8,10},{10,12},{12... | collective-permute-start | bytes 3932168 | tf_op jit(solution)/shard_map/ppermute | solution.py:36
  369.7 53.8 %collective-permute-start.29 = (bf16[1024,896]{1,0:T(8,128)(2,1)}, bf16[1024,896]{1,0:T(8,128)(2,1)}, u32[]{:S(2)}, u32[]{:S(2)}) collective-permute-start(bf16[1024,896]{1,0:T(8,128)(2,1)} %pad_maximum_fusion), channel_id=1, source_target_pairs={{0,16},{16,32},{32,48},{48,0},{1,17},{17,33},{33,49},{49,1},{2,18}... | collective-permute-start | bytes 5505032 | tf_op jit(solution)/shard_map/ppermute | solution.py:28
  372.9 5.3 collective-permute-start.34
  375.3 54.4 %collective-permute-start.31 = (bf16[1024,896]{1,0:T(8,128)(2,1)}, bf16[1024,896]{1,0:T(8,128)(2,1)}, u32[]{:S(2)}, u32[]{:S(2)}) collective-permute-start(bf16[1024,896]{1,0:T(8,128)(2,1)} %pad_maximum_fusion.1), channel_id=1, source_target_pairs={{0,48},{16,0},{32,16},{48,32},{1,49},{17,1},{33,17},{49,33},{2,50}... | collective-permute-start | bytes 5505032 | tf_op jit(solution)/shard_map/ppermute | solution.py:32
  391.7 43.9 %all-to-all-start.5 = ((bf16[16,40,1024]{2,1,0:T(8,128)(2,1)}), bf16[16,40,1024]{2,1,0:T(8,128)(2,1)}, u32[]{:S(2)}, u32[]{:S(2)}) async-start(bf16[16,40,1024]{2,1,0:T(8,128)(2,1)} %bitcast.228), calls=%async_computation.5 | async-start | bytes 2621440 | tf_op jit(solution)/shard_map/all_to_all | solution.py:56
  399.2 17.6 %collective-permute-start.35 = (bf16[320,1024]{1,0:T(8,128)(2,1)S(1)}, bf16[320,1024]{1,0:T(8,128)(2,1)S(1)}, u32[]{:S(2)}, u32[]{:S(2)}) collective-permute-start(bf16[320,1024]{1,0:T(8,128)(2,1)S(1)} %get-tuple-element.133), channel_id=1, source_target_pairs={{0,2},{2,4},{4,6},{6,0},{1,3},{3,5},{5,7},{7,1},{8,10},{10,12},{12... | collective-permute-start | bytes 1966088 | tf_op jit(solution)/shard_map/ppermute | solution.py:36
  399.2 18.9 %collective-permute-start.36 = (bf16[320,1024]{1,0:T(8,128)(2,1)S(1)}, bf16[320,1024]{1,0:T(8,128)(2,1)S(1)}, u32[]{:S(2)}, u32[]{:S(2)}) collective-permute-start(bf16[320,1024]{1,0:T(8,128)(2,1)S(1)} %get-tuple-element.132), channel_id=1, source_target_pairs={{0,6},{2,0},{4,2},{6,4},{1,7},{3,1},{5,3},{7,5},{8,14},{10,8},{12,... | collective-permute-start | bytes 1966088 | tf_op jit(solution)/shard_map/ppermute | solution.py:40
  435.6 35.9 %all-to-all-start.4 = ((bf16[16,64,896]{2,1,0:T(8,128)(2,1)}), bf16[16,64,896]{2,1,0:T(8,128)(2,1)}, u32[]{:S(2)}, u32[]{:S(2)}) async-start(bf16[16,64,896]{2,1,0:T(8,128)(2,1)} %bitcast.223), calls=%async_computation.4 | async-start | bytes 3670016 | tf_op jit(solution)/shard_map/all_to_all | solution.py:56
  440.6 201.0 %all-gather.10.cloned.1.call-start = ((), (), s32[]{:S(2)}) async-start(), calls=%async_computation.10 | async-start | bytes 3342336 | tf_op jit(solution)/shard_map/all_gather | solution.py:572
  445.4 22.4 %collective-permute-start.37 = (bf16[512,896]{1,0:T(8,128)(2,1)}, bf16[512,896]{1,0:T(8,128)(2,1)}, u32[]{:S(2)}, u32[]{:S(2)}) collective-permute-start(bf16[512,896]{1,0:T(8,128)(2,1)} %get-tuple-element.141), channel_id=1, source_target_pairs={{0,16},{16,32},{32,48},{48,0},{1,17},{17,33},{33,49},{49,1},{2,18}... | collective-permute-start | bytes 2752520 | tf_op jit(solution)/shard_map/ppermute | solution.py:28
  445.4 24.3 %collective-permute-start.38 = (bf16[512,896]{1,0:T(8,128)(2,1)}, bf16[512,896]{1,0:T(8,128)(2,1)}, u32[]{:S(2)}, u32[]{:S(2)}) collective-permute-start(bf16[512,896]{1,0:T(8,128)(2,1)} %get-tuple-element.140), channel_id=1, source_target_pairs={{0,48},{16,0},{32,16},{48,32},{1,49},{17,1},{33,17},{49,33},{2,50}... | collective-permute-start | bytes 2752520 | tf_op jit(solution)/shard_map/ppermute | solution.py:32
  477.6 27.7 %collective-permute-start.43 = (bf16[640,1024]{1,0:T(8,128)(2,1)S(1)}, bf16[640,1024]{1,0:T(8,128)(2,1)S(1)}, u32[]{:S(2)}, u32[]{:S(2)}) collective-permute-start(bf16[640,1024]{1,0:T(8,128)(2,1)S(1)} %pad_maximum_fusion.5), channel_id=1, source_target_pairs={{0,6},{2,0},{4,2},{6,4},{1,7},{3,1},{5,3},{7,5},{8,14},{10,8},{12,... | collective-permute-start | bytes 3932168 | tf_op jit(solution)/shard_map/ppermute | solution.py:40
  480.0 28.3 %collective-permute-start.42 = (bf16[640,1024]{1,0:T(8,128)(2,1)S(1)}, bf16[640,1024]{1,0:T(8,128)(2,1)S(1)}, u32[]{:S(2)}, u32[]{:S(2)}) collective-permute-start(bf16[640,1024]{1,0:T(8,128)(2,1)S(1)} %pad_maximum_fusion.4), channel_id=1, source_target_pairs={{0,2},{2,4},{4,6},{6,0},{1,3},{3,5},{5,7},{7,1},{8,10},{10,12},{12... | collective-permute-start | bytes 3932168 | tf_op jit(solution)/shard_map/ppermute | solution.py:36
  487.9 64.0 %collective-permute-start.41 = (bf16[1024,896]{1,0:T(8,128)(2,1)}, bf16[1024,896]{1,0:T(8,128)(2,1)}, u32[]{:S(2)}, u32[]{:S(2)}) collective-permute-start(bf16[1024,896]{1,0:T(8,128)(2,1)} %pad_maximum_fusion.3), channel_id=1, source_target_pairs={{0,48},{16,0},{32,16},{48,32},{1,49},{17,1},{33,17},{49,33},{2,50}... | collective-permute-start | bytes 5505032 | tf_op jit(solution)/shard_map/ppermute | solution.py:32
  492.2 59.7 %collective-permute-start.40 = (bf16[1024,896]{1,0:T(8,128)(2,1)}, bf16[1024,896]{1,0:T(8,128)(2,1)}, u32[]{:S(2)}, u32[]{:S(2)}) collective-permute-start(bf16[1024,896]{1,0:T(8,128)(2,1)} %pad_maximum_fusion.2), channel_id=1, source_target_pairs={{0,16},{16,32},{32,48},{48,0},{1,17},{17,33},{33,49},{49,1},{2,18}... | collective-permute-start | bytes 5505032 | tf_op jit(solution)/shard_map/ppermute | solution.py:28
  510.7 45.2 %all-to-all-start.3 = ((bf16[16,40,1024]{2,1,0:T(8,128)(2,1)}), bf16[16,40,1024]{2,1,0:T(8,128)(2,1)}, u32[]{:S(2)}, u32[]{:S(2)}) async-start(bf16[16,40,1024]{2,1,0:T(8,128)(2,1)} %bitcast.229), calls=%async_computation.3 | async-start | bytes 2621440 | tf_op jit(solution)/shard_map/all_to_all | solution.py:56
  555.8 28.1 %all-to-all-start.2 = ((bf16[16,64,896]{2,1,0:T(8,128)(2,1)}), bf16[16,64,896]{2,1,0:T(8,128)(2,1)S(1)}, u32[]{:S(2)}, u32[]{:S(2)}) async-start(bf16[16,64,896]{2,1,0:T(8,128)(2,1)} %bitcast.47), calls=%async_computation.2 | async-start | bytes 3670016 | tf_op jit(solution)/shard_map/all_to_all | solution.py:56
  562.2 79.4 %all-gather.8.cloned.1.call-start = ((), (), s32[]{:S(2)}) async-start(), calls=%async_computation.9 | async-start | bytes 3342336 | tf_op jit(solution)/shard_map/all_gather | solution.py:572
  587.9 7.2 %collective-permute-start.21 = (f32[128,1024]{1,0:T(8,128)S(1)}, f32[128,1024]{1,0:T(8,128)S(1)}, u32[]{:S(2)}, u32[]{:S(2)}) collective-permute-start(f32[128,1024]{1,0:T(8,128)S(1)} %fusion.36), channel_id=1, source_target_pairs={{0,8},{8,0},{1,9},{9,1},{2,10},{10,2},{3,11},{11,3},{4,12},{12,4},... | collective-permute-start | bytes 1572872 | tf_op jit(solution)/shard_map/ppermute | solution.py:48
  614.8 10.0 %all-to-all-start.6 = ((f32[8,24,128]{2,1,0:T(8,128)}), f32[8,24,128]{2,1,0:T(8,128)S(1)}, u32[]{:S(2)}, u32[]{:S(2)}) async-start(f32[8,24,128]{2,1,0:T(8,128)} %copy.72), calls=%async_computation.6 | async-start | bytes 196608 | tf_op jit(solution)/shard_map/all_to_all | solution.py:56
  625.5 14.2 %all-to-all-start.7 = ((f32[16,24,128]{2,1,0:T(8,128)}), f32[16,24,128]{2,1,0:T(8,128)S(1)}, u32[]{:S(2)}, u32[]{:S(2)}) async-start(f32[16,24,128]{2,1,0:T(8,128)} %broadcast_in_dim.115), calls=%async_computation.7 | async-start | bytes 393216 | tf_op jit(solution)/shard_map/all_to_all | solution.py:56
  (129 other events, 837.0 us)
Sparse Core Ops, SparseCore 0:
  106.1 97.6 all-gather.5
  474.2 44.2 all-gather.9
  585.1 41.0 all-gather.7

commit v8 on v7

--- a/solution.py
+++ b/solution.py
@@ -495,6 +495,7 @@
     piece_x = jnp.concatenate([jnp.where(yhi == 0, mine_x[0], other), jnp.where(yhi == 0, other, mine_x[0])])
     own, following, (top, bottom), previous = ring_gather(after(piece_x, block_z), x_up, x_down)
     all_x = jnp.concatenate([own, following, top, bottom, previous]).reshape(8, 320, D)
+    first_ring_x = (previous, following)
     next_x = lax.all_gather(after(mine_x[1], block_z), SHARD, axis=0)
     for layer in range(LAYERS):
         own, following, (top, bottom), previous = ring_gather(block_z, z_up, z_down)
@@ -502,7 +503,7 @@
         wdown, wproj = split_x(at_x if layer == 0 else at, all_x)
         weights.append((wqkv, wproj, wup, wdown))
         if layer == 0:
-            next_z = to_all(after(mine_z[1], previous, following), SHARD, 8).reshape(D, 896)
+            next_z = to_all(after(mine_z[1], previous, following, *first_ring_x), SHARD, 8).reshape(D, 896)
             block_z, all_x = after(next_z, top, bottom), next_x
         else:
             second_ring = (previous, following)

time: 669 us -> 651 us (0.973)
  waiting for transfers between devices: 230 us -> 208 us
    ppermute x6, waiting for transfers between devices: 57.9 us -> 35.3 us  [x_up(): return lax.ppermute(a, 'x', ring(1))]
    ppermute x1, waiting for transfers between devices: 0.01 us -> 10.6 us  [y_pair(): return lax.ppermute(a, ('ylo', 'yhi'), [(0, 3), (3, 0), (1, 2), (2, 1)])]
    ppermute x17, starting transfers between devices: 27.6 us -> 20.1 us  [swap(): return lax.ppermute(a, 'core', [(0, 1), (1, 0)])]
    unnamed x254 -> x266, local copies, waits for them, and re-layouts: 35.9 us -> 37.2 us
    slice x23 -> x25, local copies, waits for them, and re-layouts: 21.3 us -> 22 us  [after(): e[0, 0].astype(f32)]
  transfers between devices with their start and end apart: 56 -> 56, of which waited for: 27 -> 26; matrix products, arithmetic and copies ran while one was open for 21% -> 22% of each run, Pallas kernels for 8% -> 8%
where the time goes in v8:
time: 651 us; the launch traced here: 639 us
  waiting for transfers between devices  208 us (32%)
  starting transfers between devices  102 us (16%)
  local copies, waits for them, and re-layouts  93.8 us (14%)
  Pallas kernels  76.1 us (12%)
  other arithmetic  53.1 us (8%)
  matrix products  39.9 us (6%)
  between operations  33.2 us (5%)
  blocking collectives  32.8 us (5%)
    ppermute x8, waiting for transfers between devices, z_up(): return lax.ppermute(a, 'z', ring(1))  67.1 us
    pallas_call x15, Pallas kernels, call(): pl.pallas_call(kernel, out_shape=out_shape, grid_spec=pltpu.PrefetchScala...  42.2 us
    all_to_all x7, starting transfers between devices, exchange(): return lax.all_to_all(blocks, axes, 0, 0, tiled=True)  40.9 us
    ppermute x8, waiting for transfers between devices, z_down(): return lax.ppermute(a, 'z', ring(3))  40 us
    unnamed x266, local copies, waits for them, and re-layouts  37.2 us
    ppermute x6, waiting for transfers between devices, x_up(): return lax.ppermute(a, 'x', ring(1))  35.3 us
    all_to_all x1, blocking collectives, exchange(): return lax.all_to_all(blocks, axes, 0, 0, tiled=True)  32.8 us
    all_to_all x7, waiting for transfers between devices, exchange(): return lax.all_to_all(blocks, axes, 0, 0, tiled=True)  31.2 us
  transfers between devices with their start and end apart: 56, of which 26 were waited for; matrix products, arithmetic and copies ran while one was open for 22% of the time, Pallas kernels for 8%

profile of v8, /device:TPU:1, one launch (start us, length us, event | category | flops | bytes accessed | tf_op | source)
XLA Modules:
  0.0 639.4 jit_solution(15846936769684871322)
XLA Ops:
  17.5 32.8 %all_to_all.40 = bf16[8,136,896]{2,1,0:T(8,128)(2,1)S(1)} all-to-all(bf16[8,136,896]{2,1,0:T(8,128)(2,1)S(1)} %broadcast_in_dim.97), channel_id=1, replica_groups=mesh['ylo'=2,'z'=4,'core'=2,'x'=4,'yhi'=2] {'x','yhi'}, dimensions={0} | all-to-all | bytes 3899392 | tf_op jit(solution)/shard_map/all_to_all | solution.py:56
  57.8 10.6 %collective-permute-done.4 = bf16[320,1024]{1,0:T(8,128)(2,1)} collective-permute-done((bf16[320,1024]{1,0:T(8,128)(2,1)}, bf16[320,1024]{1,0:T(8,128)(2,1)}, u32[]{:S(2)}, u32[]{:S(2)}) %collective-permute-start.4) | collective-permute-done | bytes 655392 | tf_op jit(solution)/shard_map/ppermute | solution.py:44
  73.8 22.4 %collective-permute-done.last_ref = bf16[1024,896]{1,0:T(8,128)(2,1)} collective-permute-done((bf16[1024,896]{1,0:T(8,128)(2,1)S(1)}, bf16[1024,896]{1,0:T(8,128)(2,1)}, u32[]{:S(2)}, u32[]{:S(2)}) %collective-permute-start) | collective-permute-done | bytes 1835040 | tf_op jit(solution)/shard_map/ppermute | solution.py:28
  104.8 4.4 all-to-all-start.1
  109.3 3.7 collective-permute-start.9
  130.0 10.0 %collective-permute-done.1.top_ref = bf16[512,896]{1,0:T(8,128)(2,1)S(1)} collective-permute-done((bf16[512,896]{1,0:T(8,128)(2,1)}, bf16[512,896]{1,0:T(8,128)(2,1)S(1)}, u32[]{:S(2)}, u32[]{:S(2)}) %collective-permute-start.1) | collective-permute-done | bytes 917536 | tf_op jit(solution)/shard_map/ppermute | solution.py:28
  143.1 2.9 broadcast_select_fusion.own_ref
  160.5 19.6 %collective-permute-done.11 = bf16[320,1024]{1,0:T(8,128)(2,1)} collective-permute-done((bf16[320,1024]{1,0:T(8,128)(2,1)}, bf16[320,1024]{1,0:T(8,128)(2,1)}, u32[]{:S(2)}, u32[]{:S(2)}) %collective-permute-start.11) | collective-permute-done | bytes 655392 | tf_op jit(solution)/shard_map/ppermute | solution.py:36
  185.3 2.7 copy-done.22
  191.0 5.7 shard_map.170
  201.3 7.0 %shard_map.171 = bf16[256,512]{1,0:T(8,128)(2,1)S(1)} custom-call(f32[8]{0:T(128)S(1)} %fusion.85.slope_ref, s32[2,128,1]{2,1,0:T(8,128)S(1)} %copy.62.rows_ref, s32[2,1,128]{2,1,0:T(1,128)S(1)} %bitcast.219, bf16[256,1536]{1,0:T(8,128)(2,1)S(1)} %fusion.4.qkv_ref), custom_call_target="tpu_custom_call" | custom-call | flops 67108864 | bytes 1048576 | tf_op jit(solution)/shard_map/pallas_call | solution.py:384
  218.5 3.1 multiply_convert_fusion.1
  233.2 15.0 %collective-permute-done.17.top_ref = bf16[512,896]{1,0:T(8,128)(2,1)S(1)} collective-permute-done((bf16[512,896]{1,0:T(8,128)(2,1)}, bf16[512,896]{1,0:T(8,128)(2,1)S(1)}, u32[]{:S(2)}, u32[]{:S(2)}) %collective-permute-start.17) | collective-permute-done | bytes 917536 | tf_op jit(solution)/shard_map/ppermute | solution.py:28
  249.4 5.7 shard_map.173
  258.3 7.0 %shard_map.174.ctx_ref = bf16[256,512]{1,0:T(8,128)(2,1)S(1)} custom-call(f32[8]{0:T(128)S(1)} %fusion.85.slope_ref, s32[2,128,1]{2,1,0:T(8,128)S(1)} %copy.62.rows_ref, s32[2,1,128]{2,1,0:T(1,128)S(1)} %bitcast.220, bf16[256,1536]{1,0:T(8,128)(2,1)S(1)} %fusion.5.qkv_ref), custom_call_target="tpu_custom_call" | custom-call | flops 67108864 | bytes 1048576 | tf_op jit(solution)/shard_map/pallas_call | solution.py:384
  276.5 3.0 fusion.93
  288.3 9.4 %shard_map.176 = (bf16[256,1536]{1,0:T(8,128)(2,1)S(1)}, f32[2,2,1,256]{3,2,1,0:T(1,128)S(1)}, f32[2,2,1,256]{3,2,1,0:T(1,128)S(1)}) custom-call(f32[8]{0:T(128)S(1)} %fusion.85.slope_ref, s32[2,128,1]{2,1,0:T(8,128)S(1)} %copy.62.rows_ref, s32[2,1,128]{2,1,0:T(1,128)S(1)} %bitcast.221, bf16[256,1536]{1,0:T(8,128)(2,1)S(1)} %fusion.5.qkv_ref, ...), custom_call_target="tpu_custom_call" | custom-call | flops 167772160 | bytes 2097152 | tf_op jit(solution)/shard_map/pallas_call | solution.py:403
  308.7 3.4 collective-permute-start.30
  312.2 3.2 shard_map.180
  322.2 10.6 %collective-permute-done.32 = bf16[320,1024]{1,0:T(8,128)(2,1)S(1)} collective-permute-done((bf16[320,1024]{1,0:T(8,128)(2,1)S(1)}, bf16[320,1024]{1,0:T(8,128)(2,1)S(1)}, u32[]{:S(2)}, u32[]{:S(2)}) %collective-permute-start.32) | collective-permute-done | bytes 655392 | tf_op jit(solution)/shard_map/ppermute | solution.py:36
  338.2 3.0 fusion.94
  353.7 2.9 collective-permute-start.31
  356.6 3.2 shard_map.181
  362.2 2.9 collective-permute-done.45
  369.4 6.4 %all-to-all-start.5 = ((bf16[16,40,1024]{2,1,0:T(8,128)(2,1)}), bf16[16,40,1024]{2,1,0:T(8,128)(2,1)}, u32[]{:S(2)}, u32[]{:S(2)}) async-start(bf16[16,40,1024]{2,1,0:T(8,128)(2,1)} %bitcast.228), calls=%async_computation.5 | async-start | bytes 2621440 | tf_op jit(solution)/shard_map/all_to_all | solution.py:56
  375.9 3.1 slice_bitcast_fusion.6
  385.9 9.3 %shard_map.182 = (bf16[256,1536]{1,0:T(8,128)(2,1)S(1)}, f32[2,2,1,256]{3,2,1,0:T(1,128)S(1)}, f32[2,2,1,256]{3,2,1,0:T(1,128)S(1)}) custom-call(f32[8]{0:T(128)S(1)} %fusion.85.slope_ref, s32[2,128,1]{2,1,0:T(8,128)S(1)} %copy.62.rows_ref, s32[2,1,128]{2,1,0:T(1,128)S(1)} %bitcast.222, bf16[256,1536]{1,0:T(8,128)(2,1)S(1)} %copy-done.38, ...), custom_call_target="tpu_custom_call" | custom-call | flops 167772160 | bytes 2097152 | tf_op jit(solution)/shard_map/pallas_call | solution.py:403
  403.7 4.3 collective-permute-done.31
  409.9 4.1 fusion.16
  414.0 8.3 %all-to-all-start.4 = ((bf16[16,64,896]{2,1,0:T(8,128)(2,1)}), bf16[16,64,896]{2,1,0:T(8,128)(2,1)}, u32[]{:S(2)}, u32[]{:S(2)}) async-start(bf16[16,64,896]{2,1,0:T(8,128)(2,1)} %bitcast.223), calls=%async_computation.4 | async-start | bytes 3670016 | tf_op jit(solution)/shard_map/all_to_all | solution.py:56
  427.1 3.6 collective-permute-start.38
  432.3 17.3 %collective-permute-done.37 = bf16[512,896]{1,0:T(8,128)(2,1)} collective-permute-done((bf16[512,896]{1,0:T(8,128)(2,1)}, bf16[512,896]{1,0:T(8,128)(2,1)}, u32[]{:S(2)}, u32[]{:S(2)}) %collective-permute-start.37) | collective-permute-done | bytes 917536 | tf_op jit(solution)/shard_map/ppermute | solution.py:28
  474.2 12.8 %collective-permute-done.43 = bf16[640,1024]{1,0:T(8,128)(2,1)S(1)} collective-permute-done((bf16[640,1024]{1,0:T(8,128)(2,1)S(1)}, bf16[640,1024]{1,0:T(8,128)(2,1)S(1)}, u32[]{:S(2)}, u32[]{:S(2)}) %collective-permute-start.43) | collective-permute-done | bytes 1310752 | tf_op jit(solution)/shard_map/ppermute | solution.py:40
  487.0 3.1 collective-permute-done.42
  492.4 4.7 all-to-all-start.3
  499.3 34.3 %collective-permute-done.41 = bf16[1024,896]{1,0:T(8,128)(2,1)} collective-permute-done((bf16[1024,896]{1,0:T(8,128)(2,1)}, bf16[1024,896]{1,0:T(8,128)(2,1)}, u32[]{:S(2)}, u32[]{:S(2)}) %collective-permute-start.41) | collective-permute-done | bytes 1835040 | tf_op jit(solution)/shard_map/ppermute | solution.py:32
  533.6 3.9 add_convert_fusion.1
  537.6 6.4 %all-to-all-start.2 = ((bf16[16,64,896]{2,1,0:T(8,128)(2,1)}), bf16[16,64,896]{2,1,0:T(8,128)(2,1)S(1)}, u32[]{:S(2)}, u32[]{:S(2)}) async-start(bf16[16,64,896]{2,1,0:T(8,128)(2,1)} %bitcast.47), calls=%async_computation.2 | async-start | bytes 3670016 | tf_op jit(solution)/shard_map/all_to_all | solution.py:56
  545.7 20.2 %all-to-all-done.2 = bf16[16,64,896]{2,1,0:T(8,128)(2,1)S(1)} async-done(((bf16[16,64,896]{2,1,0:T(8,128)(2,1)}), bf16[16,64,896]{2,1,0:T(8,128)(2,1)S(1)}, u32[]{:S(2)}, u32[]{:S(2)}) %all-to-all-start.2) | async-done | bytes 1835040 | tf_op jit(solution)/shard_map/all_to_all | solution.py:56
  566.9 2.9 fusion.36
  569.8 5.6 collective-permute-start.21
  577.8 4.3 fusion.28
  592.4 3.3 multiply_reduce_fusion.3
  596.7 3.4 all-to-all-start.6
  600.1 6.7 %all-to-all-done.6 = f32[8,24,128]{2,1,0:T(8,128)S(1)} async-done(((f32[8,24,128]{2,1,0:T(8,128)}), f32[8,24,128]{2,1,0:T(8,128)S(1)}, u32[]{:S(2)}, u32[]{:S(2)}) %all-to-all-start.6) | async-done | bytes 98336 | tf_op jit(solution)/shard_map/all_to_all | solution.py:56
  607.5 7.2 %all-to-all-start.7 = ((f32[16,24,128]{2,1,0:T(8,128)}), f32[16,24,128]{2,1,0:T(8,128)S(1)}, u32[]{:S(2)}, u32[]{:S(2)}) async-start(f32[16,24,128]{2,1,0:T(8,128)} %broadcast_in_dim.115), calls=%async_computation.7 | async-start | bytes 393216 | tf_op jit(solution)/shard_map/all_to_all | solution.py:56
  617.1 4.3 all-to-all-done.7
  627.0 5.4 shard_map.188
  (604 shorter events, 227.0 us)
Async XLA Ops:
  53.1 15.4 %collective-permute-start.4 = (bf16[320,1024]{1,0:T(8,128)(2,1)}, bf16[320,1024]{1,0:T(8,128)(2,1)}, u32[]{:S(2)}, u32[]{:S(2)}) collective-permute-start(bf16[320,1024]{1,0:T(8,128)(2,1)} %get-tuple-element.145), channel_id=1, source_target_pairs={{0,65},{65,0},{1,64},{64,1},{2,67},{67,2},{3,66},{66,3},{4,69},{69... | collective-permute-start | bytes 1966088 | tf_op jit(solution)/shard_map/ppermute | solution.py:44
  54.1 42.0 %collective-permute-start = (bf16[1024,896]{1,0:T(8,128)(2,1)S(1)}, bf16[1024,896]{1,0:T(8,128)(2,1)}, u32[]{:S(2)}, u32[]{:S(2)}) collective-permute-start(bf16[1024,896]{1,0:T(8,128)(2,1)S(1)} %bitcast.214), channel_id=1, source_target_pairs={{0,16},{16,32},{32,48},{48,0},{1,17},{17,33},{33,49},{49,1},{2,18}... | collective-permute-start | bytes 5505032 | tf_op jit(solution)/shard_map/ppermute | solution.py:28
  55.7 42.2 %collective-permute-start.2 = (bf16[1024,896]{1,0:T(8,128)(2,1)S(1)}, bf16[1024,896]{1,0:T(8,128)(2,1)}, u32[]{:S(2)}, u32[]{:S(2)}) collective-permute-start(bf16[1024,896]{1,0:T(8,128)(2,1)S(1)} %bitcast.215), channel_id=1, source_target_pairs={{0,48},{16,0},{32,16},{48,32},{1,49},{17,1},{33,17},{49,33},{2,50}... | collective-permute-start | bytes 5505032 | tf_op jit(solution)/shard_map/ppermute | solution.py:32
  71.1 28.7 %collective-permute-start.5 = (bf16[640,1024]{1,0:T(8,128)(2,1)S(1)}, bf16[640,1024]{1,0:T(8,128)(2,1)S(1)}, u32[]{:S(2)}, u32[]{:S(2)}) collective-permute-start(bf16[640,1024]{1,0:T(8,128)(2,1)S(1)} %get-tuple-element.121), channel_id=1, source_target_pairs={{0,2},{2,4},{4,6},{6,0},{1,3},{3,5},{5,7},{7,1},{8,10},{10,12},{12... | collective-permute-start | bytes 3932168 | tf_op jit(solution)/shard_map/ppermute | solution.py:36
  71.4 29.6 %collective-permute-start.6 = (bf16[640,1024]{1,0:T(8,128)(2,1)S(1)}, bf16[640,1024]{1,0:T(8,128)(2,1)S(1)}, u32[]{:S(2)}, u32[]{:S(2)}) collective-permute-start(bf16[640,1024]{1,0:T(8,128)(2,1)S(1)} %get-tuple-element.121), channel_id=1, source_target_pairs={{0,6},{2,0},{4,2},{6,4},{1,7},{3,1},{5,3},{7,5},{8,14},{10,8},{12,... | collective-permute-start | bytes 3932168 | tf_op jit(solution)/shard_map/ppermute | solution.py:40
  104.8 38.3 %all-to-all-start.1 = ((bf16[8,128,896]{2,1,0:T(8,128)(2,1)}), bf16[8,128,896]{2,1,0:T(8,128)(2,1)}, u32[]{:S(2)}, u32[]{:S(2)}) async-start(bf16[8,128,896]{2,1,0:T(8,128)(2,1)} %broadcast_in_dim.101), calls=%async_computation.1 | async-start | bytes 3670016 | tf_op jit(solution)/shard_map/all_to_all | solution.py:56
  109.3 156.1 %all-gather.6.cloned.1.call-start = ((), (), s32[]{:S(2)}) async-start(), calls=%async_computation.8 | async-start | bytes 5898240 | tf_op jit(solution)/shard_map/all_gather | solution.py:499
  109.3 13.5 %collective-permute-start.9 = (s32[1,128]{1,0:T(1,128)S(1)}, s32[1,128]{1,0:T(1,128)S(1)}, u32[]{:S(2)}, u32[]{:S(2)}) collective-permute-start(s32[1,128]{1,0:T(1,128)S(1)} %bitcast.293), channel_id=1, source_target_pairs={{0,8},{8,0},{1,9},{9,1},{2,10},{10,2},{3,11},{11,3},{4,12},{12,4},... | collective-permute-start | bytes 1544 | tf_op jit(solution)/shard_map/ppermute | solution.py:48
  115.6 24.4 %collective-permute-start.1 = (bf16[512,896]{1,0:T(8,128)(2,1)}, bf16[512,896]{1,0:T(8,128)(2,1)S(1)}, u32[]{:S(2)}, u32[]{:S(2)}) collective-permute-start(bf16[512,896]{1,0:T(8,128)(2,1)} %slice.556), channel_id=1, source_target_pairs={{0,16},{16,32},{32,48},{48,0},{1,17},{17,33},{33,49},{49,1},{2,18}... | collective-permute-start | bytes 2752520 | tf_op jit(solution)/shard_map/ppermute | solution.py:28
  119.5 21.8 %collective-permute-start.3 = (bf16[512,896]{1,0:T(8,128)(2,1)}, bf16[512,896]{1,0:T(8,128)(2,1)}, u32[]{:S(2)}, u32[]{:S(2)}) collective-permute-start(bf16[512,896]{1,0:T(8,128)(2,1)} %slice.558), channel_id=1, source_target_pairs={{0,48},{16,0},{32,16},{48,32},{1,49},{17,1},{33,17},{49,33},{2,50}... | collective-permute-start | bytes 2752520 | tf_op jit(solution)/shard_map/ppermute | solution.py:32
  128.3 70.7 %collective-permute-start.10 = (bf16[128,1024]{1,0:T(8,128)(2,1)}, bf16[128,1024]{1,0:T(8,128)(2,1)}, u32[]{:S(2)}, u32[]{:S(2)}) collective-permute-start(bf16[128,1024]{1,0:T(8,128)(2,1)} %add_convert_fusion.9), channel_id=1, source_target_pairs={{0,8},{8,0},{1,9},{9,1},{2,10},{10,2},{3,11},{11,3},{4,12},{12,4},... | collective-permute-start | bytes 786440 | tf_op jit(solution)/shard_map/ppermute | solution.py:48
  146.1 62.3 %collective-permute-start.7 = (bf16[1024,896]{1,0:T(8,128)(2,1)}, bf16[1024,896]{1,0:T(8,128)(2,1)}, u32[]{:S(2)}, u32[]{:S(2)}) collective-permute-start(bf16[1024,896]{1,0:T(8,128)(2,1)} %broadcast_select_fusion.own_ref), channel_id=1, source_target_pairs={{0,16},{16,32},{32,48},{48,0},{1,17},{17,33},{33,49},{49,1},{2,18}... | collective-permute-start | bytes 5505032 | tf_op jit(solution)/shard_map/ppermute | solution.py:28
  147.4 62.8 %collective-permute-start.8 = (bf16[1024,896]{1,0:T(8,128)(2,1)}, bf16[1024,896]{1,0:T(8,128)(2,1)}, u32[]{:S(2)}, u32[]{:S(2)}) collective-permute-start(bf16[1024,896]{1,0:T(8,128)(2,1)} %broadcast_select_fusion.own_ref), channel_id=1, source_target_pairs={{0,48},{16,0},{32,16},{48,32},{1,49},{17,1},{33,17},{49,33},{2,50}... | collective-permute-start | bytes 5505032 | tf_op jit(solution)/shard_map/ppermute | solution.py:32
  152.4 27.8 %collective-permute-start.11 = (bf16[320,1024]{1,0:T(8,128)(2,1)}, bf16[320,1024]{1,0:T(8,128)(2,1)}, u32[]{:S(2)}, u32[]{:S(2)}) collective-permute-start(bf16[320,1024]{1,0:T(8,128)(2,1)} %slice.576), channel_id=1, source_target_pairs={{0,2},{2,4},{4,6},{6,0},{1,3},{3,5},{5,7},{7,1},{8,10},{10,12},{12... | collective-permute-start | bytes 1966088 | tf_op jit(solution)/shard_map/ppermute | solution.py:36
  156.1 26.1 %collective-permute-start.12 = (bf16[320,1024]{1,0:T(8,128)(2,1)}, bf16[320,1024]{1,0:T(8,128)(2,1)}, u32[]{:S(2)}, u32[]{:S(2)}) collective-permute-start(bf16[320,1024]{1,0:T(8,128)(2,1)} %slice.577), channel_id=1, source_target_pairs={{0,6},{2,0},{4,2},{6,4},{1,7},{3,1},{5,3},{7,5},{8,14},{10,8},{12,... | collective-permute-start | bytes 1966088 | tf_op jit(solution)/shard_map/ppermute | solution.py:40
  222.3 7.5 %collective-permute-start.15 = (f32[128,1024]{1,0:T(8,128)S(1)}, f32[128,1024]{1,0:T(8,128)S(1)}, u32[]{:S(2)}, u32[]{:S(2)}) collective-permute-start(f32[128,1024]{1,0:T(8,128)S(1)} %fusion.39), channel_id=1, source_target_pairs={{0,8},{8,0},{1,9},{9,1},{2,10},{10,2},{3,11},{11,3},{4,12},{12,4},... | collective-permute-start | bytes 1572872 | tf_op jit(solution)/shard_map/ppermute | solution.py:48
  224.9 23.2 %collective-permute-start.17 = (bf16[512,896]{1,0:T(8,128)(2,1)}, bf16[512,896]{1,0:T(8,128)(2,1)S(1)}, u32[]{:S(2)}, u32[]{:S(2)}) collective-permute-start(bf16[512,896]{1,0:T(8,128)(2,1)} %slice.589), channel_id=1, source_target_pairs={{0,16},{16,32},{32,48},{48,0},{1,17},{17,33},{33,49},{49,1},{2,18}... | collective-permute-start | bytes 2752520 | tf_op jit(solution)/shard_map/ppermute | solution.py:28
  227.2 22.3 %collective-permute-start.18 = (bf16[512,896]{1,0:T(8,128)(2,1)}, bf16[512,896]{1,0:T(8,128)(2,1)S(1)}, u32[]{:S(2)}, u32[]{:S(2)}) collective-permute-start(bf16[512,896]{1,0:T(8,128)(2,1)} %slice.590), channel_id=1, source_target_pairs={{0,48},{16,0},{32,16},{48,32},{1,49},{17,1},{33,17},{49,33},{2,50}... | collective-permute-start | bytes 2752520 | tf_op jit(solution)/shard_map/ppermute | solution.py:32
  231.7 23.5 %collective-permute-start.16 = (bf16[128,1024]{1,0:T(8,128)(2,1)S(1)}, bf16[128,1024]{1,0:T(8,128)(2,1)S(1)}, u32[]{:S(2)}, u32[]{:S(2)}) collective-permute-start(bf16[128,1024]{1,0:T(8,128)(2,1)S(1)} %add_convert_fusion.7), channel_id=1, source_target_pairs={{0,8},{8,0},{1,9},{9,1},{2,10},{10,2},{3,11},{11,3},{4,12},{12,4},... | collective-permute-start | bytes 786440 | tf_op jit(solution)/shard_map/ppermute | solution.py:48
  306.5 11.9 %collective-permute-start.25 = (f32[128,1024]{1,0:T(8,128)S(1)}, f32[128,1024]{1,0:T(8,128)S(1)}, u32[]{:S(2)}, u32[]{:S(2)}) collective-permute-start(f32[128,1024]{1,0:T(8,128)S(1)} %fusion.45), channel_id=1, source_target_pairs={{0,8},{8,0},{1,9},{9,1},{2,10},{10,2},{3,11},{11,3},{4,12},{12,4},... | collective-permute-start | bytes 1572872 | tf_op jit(solution)/shard_map/ppermute | solution.py:48
  308.5 35.6 %collective-permute-start.28 = (bf16[512,896]{1,0:T(8,128)(2,1)S(1)}, bf16[512,896]{1,0:T(8,128)(2,1)S(1)}, u32[]{:S(2)}, u32[]{:S(2)}) collective-permute-start(bf16[512,896]{1,0:T(8,128)(2,1)S(1)} %get-tuple-element.143), channel_id=1, source_target_pairs={{0,16},{16,32},{32,48},{48,0},{1,17},{17,33},{33,49},{49,1},{2,18}... | collective-permute-start | bytes 2752520 | tf_op jit(solution)/shard_map/ppermute | solution.py:28
  308.7 36.6 %collective-permute-start.30 = (bf16[512,896]{1,0:T(8,128)(2,1)S(1)}, bf16[512,896]{1,0:T(8,128)(2,1)S(1)}, u32[]{:S(2)}, u32[]{:S(2)}) collective-permute-start(bf16[512,896]{1,0:T(8,128)(2,1)S(1)} %get-tuple-element.142), channel_id=1, source_target_pairs={{0,48},{16,0},{32,16},{48,32},{1,49},{17,1},{33,17},{49,33},{2,50}... | collective-permute-start | bytes 2752520 | tf_op jit(solution)/shard_map/ppermute | solution.py:32
  315.7 17.2 %collective-permute-start.32 = (bf16[320,1024]{1,0:T(8,128)(2,1)S(1)}, bf16[320,1024]{1,0:T(8,128)(2,1)S(1)}, u32[]{:S(2)}, u32[]{:S(2)}) collective-permute-start(bf16[320,1024]{1,0:T(8,128)(2,1)S(1)} %get-tuple-element.127), channel_id=1, source_target_pairs={{0,2},{2,4},{4,6},{6,0},{1,3},{3,5},{5,7},{7,1},{8,10},{10,12},{12... | collective-permute-start | bytes 1966088 | tf_op jit(solution)/shard_map/ppermute | solution.py:36
  315.8 18.2 %collective-permute-start.33 = (bf16[320,1024]{1,0:T(8,128)(2,1)S(1)}, bf16[320,1024]{1,0:T(8,128)(2,1)S(1)}, u32[]{:S(2)}, u32[]{:S(2)}) collective-permute-start(bf16[320,1024]{1,0:T(8,128)(2,1)S(1)} %get-tuple-element.126), channel_id=1, source_target_pairs={{0,6},{2,0},{4,2},{6,4},{1,7},{3,1},{5,3},{7,5},{8,14},{10,8},{12,... | collective-permute-start | bytes 1966088 | tf_op jit(solution)/shard_map/ppermute | solution.py:40
  321.2 16.4 %collective-permute-start.26 = (bf16[128,1024]{1,0:T(8,128)(2,1)S(1)}, bf16[128,1024]{1,0:T(8,128)(2,1)S(1)}, u32[]{:S(2)}, u32[]{:S(2)}) collective-permute-start(bf16[128,1024]{1,0:T(8,128)(2,1)S(1)} %convert_element_type.333), channel_id=1, source_target_pairs={{0,8},{8,0},{1,9},{9,1},{2,10},{10,2},{3,11},{11,3},{4,12},{12,4},... | collective-permute-start | bytes 786440 | tf_op jit(solution)/shard_map/ppermute | solution.py:48
  335.9 29.2 %collective-permute-start.45 = (bf16[640,1024]{1,0:T(8,128)(2,1)S(1)}, bf16[640,1024]{1,0:T(8,128)(2,1)S(1)}, u32[]{:S(2)}, u32[]{:S(2)}) collective-permute-start(bf16[640,1024]{1,0:T(8,128)(2,1)S(1)} %pad_maximum_fusion.7), channel_id=1, source_target_pairs={{0,6},{2,0},{4,2},{6,4},{1,7},{3,1},{5,3},{7,5},{8,14},{10,8},{12,... | collective-permute-start | bytes 3932168 | tf_op jit(solution)/shard_map/ppermute | solution.py:40
  337.2 29.8 %collective-permute-start.44 = (bf16[640,1024]{1,0:T(8,128)(2,1)S(1)}, bf16[640,1024]{1,0:T(8,128)(2,1)S(1)}, u32[]{:S(2)}, u32[]{:S(2)}) collective-permute-start(bf16[640,1024]{1,0:T(8,128)(2,1)S(1)} %pad_maximum_fusion.6), channel_id=1, source_target_pairs={{0,2},{2,4},{4,6},{6,0},{1,3},{3,5},{5,7},{7,1},{8,10},{10,12},{12... | collective-permute-start | bytes 3932168 | tf_op jit(solution)/shard_map/ppermute | solution.py:36
  342.7 5.4 collective-permute-start.27
  348.1 53.8 %collective-permute-start.29 = (bf16[1024,896]{1,0:T(8,128)(2,1)}, bf16[1024,896]{1,0:T(8,128)(2,1)}, u32[]{:S(2)}, u32[]{:S(2)}) collective-permute-start(bf16[1024,896]{1,0:T(8,128)(2,1)} %pad_maximum_fusion), channel_id=1, source_target_pairs={{0,16},{16,32},{32,48},{48,0},{1,17},{17,33},{33,49},{49,1},{2,18}... | collective-permute-start | bytes 5505032 | tf_op jit(solution)/shard_map/ppermute | solution.py:28
  351.3 5.2 collective-permute-start.34
  353.7 54.4 %collective-permute-start.31 = (bf16[1024,896]{1,0:T(8,128)(2,1)}, bf16[1024,896]{1,0:T(8,128)(2,1)}, u32[]{:S(2)}, u32[]{:S(2)}) collective-permute-start(bf16[1024,896]{1,0:T(8,128)(2,1)} %pad_maximum_fusion.1), channel_id=1, source_target_pairs={{0,48},{16,0},{32,16},{48,32},{1,49},{17,1},{33,17},{49,33},{2,50}... | collective-permute-start | bytes 5505032 | tf_op jit(solution)/shard_map/ppermute | solution.py:32
  369.4 44.6 %all-to-all-start.5 = ((bf16[16,40,1024]{2,1,0:T(8,128)(2,1)}), bf16[16,40,1024]{2,1,0:T(8,128)(2,1)}, u32[]{:S(2)}, u32[]{:S(2)}) async-start(bf16[16,40,1024]{2,1,0:T(8,128)(2,1)} %bitcast.228), calls=%async_computation.5 | async-start | bytes 2621440 | tf_op jit(solution)/shard_map/all_to_all | solution.py:56
  379.0 17.6 %collective-permute-start.35 = (bf16[320,1024]{1,0:T(8,128)(2,1)S(1)}, bf16[320,1024]{1,0:T(8,128)(2,1)S(1)}, u32[]{:S(2)}, u32[]{:S(2)}) collective-permute-start(bf16[320,1024]{1,0:T(8,128)(2,1)S(1)} %get-tuple-element.133), channel_id=1, source_target_pairs={{0,2},{2,4},{4,6},{6,0},{1,3},{3,5},{5,7},{7,1},{8,10},{10,12},{12... | collective-permute-start | bytes 1966088 | tf_op jit(solution)/shard_map/ppermute | solution.py:36
  379.0 19.0 %collective-permute-start.36 = (bf16[320,1024]{1,0:T(8,128)(2,1)S(1)}, bf16[320,1024]{1,0:T(8,128)(2,1)S(1)}, u32[]{:S(2)}, u32[]{:S(2)}) collective-permute-start(bf16[320,1024]{1,0:T(8,128)(2,1)S(1)} %get-tuple-element.132), channel_id=1, source_target_pairs={{0,6},{2,0},{4,2},{6,4},{1,7},{3,1},{5,3},{7,5},{8,14},{10,8},{12,... | collective-permute-start | bytes 1966088 | tf_op jit(solution)/shard_map/ppermute | solution.py:40
  414.0 39.2 %all-to-all-start.4 = ((bf16[16,64,896]{2,1,0:T(8,128)(2,1)}), bf16[16,64,896]{2,1,0:T(8,128)(2,1)}, u32[]{:S(2)}, u32[]{:S(2)}) async-start(bf16[16,64,896]{2,1,0:T(8,128)(2,1)} %bitcast.223), calls=%async_computation.4 | async-start | bytes 3670016 | tf_op jit(solution)/shard_map/all_to_all | solution.py:56
  422.3 200.9 %all-gather.10.cloned.1.call-start = ((), (), s32[]{:S(2)}) async-start(), calls=%async_computation.10 | async-start | bytes 3342336 | tf_op jit(solution)/shard_map/all_gather | solution.py:573
  427.1 22.4 %collective-permute-start.37 = (bf16[512,896]{1,0:T(8,128)(2,1)}, bf16[512,896]{1,0:T(8,128)(2,1)}, u32[]{:S(2)}, u32[]{:S(2)}) collective-permute-start(bf16[512,896]{1,0:T(8,128)(2,1)} %get-tuple-element.141), channel_id=1, source_target_pairs={{0,16},{16,32},{32,48},{48,0},{1,17},{17,33},{33,49},{49,1},{2,18}... | collective-permute-start | bytes 2752520 | tf_op jit(solution)/shard_map/ppermute | solution.py:28
  427.1 24.3 %collective-permute-start.38 = (bf16[512,896]{1,0:T(8,128)(2,1)}, bf16[512,896]{1,0:T(8,128)(2,1)}, u32[]{:S(2)}, u32[]{:S(2)}) collective-permute-start(bf16[512,896]{1,0:T(8,128)(2,1)} %get-tuple-element.140), channel_id=1, source_target_pairs={{0,48},{16,0},{32,16},{48,32},{1,49},{17,1},{33,17},{49,33},{2,50}... | collective-permute-start | bytes 2752520 | tf_op jit(solution)/shard_map/ppermute | solution.py:32
  459.3 27.7 %collective-permute-start.43 = (bf16[640,1024]{1,0:T(8,128)(2,1)S(1)}, bf16[640,1024]{1,0:T(8,128)(2,1)S(1)}, u32[]{:S(2)}, u32[]{:S(2)}) collective-permute-start(bf16[640,1024]{1,0:T(8,128)(2,1)S(1)} %pad_maximum_fusion.5), channel_id=1, source_target_pairs={{0,6},{2,0},{4,2},{6,4},{1,7},{3,1},{5,3},{7,5},{8,14},{10,8},{12,... | collective-permute-start | bytes 3932168 | tf_op jit(solution)/shard_map/ppermute | solution.py:40
  461.7 28.3 %collective-permute-start.42 = (bf16[640,1024]{1,0:T(8,128)(2,1)S(1)}, bf16[640,1024]{1,0:T(8,128)(2,1)S(1)}, u32[]{:S(2)}, u32[]{:S(2)}) collective-permute-start(bf16[640,1024]{1,0:T(8,128)(2,1)S(1)} %pad_maximum_fusion.4), channel_id=1, source_target_pairs={{0,2},{2,4},{4,6},{6,0},{1,3},{3,5},{5,7},{7,1},{8,10},{10,12},{12... | collective-permute-start | bytes 3932168 | tf_op jit(solution)/shard_map/ppermute | solution.py:36
  469.6 64.0 %collective-permute-start.41 = (bf16[1024,896]{1,0:T(8,128)(2,1)}, bf16[1024,896]{1,0:T(8,128)(2,1)}, u32[]{:S(2)}, u32[]{:S(2)}) collective-permute-start(bf16[1024,896]{1,0:T(8,128)(2,1)} %pad_maximum_fusion.3), channel_id=1, source_target_pairs={{0,48},{16,0},{32,16},{48,32},{1,49},{17,1},{33,17},{49,33},{2,50}... | collective-permute-start | bytes 5505032 | tf_op jit(solution)/shard_map/ppermute | solution.py:32
  473.9 59.7 %collective-permute-start.40 = (bf16[1024,896]{1,0:T(8,128)(2,1)}, bf16[1024,896]{1,0:T(8,128)(2,1)}, u32[]{:S(2)}, u32[]{:S(2)}) collective-permute-start(bf16[1024,896]{1,0:T(8,128)(2,1)} %pad_maximum_fusion.2), channel_id=1, source_target_pairs={{0,16},{16,32},{32,48},{48,0},{1,17},{17,33},{33,49},{49,1},{2,18}... | collective-permute-start | bytes 5505032 | tf_op jit(solution)/shard_map/ppermute | solution.py:28
  492.4 45.1 %all-to-all-start.3 = ((bf16[16,40,1024]{2,1,0:T(8,128)(2,1)}), bf16[16,40,1024]{2,1,0:T(8,128)(2,1)}, u32[]{:S(2)}, u32[]{:S(2)}) async-start(bf16[16,40,1024]{2,1,0:T(8,128)(2,1)} %bitcast.229), calls=%async_computation.3 | async-start | bytes 2621440 | tf_op jit(solution)/shard_map/all_to_all | solution.py:56
  537.6 28.3 %all-to-all-start.2 = ((bf16[16,64,896]{2,1,0:T(8,128)(2,1)}), bf16[16,64,896]{2,1,0:T(8,128)(2,1)S(1)}, u32[]{:S(2)}, u32[]{:S(2)}) async-start(bf16[16,64,896]{2,1,0:T(8,128)(2,1)} %bitcast.47), calls=%async_computation.2 | async-start | bytes 3670016 | tf_op jit(solution)/shard_map/all_to_all | solution.py:56
  544.0 79.2 %all-gather.8.cloned.1.call-start = ((), (), s32[]{:S(2)}) async-start(), calls=%async_computation.9 | async-start | bytes 3342336 | tf_op jit(solution)/shard_map/all_gather | solution.py:573
  569.8 7.1 %collective-permute-start.21 = (f32[128,1024]{1,0:T(8,128)S(1)}, f32[128,1024]{1,0:T(8,128)S(1)}, u32[]{:S(2)}, u32[]{:S(2)}) collective-permute-start(f32[128,1024]{1,0:T(8,128)S(1)} %fusion.36), channel_id=1, source_target_pairs={{0,8},{8,0},{1,9},{9,1},{2,10},{10,2},{3,11},{11,3},{4,12},{12,4},... | collective-permute-start | bytes 1572872 | tf_op jit(solution)/shard_map/ppermute | solution.py:48
  596.7 10.1 %all-to-all-start.6 = ((f32[8,24,128]{2,1,0:T(8,128)}), f32[8,24,128]{2,1,0:T(8,128)S(1)}, u32[]{:S(2)}, u32[]{:S(2)}) async-start(f32[8,24,128]{2,1,0:T(8,128)} %copy.72), calls=%async_computation.6 | async-start | bytes 196608 | tf_op jit(solution)/shard_map/all_to_all | solution.py:56
  607.5 13.9 %all-to-all-start.7 = ((f32[16,24,128]{2,1,0:T(8,128)}), f32[16,24,128]{2,1,0:T(8,128)S(1)}, u32[]{:S(2)}, u32[]{:S(2)}) async-start(f32[16,24,128]{2,1,0:T(8,128)} %broadcast_in_dim.115), calls=%async_computation.7 | async-start | bytes 393216 | tf_op jit(solution)/shard_map/all_to_all | solution.py:56
  (135 other events, 855.2 us)
Sparse Core Ops, SparseCore 0:
  113.3 84.9 all-gather.5
  455.9 44.1 all-gather.9
  567.0 40.6 all-gather.7
